TPU v7x, 32 devices: a whole 2x2x4 slice. The times are simulated.
32 devices in a mesh: dp: 8 (over y, x, core), tensor: 4 (over z).
Axes of the slice: x: 2, y: 2, z: 4, core: 2. Of those that a mesh axis runs over, the one named last changes fastest.
Arguments:
- inputs: bfloat16 [32768, 768], P(('dp', 'tensor')), may hold values from -6 to 6
- cotangent: bfloat16 [32768, 768], P(('dp', 'tensor')), may hold values from -6 to 6
- w_query: bfloat16 [768, 768], P('dp', 'tensor'), may hold values from -0.21875 to 0.21875
- w_key: bfloat16 [768, 768], P('dp', 'tensor'), may hold values from -0.21875 to 0.21875
- w_value: bfloat16 [768, 768], P('dp', 'tensor'), may hold values from -0.21875 to 0.21875
- w_output: bfloat16 [768, 768], P('tensor', 'dp'), may hold values from -2.5 to 2.5
- w_up: bfloat16 [768, 3072], P('dp', 'tensor'), may hold values from -0.21875 to 0.21875
- w_down: bfloat16 [3072, 768], P('tensor', 'dp'), may hold values from -0.109375 to 0.109375
- b_query: float32 [768], P('tensor'), may hold values from -3 to 3
- b_value: float32 [768], P('tensor'), may hold values from -3 to 3
- b_output: float32 [768], replicated, may hold values from -3 to 3
- gain_attn: float32 [768], replicated, may hold values from 0.1 to 1.9
- bias_attn: float32 [768], replicated, may hold values from -3 to 3
- b_up: float32 [3072], P('tensor'), may hold values from -3 to 3
- b_down: float32 [768], replicated, may hold values from -3 to 3
- gain_mlp: float32 [768], replicated, may hold values from 0.1 to 1.9
- bias_mlp: float32 [768], replicated, may hold values from -3 to 3
- random_blocks: int32 [12, 64, 3], P('tensor'), may hold values from 1 to 62, as said below
Outputs:
- layer_out: bfloat16 [32768, 768], P(('dp', 'tensor'))
- grad_input: bfloat16 [32768, 768], P(('dp', 'tensor'))
- grad_w_query: float32 [768, 768], P('dp', 'tensor')
- grad_w_key: float32 [768, 768], P('dp', 'tensor')
- grad_w_value: float32 [768, 768], P('dp', 'tensor')
- grad_w_output: float32 [768, 768], P('tensor', 'dp')
- grad_w_up: float32 [768, 3072], P('dp', 'tensor')
- grad_w_down: float32 [3072, 768], P('tensor', 'dp')
- grad_b_query: float32 [768], P('tensor')
- grad_b_value: float32 [768], P('tensor')
- grad_b_output: float32 [768], replicated
- grad_gain_attn: float32 [768], replicated
- grad_bias_attn: float32 [768], replicated
- grad_b_up: float32 [3072], P('tensor')
- grad_b_down: float32 [768], replicated
- grad_gain_mlp: float32 [768], replicated
- grad_bias_mlp: float32 [768], replicated
Inputs may be any that keep to these rules, and one draw needn't show every extreme that they name: random_blocks[h, i] names 3 different blocks of the same sequence, none of them 0, 63, i - 1, i or i + 1.
All inputs are finite; a program needn't handle non-finite values.
Results may differ from a plain program's by a relative error of at most 0.02.
Values may be sent and summed in bfloat16 or wider, within the bound.
No kernel may reach another device: no remote copies, remote signals or barrier semaphores. Data moves between devices by JAX's collectives and lax.ppermute only.
A program may use at most 256 MiB of HBM per device.

v0:
```python
import jax
import jax.numpy as jnp
from jax import lax
from jax.sharding import PartitionSpec as P

HD = 64
BLOCK = 64
LENGTH = 4096


negative = -1e30
epsilon = 1e-05
group_blocks = 8


def build_keys(random_blocks, nblocks):
    block_index = jnp.arange(nblocks, dtype=jnp.int32)
    fixed_blocks = jnp.stack(
        [
            jnp.zeros_like(block_index),
            jnp.full_like(block_index, nblocks - 1),
            block_index - 1,
            block_index,
            block_index + 1,
        ],
        axis=-1,
    )
    fixed_blocks = jnp.clip(fixed_blocks, 0, nblocks - 1)
    always_on = jnp.ones((nblocks,), dtype=bool)
    valid_keys = jnp.stack(
        [
            always_on,
            always_on,
            (block_index - 1 >= 1) & (block_index - 1 <= nblocks - 2),
            (block_index >= 1) & (block_index <= nblocks - 2),
            block_index + 1 <= nblocks - 2,
        ]
        + [always_on] * random_blocks.shape[-1],
        axis=-1,
    )
    head_count = random_blocks.shape[0]
    key_table = jnp.concatenate(
        [jnp.broadcast_to(fixed_blocks[None], (head_count, nblocks, 5)), random_blocks], axis=-1
    )
    return (key_table, valid_keys)


def rows_to_heads(matrix, head_count):
    return matrix.reshape(-1, BLOCK, head_count, HD).transpose(2, 0, 1, 3)


def groups_to_rows(blocks):
    return blocks.transpose(0, 2, 3, 1, 4).reshape(-1, blocks.shape[1] * blocks.shape[4])


def heads_to_rows(blocks):
    return blocks.transpose(1, 2, 0, 3).reshape(-1, blocks.shape[0] * blocks.shape[3])


def dot_rows(left, right):
    return lax.dot_general(
        left, right, (((0,), (0,)), ((), ())), preferred_element_type=jnp.float32
    )


def dot_cols(left, right):
    return lax.dot_general(
        left, right, (((1,), (1,)), ((), ())), preferred_element_type=jnp.float32
    )


def layer_stats(hidden):
    center = hidden - jnp.mean(hidden, axis=-1, keepdims=True)
    scale_inv = lax.rsqrt(jnp.mean(center * center, axis=-1, keepdims=True) + epsilon)
    return (center * scale_inv, scale_inv)


def layer_back(grad_out, normal, scale_inv, gain):
    grad_norm = grad_out * gain
    return scale_inv * (
        grad_norm
        - jnp.mean(grad_norm, axis=-1, keepdims=True)
        - normal * jnp.mean(grad_norm * normal, axis=-1, keepdims=True)
    )


def gelu_slope(values):
    return (
        0.5 * (1.0 + lax.erf(values * 0.7071067811865476))
        + values * jnp.exp(-0.5 * values * values) * 0.3989422804014327
    )


def pick_blocks(selector, seq_heads):
    head_count = seq_heads.shape[0]
    flat = seq_heads.reshape(head_count, seq_heads.shape[1], BLOCK * HD)
    picked = jnp.einsum(
        "hgrn,hnx->hgrx", selector, flat, preferred_element_type=jnp.float32
    ).astype(jnp.bfloat16)
    return picked.reshape(head_count, selector.shape[1], -1, HD)


def spread_blocks(accumulator, selector, contrib):
    head_count = accumulator.shape[0]
    nblocks = selector.shape[3]
    flat = contrib.reshape(head_count, selector.shape[1], selector.shape[2], BLOCK * HD)
    added = jnp.einsum(
        "hgrn,hgrx->hnx",
        selector.astype(jnp.float32),
        flat,
        preferred_element_type=jnp.float32,
        precision=lax.Precision.HIGHEST,
    )
    updated = accumulator + added.reshape(head_count, nblocks, BLOCK, HD)
    return updated


def group_inputs(query_heads, key_heads, value_heads, seq_table, key_mask, group_id):
    nblocks = LENGTH // BLOCK
    first_block = group_id * group_blocks
    seq_start = first_block // nblocks * nblocks
    query_part = lax.dynamic_slice_in_dim(query_heads, first_block, group_blocks, 1)
    chosen = lax.dynamic_slice_in_dim(seq_table, first_block, group_blocks, 1) - seq_start
    allowed = lax.dynamic_slice_in_dim(key_mask, first_block, group_blocks, 0)
    selector = (chosen[..., None] == jnp.arange(nblocks, dtype=jnp.int32)).astype(jnp.bfloat16)
    key_part = pick_blocks(selector, key_heads)
    value_part = pick_blocks(selector, value_heads)
    return (first_block, seq_start, query_part, selector, allowed, key_part, value_part)


def attend_forward(query_heads, key_heads, value_heads, seq_table, key_mask, score_scale):
    groups = query_heads.shape[1] // group_blocks

    def one_group(group_id):
        first_block, seq_start, query_part, selector, allowed, key_part, value_part = group_inputs(
            query_heads, key_heads, value_heads, seq_table, key_mask, group_id
        )
        scores = (
            jnp.einsum("hgqd,hgkd->hgqk", query_part, key_part, preferred_element_type=jnp.float32)
            * score_scale
        )
        scores = jnp.where(allowed[None, :, None, :], scores, negative)
        row_max = jnp.max(scores, axis=-1, keepdims=True)
        expo_scores = jnp.exp(scores - row_max)
        row_total = jnp.sum(expo_scores, axis=-1, keepdims=True)
        softmax_low = (expo_scores / row_total).astype(jnp.bfloat16)
        attended = jnp.einsum(
            "hgqk,hgkd->hgqd", softmax_low, value_part, preferred_element_type=jnp.float32
        )
        return (attended, (row_max + jnp.log(row_total))[..., 0])

    return lax.map(one_group, jnp.arange(groups))


def attend_backward(
    query_heads, key_heads, value_heads, grad_heads, logsum, seq_table, key_mask, score_scale
):
    groups = query_heads.shape[1] // group_blocks
    initial = (jnp.zeros(key_heads.shape, jnp.float32), jnp.zeros(value_heads.shape, jnp.float32))

    def one_group(accumulators, group_id):
        key_acc, value_acc = accumulators
        first_block, seq_start, query_part, selector, allowed, key_part, value_part = group_inputs(
            query_heads, key_heads, value_heads, seq_table, key_mask, group_id
        )
        grad_part = lax.dynamic_slice_in_dim(grad_heads, first_block, group_blocks, 1)
        logsum_part = lax.dynamic_slice_in_dim(logsum, first_block, group_blocks, 1)
        scores = (
            jnp.einsum("hgqd,hgkd->hgqk", query_part, key_part, preferred_element_type=jnp.float32)
            * score_scale
        )
        scores = jnp.where(allowed[None, :, None, :], scores, negative)
        softmax_probs = jnp.exp(scores - logsum_part[..., None])
        softmax_low = softmax_probs.astype(jnp.bfloat16)
        grad_probs = jnp.einsum(
            "hgqd,hgkd->hgqk", grad_part, value_part, preferred_element_type=jnp.float32
        )
        grad_values = jnp.einsum(
            "hgqk,hgqd->hgkd", softmax_low, grad_part, preferred_element_type=jnp.float32
        )
        grad_scores = (
            softmax_probs
            * (grad_probs - jnp.sum(softmax_probs * grad_probs, axis=-1, keepdims=True))
        ).astype(jnp.bfloat16)
        grad_query = (
            jnp.einsum("hgqk,hgkd->hgqd", grad_scores, key_part, preferred_element_type=jnp.float32)
            * score_scale
        )
        grad_keys = (
            jnp.einsum(
                "hgqk,hgqd->hgkd", grad_scores, query_part, preferred_element_type=jnp.float32
            )
            * score_scale
        )
        key_acc = spread_blocks(key_acc, selector, grad_keys)
        value_acc = spread_blocks(value_acc, selector, grad_values)
        return ((key_acc, value_acc), grad_query)

    (key_acc, value_acc), grad_query = lax.scan(one_group, initial, jnp.arange(groups))
    return (grad_query, key_acc, value_acc)


def per_device(
    inputs,
    cotangent,
    w_query,
    w_key,
    w_value,
    w_output,
    w_up,
    w_down,
    b_query,
    b_value,
    b_output,
    gain_attn,
    bias_attn,
    b_up,
    b_down,
    gain_mlp,
    bias_mlp,
    random_blocks,
):
    model_width = inputs.shape[1]
    tensor_size = lax.axis_size("tensor")
    tensor_index = lax.axis_index("tensor")
    head_count = random_blocks.shape[0]
    nblocks = LENGTH // BLOCK
    score_scale = HD ** (-0.5)
    query_weight, key_weight, value_weight, output_weight = (
        lax.all_gather(w_query, "dp", axis=0, tiled=True),
        lax.all_gather(w_key, "dp", axis=0, tiled=True),
        lax.all_gather(w_value, "dp", axis=0, tiled=True),
        lax.all_gather(w_output, "dp", axis=1, tiled=True),
    )
    up_weight, down_weight = (
        lax.all_gather(w_up, "dp", axis=0, tiled=True),
        lax.all_gather(w_down, "dp", axis=1, tiled=True),
    )
    seq_inputs = lax.all_gather(inputs, "tensor", axis=0, tiled=True)
    sequences = seq_inputs.shape[0] // LENGTH
    query_low = (
        jnp.dot(seq_inputs, query_weight, preferred_element_type=jnp.float32) + b_query
    ).astype(jnp.bfloat16)
    key_low = jnp.dot(seq_inputs, key_weight, preferred_element_type=jnp.float32).astype(
        jnp.bfloat16
    )
    value_low = (
        jnp.dot(seq_inputs, value_weight, preferred_element_type=jnp.float32) + b_value
    ).astype(jnp.bfloat16)
    key_table, valid_keys = build_keys(random_blocks, nblocks)
    offsets = jnp.arange(sequences, dtype=jnp.int32) * nblocks
    seq_table = (key_table[:, None] + offsets[None, :, None, None]).reshape(
        head_count, sequences * nblocks, -1
    )
    key_mask = jnp.tile(jnp.repeat(valid_keys, BLOCK, axis=1), (sequences, 1))
    query_heads = rows_to_heads(query_low, head_count)
    key_heads = rows_to_heads(key_low, head_count)
    value_heads = rows_to_heads(value_low, head_count)
    attended, logsum_groups = attend_forward(
        query_heads, key_heads, value_heads, seq_table, key_mask, score_scale
    )
    mixed_low = groups_to_rows(attended).astype(jnp.bfloat16)
    logsum = logsum_groups.transpose(1, 0, 2, 3).reshape(head_count, -1, BLOCK)
    attn_own = lax.psum_scatter(
        jnp.dot(mixed_low, output_weight, preferred_element_type=jnp.float32).astype(jnp.bfloat16),
        "tensor",
        scatter_dimension=0,
        tiled=True,
    ).astype(jnp.float32)
    residual = inputs.astype(jnp.float32) + attn_own + b_output
    normal_first, scale_first = layer_stats(residual)
    normed = normal_first * gain_attn + bias_attn
    normed_own_low = normed.astype(jnp.bfloat16)
    normed_low = lax.all_gather(normed_own_low, "tensor", axis=0, tiled=True)
    hidden_pre = jnp.dot(normed_low, up_weight, preferred_element_type=jnp.float32) + b_up
    hidden_low = jax.nn.gelu(hidden_pre, approximate=False).astype(jnp.bfloat16)
    mlp_own = lax.psum_scatter(
        jnp.dot(hidden_low, down_weight, preferred_element_type=jnp.float32).astype(jnp.bfloat16),
        "tensor",
        scatter_dimension=0,
        tiled=True,
    ).astype(jnp.float32)
    second = normed + mlp_own + b_down
    normal_second, scale_second = layer_stats(second)
    layer_out = (normal_second * gain_mlp + bias_mlp).astype(jnp.bfloat16)
    grad_out = cotangent.astype(jnp.float32)
    grad_gain_mlp_part = jnp.sum(grad_out * normal_second, axis=0)
    grad_bias_mlp_part = jnp.sum(grad_out, axis=0)
    grad_second = layer_back(grad_out, normal_second, scale_second, gain_mlp)
    grad_b_down_part = jnp.sum(grad_second, axis=0)
    grad_second_low = grad_second.astype(jnp.bfloat16)
    hidden_width = b_up.shape[0]
    grad_mlp_seq = lax.all_gather(grad_second_low, "tensor", axis=0, tiled=True)
    grad_down = dot_rows(hidden_low, grad_mlp_seq)
    grad_hidden = (dot_cols(grad_mlp_seq, down_weight) * gelu_slope(hidden_pre)).astype(
        jnp.bfloat16
    )
    grad_b_up_part = jnp.sum(grad_hidden.astype(jnp.float32), axis=0)
    grad_up = dot_rows(normed_low, grad_hidden)
    grad_normed = grad_second + lax.psum_scatter(
        dot_cols(grad_hidden, up_weight).astype(jnp.bfloat16),
        "tensor",
        scatter_dimension=0,
        tiled=True,
    ).astype(jnp.float32)
    padded_up = lax.dynamic_update_slice_in_dim(
        jnp.zeros((hidden_width * tensor_size,), jnp.float32),
        grad_b_up_part,
        tensor_index * hidden_width,
        0,
    )
    grad_gain_attn_part = jnp.sum(grad_normed * normal_first, axis=0)
    grad_bias_attn_part = jnp.sum(grad_normed, axis=0)
    grad_residual = layer_back(grad_normed, normal_first, scale_first, gain_attn)
    grad_b_output_part = jnp.sum(grad_residual, axis=0)
    grad_attn_seq = lax.all_gather(grad_residual.astype(jnp.bfloat16), "tensor", axis=0, tiled=True)
    grad_output = dot_rows(mixed_low, grad_attn_seq)
    grad_mixed = dot_cols(grad_attn_seq, output_weight).astype(jnp.bfloat16)
    grad_query_groups, grad_key_heads, grad_value_heads = attend_backward(
        query_heads,
        key_heads,
        value_heads,
        rows_to_heads(grad_mixed, head_count),
        logsum,
        seq_table,
        key_mask,
        score_scale,
    )
    grad_query_low = groups_to_rows(grad_query_groups).astype(jnp.bfloat16)
    grad_key_low = heads_to_rows(grad_key_heads).astype(jnp.bfloat16)
    grad_value_low = heads_to_rows(grad_value_heads).astype(jnp.bfloat16)
    grad_b_query_part = jnp.sum(grad_query_low.astype(jnp.float32), axis=0)
    grad_b_value_part = jnp.sum(grad_value_low.astype(jnp.float32), axis=0)
    grad_query_w = dot_rows(seq_inputs, grad_query_low)
    grad_key_w = dot_rows(seq_inputs, grad_key_low)
    grad_value_w = dot_rows(seq_inputs, grad_value_low)
    grad_input = (
        grad_residual
        + lax.psum_scatter(
            (
                dot_cols(grad_query_low, query_weight)
                + dot_cols(grad_key_low, key_weight)
                + dot_cols(grad_value_low, value_weight)
            ).astype(jnp.bfloat16),
            "tensor",
            scatter_dimension=0,
            tiled=True,
        ).astype(jnp.float32)
    ).astype(jnp.bfloat16)
    shard_query, shard_key, shard_value, shard_output, shard_up, shard_down = (
        lax.psum_scatter(grad_query_w, "dp", scatter_dimension=0, tiled=True),
        lax.psum_scatter(grad_key_w, "dp", scatter_dimension=0, tiled=True),
        lax.psum_scatter(grad_value_w, "dp", scatter_dimension=0, tiled=True),
        lax.psum_scatter(grad_output, "dp", scatter_dimension=1, tiled=True),
        lax.psum_scatter(grad_up, "dp", scatter_dimension=0, tiled=True),
        lax.psum_scatter(grad_down, "dp", scatter_dimension=1, tiled=True),
    )
    local_width = grad_b_query_part.shape[0]
    zero_width = jnp.zeros((model_width,), jnp.float32)
    padded_query = lax.dynamic_update_slice_in_dim(
        zero_width, grad_b_query_part, tensor_index * local_width, 0
    )
    padded_value = lax.dynamic_update_slice_in_dim(
        zero_width, grad_b_value_part, tensor_index * local_width, 0
    )
    stacked = jnp.stack(
        [
            padded_query,
            padded_value,
            grad_b_output_part,
            grad_gain_attn_part,
            grad_bias_attn_part,
            grad_b_down_part,
            grad_gain_mlp_part,
            grad_bias_mlp_part,
        ]
    )
    summed, summed_up = lax.psum((stacked, padded_up), ("dp", "tensor"))
    grad_b_query = lax.dynamic_slice_in_dim(summed[0], tensor_index * local_width, local_width, 0)
    grad_b_value = lax.dynamic_slice_in_dim(summed[1], tensor_index * local_width, local_width, 0)
    grad_b_up = lax.dynamic_slice_in_dim(summed_up, tensor_index * hidden_width, hidden_width, 0)
    return (
        layer_out,
        grad_input,
        shard_query,
        shard_key,
        shard_value,
        shard_output,
        shard_up,
        shard_down,
        grad_b_query,
        grad_b_value,
        summed[2],
        summed[3],
        summed[4],
        grad_b_up,
        summed[5],
        summed[6],
        summed[7],
    )


def solution(mesh):
    in_specs = (
        P(("dp", "tensor"), None),
        P(("dp", "tensor"), None),
        P("dp", "tensor"),
        P("dp", "tensor"),
        P("dp", "tensor"),
        P("tensor", "dp"),
        P("dp", "tensor"),
        P("tensor", "dp"),
        P("tensor"),
        P("tensor"),
        P(),
        P(),
        P(),
        P("tensor"),
        P(),
        P(),
        P(),
        P("tensor", None, None),
    )
    out_specs = (
        P(("dp", "tensor"), None),
        P(("dp", "tensor"), None),
        P("dp", "tensor"),
        P("dp", "tensor"),
        P("dp", "tensor"),
        P("tensor", "dp"),
        P("dp", "tensor"),
        P("tensor", "dp"),
        P("tensor"),
        P("tensor"),
        P(),
        P(),
        P(),
        P("tensor"),
        P(),
        P(),
        P(),
    )
    return jax.shard_map(
        per_device, mesh=mesh, in_specs=in_specs, out_specs=out_specs, check_vma=False
    )
```

profile of v0, /device:TPU:1, one launch (start us, length us, event | category | flops | bytes accessed | tf_op | source)
XLA Modules:
  0.0 2174.2 jit_solution(7546845430186548512)
XLA Ops:
  12.3 10.9 all_gather.34
  23.3 10.5 all_gather.31
  33.8 10.4 all_gather.32
  44.2 9.6 all_gather.33
  53.9 74.3 %all-gather.7.cloned.1.call-done = bf16[4096,768]{1,0:T(8,128)(2,1)} async-done(((bf16[1024,768]{1,0:T(8,128)(2,1)}), bf16[4096,768]{1,0:T(8,128)(2,1)}) %all-gather.7.cloned.1.call-update) | async-done | bytes 6291472 | tf_op jit(solution)/shard_map/all_gather | solution.py:239
  128.1 6.1 fusion.51
  165.8 6.2 fusion.50
  185.3 165.0 %while.33 = (s32[]{:T(128)}, bf16[8,3,8,64,64]{4,3,2,1,0:T(8,128)(2,1)}, f32[8,3,8,64]{3,2,1,0:T(8,128)}, s32[8]{0:T(128)S(1)}, pred[64,512]{1,0:T(8,128)(4,1)},...) while((s32[]{:T(128)}, ...), condition=%wide.wide.region_3.4_spmd, body=%wide.wide.region_0.3_spmd.sunk | while | flops 413686464 | bytes 57882148 | solution.py:152
  364.6 108.3 %reduce-scatter.19.cloned.1.call-done = bf16[1024,768]{1,0:T(8,128)(2,1)} async-done(((bf16[4096,768]{1,0:T(8,128)(2,1)}), bf16[1024,768]{1,0:T(8,128)(2,1)}) %reduce-scatter.19.cloned.1.call-update) | async-done | bytes 1572880 | tf_op jit(solution)/shard_map/reduce_scatter | solution.py:264
  478.6 115.3 %all-gather.9.cloned.1.call-done = bf16[4096,768]{1,0:T(8,128)(2,1)} async-done(((bf16[1024,768]{1,0:T(8,128)(2,1)}), bf16[4096,768]{1,0:T(8,128)(2,1)}) %all-gather.9.cloned.1.call-update) | async-done | bytes 6291472 | tf_op jit(solution)/shard_map/all_gather | solution.py:274
  594.0 34.7 %fusion.36 = (bf16[4096,768]{1,0:T(8,128)(2,1)}, f32[4096,768]{1,0:T(8,128)}) fusion(f32[768]{0:T(1024)S(1)} %copy-done.44, bf16[4096,768]{1,0:T(8,128)(2,1)} %all-gather.9.cloned.1.call-done, bf16[768,768]{1,0:T(8,128)(2,1)} %all-gather.11.cloned.1.call-done), kind=kOutput, calls=%fused_computation.62 | convolution fusion | flops 5039456256 | bytes 26348544 | tf_op jit(solution)/shard_map/dot_general | solution.py:275
  628.6 9.2 convolution_convert_fusion.6
  637.9 108.7 %reduce-scatter.21.cloned.1.call-done = bf16[1024,768]{1,0:T(8,128)(2,1)} async-done(((bf16[4096,768]{1,0:T(8,128)(2,1)}), bf16[1024,768]{1,0:T(8,128)(2,1)}) %reduce-scatter.21.cloned.1.call-update) | async-done | bytes 1572880 | tf_op jit(solution)/shard_map/reduce_scatter | solution.py:277
  756.7 116.2 %all-gather.15.cloned.1.call-done = bf16[4096,768]{1,0:T(8,128)(2,1)} async-done(((bf16[1024,768]{1,0:T(8,128)(2,1)}), bf16[4096,768]{1,0:T(8,128)(2,1)}) %all-gather.15.cloned.1.call-update) | async-done | bytes 6291472 | tf_op jit(solution)/shard_map/all_gather | solution.py:293
  872.9 12.9 convert_reduce_fusion
  888.4 7.1 convolution_convert_fusion.5
  895.6 108.7 %reduce-scatter.23.cloned.1.call-done = bf16[1024,768]{1,0:T(8,128)(2,1)} async-done(((bf16[4096,768]{1,0:T(8,128)(2,1)}), bf16[1024,768]{1,0:T(8,128)(2,1)}) %reduce-scatter.23.cloned.1.call-update) | async-done | bytes 1572880 | tf_op jit(solution)/shard_map/reduce_scatter | solution.py:300
  1023.9 106.5 %all-gather.17.cloned.1.call-done = bf16[4096,768]{1,0:T(8,128)(2,1)} async-done(((bf16[1024,768]{1,0:T(8,128)(2,1)}), bf16[4096,768]{1,0:T(8,128)(2,1)}) %all-gather.17.cloned.1.call-update) | async-done | bytes 6291472 | tf_op jit(solution)/shard_map/all_gather | solution.py:316
  1130.5 6.2 convolution_bitcast_fusion.2
  1154.0 635.1 %while.34 = (s32[]{:T(128)}, f32[3,64,64,64]{3,2,1,0:T(8,128)}, f32[3,64,64,64]{3,2,1,0:T(8,128)}, bf16[8,3,8,64,64]{4,3,2,1,0:T(8,128)(2,1)}, s32[8]{0:T(128)S(...) while((s32[]{:T(128)}, f32[3,64,64,64]{3,2,1,0:T(8,128)}, ...), condition=%wide.wide.region_17.18_spmd.clone, body=%wide.wide.region_15.17_spmd.clone.sunk | while | flops 1925331712 | bytes 139246608 | solution.py:199
  1196.0 6.3 reshape.362
  1220.2 10.0 select_add_fusion.4
  1271.8 6.3 reshape.362
  1296.0 14.0 select_add_fusion.4
  1351.6 6.3 reshape.362
  1375.8 14.0 select_add_fusion.4
  1431.4 6.3 reshape.362
  1455.7 14.0 select_add_fusion.4
  1511.2 6.3 reshape.362
  1535.5 14.0 select_add_fusion.4
  1591.1 6.3 reshape.362
  1615.3 14.0 select_add_fusion.4
  1670.9 6.3 reshape.362
  1695.1 14.0 select_add_fusion.4
  1750.7 6.3 reshape.362
  1775.0 14.0 select_add_fusion.4
  1823.4 6.4 fusion.66
  1829.8 6.4 fusion.67
  1836.2 12.0 add_convert_fusion
  1848.3 10.3 fusion.68
  1858.7 10.1 fusion.69
  1894.7 46.7 %all-reduce = (f32[8,768]{1,0:T(8,128)S(1)}, f32[3072]{0:T(1024)S(1)}) all-reduce(f32[8,768]{1,0:T(8,128)S(1)} %stack.49, f32[3072]{0:T(1024)S(1)} %dynamic_update_slice.33), channel_id=1, replica_groups=mesh['dp'=8,'tensor'=4] {'dp','tensor'}, use_global_device_ids=true, to_apply=%region_33.34 | all-reduce | flops 9216 | bytes 73728 | tf_op jit(solution)/shard_map/psum | solution.py:378
  1945.6 12.5 reduce-scatter.25.cloned.1.call-done
  1961.0 43.7 %reduce-scatter.27.cloned.1.call-done = f32[96,768]{1,0:T(8,128)} async-done(((f32[768,768]{1,0:T(8,128)}), f32[96,768]{1,0:T(8,128)}) %reduce-scatter.27.cloned.1.call-update) | async-done | bytes 294928 | tf_op jit(solution)/shard_map/reduce_scatter | solution.py:355
  2004.7 46.5 %reduce-scatter.29.cloned.1.call-done = f32[768,96]{0,1:T(8,128)} async-done(((f32[768,768]{0,1:T(8,128)}), f32[768,96]{0,1:T(8,128)}) %reduce-scatter.29.cloned.1.call-update) | async-done | bytes 294928 | tf_op jit(solution)/shard_map/reduce_scatter | solution.py:356
  2051.2 38.3 %reduce-scatter.33.cloned.1.call-done = f32[96,192]{1,0:T(8,128)} async-done(((f32[768,192]{1,0:T(8,128)}), f32[96,192]{1,0:T(8,128)}) %reduce-scatter.33.cloned.1.call-update) | async-done | bytes 73744
  2089.5 38.6 %reduce-scatter.31.cloned.1.call-done = f32[96,192]{1,0:T(8,128)} async-done(((f32[768,192]{1,0:T(8,128)}), f32[96,192]{1,0:T(8,128)}) %reduce-scatter.31.cloned.1.call-update) | async-done | bytes 73744
  2128.1 38.7 %reduce-scatter.35.cloned.1.call-done = f32[96,192]{1,0:T(8,128)} async-done(((f32[768,192]{1,0:T(8,128)}), f32[96,192]{1,0:T(8,128)}) %reduce-scatter.35.cloned.1.call-update) | async-done | bytes 73744
  (588 shorter events, 814.8 us)
Async XLA Ops:
  8.0 36.2 %copy-start.31 = (bf16[96,192]{1,0:T(8,128)(2,1)S(1)}, bf16[96,192]{1,0:T(8,128)(2,1)}, u32[]{:S(2)}) copy-start(bf16[96,192]{1,0:T(8,128)(2,1)} %param.26) | copy-start | bytes 110596
  8.0 120.1 %copy-start.45 = (f32[192]{0:T(256)S(1)}, f32[192]{0:T(256)}, u32[]{:S(2)}) copy-start(f32[192]{0:T(256)} %param.31) | copy-start | bytes 2308
  8.0 120.1 %all-gather.7.cloned.1.call-start = ((), (), s32[]{:S(2)}) async-start(), calls=%async_computation.10 | async-start | bytes 7864320 | tf_op jit(solution)/shard_map/all_gather | solution.py:239
  8.8 464.1 %reduce-scatter.19.cloned.1.call-start = ((), (), s32[]{:S(2)}) async-start(), calls=%async_computation.11 | async-start | bytes 7864320 | tf_op jit(solution)/shard_map/reduce_scatter | solution.py:264
  23.3 334.7 %copy-start.22 = (bf16[192,768]{0,1:T(8,128)(2,1)}, bf16[192,768]{0,1:T(8,128)(2,1)S(1)}, u32[]{:S(2)}) copy-start(bf16[192,768]{0,1:T(8,128)(2,1)S(1)} %all_gather.34) | copy-start | bytes 884740
  53.8 74.3 %copy-start.25 = (bf16[768,192]{1,0:T(8,128)(2,1)}, bf16[768,192]{1,0:T(8,128)(2,1)S(1)}, u32[]{:S(2)}) copy-start(bf16[768,192]{1,0:T(8,128)(2,1)S(1)} %all_gather.33) | copy-start | bytes 884740
  363.9 109.0 %copy-start.8 = (bf16[1024,768]{1,0:T(8,128)(2,1)S(1)}, bf16[1024,768]{1,0:T(8,128)(2,1)}, u32[]{:S(2)}) copy-start(bf16[1024,768]{1,0:T(8,128)(2,1)} %param.22) | copy-start | bytes 4718596
  363.9 109.0 %copy-start.28 = (f32[768]{0:T(1024)S(1)}, f32[768]{0:T(1024)}, u32[]{:S(2)}) copy-start(f32[768]{0:T(1024)} %param.32) | copy-start | bytes 9220
  363.9 114.7 %all-gather.11.cloned.1.call-start = ((), (), s32[]{:S(2)}) async-start(), calls=%async_computation.13 | async-start | bytes 1327104 | tf_op jit(solution)/shard_map/all_gather | solution.py:236
  364.5 111.4 %copy-start.30 = (f32[768]{0:T(1024)S(1)}, f32[768]{0:T(1024)}, u32[]{:S(2)}) copy-start(f32[768]{0:T(1024)} %param.33) | copy-start | bytes 9220
  364.5 111.4 %copy-start.36 = (f32[768]{0:T(1024)S(1)}, f32[768]{0:T(1024)}, u32[]{:S(2)}) copy-start(f32[768]{0:T(1024)} %param.34) | copy-start | bytes 9220
  364.5 229.4 %all-gather.9.cloned.1.call-start = ((), (), s32[]{:S(2)}) async-start(), calls=%async_computation.12 | async-start | bytes 7864320 | tf_op jit(solution)/shard_map/all_gather | solution.py:274
  475.9 118.1 %copy-start.44 = (f32[768]{0:T(1024)S(1)}, f32[768]{0:T(1024)}, u32[]{:S(2)}) copy-start(f32[768]{0:T(1024)} %param.35) | copy-start | bytes 9220
  478.0 150.7 %all-gather.13.cloned.1.call-start = ((), (), s32[]{:S(2)}) async-start(), calls=%async_computation.14 | async-start | bytes 1327104 | tf_op jit(solution)/shard_map/all_gather | solution.py:237
  478.5 268.0 %reduce-scatter.21.cloned.1.call-start = ((), (), s32[]{:S(2)}) async-start(), calls=%async_computation.15 | async-start | bytes 7864320 | tf_op jit(solution)/shard_map/reduce_scatter | solution.py:277
  637.8 108.8 %copy-start.40 = (f32[768]{0:T(1024)S(1)}, f32[768]{0:T(1024)}, u32[]{:S(2)}) copy-start(f32[768]{0:T(1024)} %param.36) | copy-start | bytes 9220
  637.9 235.1 %all-gather.15.cloned.1.call-start = ((), (), s32[]{:S(2)}) async-start(), calls=%async_computation.16 | async-start | bytes 7864320 | tf_op jit(solution)/shard_map/all_gather | solution.py:293
  756.7 247.6 %reduce-scatter.23.cloned.1.call-start = ((), (), s32[]{:S(2)}) async-start(), calls=%async_computation.17 | async-start | bytes 7864320 | tf_op jit(solution)/shard_map/reduce_scatter | solution.py:300
  872.9 15.5 copy-start.43
  895.6 234.9 %all-gather.17.cloned.1.call-start = ((), (), s32[]{:S(2)}) async-start(), calls=%async_computation.18 | async-start | bytes 7864320 | tf_op jit(solution)/shard_map/all_gather | solution.py:316
  1014.2 929.7 %reduce-scatter.37.cloned.1.call-start = ((), (), s32[]{:S(2)}) async-start(), calls=%async_computation.25 | async-start | bytes 884736
  1018.8 111.7 %copy-start.15 = (bf16[4096,192]{0,1:T(8,128)(2,1)S(1)}, bf16[4096,192]{0,1:T(8,128)(2,1)}, u32[]{:S(2)}) copy-start(bf16[4096,192]{0,1:T(8,128)(2,1)} %convert_element_type.168) | copy-start | bytes 4718596
  1023.9 112.8 %copy-start.23 = (bf16[192,768]{0,1:T(8,128)(2,1)S(1)}, bf16[192,768]{0,1:T(8,128)(2,1)}, u32[]{:S(2)}) copy-start(bf16[192,768]{0,1:T(8,128)(2,1)} %copy-done.22) | copy-start | bytes 884740
  1136.7 821.4 %reduce-scatter.25.cloned.1.call-start = ((), (), s32[]{:S(2)}) async-start(), calls=%async_computation.19 | async-start | bytes 7864320 | tf_op jit(solution)/shard_map/reduce_scatter | solution.py:339
  1220.2 10.0 copy-start.2
  1296.0 14.0 copy-start.2
  1375.8 14.0 copy-start.2
  1455.7 14.0 copy-start.2
  1535.5 14.0 copy-start.2
  1615.3 14.0 copy-start.2
  1695.1 14.0 copy-start.2
  1775.0 14.0 copy-start.2
  1823.3 6.5 copy-start.17
  1823.3 6.5 copy-start.24
  1848.3 156.4 %reduce-scatter.27.cloned.1.call-start = ((), (), s32[]{:S(2)}) async-start(), calls=%async_computation.20 | async-start | bytes 2654208 | tf_op jit(solution)/shard_map/reduce_scatter | solution.py:355
  1858.6 192.6 %reduce-scatter.29.cloned.1.call-start = ((), (), s32[]{:S(2)}) async-start(), calls=%async_computation.21 | async-start | bytes 2654208 | tf_op jit(solution)/shard_map/reduce_scatter | solution.py:356
  1868.8 220.7 %reduce-scatter.33.cloned.1.call-start = ((), (), s32[]{:S(2)}) async-start(), calls=%async_computation.23 | async-start | bytes 884736
  1876.1 7.6 copy-start.39
  1876.1 7.6 copy-start.38
  1876.1 7.6 copy-start.42
  1876.1 7.9 copy-start.34
  1876.1 7.9 copy-start.33
  1876.2 7.9 copy-start.32
  1876.2 7.9 copy-start.35
  1876.2 7.9 copy-start.19
  1876.2 251.9 %reduce-scatter.31.cloned.1.call-start = ((), (), s32[]{:S(2)}) async-start(), calls=%async_computation.22 | async-start | bytes 884736
  1883.6 283.2 %reduce-scatter.35.cloned.1.call-start = ((), (), s32[]{:S(2)}) async-start(), calls=%async_computation.24 | async-start | bytes 884736
  1889.1 68.9 %copy-start.12 = (f32[1024,768]{1,0:T(8,128)S(1)}, f32[1024,768]{1,0:T(8,128)}, u32[]{:S(2)}) copy-start(f32[1024,768]{1,0:T(8,128)} %copy-done.11) | copy-start | bytes 9437188
  (72 other events, 258.6 us)
Sparse Core Ops, SparseCore 0:
  10.4 117.6 all-gather.6
  364.0 108.8 reduce-scatter.18
  756.8 116.1 all-gather.14
  1014.3 116.1 all-gather.16
Sparse Core Ops, SparseCore 1:
  366.3 22.3 all-gather.10
  478.1 115.9 all-gather.8
  595.7 22.3 all-gather.12
  637.9 108.6 reduce-scatter.20
  895.6 108.6 reduce-scatter.22
  1136.8 32.4 reduce-scatter.36
  1848.3 109.7 reduce-scatter.24
  1961.9 42.8 reduce-scatter.26
  2008.9 42.3 reduce-scatter.28
  2055.0 34.5 reduce-scatter.32
  2093.1 34.9 reduce-scatter.30
  2131.8 34.9 reduce-scatter.34
where the time goes:
time: 2190 us; the launch traced here: 2170 us
  waiting for transfers between devices  958 us (44%)
  local copies, waits for them, and re-layouts  501 us (23%)
  matrix products  426 us (19%)
  other arithmetic  171 us (8%)
  blocking collectives  88.2 us (4%)
    reshape x32, local copies, waits for them, and re-layouts, pick_blocks(): return picked.reshape(head_count, selector.shape[1], -1, HD)  148 us
    unnamed x20, waiting for transfers between devices  118 us
    all_gather x1, waiting for transfers between devices, per_device(): grad_mlp_seq = lax.all_gather(grad_second_low, 'tensor', axis=0, tiled=True)  116 us
    all_gather x1, waiting for transfers between devices, per_device(): normed_low = lax.all_gather(normed_own_low, 'tensor', axis=0, tiled=True)  115 us
    reduce_scatter x1, waiting for transfers between devices, per_device(): lax.psum_scatter(jnp.dot(hidden_low, down_weight, preferred_element_type=...  109 us
    reduce_scatter x1, waiting for transfers between devices, per_device(): lax.psum_scatter(dot_cols(grad_hidden, up_weight).astype(jnp.bfloat16), '...  109 us
    reduce_scatter x1, waiting for transfers between devices, per_device(): lax.psum_scatter(jnp.dot(mixed_low, output_weight, preferred_element_type...  108 us
    add x8, other arithmetic, spread_blocks(): updated = accumulator + added.reshape(head_count, nblocks, BLOCK, HD)  108 us
  transfers between devices with their start and end apart: 16, of which 13 were waited for; matrix products, arithmetic and copies ran while one was open for 37% of the time, Pallas kernels for 0%

commit v1 on v0

v1 whole, which is shorter than its diff:
```python
import functools

import jax
import jax.numpy as jnp
from jax import lax
from jax.experimental import pallas as pl
from jax.experimental.pallas import tpu as pltpu
from jax.sharding import PartitionSpec as P

HD = 64
BLOCK = 64
LENGTH = 4096
NB = LENGTH // BLOCK
GROUP = 4
QROWS = LENGTH // GROUP
QB = QROWS // BLOCK
HEADS = 3
KEYS = 8 * BLOCK
KV = 128 * HEADS
QKV = KV + 256

negative = -1e30
epsilon = 1e-05
both = ("dp", "tensor")
flipped = ("tensor", "dp")
vmem_limit = 56 * 1024 * 1024


def dot_nn(left, right):
    return jnp.dot(left, right, preferred_element_type=jnp.float32)


def dot_tn(left, right):
    return lax.dot_general(
        left, right, (((0,), (0,)), ((), ())), preferred_element_type=jnp.float32
    )


def dot_nt(left, right):
    return lax.dot_general(
        left, right, (((1,), (1,)), ((), ())), preferred_element_type=jnp.float32
    )


def lane_masks(dtype):
    lane = lax.broadcasted_iota(jnp.int32, (1, 128), 1)
    low = (lane < 64).astype(jnp.float32).astype(dtype)
    high = (lane >= 64).astype(jnp.float32).astype(dtype)
    return low, high


def key_bias(block):
    lane = lax.broadcasted_iota(jnp.int32, (1, KEYS), 1)
    entry = lane // BLOCK
    key = jnp.where(entry == 2, block - 1, jnp.where(entry == 3, block, block + 1))
    window = (entry >= 2) & (entry <= 4)
    off = window & ((key < 1) | (key > NB - 2))
    return jnp.where(off, negative, 0.0).astype(jnp.float32)


def gather_keys(table, source, head, block):
    rows = []
    for entry in range(8):
        place = table[(head * NB + block) * 8 + entry]
        rows.append(source[pl.ds(pl.multiple_of(place * BLOCK, BLOCK), BLOCK), head * 128 : head * 128 + 128])
    return jnp.concatenate(rows, axis=0)


def head_queries(first, second, low, high):
    return (first * high, first * low, second)


def forward_kernel(steps, table, place, q_first, q_second, kv0, kv1, kv2, kv3, _, o_ref, p_ref, kv_scr, sems):
    step = pl.program_id(0)

    @pl.when(step == 0)
    def _load():
        copies = [
            pltpu.make_async_copy(
                src.at[:, pl.ds(0, KV)], kv_scr.at[pl.ds(n * QROWS, QROWS)], sems.at[n]
            )
            for n, src in enumerate((kv0, kv1, kv2, kv3))
        ]
        for copy in copies:
            copy.start()
        for copy in copies:
            copy.wait()

    low, high = lane_masks(jnp.bfloat16)
    lane = lax.broadcasted_iota(jnp.int32, (1, 128), 1)
    per = QB // steps
    for sub in range(per):
        local = place[0] * QB + step * per + sub
        bias = key_bias(local ^ (place[1] * QB))
        rows = slice(sub * BLOCK, (sub + 1) * BLOCK)
        queries = head_queries(q_first[rows], q_second[rows], low, high)
        outs = []
        for head in range(HEADS):
            keys = gather_keys(table, kv_scr, head, local)
            scores = dot_nt(queries[head], keys) + bias
            expo = jnp.exp(scores - jnp.max(scores, axis=1, keepdims=True))
            inverse = 1.0 / jnp.sum(expo, axis=1, keepdims=True)
            probs = (expo * inverse).astype(jnp.bfloat16)
            p_ref[sub, head] = probs
            outs.append(dot_nn(probs, keys))
        o_ref[rows, 0:128] = jnp.where(lane < 64, outs[0], outs[1]).astype(jnp.bfloat16)
        o_ref[rows, 128:192] = outs[2][:, 0:64].astype(jnp.bfloat16)


def attend_forward(slot, table, place, qkv, probs):
    steps = 4
    per = QB // steps
    any_spec = pl.BlockSpec(memory_space=pl.ANY)
    p_shape = jax.ShapeDtypeStruct((NB, HEADS, BLOCK, KEYS), jnp.bfloat16)
    operands = [table, place, qkv[slot], qkv[slot], *qkv]
    alias = {}
    kernel = functools.partial(forward_kernel, steps)
    if probs is None:
        probs = jnp.zeros((8, 128), jnp.bfloat16)
    else:
        alias = {8: 1}
    operands.append(probs)
    return pl.pallas_call(
        kernel,
        grid_spec=pltpu.PrefetchScalarGridSpec(
            num_scalar_prefetch=2,
            grid=(steps,),
            in_specs=[
                pl.BlockSpec((per * BLOCK, 128), lambda g, *_: (g, 3)),
                pl.BlockSpec((per * BLOCK, 128), lambda g, *_: (g, 4)),
                any_spec,
                any_spec,
                any_spec,
                any_spec,
                any_spec,
            ],
            out_specs=[
                pl.BlockSpec((per * BLOCK, 192), lambda g, *_: (g, 0)),
                pl.BlockSpec(
                    (per, HEADS, BLOCK, KEYS), lambda g, t, pos: (pos[0] * steps + g, 0, 0, 0)
                ),
            ],
            scratch_shapes=[
                pltpu.VMEM((LENGTH, KV), jnp.bfloat16),
                pltpu.SemaphoreType.DMA((4,)),
            ],
        ),
        out_shape=[jax.ShapeDtypeStruct((QROWS, 192), jnp.bfloat16), p_shape],
        input_output_aliases=alias,
        compiler_params=pltpu.CompilerParams(
            dimension_semantics=("arbitrary",), vmem_limit_bytes=vmem_limit
        ),
        name="attend_forward",
    )(*operands)


def backward_kernel(
    steps, table, p_ref, qkv0, qkv1, qkv2, qkv3, do0, do1, do2, do3, out_ref, qkv_scr, do_scr, acc, sems
):
    step = pl.program_id(0)

    @pl.when(step == 0)
    def _load():
        copies = [
            pltpu.make_async_copy(src, qkv_scr.at[pl.ds(n * QROWS, QROWS)], sems.at[n])
            for n, src in enumerate((qkv0, qkv1, qkv2, qkv3))
        ] + [
            pltpu.make_async_copy(src, do_scr.at[pl.ds(n * QROWS, QROWS)], sems.at[4 + n])
            for n, src in enumerate((do0, do1, do2, do3))
        ]
        for copy in copies:
            copy.start()
        acc[...] = jnp.zeros_like(acc)
        for copy in copies:
            copy.wait()

    low, high = lane_masks(jnp.bfloat16)
    lane = lax.broadcasted_iota(jnp.int32, (1, 128), 1)
    per = NB // steps
    for sub in range(per):
        local = step * per + sub
        rows = pl.ds(pl.multiple_of(local * BLOCK, BLOCK), BLOCK)
        queries = head_queries(
            qkv_scr[rows, KV : KV + 128], qkv_scr[rows, KV + 128 : KV + 256], low, high
        )
        g_first = do_scr[rows, 0:128]
        g_second = do_scr[rows, 128:192]
        grads = (
            g_first * low,
            g_first * high,
            jnp.concatenate([g_second, jnp.zeros_like(g_second)], axis=1),
        )
        backs = []
        for head in range(HEADS):
            keys = gather_keys(table, qkv_scr, head, local)
            probs = p_ref[sub, head]
            wide = probs.astype(jnp.float32)
            weighted = wide * dot_nt(grads[head], keys)
            total = jnp.sum(weighted, axis=1, keepdims=True)
            slopes = (weighted - wide * total).astype(jnp.bfloat16)
            backs.append(dot_nn(slopes, keys) * 0.125)
            stack = jnp.concatenate([slopes, probs], axis=0)
            right = jnp.concatenate([queries[head], grads[head]], axis=0)
            spread = dot_tn(stack, right)
            for entry in range(8):
                spot = table[(head * NB + local) * 8 + entry]
                where = pl.ds(pl.multiple_of(spot * BLOCK, BLOCK), BLOCK)
                acc[where, head * 128 : head * 128 + 128] += spread[
                    entry * BLOCK : (entry + 1) * BLOCK
                ]
        out_ref[rows, KV : KV + 128] = jnp.where(lane < 64, backs[1], backs[0]).astype(jnp.bfloat16)
        out_ref[rows, KV + 128 : KV + 256] = jnp.where(lane < 64, 0.0, backs[2]).astype(
            jnp.bfloat16
        )

    @pl.when(step == steps - 1)
    def _store():
        out_ref[:, 0:KV] = acc[...].astype(jnp.bfloat16)


def attend_backward(table, probs, qkv, grads):
    steps = 16
    per = NB // steps
    any_spec = pl.BlockSpec(memory_space=pl.ANY)
    return pl.pallas_call(
        functools.partial(backward_kernel, steps),
        grid_spec=pltpu.PrefetchScalarGridSpec(
            num_scalar_prefetch=1,
            grid=(steps,),
            in_specs=[pl.BlockSpec((per, HEADS, BLOCK, KEYS), lambda g, *_: (g, 0, 0, 0))]
            + [any_spec] * 8,
            out_specs=pl.BlockSpec((LENGTH, QKV), lambda g, *_: (0, 0)),
            scratch_shapes=[
                pltpu.VMEM((LENGTH, QKV), jnp.bfloat16),
                pltpu.VMEM((LENGTH, 192), jnp.bfloat16),
                pltpu.VMEM((LENGTH, KV), jnp.float32),
                pltpu.SemaphoreType.DMA((8,)),
            ],
        ),
        out_shape=jax.ShapeDtypeStruct((LENGTH, QKV), jnp.bfloat16),
        compiler_params=pltpu.CompilerParams(
            dimension_semantics=("arbitrary",), vmem_limit_bytes=vmem_limit
        ),
        name="attend_backward",
    )(table, probs, *qkv, *grads)


def pack_columns(query, key, value, axis):
    def piece(matrix, head):
        return lax.slice_in_dim(matrix, head * HD, (head + 1) * HD, axis=axis)

    return jnp.concatenate(
        [
            piece(value, 0),
            piece(key, 0),
            piece(key, 1),
            piece(value, 1),
            piece(value, 2),
            piece(key, 2),
            piece(query, 1),
            piece(query, 0),
            piece(query, 2),
        ],
        axis=axis,
    )


def insert_zero(packed, axis):
    head = lax.slice_in_dim(packed, 0, KV + 128, axis=axis)
    tail = lax.slice_in_dim(packed, KV + 128, KV + 192, axis=axis)
    return jnp.concatenate([head, jnp.zeros_like(tail), tail], axis=axis)


def drop_zero(packed, axis):
    head = lax.slice_in_dim(packed, 0, KV + 128, axis=axis)
    tail = lax.slice_in_dim(packed, KV + 192, KV + 256, axis=axis)
    return jnp.concatenate([head, tail], axis=axis)


def unpack_columns(packed, axis):
    def piece(n):
        return lax.slice_in_dim(packed, n * HD, (n + 1) * HD, axis=axis)

    query = jnp.concatenate([piece(7), piece(6), piece(8)], axis=axis)
    key = jnp.concatenate([piece(1), piece(2), piece(5)], axis=axis)
    value = jnp.concatenate([piece(0), piece(3), piece(4)], axis=axis)
    return query, key, value


def layer_stats(hidden):
    center = hidden - jnp.mean(hidden, axis=-1, keepdims=True)
    scale_inv = lax.rsqrt(jnp.mean(center * center, axis=-1, keepdims=True) + epsilon)
    return (center * scale_inv, scale_inv)


def layer_back(grad_out, normal, scale_inv, gain):
    grad_norm = grad_out * gain
    return scale_inv * (
        grad_norm
        - jnp.mean(grad_norm, axis=-1, keepdims=True)
        - normal * jnp.mean(grad_norm * normal, axis=-1, keepdims=True)
    )


def per_device(
    dp_size,
    tensor_size,
    inputs,
    cotangent,
    w_query,
    w_key,
    w_value,
    w_output,
    w_up,
    w_down,
    b_query,
    b_value,
    b_output,
    gain_attn,
    bias_attn,
    b_up,
    b_down,
    gain_mlp,
    bias_mlp,
    random_blocks,
):
    width = inputs.shape[1]
    dp_index = lax.axis_index("dp")
    tensor_index = lax.axis_index("tensor")
    core = dp_index % 2
    rank = 2 * core + tensor_index % 2
    devices = [(d, t) for d in range(dp_size) for t in range(tensor_size)]

    def flat(d, t):
        return d * tensor_size + t

    def stays(d, t):
        return d % 2 == t // 2

    move_pairs = [
        (flat(d, t), flat(d, t) if stays(d, t) else flat(d ^ 1, t ^ 2)) for d, t in devices
    ]
    stay_pairs = [(flat(d, t), flat(d, t ^ 1)) for d, t in devices if stays(d, t)]
    moved_pairs = [(flat(d, t), flat(d, t ^ 1)) for d, t in devices if not stays(d, t)]
    peer_pairs = {
        1: [(flat(d, t), flat(d, t ^ 1)) for d, t in devices],
        2: [(flat(d, t), flat(d ^ 1, t)) for d, t in devices],
        3: [(flat(d, t), flat(d ^ 1, t ^ 1)) for d, t in devices],
    }
    here = core == tensor_index // 2

    packed = pack_columns(w_query, w_key, w_value, 1)
    qkv_all = lax.all_gather(packed, flipped, axis=0, tiled=True).reshape(GROUP, width, 3 * 192)
    rest = jnp.concatenate([w_up, w_down.T, w_output.T], axis=1)
    rest_all = lax.all_gather(rest, flipped, axis=0, tiled=True).reshape(GROUP, width, -1)
    small = jnp.concatenate(
        [b_query, b_value, b_up, random_blocks.astype(jnp.float32).reshape(-1)]
    )
    small_all = lax.all_gather(small, "tensor", axis=0)
    b_up_all = small_all[:, 384 : 384 + b_up.shape[0]].reshape(-1)
    mine = lax.dynamic_index_in_dim(small_all, rank, 0, keepdims=False)
    my_random = mine[384 + b_up.shape[0] :].reshape(HEADS, NB, -1).astype(jnp.int32)

    own = lax.ppermute(inputs, both, move_pairs)
    near_stay = lax.ppermute(inputs, both, stay_pairs)
    near_move = lax.ppermute(own, both, moved_pairs)
    near = jnp.where(here, near_stay, near_move)
    side = lax.ppermute(own, both, peer_pairs[2])
    far = lax.ppermute(near, both, peer_pairs[2])
    rows = (own, near, side, far)
    grad_top = lax.ppermute(cotangent, both, move_pairs)

    w_qkv = insert_zero(lax.dynamic_index_in_dim(qkv_all, rank, 0, keepdims=False), 1)
    b_key = jnp.zeros_like(b_query)
    b_qkv = insert_zero(pack_columns(mine[:192], b_key, mine[192:384], 0), 0)
    scale = jnp.concatenate([jnp.ones((KV,), jnp.float32), jnp.full((256,), 0.125, jnp.float32)])
    qkv = [((dot_nn(part, w_qkv) + b_qkv) * scale).astype(jnp.bfloat16) for part in rows]

    block = jnp.arange(NB, dtype=jnp.int32)
    block = block ^ (rank * QB)
    fixed = jnp.clip(
        jnp.stack(
            [
                jnp.zeros_like(block),
                jnp.full_like(block, NB - 1),
                block - 1,
                block,
                block + 1,
            ],
            axis=-1,
        ),
        0,
        NB - 1,
    )
    local_random = jnp.take(my_random, block, axis=1)
    table = jnp.concatenate(
        [jnp.broadcast_to(fixed[None], (HEADS, NB, 5)), local_random], axis=-1
    )
    table = (table ^ (rank * QB)).reshape(-1)

    probs = None
    outs = [None] * 4
    for slot in (1, 3, 2, 0):
        place = jnp.stack([jnp.int32(slot), rank.astype(jnp.int32)])
        outs[slot], probs = attend_forward(slot, table, place, qkv, probs)
    mixed = jnp.concatenate(
        [outs[0]] + [lax.ppermute(outs[n], both, peer_pairs[n]) for n in (1, 2, 3)], axis=1
    )

    hidden_width = b_up.shape[0]
    up_all = rest_all[:, :, :hidden_width].transpose(1, 0, 2).reshape(width, -1)
    down_all = rest_all[:, :, hidden_width : 2 * hidden_width].transpose(1, 0, 2).reshape(width, -1)
    out_parts = rest_all[:, :, 2 * hidden_width :]
    out_all = jnp.concatenate(
        [
            lax.dynamic_index_in_dim(out_parts, rank ^ n, 0, keepdims=False)
            for n in range(GROUP)
        ],
        axis=1,
    )
    residual = own.astype(jnp.float32) + dot_nt(mixed, out_all) + b_output
    normal_first, scale_first = layer_stats(residual)
    normed = normal_first * gain_attn + bias_attn
    normed_low = normed.astype(jnp.bfloat16)
    hidden_pre = dot_nn(normed_low, up_all) + b_up_all
    cdf = 0.5 * (1.0 + lax.erf(hidden_pre * 0.7071067811865476))
    hidden_low = (hidden_pre * cdf).astype(jnp.bfloat16)
    slope = cdf + hidden_pre * jnp.exp(-0.5 * hidden_pre * hidden_pre) * 0.3989422804014327
    second = normed + dot_nt(hidden_low, down_all) + b_down
    normal_second, scale_second = layer_stats(second)
    layer_out = (normal_second * gain_mlp + bias_mlp).astype(jnp.bfloat16)
    grad_out = grad_top.astype(jnp.float32)
    grad_second = layer_back(grad_out, normal_second, scale_second, gain_mlp)
    grad_second_low = grad_second.astype(jnp.bfloat16)
    grad_hidden = (dot_nn(grad_second_low, down_all) * slope).astype(jnp.bfloat16)
    grad_normed = grad_second + dot_nt(grad_hidden, up_all)
    grad_residual = layer_back(grad_normed, normal_first, scale_first, gain_attn)
    grad_residual_low = grad_residual.astype(jnp.bfloat16)
    grad_mixed = dot_nn(grad_residual_low, out_all).astype(jnp.bfloat16)

    layer_out = lax.ppermute(layer_out, both, move_pairs)
    grad_parts = [grad_mixed[:, n * 192 : (n + 1) * 192] for n in range(GROUP)]
    grads = [grad_parts[0]] + [
        lax.ppermute(grad_parts[n], both, peer_pairs[n]) for n in (1, 2, 3)
    ]

    grad_down = dot_tn(grad_second_low, hidden_low).astype(jnp.bfloat16)
    grad_up = dot_tn(normed_low, grad_hidden).astype(jnp.bfloat16)
    grad_output = dot_tn(grad_residual_low, mixed).astype(jnp.bfloat16)
    grad_output = grad_output.reshape(width, GROUP, -1)
    rest_grad = jnp.concatenate(
        [
            grad_up.reshape(width, GROUP, -1).transpose(1, 0, 2),
            grad_down.reshape(width, GROUP, -1).transpose(1, 0, 2),
            jnp.stack(
                [
                    lax.dynamic_index_in_dim(grad_output, rank ^ n, 1, keepdims=False)
                    for n in range(GROUP)
                ]
            ),
        ],
        axis=2,
    )
    rest_sum = lax.psum_scatter(
        rest_grad.reshape(GROUP * width, -1), flipped, scatter_dimension=0, tiled=True
    ).astype(jnp.float32)
    shard_up = rest_sum[:, :hidden_width]
    shard_down = rest_sum[:, hidden_width : 2 * hidden_width].T
    shard_output = rest_sum[:, 2 * hidden_width :].T
    vectors = jnp.concatenate(
        [
            jnp.sum(grad_residual, axis=0),
            jnp.sum(grad_normed * normal_first, axis=0),
            jnp.sum(grad_normed, axis=0),
            jnp.sum(grad_second, axis=0),
            jnp.sum(grad_out * normal_second, axis=0),
            jnp.sum(grad_out, axis=0),
            jnp.sum(grad_hidden.astype(jnp.float32), axis=0),
        ]
    )
    vectors = lax.psum(vectors, both)

    grad_qkv = attend_backward(table, probs, qkv, grads)
    partial = [
        dot_nt(grad_qkv[n * QROWS : (n + 1) * QROWS], w_qkv8(w_qkv)) for n in range(GROUP)
    ]
    from_side = [
        lax.ppermute(partial[n].astype(jnp.bfloat16), both, peer_pairs[2]) for n in (2, 3)
    ]
    to_near = (partial[1] + from_side[1].astype(jnp.float32)).astype(jnp.bfloat16)
    from_near = lax.ppermute(to_near, both, peer_pairs[1])
    grad_own = (
        grad_residual
        + partial[0]
        + from_side[0].astype(jnp.float32)
        + from_near.astype(jnp.float32)
    ).astype(jnp.bfloat16)
    grad_input = lax.ppermute(grad_own, both, move_pairs)

    all_rows = jnp.concatenate(rows, axis=0)
    grad_w = drop_zero(dot_tn(all_rows, grad_qkv), 1).astype(jnp.bfloat16)
    groups = jnp.arange(GROUP, dtype=jnp.int32)[:, None, None]
    spread_w = jnp.where(groups == rank, grad_w[None], jnp.zeros((), jnp.bfloat16))
    shard_qkv = lax.psum_scatter(
        spread_w.reshape(GROUP * width, -1), flipped, scatter_dimension=0, tiled=True
    ).astype(jnp.float32)
    shard_query, shard_key, shard_value = unpack_columns(shard_qkv, 1)
    shard_query = shard_query
    bias_sum = drop_zero(jnp.sum(grad_qkv.astype(jnp.float32), axis=0), 0)
    bias_query, _, bias_value = unpack_columns(bias_sum, 0)
    bias_pair = jnp.concatenate([bias_query, bias_value])
    bias_pair = lax.psum(
        jnp.where(groups[:, :, 0] == rank, bias_pair[None], 0.0), both
    )
    bias_pair = lax.dynamic_index_in_dim(bias_pair, tensor_index, 0, keepdims=False)
    grad_b_up = lax.dynamic_slice_in_dim(
        vectors[6 * width :], tensor_index * hidden_width, hidden_width, 0
    )
    return (
        layer_out,
        grad_input,
        shard_query,
        shard_key,
        shard_value,
        shard_output,
        shard_up,
        shard_down,
        bias_pair[:192],
        bias_pair[192:],
        vectors[0:width],
        vectors[width : 2 * width],
        vectors[2 * width : 3 * width],
        grad_b_up,
        vectors[3 * width : 4 * width],
        vectors[4 * width : 5 * width],
        vectors[5 * width : 6 * width],
    )


def w_qkv8(w_qkv):
    return w_qkv


def solution(mesh):
    in_specs = (
        P(("dp", "tensor"), None),
        P(("dp", "tensor"), None),
        P("dp", "tensor"),
        P("dp", "tensor"),
        P("dp", "tensor"),
        P("tensor", "dp"),
        P("dp", "tensor"),
        P("tensor", "dp"),
        P("tensor"),
        P("tensor"),
        P(),
        P(),
        P(),
        P("tensor"),
        P(),
        P(),
        P(),
        P("tensor", None, None),
    )
    out_specs = (
        P(("dp", "tensor"), None),
        P(("dp", "tensor"), None),
        P("dp", "tensor"),
        P("dp", "tensor"),
        P("dp", "tensor"),
        P("tensor", "dp"),
        P("dp", "tensor"),
        P("tensor", "dp"),
        P("tensor"),
        P("tensor"),
        P(),
        P(),
        P(),
        P("tensor"),
        P(),
        P(),
        P(),
    )
    body = functools.partial(per_device, mesh.shape["dp"], mesh.shape["tensor"])
    return jax.shard_map(body, mesh=mesh, in_specs=in_specs, out_specs=out_specs, check_vma=False)
```

time: 2190 us -> 723 us (0.33)
  waiting for transfers between devices: 958 us -> 163 us
  local copies, waits for them, and re-layouts: 501 us -> 86.9 us
  matrix products: 426 us -> 111 us
  Pallas kernels: 0 us -> 152 us
  other arithmetic: 171 us -> 33.9 us
  blocking collectives: 88.2 us -> 121 us
  starting transfers between devices: 0.68 us -> 30.1 us
    all_gather x6 -> x2, waiting for transfers between devices: 412 us -> 0.02 us  [the longest x1 0.02 us: per_device(): lax.all_gather(rest, flipped, axis=0, tiled=True).reshape(GROUP, width, -1)]
    reduce_scatter x6 -> x2, waiting for transfers between devices: 428 us -> 48.6 us  [the longest x1 48.6 us: per_device(): lax.psum_scatter(rest_grad.reshape(GROUP * width, -1), flipped, scatter_d...]
    reshape x77 -> x3, local copies, waits for them, and re-layouts: 374 us -> 19.9 us  [the longest x1 9.87 us: per_device(): grad_up.reshape(width, GROUP, -1).transpose(1, 0, 2)]
    dot_general x121 -> x18, matrix products: 420 us -> 111 us  [the longest x7 42.3 us: dot_nn(): return jnp.dot(left, right, preferred_element_type=jnp.float32)]
    pallas_call x0 -> x5, Pallas kernels: none -> 152 us  [the longest x4 85.9 us: attend_forward(): pl.pallas_call(kernel, grid_spec=pltpu.PrefetchScalarGridSpec(num_scalar_...]
    unnamed x20 -> x4, waiting for transfers between devices: 118 us -> 0.07 us
    ppermute x0 -> x17, waiting for transfers between devices: none -> 114 us  [the longest x1 49.3 us: per_device(): from_near = lax.ppermute(to_near, both, peer_pairs[1])]
    add x9 -> x0, other arithmetic: 108 us -> none  [the longest x8 108 us: spread_blocks(): updated = accumulator + added.reshape(head_count, nblocks, BLOCK, HD)]
  transfers between devices with their start and end apart: 16 -> 21, of which waited for: 13 -> 5; matrix products, arithmetic and copies ran while one was open for 37% -> 24% of each run, Pallas kernels for 0% -> 12%
where the time goes in v1:
time: 723 us; the launch traced here: 714 us
  waiting for transfers between devices  163 us (23%)
  Pallas kernels  152 us (21%)
  blocking collectives  121 us (17%)
  matrix products  111 us (15%)
  local copies, waits for them, and re-layouts  86.9 us (12%)
  other arithmetic  33.9 us (5%)
  starting transfers between devices  30.1 us (4%)
  between operations  16.2 us (2%)
    pallas_call x4, Pallas kernels, attend_forward(): pl.pallas_call(kernel, grid_spec=pltpu.PrefetchScalarGridSpec(num_scalar_...  85.9 us
    psum x1, blocking collectives, per_device(): lax.psum(jnp.where(groups[:, :, 0] == rank, bias_pair[None], 0.0), both)  68.2 us
    pallas_call x1, Pallas kernels, attend_backward(): pl.pallas_call(functools.partial(backward_kernel, steps), grid_spec=pltpu...  66.4 us
    unnamed x1, blocking collectives  52.5 us
    ppermute x1, waiting for transfers between devices, per_device(): from_near = lax.ppermute(to_near, both, peer_pairs[1])  49.3 us
    reduce_scatter x1, waiting for transfers between devices, per_device(): lax.psum_scatter(rest_grad.reshape(GROUP * width, -1), flipped, scatter_d...  48.6 us
    dot_general x7, matrix products, dot_nn(): return jnp.dot(left, right, preferred_element_type=jnp.float32)  42.3 us
    ppermute x1, waiting for transfers between devices, per_device(): own = lax.ppermute(inputs, both, move_pairs)  42 us
  transfers between devices with their start and end apart: 21, of which 5 were waited for; matrix products, arithmetic and copies ran while one was open for 24% of the time, Pallas kernels for 12%

profile of v1, /device:TPU:1, one launch (start us, length us, event | category | flops | bytes accessed | tf_op | source)
XLA Modules:
  0.0 714.1 jit_solution(13532797172280158062)
XLA Ops:
  15.0 2.6 copy.109
  17.6 5.6 collective-permute-start
  23.9 42.0 %collective-permute-done = bf16[1024,768]{0,1:T(8,128)(2,1)} collective-permute-done((bf16[1024,768]{0,1:T(8,128)(2,1)}, bf16[1024,768]{0,1:T(8,128)(2,1)}, u32[]{:S(2)}, u32[]{:S(2)}) %collective-permute-start) | collective-permute-done | bytes 1572896 | tf_op jit(solution)/shard_map/ppermute | solution.py:364
  66.0 2.5 collective-permute-start.2
  70.1 5.6 collective-permute-start.9
  77.7 52.5 %all-reduce = f32[6912]{0:T(1024)S(1)} all-reduce(f32[6912]{0:T(1024)S(1)} %dynamic-update-slice), channel_id=2, replica_groups=mesh['dp'=8,'tensor'=4] {'tensor'}, use_global_device_ids=true, to_apply=%add | all-reduce | flops 6912 | bytes 55296
  131.6 6.8 collective-permute-start.3
  144.6 4.3 fusion.25.kv0.q_first.q_second.qkv0
  148.9 4.0 fusion.26.kv2.q_first.q_second.qkv2
  152.9 2.6 multiply_convert_fusion.3.q_first.q_second.kv1.qkv1
  155.6 4.0 multiply_convert_fusion.1.kv3.q_first.q_second.qkv3
  160.2 22.0 %attend_forward.4 = (bf16[1024,192]{1,0:T(8,128)(2,1)}, bf16[64,3,64,512]{3,2,1,0:T(8,128)(2,1)}) custom-call(s32[1536]{0:T(1024)} %xor.65.table, s32[2]{0:T(128)} %get-tuple-element.169.place, bf16[1024,640]{1,0:T(8,128)(2,1)} %multiply_convert_fusion.3.q_first.q_second.kv1.qkv1, bf16[1024,640]{1,0:T(8,128)(2,1)} %multiply_convert_fusion.3.q_first.q_second.kv1.qkv1, ...), custom_call_target="tpu_custom_call" | custom-call | tf_op jit(solution)/shard_map/attend_forward/pallas_call | solution.py:123
  182.1 21.3 %attend_forward.5 = (bf16[1024,192]{1,0:T(8,128)(2,1)}, bf16[64,3,64,512]{3,2,1,0:T(8,128)(2,1)}) custom-call(s32[1536]{0:T(1024)} %xor.65.table, s32[2]{0:T(128)} %get-tuple-element.168.place, bf16[1024,640]{1,0:T(8,128)(2,1)} %multiply_convert_fusion.1.kv3.q_first.q_second.qkv3, ...), custom_call_target="tpu_custom_call", output_to_operand_aliasing={{1}: (8, {})} | custom-call | tf_op jit(solution)/shard_map/attend_forward/pallas_call | solution.py:123
  203.4 21.6 %attend_forward.6 = (bf16[1024,192]{1,0:T(8,128)(2,1)}, bf16[64,3,64,512]{3,2,1,0:T(8,128)(2,1)}) custom-call(s32[1536]{0:T(1024)} %xor.65.table, s32[2]{0:T(128)} %get-tuple-element.167.place, bf16[1024,640]{1,0:T(8,128)(2,1)} %fusion.26.kv2.q_first.q_second.qkv2, ...), custom_call_target="tpu_custom_call", output_to_operand_aliasing={{1}: (8, {})} | custom-call | tf_op jit(solution)/shard_map/attend_forward/pallas_call | solution.py:123
  226.9 21.1 %attend_forward.7 = (bf16[1024,192]{1,0:T(8,128)(2,1)}, bf16[64,3,64,512]{3,2,1,0:T(8,128)(2,1)}) custom-call(s32[1536]{0:T(1024)} %xor.65.table, s32[2]{0:T(128)} %get-tuple-element.166.place, bf16[1024,640]{1,0:T(8,128)(2,1)} %fusion.25.kv0.q_first.q_second.qkv0, ...), custom_call_target="tpu_custom_call", output_to_operand_aliasing={{1}: (8, {})} | custom-call | tf_op jit(solution)/shard_map/attend_forward/pallas_call | solution.py:123
  249.8 8.4 %slice_bitcast_fusion = (bf16[768,4,768]{2,0,1:T(8,128)(2,1)}, bf16[768,4,768]{2,0,1:T(8,128)(2,1)}) fusion(bf16[4,768,1728]{2,1,0:T(8,128)(2,1)} %bitcast.81), kind=kLoop, calls=%fused_computation.26 | loop fusion | bytes 18874368 | tf_op jit(solution)/shard_map/transpose | solution.py:412
  259.4 3.7 fusion.58
  263.5 7.2 %copy.118 = bf16[768,4,768]{0,2,1:T(8,128)(2,1)} copy(bf16[768,4,768]{2,0,1:T(8,128)(2,1)} %get-tuple-element.115) | data formatting | bytes 9437184 | tf_op jit(solution)/shard_map/transpose | solution.py:411
  270.7 6.7 copy.119
  277.4 12.2 %multiply_convert_fusion = (bf16[1024,3072]{1,0:T(8,128)(2,1)S(1)}, f32[1024,3072]{1,0:T(8,128)}) fusion(f32[3072]{0:T(1024)} %add.233, bf16[768,3072]{0,1:T(8,128)(2,1)} %bitcast.82, f32[1024,768]{0,1:T(8,128)S(1)} %get-tuple-element.158, f32[768]{0:T(1024)S(1)} %copy-done.48, f32[768]{0:T(1024)S(1)} %copy-done.29, f32[1024]{0:T(1024)S(1)} %add_rsqrt_fusion.1, ...), kind=kOutput, calls=%fused_computation.9 | convolution fusion | flops 4854644736 | bytes 26765312 | tf_op jit(solution)/shard_map/dot_general | solution.py:30
  289.7 10.0 %fusion.59 = (f32[1024]{0:T(1024)S(1)}, f32[1024,768]{0,1:T(8,128)S(1)}) fusion(f32[768]{0:T(1024)S(1)} %copy-done.47, bf16[1024,3072]{1,0:T(8,128)(2,1)S(1)} %get-tuple-element.159, bf16[768,3072]{0,1:T(8,128)(2,1)S(1)} %bitcast.86, f32[768]{0:T(1024)S(1)} %copy-done.49, f32[768]{0:T(1024)S(1)} %copy-done.29, f32[1024]{0:T(1024)S(1)} %add_rsqrt_fusion.1, ...), kind=kOutput, calls=%fused_computation.151 | convolution fusion | flops 4837342208 | bytes 17323008 | tf_op jit(solution)/shard_map/dot_general | solution.py:40
  300.4 2.3 fusion.16
  302.8 13.6 %convert_reduce_fusion = (f32[3072]{0:T(1024)}, bf16[1024,3072]{1,0:T(8,128)(2,1)}) fusion(f32[1024,3072]{1,0:T(8,128)} %get-tuple-element.160, f32[3072]{0:T(1024)S(1)} %copy-done.27, bf16[768,3072]{0,1:T(8,128)(2,1)S(1)} %bitcast.87, f32[1024]{0:T(1024)S(1)} %broadcast_multiply_fusion.2, f32[1024,768]{0,1:T(8,128)S(1)} %get-tuple-element.162, ...), kind=kOutput, calls=%fused_computation.8 | convolution fusion | flops 4879807488 | bytes 28355584 | tf_op jit(solution)/shard_map/dot_general | solution.py:30
  316.4 10.0 %multiply_reduce_fusion = (f32[768]{0:T(1024)}, f32[1024]{0:T(1024)S(1)}, f32[1024]{0:T(1024)S(1)}, f32[768]{0:T(1024)}, f32[1024,768]{0,1:T(8,128)S(1)}) fusion(f32[1024,768]{0,1:T(8,128)S(1)} %copy-done.1, f32[1024]{0:T(1024)S(1)} %add_rsqrt_fusion.1, f32[1024]{0:T(1024)S(1)} %broadcast_multiply_fusion.5, f32[768]{0:T(1024)S(1)} %copy-done.30, ...), kind=kOutput, calls=%fused_computation.36 | convolution fusion | flops 4845989888 | bytes 22065152 | tf_op jit(solution)/shard_map/dot_general | solution.py:40
  334.1 10.8 %collective-permute-done.10.do1 = bf16[1024,192]{1,0:T(8,128)(2,1)} collective-permute-done((bf16[1024,192]{1,0:T(8,128)(2,1)}, bf16[1024,192]{1,0:T(8,128)(2,1)}, u32[]{:S(2)}, u32[]{:S(2)}) %collective-permute-start.10) | collective-permute-done | bytes 393248 | tf_op jit(solution)/shard_map/ppermute | solution.py:444
  344.8 12.1 %collective-permute-done.12.do3 = bf16[1024,192]{1,0:T(8,128)(2,1)} collective-permute-done((bf16[1024,192]{1,0:T(8,128)(2,1)}, bf16[1024,192]{1,0:T(8,128)(2,1)}, u32[]{:S(2)}, u32[]{:S(2)}) %collective-permute-start.12) | collective-permute-done | bytes 393248 | tf_op jit(solution)/shard_map/ppermute | solution.py:444
  356.9 66.4 %attend_backward.1 = bf16[4096,640]{1,0:T(8,128)(2,1)} custom-call(s32[1536]{0:T(1024)} %xor.65.table, bf16[64,3,64,512]{3,2,1,0:T(8,128)(2,1)} %get-tuple-element.32.p_ref, bf16[1024,640]{1,0:T(8,128)(2,1)} %fusion.25.kv0.q_first.q_second.qkv0, bf16[1024,640]{1,0:T(8,128)(2,1)} %multiply_convert_fusion.3.q_first.q_second.kv1.qkv1, ...), custom_call_target="tpu_custom_call" | custom-call | tf_op jit(solution)/shard_map/attend_backward/pallas_call | solution.py:225
  423.3 9.3 %fusion.22 = bf16[768,640]{0,1:T(8,128)(2,1)S(1)} fusion(bf16[4096,640]{1,0:T(8,128)(2,1)} %attend_backward.1, bf16[1024,768]{0,1:T(8,128)(2,1)} %collective-permute-done.4, bf16[1024,768]{0,1:T(8,128)(2,1)} %collective-permute-done.3, bf16[1024,768]{0,1:T(8,128)(2,1)S(1)} %copy-done.6, bf16[1024,768]{0,1:T(8,128)(2,1)} %collective-permute-done), kind=kOutput, calls=%fused_computation.62 | convolution fusion | flops 4052189184 | bytes 12517376 | tf_op jit(solution)/shard_map/dot_general | solution.py:34
  433.7 2.2 copy.128
  435.9 3.8 bitcast_select_fusion
  440.4 9.9 %convolution_convert_fusion.1 = bf16[768,3072]{1,0:T(8,128)(2,1)} fusion(bf16[1024,3072]{1,0:T(8,128)(2,1)} %get-tuple-element.165, f32[1024,768]{0,1:T(8,128)} %copy-done, f32[768]{0:T(1024)S(1)} %copy-done.50, f32[768]{0:T(1024)S(1)} %copy-done.31, f32[1024]{0:T(1024)S(1)} %copy-done.19, f32[1024]{0:T(1024)S(1)} %broadcast_multiply_fusion.5), kind=kOutput, calls=%fused_computation.22 | convolution fusion | flops 4838129664 | bytes 14170112 | tf_op jit(solution)/shard_map/dot_general | solution.py:34
  450.4 9.9 %reshape.222 = bf16[768,4,768]{2,1,0:T(4,128)(2,1)} reshape(bf16[768,3072]{1,0:T(8,128)(2,1)} %convolution_convert_fusion.1) | data formatting | bytes 9437184 | tf_op jit(solution)/shard_map/reshape | solution.py:453
  460.3 9.7 %convolution_convert_fusion = bf16[768,3072]{1,0:T(8,128)(2,1)} fusion(bf16[1024,3072]{1,0:T(8,128)(2,1)} %copy-done.53, bf16[1024,768]{0,1:T(8,128)(2,1)} %collective-permute-done.9, f32[1024,768]{0,1:T(8,128)S(1)} %get-tuple-element.162, f32[1024]{0:T(1024)S(1)} %copy-done.21, f32[1024]{0:T(1024)S(1)} %copy-done.23, f32[768]{0:T(1024)S(1)} %copy-done.25, ...), kind=kOutput, calls=%fused_computation.21 | convolution fusion | flops 4841275392 | bytes 15748096 | tf_op jit(solution)/shard_map/dot_general | solution.py:34
  470.0 9.8 %reshape.223 = bf16[768,4,768]{2,1,0:T(4,128)(2,1)} reshape(bf16[768,3072]{1,0:T(8,128)(2,1)} %convolution_convert_fusion) | data formatting | bytes 9437184 | tf_op jit(solution)/shard_map/reshape | solution.py:454
  479.8 4.3 convolution_convert_fusion.5
  485.4 3.6 copy.129
  489.0 7.5 %pad_maximum_fusion = bf16[4,768,1728]{2,0,1:T(4,128)(2,1)S(1)} fusion(bf16[4,768,192]{2,0,1:T(4,128)(2,1)} %copy.129, bf16[4,768,768]{2,0,1:T(4,128)(2,1)} %bitcast.79, bf16[4,768,768]{2,0,1:T(4,128)(2,1)} %bitcast.78), kind=kLoop, calls=%fused_computation.11 | loop fusion | flops 31850496 | bytes 21233664 | tf_op jit(solution)/shard_map/concatenate | solution.py:451
  496.5 6.0 copy.130
  503.4 4.1 convolution_convert_fusion.2
  507.5 3.3 convolution_convert_fusion.3
  511.4 3.2 add_convert_fusion.1
  514.7 4.1 fusion.20
  518.9 1.9 collective-permute-start.8
  523.3 49.3 %collective-permute-done.15 = bf16[1024,768]{0,1:T(8,128)(2,1)S(1)} collective-permute-done((bf16[1024,768]{0,1:T(8,128)(2,1)S(1)}, bf16[1024,768]{0,1:T(8,128)(2,1)S(1)}, u32[]{:S(2)}, u32[]{:S(2)}) %collective-permute-start.15) | collective-permute-done | bytes 1572896 | tf_op jit(solution)/shard_map/ppermute | solution.py:491
  572.6 2.4 add_convert_fusion
  575.0 1.9 collective-permute-start.16
  577.1 68.2 %all-reduce.1 = (f32[4,384]{1,0:T(4,128)S(1)}, f32[7680]{0:T(1024)S(1)}) all-reduce(f32[4,384]{1,0:T(4,128)S(1)} %broadcast_select_fusion.1, f32[7680]{0:T(1024)S(1)} %constant_dynamic-update-slice_fusion), channel_id=1, replica_groups=mesh['dp'=8,'tensor'=4] {'dp','tensor'}, use_global_device_ids=true, to_apply=%region_11.12 | all-reduce | flops 9216 | bytes 73728 | tf_op jit(solution)/shard_map/psum | solution.py:512
  654.4 48.6 %reduce-scatter.5.cloned.1.call-done = bf16[96,1728]{1,0:T(8,128)(2,1)} async-done(((bf16[3072,1728]{1,0:T(8,128)(2,1)}), bf16[96,1728]{1,0:T(8,128)(2,1)}) %reduce-scatter.5.cloned.1.call-update) | async-done | bytes 331792 | tf_op jit(solution)/shard_map/reduce_scatter | solution.py:464
  (257 shorter events, 53.2 us)
Async XLA Ops:
  7.2 61.2 %copy-start.7 = (bf16[1024,768]{1,0:T(8,128)(2,1)S(1)}, bf16[1024,768]{1,0:T(8,128)(2,1)}, u32[]{:S(2)}) copy-start(bf16[1024,768]{1,0:T(8,128)(2,1)} %param.19) | copy-start | bytes 4718596
  7.2 136.0 %all-gather.4.cloned.1.call-start = ((), (), s32[]{:S(2)}) async-start(), calls=%async_computation.2 | async-start | bytes 4055040 | tf_op jit(solution)/shard_map/all_gather | solution.py:353
  12.1 236.0 %all-gather.6.cloned.1.call-start = ((), (), s32[]{:S(2)}) async-start(), calls=%async_computation.3 | async-start | bytes 11354112 | tf_op jit(solution)/shard_map/all_gather | solution.py:355
  14.9 60.8 %copy-start.28 = (s32[3,64,3]{1,2,0:T(4,128)S(1)}, s32[3,64,3]{1,2,0:T(4,128)}, u32[]{:S(2)}) copy-start(s32[3,64,3]{1,2,0:T(4,128)} %param.35) | copy-start | bytes 6916
  14.9 61.2 %copy-start.51 = (u32[32]{0:T(128)S(1)}, u32[32]{0:T(128)}, u32[]{:S(2)}) copy-start(u32[32]{0:T(128)} %constant.144) | copy-start | bytes 388
  14.9 62.4 %copy-start.34 = (f32[768]{0:T(1024)S(1)}, f32[768]{0:T(1024)}, u32[]{:S(2)}) copy-start(f32[768]{0:T(1024)} %param.31) | copy-start | bytes 9220
  14.9 62.4 %copy-start.38 = (f32[192]{0:T(256)S(1)}, f32[192]{0:T(256)}, u32[]{:S(2)}) copy-start(f32[192]{0:T(256)} %param.26) | copy-start | bytes 2308
  14.9 62.4 %copy-start.39 = (f32[192]{0:T(256)S(1)}, f32[192]{0:T(256)}, u32[]{:S(2)}) copy-start(f32[192]{0:T(256)} %param.27) | copy-start | bytes 2308
  14.9 633.9 %reduce-scatter.3.cloned.1.call-start = ((), (), s32[]{:S(2)}) async-start(), calls=%async_computation.4 | async-start | bytes 4055040 | tf_op jit(solution)/shard_map/reduce_scatter | solution.py:504
  17.6 48.4 %collective-permute-start = (bf16[1024,768]{0,1:T(8,128)(2,1)}, bf16[1024,768]{0,1:T(8,128)(2,1)}, u32[]{:S(2)}, u32[]{:S(2)}) collective-permute-start(bf16[1024,768]{0,1:T(8,128)(2,1)} %copy.109), channel_id=1, source_target_pairs={{0,0},{1,1},{2,4},{3,5},{4,2},{5,3},{6,6},{7,7},{8,8},{9,9},{10,12... | collective-permute-start | bytes 4718600 | tf_op jit(solution)/shard_map/ppermute | solution.py:364
  23.2 115.3 %collective-permute-start.1 = (bf16[1024,768]{0,1:T(8,128)(2,1)}, bf16[1024,768]{0,1:T(8,128)(2,1)S(1)}, u32[]{:S(2)}, u32[]{:S(2)}) collective-permute-start(bf16[1024,768]{0,1:T(8,128)(2,1)} %copy.109), channel_id=1, source_target_pairs={{0,1},{1,0},{6,7},{7,6},{8,9},{9,8},{14,15},{15,14},{16,17},{17,16... | collective-permute-start | bytes 4718600 | tf_op jit(solution)/shard_map/ppermute | solution.py:365
  66.0 72.5 %collective-permute-start.2 = (bf16[1024,768]{0,1:T(8,128)(2,1)}, bf16[1024,768]{0,1:T(8,128)(2,1)}, u32[]{:S(2)}, u32[]{:S(2)}) collective-permute-start(bf16[1024,768]{0,1:T(8,128)(2,1)} %collective-permute-done), channel_id=1, source_target_pairs={{2,3},{3,2},{4,5},{5,4},{10,11},{11,10},{12,13},{13,12},{18,19},{1... | collective-permute-start | bytes 4718600 | tf_op jit(solution)/shard_map/ppermute | solution.py:366
  70.1 230.0 %collective-permute-start.9 = (bf16[1024,768]{0,1:T(8,128)(2,1)}, bf16[1024,768]{0,1:T(8,128)(2,1)}, u32[]{:S(2)}, u32[]{:S(2)}) collective-permute-start(bf16[1024,768]{0,1:T(8,128)(2,1)} %copy.121), channel_id=1, source_target_pairs={{0,0},{1,1},{2,4},{3,5},{4,2},{5,3},{6,6},{7,7},{8,8},{9,9},{10,12... | collective-permute-start | bytes 4718600 | tf_op jit(solution)/shard_map/ppermute | solution.py:371
  131.6 17.3 %collective-permute-start.3 = (bf16[1024,768]{0,1:T(8,128)(2,1)}, bf16[1024,768]{0,1:T(8,128)(2,1)}, u32[]{:S(2)}, u32[]{:S(2)}) collective-permute-start(bf16[1024,768]{0,1:T(8,128)(2,1)} %collective-permute-done), channel_id=1, source_target_pairs={{0,4},{1,5},{2,6},{3,7},{4,0},{5,1},{6,2},{7,3},{8,12},{9,13},{10,... | collective-permute-start | bytes 4718600 | tf_op jit(solution)/shard_map/ppermute | solution.py:368
  140.1 12.8 %copy-start.5 = (bf16[1024,768]{0,1:T(8,128)(2,1)}, bf16[1024,768]{0,1:T(8,128)(2,1)S(1)}, u32[]{:S(2)}) copy-start(bf16[1024,768]{0,1:T(8,128)(2,1)S(1)} %broadcast_select_fusion) | copy-start | bytes 4718596
  140.1 15.5 %collective-permute-start.4 = (bf16[1024,768]{0,1:T(8,128)(2,1)S(1)}, bf16[1024,768]{0,1:T(8,128)(2,1)}, u32[]{:S(2)}, u32[]{:S(2)}) collective-permute-start(bf16[1024,768]{0,1:T(8,128)(2,1)S(1)} %broadcast_select_fusion), channel_id=1, source_target_pairs={{0,4},{1,5},{2,6},{3,7},{4,0},{5,1},{6,2},{7,3},{8,12},{9,13},{10,... | collective-permute-start | bytes 4718600 | tf_op jit(solution)/shard_map/ppermute | solution.py:369
  141.8 13.7 %copy-start.36 = (bf16[640]{0:T(1024)(128)(2,1)}, bf16[640]{0:T(1024)(128)(2,1)S(1)}, u32[]{:S(2)}) copy-start(bf16[640]{0:T(1024)(128)(2,1)S(1)} %pad.38.clone) | copy-start | bytes 3844
  144.6 11.0 %copy-start.8 = (bf16[768,512]{1,0:T(8,128)(2,1)}, bf16[768,512]{1,0:T(8,128)(2,1)S(1)}, u32[]{:S(2)}) copy-start(bf16[768,512]{1,0:T(8,128)(2,1)S(1)} %slice.279) | copy-start | bytes 2359300
  144.6 11.0 %copy-start.16 = (bf16[768,64]{1,0:T(8,128)(2,1)}, bf16[768,64]{1,0:T(8,128)(2,1)S(1)}, u32[]{:S(2)}) copy-start(bf16[768,64]{1,0:T(8,128)(2,1)S(1)} %slice.280) | copy-start | bytes 294916
  203.4 22.0 %copy-start.45 = (bf16[1024,192]{1,0:T(8,128)(2,1)S(1)}, bf16[1024,192]{1,0:T(8,128)(2,1)}, u32[]{:S(2)}) copy-start(bf16[1024,192]{1,0:T(8,128)(2,1)} %get-tuple-element.31) | copy-start | bytes 1179652
  203.4 22.0 %copy-start.44 = (bf16[1024,192]{1,0:T(8,128)(2,1)S(1)}, bf16[1024,192]{1,0:T(8,128)(2,1)}, u32[]{:S(2)}) copy-start(bf16[1024,192]{1,0:T(8,128)(2,1)} %get-tuple-element.29) | copy-start | bytes 1179652
  225.0 33.2 %collective-permute-start.6 = (bf16[1024,192]{1,0:T(8,128)(2,1)}, bf16[1024,192]{1,0:T(8,128)(2,1)S(1)}, u32[]{:S(2)}, u32[]{:S(2)}) collective-permute-start(bf16[1024,192]{1,0:T(8,128)(2,1)} %get-tuple-element.30), channel_id=1, source_target_pairs={{0,4},{1,5},{2,6},{3,7},{4,0},{5,1},{6,2},{7,3},{8,12},{9,13},{10,... | collective-permute-start | bytes 1179656 | tf_op jit(solution)/shard_map/ppermute | solution.py:407
  225.4 32.7 %collective-permute-start.7 = (bf16[1024,192]{1,0:T(8,128)(2,1)S(1)}, bf16[1024,192]{1,0:T(8,128)(2,1)S(1)}, u32[]{:S(2)}, u32[]{:S(2)}) collective-permute-start(bf16[1024,192]{1,0:T(8,128)(2,1)S(1)} %copy-done.45), channel_id=1, source_target_pairs={{0,5},{1,4},{2,7},{3,6},{4,1},{5,0},{6,3},{7,2},{8,13},{9,12},{10,... | collective-permute-start | bytes 1179656 | tf_op jit(solution)/shard_map/ppermute | solution.py:407
  225.4 32.7 %collective-permute-start.5 = (bf16[1024,192]{1,0:T(8,128)(2,1)S(1)}, bf16[1024,192]{1,0:T(8,128)(2,1)S(1)}, u32[]{:S(2)}, u32[]{:S(2)}) collective-permute-start(bf16[1024,192]{1,0:T(8,128)(2,1)S(1)} %copy-done.44), channel_id=1, source_target_pairs={{0,1},{1,0},{2,3},{3,2},{4,5},{5,4},{6,7},{7,6},{8,9},{9,8},{10,11... | collective-permute-start | bytes 1179656 | tf_op jit(solution)/shard_map/ppermute | solution.py:407
  263.0 14.3 %copy-start = (f32[1024,768]{0,1:T(8,128)}, f32[1024,768]{0,1:T(8,128)S(1)}, u32[]{:S(2)}) copy-start(f32[1024,768]{0,1:T(8,128)S(1)} %get-tuple-element.158) | copy-start | bytes 9437188
  263.4 52.9 %copy-start.18 = (f32[1024]{0:T(1024)}, f32[1024]{0:T(1024)S(1)}, u32[]{:S(2)}) copy-start(f32[1024]{0:T(1024)S(1)} %add_rsqrt_fusion.1) | copy-start | bytes 12292
  277.4 12.3 %copy-start.4 = (bf16[768,4,768]{0,2,1:T(8,128)(2,1)S(1)}, bf16[768,4,768]{0,2,1:T(8,128)(2,1)}, u32[]{:S(2)}) copy-start(bf16[768,4,768]{0,2,1:T(8,128)(2,1)} %copy.119) | copy-start | bytes 14155780
  277.4 12.3 %copy-start.47 = (f32[768]{0:T(1024)S(1)}, f32[768]{0:T(1024)}, u32[]{:S(2)}) copy-start(f32[768]{0:T(1024)} %param.32) | copy-start | bytes 9220
  277.4 12.3 %copy-start.49 = (f32[768]{0:T(1024)S(1)}, f32[768]{0:T(1024)}, u32[]{:S(2)}) copy-start(f32[768]{0:T(1024)} %param.30) | copy-start | bytes 9220
  300.4 16.0 %slice-start.2 = ((s8[4718592]{0:T(1024)(128)(4,1)}), s8[4194304]{0:T(1024)(128)(4,1)S(1)}, s32[]{:S(2)}) async-start(s8[4718592]{0:T(1024)(128)(4,1)} %bitcast.83), calls=%async_computation.8 | async-start | bytes 8388608
  302.7 13.7 %copy-start.20 = (f32[1024]{0:T(1024)}, f32[1024]{0:T(1024)S(1)}, u32[]{:S(2)}) copy-start(f32[1024]{0:T(1024)S(1)} %broadcast_multiply_fusion.2) | copy-start | bytes 12292
  302.7 13.7 %copy-start.22 = (f32[1024]{0:T(1024)}, f32[1024]{0:T(1024)S(1)}, u32[]{:S(2)}) copy-start(f32[1024]{0:T(1024)S(1)} %broadcast_multiply_fusion.3) | copy-start | bytes 12292
  302.7 13.6 %copy-start.1 = (f32[1024,768]{0,1:T(8,128)S(1)}, f32[1024,768]{0,1:T(8,128)}, u32[]{:S(2)}) copy-start(f32[1024,768]{0,1:T(8,128)} %copy-done) | copy-start | bytes 9437188
  302.8 13.6 %slice-start.3 = ((s8[4718592]{0:T(1024)(128)(4,1)}), s8[524288]{0:T(1024)(128)(4,1)S(1)}, s32[]{:S(2)}) async-start(s8[4718592]{0:T(1024)(128)(4,1)} %bitcast.83), calls=%async_computation.9 | async-start | bytes 1048576
  302.8 13.6 %copy-start.30 = (f32[768]{0:T(1024)S(1)}, f32[768]{0:T(1024)}, u32[]{:S(2)}) copy-start(f32[768]{0:T(1024)} %param.29) | copy-start | bytes 9220
  331.7 13.1 %collective-permute-start.10 = (bf16[1024,192]{1,0:T(8,128)(2,1)}, bf16[1024,192]{1,0:T(8,128)(2,1)}, u32[]{:S(2)}, u32[]{:S(2)}) collective-permute-start(bf16[1024,192]{1,0:T(8,128)(2,1)} %get-tuple-element.119), channel_id=1, source_target_pairs={{0,1},{1,0},{2,3},{3,2},{4,5},{5,4},{6,7},{7,6},{8,9},{9,8},{10,11... | collective-permute-start | bytes 1179656 | tf_op jit(solution)/shard_map/ppermute | solution.py:444
  331.7 13.1 %collective-permute-start.11 = (bf16[1024,192]{1,0:T(8,128)(2,1)}, bf16[1024,192]{1,0:T(8,128)(2,1)}, u32[]{:S(2)}, u32[]{:S(2)}) collective-permute-start(bf16[1024,192]{1,0:T(8,128)(2,1)} %get-tuple-element.118), channel_id=1, source_target_pairs={{0,4},{1,5},{2,6},{3,7},{4,0},{5,1},{6,2},{7,3},{8,12},{9,13},{10,... | collective-permute-start | bytes 1179656 | tf_op jit(solution)/shard_map/ppermute | solution.py:444
  332.5 24.4 %collective-permute-start.12 = (bf16[1024,192]{1,0:T(8,128)(2,1)}, bf16[1024,192]{1,0:T(8,128)(2,1)}, u32[]{:S(2)}, u32[]{:S(2)}) collective-permute-start(bf16[1024,192]{1,0:T(8,128)(2,1)} %get-tuple-element.117), channel_id=1, source_target_pairs={{0,5},{1,4},{2,7},{3,6},{4,1},{5,0},{6,3},{7,2},{8,13},{9,12},{10,... | collective-permute-start | bytes 1179656 | tf_op jit(solution)/shard_map/ppermute | solution.py:444
  356.9 66.4 %copy-start.6 = (bf16[1024,768]{0,1:T(8,128)(2,1)S(1)}, bf16[1024,768]{0,1:T(8,128)(2,1)}, u32[]{:S(2)}) copy-start(bf16[1024,768]{0,1:T(8,128)(2,1)} %copy-done.5) | copy-start | bytes 4718596
  439.7 263.2 %reduce-scatter.5.cloned.1.call-start = ((), (), s32[]{:S(2)}) async-start(), calls=%async_computation.5 | async-start | bytes 11354112 | tf_op jit(solution)/shard_map/reduce_scatter | solution.py:464
  507.5 3.8 collective-permute-start.14
  507.5 13.4 %slice-start = ((s8[5242880]{0:T(1024)(128)(4,1)}), s8[4194304]{0:T(1024)(128)(4,1)S(1)}, s32[]{:S(2)}) async-start(s8[5242880]{0:T(1024)(128)(4,1)} %bitcast.76), calls=%async_computation.6 | async-start | bytes 8388608
  510.8 10.1 %slice-start.1 = ((s8[5242880]{0:T(1024)(128)(4,1)}), s8[1048576]{0:T(1024)(128)(4,1)S(1)}, s32[]{:S(2)}) async-start(s8[5242880]{0:T(1024)(128)(4,1)} %bitcast.76), calls=%async_computation.7 | async-start | bytes 2097152
  510.9 12.5 %collective-permute-start.13 = (bf16[1024,768]{0,1:T(8,128)(2,1)S(1)}, bf16[1024,768]{0,1:T(8,128)(2,1)S(1)}, u32[]{:S(2)}, u32[]{:S(2)}) collective-permute-start(bf16[1024,768]{0,1:T(8,128)(2,1)S(1)} %convolution_convert_fusion.3), channel_id=1, source_target_pairs={{0,4},{1,5},{2,6},{3,7},{4,0},{5,1},{6,2},{7,3},{8,12},{9,13},{10,... | collective-permute-start | bytes 4718600 | tf_op jit(solution)/shard_map/ppermute | solution.py:488
  514.6 58.0 %collective-permute-start.15 = (bf16[1024,768]{0,1:T(8,128)(2,1)S(1)}, bf16[1024,768]{0,1:T(8,128)(2,1)S(1)}, u32[]{:S(2)}, u32[]{:S(2)}) collective-permute-start(bf16[1024,768]{0,1:T(8,128)(2,1)S(1)} %add_convert_fusion.1), channel_id=1, source_target_pairs={{0,1},{1,0},{2,3},{3,2},{4,5},{5,4},{6,7},{7,6},{8,9},{9,8},{10,11... | collective-permute-start | bytes 4718600 | tf_op jit(solution)/shard_map/ppermute | solution.py:491
  518.9 128.4 %collective-permute-start.8 = (bf16[1024,768]{0,1:T(8,128)(2,1)}, bf16[1024,768]{0,1:T(8,128)(2,1)S(1)}, u32[]{:S(2)}, u32[]{:S(2)}) collective-permute-start(bf16[1024,768]{0,1:T(8,128)(2,1)} %get-tuple-element.116), channel_id=1, source_target_pairs={{0,0},{1,1},{2,4},{3,5},{4,2},{5,3},{6,6},{7,7},{8,8},{9,9},{10,12... | collective-permute-start | bytes 4718600 | tf_op jit(solution)/shard_map/ppermute | solution.py:441
  521.9 50.7 %copy-start.3 = (f32[1024,768]{0,1:T(8,128)S(1)}, f32[1024,768]{0,1:T(8,128)}, u32[]{:S(2)}) copy-start(f32[1024,768]{0,1:T(8,128)} %copy-done.2) | copy-start | bytes 9437188
  575.0 77.8 %collective-permute-start.16 = (bf16[1024,768]{0,1:T(8,128)(2,1)}, bf16[1024,768]{0,1:T(8,128)(2,1)S(1)}, u32[]{:S(2)}, u32[]{:S(2)}) collective-permute-start(bf16[1024,768]{0,1:T(8,128)(2,1)} %add_convert_fusion), channel_id=1, source_target_pairs={{0,0},{1,1},{2,4},{3,5},{4,2},{5,3},{6,6},{7,7},{8,8},{9,9},{10,12... | collective-permute-start | bytes 4718600 | tf_op jit(solution)/shard_map/ppermute | solution.py:498
  (31 other events, 149.3 us)
Sparse Core Ops, SparseCore 0:
  12.3 94.3 all-gather.3
  109.5 90.8 all-gather.5
  439.9 111.5 reduce-scatter.2
  557.3 145.6 reduce-scatter.4

commit v2 on v1

v2 whole, which is shorter than its diff:
```python
import functools

import jax
import jax.numpy as jnp
from jax import lax
from jax.experimental import pallas as pl
from jax.experimental.pallas import tpu as pltpu
from jax.sharding import PartitionSpec as P

HD = 64
BLOCK = 64
LENGTH = 4096
NB = LENGTH // BLOCK
GROUP = 4
QROWS = LENGTH // GROUP
QB = QROWS // BLOCK
HEADS = 3
KEYS = 8 * BLOCK
KV = 128 * HEADS
QKV = KV + 256

negative = -1e30
epsilon = 1e-05
both = ("dp", "tensor")
vmem_limit = 56 * 1024 * 1024


def dot_nn(left, right):
    return jnp.dot(left, right, preferred_element_type=jnp.float32)


def dot_tn(left, right):
    return lax.dot_general(
        left, right, (((0,), (0,)), ((), ())), preferred_element_type=jnp.float32
    )


def dot_nt(left, right):
    return lax.dot_general(
        left, right, (((1,), (1,)), ((), ())), preferred_element_type=jnp.float32
    )


def lane_masks(dtype):
    lane = lax.broadcasted_iota(jnp.int32, (1, 128), 1)
    low = (lane < 64).astype(jnp.float32).astype(dtype)
    high = (lane >= 64).astype(jnp.float32).astype(dtype)
    return low, high


def key_bias(block):
    lane = lax.broadcasted_iota(jnp.int32, (1, KEYS), 1)
    entry = lane // BLOCK
    key = jnp.where(entry == 2, block - 1, jnp.where(entry == 3, block, block + 1))
    window = (entry >= 2) & (entry <= 4)
    off = window & ((key < 1) | (key > NB - 2))
    return jnp.where(off, negative, 0.0).astype(jnp.float32)


def gather_keys(table, source, head, block):
    rows = []
    for entry in range(8):
        place = table[(head * NB + block) * 8 + entry]
        rows.append(source[pl.ds(pl.multiple_of(place * BLOCK, BLOCK), BLOCK), head * 128 : head * 128 + 128])
    return jnp.concatenate(rows, axis=0)


def head_queries(first, second, low, high):
    return (first * high, first * low, second)


def forward_kernel(steps, fill, table, place, *refs):
    if fill:
        qkv0, qkv1, qkv2, qkv3, o_ref, p_ref, qkv_scr, s_scr, sems = refs
    else:
        qkv0, qkv1, qkv2, qkv3, _, o_ref, p_ref, qkv_scr, s_scr, sems = refs
    step = pl.program_id(0)

    @pl.when(step == 0)
    def _load():
        copies = [
            pltpu.make_async_copy(src, qkv_scr.at[pl.ds(n * QROWS, QROWS)], sems.at[n])
            for n, src in enumerate((qkv0, qkv1, qkv2, qkv3))
        ]
        for copy in copies:
            copy.start()
        for copy in copies:
            copy.wait()

    low, high = lane_masks(jnp.bfloat16)
    lane = lax.broadcasted_iota(jnp.int32, (1, 128), 1)
    per = QB // steps
    units = [(sub, head) for sub in range(per) for head in range(HEADS)]
    slot = place[1 + step // steps]
    keys = []
    for sub in range(per):
        local = slot * QB + (step % steps) * per + sub
        bias = key_bias(local ^ (place[0] * QB))
        rows = pl.ds(pl.multiple_of(local * BLOCK, BLOCK), BLOCK)
        queries = head_queries(
            qkv_scr[rows, KV : KV + 128], qkv_scr[rows, KV + 128 : KV + 256], low, high
        )
        for head in range(HEADS):
            n = sub * HEADS + head
            keys.append(gather_keys(table, qkv_scr, head, local))
            raw = dot_nt(queries[head], keys[n])
            s_scr[n, :, 0:128] = raw[:, 0:128]
            s_scr[n, :, 128:384] = raw[:, 128:384] + bias[:, 128:384]
            s_scr[n, :, 384:512] = raw[:, 384:512]
    tops = [jnp.max(s_scr[n], axis=1, keepdims=True) for n in range(len(units))]
    sums = []
    for n in range(len(units)):
        expo = jnp.exp(s_scr[n] - tops[n])
        s_scr[n] = expo
        sums.append(jnp.sum(expo, axis=1, keepdims=True))
    for n, (sub, head) in enumerate(units):
        p_ref[sub, head] = (s_scr[n] * (1.0 / sums[n])).astype(jnp.bfloat16)
    for sub in range(per):
        rows = slice(sub * BLOCK, (sub + 1) * BLOCK)
        outs = [dot_nn(p_ref[sub, head], keys[sub * HEADS + head]) for head in range(HEADS)]
        o_ref[0, rows, 0:128] = jnp.where(lane < 64, outs[0], outs[1]).astype(jnp.bfloat16)
        o_ref[0, rows, 128:192] = outs[2][:, 0:64].astype(jnp.bfloat16)


def attend_forward(slots, rank, table, qkv, probs):
    steps = 4
    per = QB // steps
    count = len(slots)
    any_spec = pl.BlockSpec(memory_space=pl.ANY)
    place = jnp.stack([rank.astype(jnp.int32)] + [jnp.int32(slot) for slot in slots])
    operands = [table, place, *qkv]
    alias = {}
    if probs is not None:
        alias = {6: 1}
        operands.append(probs)
    return pl.pallas_call(
        functools.partial(forward_kernel, steps, probs is None),
        grid_spec=pltpu.PrefetchScalarGridSpec(
            num_scalar_prefetch=2,
            grid=(count * steps,),
            in_specs=[any_spec] * (4 + len(alias)),
            out_specs=[
                pl.BlockSpec((1, per * BLOCK, 192), lambda g, *_: (g // steps, g % steps, 0)),
                pl.BlockSpec(
                    (per, HEADS, BLOCK, KEYS),
                    lambda g, t, pos: (pos[1 + g // steps] * steps + g % steps, 0, 0, 0),
                ),
            ],
            scratch_shapes=[
                pltpu.VMEM((LENGTH, QKV), jnp.bfloat16),
                pltpu.VMEM((per * HEADS, BLOCK, KEYS), jnp.float32),
                pltpu.SemaphoreType.DMA((4,)),
            ],
        ),
        out_shape=[
            jax.ShapeDtypeStruct((count, QROWS, 192), jnp.bfloat16),
            jax.ShapeDtypeStruct((NB, HEADS, BLOCK, KEYS), jnp.bfloat16),
        ],
        input_output_aliases=alias,
        compiler_params=pltpu.CompilerParams(
            dimension_semantics=("arbitrary",), vmem_limit_bytes=vmem_limit
        ),
        name="attend_forward",
    )(*operands)


def backward_kernel(
    steps, table, p_ref, qkv0, qkv1, qkv2, qkv3, do0, do1, do2, do3, out_ref, qkv_scr, do_scr, acc, dp_scr, st_scr, sems
):
    step = pl.program_id(0)

    @pl.when(step == 0)
    def _load():
        copies = [
            pltpu.make_async_copy(src, qkv_scr.at[pl.ds(n * QROWS, QROWS)], sems.at[n])
            for n, src in enumerate((qkv0, qkv1, qkv2, qkv3))
        ] + [
            pltpu.make_async_copy(src, do_scr.at[pl.ds(n * QROWS, QROWS)], sems.at[4 + n])
            for n, src in enumerate((do0, do1, do2, do3))
        ]
        for copy in copies:
            copy.start()
        acc[...] = jnp.zeros_like(acc)
        for copy in copies:
            copy.wait()

    low, high = lane_masks(jnp.bfloat16)
    lane = lax.broadcasted_iota(jnp.int32, (1, 128), 1)
    per = NB // steps
    units = [(sub, head) for sub in range(per) for head in range(HEADS)]
    keys, right = [], []
    for sub in range(per):
        local = step * per + sub
        rows = pl.ds(pl.multiple_of(local * BLOCK, BLOCK), BLOCK)
        queries = head_queries(
            qkv_scr[rows, KV : KV + 128], qkv_scr[rows, KV + 128 : KV + 256], low, high
        )
        g_first = do_scr[rows, 0:128]
        g_second = do_scr[rows, 128:192]
        grads = (
            g_first * low,
            g_first * high,
            jnp.concatenate([g_second, jnp.zeros_like(g_second)], axis=1),
        )
        for head in range(HEADS):
            n = sub * HEADS + head
            keys.append(gather_keys(table, qkv_scr, head, local))
            right.append(jnp.concatenate([queries[head], grads[head]], axis=0))
            dp_scr[n] = dot_nt(grads[head], keys[n])
    totals = []
    for n, (sub, head) in enumerate(units):
        weighted = p_ref[sub, head].astype(jnp.float32) * dp_scr[n]
        dp_scr[n] = weighted
        totals.append(jnp.sum(weighted, axis=1, keepdims=True))
    for n, (sub, head) in enumerate(units):
        probs = p_ref[sub, head]
        st_scr[n, 0:BLOCK] = (dp_scr[n] - probs.astype(jnp.float32) * totals[n]).astype(jnp.bfloat16)
        st_scr[n, BLOCK:128] = probs
    for sub in range(per):
        local = step * per + sub
        rows = pl.ds(pl.multiple_of(local * BLOCK, BLOCK), BLOCK)
        backs = [
            dot_nn(st_scr[sub * HEADS + head, 0:BLOCK], keys[sub * HEADS + head]) * 0.125
            for head in range(HEADS)
        ]
        out_ref[rows, KV : KV + 128] = jnp.where(lane < 64, backs[1], backs[0]).astype(jnp.bfloat16)
        out_ref[rows, KV + 128 : KV + 256] = jnp.where(lane < 64, 0.0, backs[2]).astype(
            jnp.bfloat16
        )
    for n, (sub, head) in enumerate(units):
        local = step * per + sub
        spread = dot_tn(st_scr[n], right[n])
        for entry in range(8):
            spot = table[(head * NB + local) * 8 + entry]
            where = pl.ds(pl.multiple_of(spot * BLOCK, BLOCK), BLOCK)
            acc[where, head * 128 : head * 128 + 128] += spread[
                entry * BLOCK : (entry + 1) * BLOCK
            ]

    @pl.when(step == steps - 1)
    def _store():
        out_ref[:, 0:KV] = acc[...].astype(jnp.bfloat16)


def attend_backward(table, probs, qkv, grads):
    steps = 16
    per = NB // steps
    any_spec = pl.BlockSpec(memory_space=pl.ANY)
    return pl.pallas_call(
        functools.partial(backward_kernel, steps),
        grid_spec=pltpu.PrefetchScalarGridSpec(
            num_scalar_prefetch=1,
            grid=(steps,),
            in_specs=[pl.BlockSpec((per, HEADS, BLOCK, KEYS), lambda g, *_: (g, 0, 0, 0))]
            + [any_spec] * 8,
            out_specs=pl.BlockSpec((LENGTH, QKV), lambda g, *_: (0, 0)),
            scratch_shapes=[
                pltpu.VMEM((LENGTH, QKV), jnp.bfloat16),
                pltpu.VMEM((LENGTH, 192), jnp.bfloat16),
                pltpu.VMEM((LENGTH, KV), jnp.float32),
                pltpu.VMEM((per * HEADS, BLOCK, KEYS), jnp.float32),
                pltpu.VMEM((per * HEADS, 128, KEYS), jnp.bfloat16),
                pltpu.SemaphoreType.DMA((8,)),
            ],
        ),
        out_shape=jax.ShapeDtypeStruct((LENGTH, QKV), jnp.bfloat16),
        compiler_params=pltpu.CompilerParams(
            dimension_semantics=("arbitrary",), vmem_limit_bytes=vmem_limit
        ),
        name="attend_backward",
    )(table, probs, *qkv, *grads)


def row_mean(values):
    return jnp.mean(values, axis=1, keepdims=True)


def fold_rows(values):
    total = values[0:8]
    for row in range(8, values.shape[0], 8):
        total = total + values[row : row + 8]
    return total


def token_kernel(
    tile,
    width,
    hidden,
    rank_ref,
    o0,
    o1,
    o2,
    o3,
    x_ref,
    cot_ref,
    vec_ref,
    up_bias_ref,
    weights,
    out_ref,
    n1_ref,
    g_ref,
    du_ref,
    dfr_ref,
    dar_ref,
    da_ref,
    do_ref,
    sum_ref,
    up_sum_ref,
    w_scr,
    acc,
    u_scr,
    slope_scr,
    xhat_scr,
    m1_scr,
    sem,
):
    step = pl.program_id(0)
    parts = GROUP
    small = 32
    cols = 256

    @pl.when(step == 0)
    def _load():
        copy = pltpu.make_async_copy(weights, w_scr, sem)
        copy.start()
        sum_ref[...] = jnp.zeros_like(sum_ref)
        up_sum_ref[...] = jnp.zeros_like(up_sum_ref)
        copy.wait()

    def vector(n):
        return vec_ref[n : n + 1, :]

    def part_rows(n):
        return slice(n * width, (n + 1) * width)

    def out_weight(n):
        place = pl.multiple_of((rank_ref[0] ^ n) * width, width)
        return w_scr[pl.ds(place, width), 2 * hidden :]

    total = dot_nt(o0[...], out_weight(0))
    for n, piece in ((1, o1), (2, o2), (3, o3)):
        total = total + dot_nt(piece[...], out_weight(n))
    acc[...] = total
    first_scale = []
    for row in range(0, tile, small):
        rows = slice(row, row + small)
        resid = acc[rows] + x_ref[rows].astype(jnp.float32) + vector(0)
        center = resid - row_mean(resid)
        scale = lax.rsqrt(row_mean(center * center) + epsilon)
        xhat = center * scale
        normed = xhat * vector(1) + vector(2)
        first_scale.append(scale)
        xhat_scr[rows] = xhat
        m1_scr[rows] = normed
        n1_ref[rows] = normed.astype(jnp.bfloat16)
    for part in range(parts):
        u_scr[part % 2] = dot_nn(n1_ref[...], w_scr[part_rows(part), 0:hidden])
        for row in range(0, tile, small):
            rows = slice(row, row + small)
            for col in range(0, hidden, cols):
                place = slice(col, col + cols)
                wide = slice(part * hidden + col, part * hidden + col + cols)
                pre = u_scr[part % 2, rows, place] + up_bias_ref[:, wide]
                cdf = 0.5 + 0.5 * lax.erf(pre * 0.7071067811865476)
                g_ref[rows, wide] = (pre * cdf).astype(jnp.bfloat16)
                slope_scr[rows, wide] = (
                    cdf + pre * jnp.exp(-0.5 * pre * pre) * 0.3989422804014327
                )
        lift = dot_nt(
            g_ref[:, part * hidden : (part + 1) * hidden],
            w_scr[part_rows(part), hidden : 2 * hidden],
        )
        if part == 0:
            acc[...] = lift
        else:
            acc[...] += lift
    sums = [jnp.zeros((8, width), jnp.float32) for _ in range(6)]
    for row in range(0, tile, small):
        rows = slice(row, row + small)
        second = m1_scr[rows] + acc[rows] + vector(3)
        center = second - row_mean(second)
        scale = lax.rsqrt(row_mean(center * center) + epsilon)
        xhat = center * scale
        out_ref[rows] = (xhat * vector(4) + vector(5)).astype(jnp.bfloat16)
        top = cot_ref[rows].astype(jnp.float32)
        gained = top * vector(4)
        down = scale * (gained - row_mean(gained) - xhat * row_mean(gained * xhat))
        sums[0] = sums[0] + fold_rows(top * xhat)
        sums[1] = sums[1] + fold_rows(top)
        sums[2] = sums[2] + fold_rows(down)
        m1_scr[rows] = down
        dfr_ref[rows] = down.astype(jnp.bfloat16)
    for part in range(parts):
        whole = slice(part * hidden, (part + 1) * hidden)
        u_scr[part % 2] = dot_nn(dfr_ref[...], w_scr[part_rows(part), hidden : 2 * hidden])
        for col in range(0, hidden, cols):
            place = slice(col, col + cols)
            wide = slice(part * hidden + col, part * hidden + col + cols)
            tally = jnp.zeros((8, cols), jnp.float32)
            for row in range(0, tile, small):
                rows = slice(row, row + small)
                low = (u_scr[part % 2, rows, place] * slope_scr[rows, wide]).astype(jnp.bfloat16)
                du_ref[rows, wide] = low
                tally = tally + fold_rows(low.astype(jnp.float32))
            up_sum_ref[:, wide] += tally
        lift = dot_nt(du_ref[:, whole], w_scr[part_rows(part), 0:hidden])
        if part == 0:
            acc[...] = lift
        else:
            acc[...] += lift
    for n, row in enumerate(range(0, tile, small)):
        rows = slice(row, row + small)
        back = m1_scr[rows] + acc[rows]
        xhat = xhat_scr[rows]
        sums[3] = sums[3] + fold_rows(back * xhat)
        sums[4] = sums[4] + fold_rows(back)
        gained = back * vector(1)
        down = first_scale[n] * (gained - row_mean(gained) - xhat * row_mean(gained * xhat))
        sums[5] = sums[5] + fold_rows(down)
        da_ref[rows] = down
        dar_ref[rows] = down.astype(jnp.bfloat16)
    for n in range(6):
        sum_ref[n] += sums[n]
    for n in range(parts):
        do_ref[n] = dot_nn(dar_ref[...], out_weight(n)).astype(jnp.bfloat16)


def token_block(rank, outs, own, cot, vectors, up_bias, weights):
    count, width = own.shape
    total_hidden = up_bias.shape[1]
    hidden = total_hidden // GROUP
    tile = 256

    def rows_of(columns):
        return pl.BlockSpec((tile, columns), lambda g, *_: (g, 0))

    def whole(shape):
        return pl.BlockSpec(shape, lambda g, *_: (0,) * len(shape))

    low = jnp.bfloat16
    head = outs[0].shape[1]
    return pl.pallas_call(
        functools.partial(token_kernel, tile, width, hidden),
        grid_spec=pltpu.PrefetchScalarGridSpec(
            num_scalar_prefetch=1,
            grid=(count // tile,),
            in_specs=[rows_of(head)] * 4
            + [rows_of(width)] * 2
            + [whole(vectors.shape), whole(up_bias.shape), pl.BlockSpec(memory_space=pl.ANY)],
            out_specs=[
                rows_of(width),
                rows_of(width),
                rows_of(total_hidden),
                rows_of(total_hidden),
                rows_of(width),
                rows_of(width),
                rows_of(width),
                pl.BlockSpec((GROUP, tile, head), lambda g, *_: (0, g, 0)),
                whole((6, 8, width)),
                whole((8, total_hidden)),
            ],
            scratch_shapes=[
                pltpu.VMEM(weights.shape, low),
                pltpu.VMEM((tile, width), jnp.float32),
                pltpu.VMEM((2, tile, hidden), jnp.float32),
                pltpu.VMEM((tile, total_hidden), jnp.float32),
                pltpu.VMEM((tile, width), jnp.float32),
                pltpu.VMEM((tile, width), jnp.float32),
                pltpu.SemaphoreType.DMA,
            ],
        ),
        out_shape=[
            jax.ShapeDtypeStruct((count, width), low),
            jax.ShapeDtypeStruct((count, width), low),
            jax.ShapeDtypeStruct((count, total_hidden), low),
            jax.ShapeDtypeStruct((count, total_hidden), low),
            jax.ShapeDtypeStruct((count, width), low),
            jax.ShapeDtypeStruct((count, width), low),
            jax.ShapeDtypeStruct((count, width), jnp.float32),
            jax.ShapeDtypeStruct((GROUP, count, head), low),
            jax.ShapeDtypeStruct((6, 8, width), jnp.float32),
            jax.ShapeDtypeStruct((8, total_hidden), jnp.float32),
        ],
        compiler_params=pltpu.CompilerParams(
            dimension_semantics=("arbitrary",), vmem_limit_bytes=vmem_limit
        ),
        name="token_block",
    )(rank.astype(jnp.int32).reshape(1), *outs, own, cot, vectors, up_bias, weights)


def weight_kernel(width, hidden, rank_ref, n1, dfr, dar, g, du, o0, o1, o2, o3, out_ref, n1_t, dfr_t, dar_t):
    part = pl.program_id(0)

    @pl.when(part == 0)
    def _turn():
        n1_t[...] = n1[...].T
        dfr_t[...] = dfr[...].T
        dar_t[...] = dar[...].T

    out_ref[:, 0:hidden] = dot_nn(n1_t[...], du[...]).astype(jnp.bfloat16)
    out_ref[:, hidden : 2 * hidden] = dot_nn(dfr_t[...], g[...]).astype(jnp.bfloat16)
    for n, piece in enumerate((o0, o1, o2, o3)):

        @pl.when(part == rank_ref[0] ^ n)
        def _out(piece=piece):
            out_ref[:, 2 * hidden :] = dot_nn(dar_t[...], piece[...]).astype(jnp.bfloat16)


def weight_block(rank, n1, dfr, dar, g, du, outs):
    count, width = n1.shape
    hidden = g.shape[1] // GROUP
    head = outs[0].shape[1]
    columns = 2 * hidden + head
    low = jnp.bfloat16

    def whole(shape):
        return pl.BlockSpec(shape, lambda g, *_: (0,) * len(shape))

    return pl.pallas_call(
        functools.partial(weight_kernel, width, hidden),
        grid_spec=pltpu.PrefetchScalarGridSpec(
            num_scalar_prefetch=1,
            grid=(GROUP,),
            in_specs=[whole((count, width))] * 3
            + [pl.BlockSpec((count, hidden), lambda g, *_: (0, g))] * 2
            + [whole((count, head))] * 4,
            out_specs=pl.BlockSpec((width, columns), lambda g, *_: (g, 0)),
            scratch_shapes=[pltpu.VMEM((width, count), low)] * 3,
        ),
        out_shape=jax.ShapeDtypeStruct((GROUP * width, columns), low),
        compiler_params=pltpu.CompilerParams(
            dimension_semantics=("arbitrary",), vmem_limit_bytes=vmem_limit
        ),
        name="weight_block",
    )(rank.astype(jnp.int32).reshape(1), n1, dfr, dar, g, du, *outs)


def pack_columns(query, key, value, axis):
    def piece(matrix, head):
        return lax.slice_in_dim(matrix, head * HD, (head + 1) * HD, axis=axis)

    return jnp.concatenate(
        [
            piece(value, 0),
            piece(key, 0),
            piece(key, 1),
            piece(value, 1),
            piece(value, 2),
            piece(key, 2),
            piece(query, 1),
            piece(query, 0),
            piece(query, 2),
        ],
        axis=axis,
    )


def insert_zero(packed, axis):
    head = lax.slice_in_dim(packed, 0, KV + 128, axis=axis)
    tail = lax.slice_in_dim(packed, KV + 128, KV + 192, axis=axis)
    return jnp.concatenate([head, jnp.zeros_like(tail), tail], axis=axis)


def drop_zero(packed, axis):
    head = lax.slice_in_dim(packed, 0, KV + 128, axis=axis)
    tail = lax.slice_in_dim(packed, KV + 192, KV + 256, axis=axis)
    return jnp.concatenate([head, tail], axis=axis)


def unpack_columns(packed, axis):
    def piece(n):
        return lax.slice_in_dim(packed, n * HD, (n + 1) * HD, axis=axis)

    query = jnp.concatenate([piece(7), piece(6), piece(8)], axis=axis)
    key = jnp.concatenate([piece(1), piece(2), piece(5)], axis=axis)
    value = jnp.concatenate([piece(0), piece(3), piece(4)], axis=axis)
    return query, key, value


def per_device(
    dp_size,
    tensor_size,
    inputs,
    cotangent,
    w_query,
    w_key,
    w_value,
    w_output,
    w_up,
    w_down,
    b_query,
    b_value,
    b_output,
    gain_attn,
    bias_attn,
    b_up,
    b_down,
    gain_mlp,
    bias_mlp,
    random_blocks,
):
    width = inputs.shape[1]
    hidden = b_up.shape[0]
    dp_index = lax.axis_index("dp")
    tensor_index = lax.axis_index("tensor")
    core = dp_index % 2
    half = tensor_index // 2
    rank = 2 * core + tensor_index % 2
    here = core == half
    devices = [(d, t) for d in range(dp_size) for t in range(tensor_size)]
    pair_bits = [bit for bit in range(1, dp_size.bit_length() - 1)]

    def flat(d, t):
        return d * tensor_size + t

    def stays(d, t):
        return d % 2 == t // 2

    def flip(value, d_bits, t_bits, chosen=None):
        pairs = [
            (flat(d, t), flat(d ^ d_bits, t ^ t_bits))
            for d, t in devices
            if chosen is None or chosen(d, t)
        ]
        return lax.ppermute(value, both, pairs)

    def moves(d, t):
        return not stays(d, t)

    def rehome(value):
        return jnp.where(here, value, flip(value, 1, 2, moves))

    def near_of(value):
        return flip(value, 0, 1)

    def side_of(value):
        return flip(value, 1, 0)

    rest = jnp.concatenate([w_up, w_down.T, w_output.T], axis=1)
    rest = lax.all_gather(rest, "tensor", axis=0)
    rest_all = lax.all_gather(rest, "dp", axis=1, tiled=True).reshape(GROUP * width, -1)

    packed = rehome(pack_columns(w_query, w_key, w_value, 1))
    packed = order_halves(half, packed, flip(packed, 0, 2))
    for bit in pair_bits:
        packed = order_halves((dp_index >> bit) % 2, packed, flip(packed, 1 << bit, 0))
    w_qkv = insert_zero(packed, 1)

    small = jnp.concatenate(
        [b_query, b_value, b_up, random_blocks.astype(jnp.float32).reshape(-1)]
    )[None]
    small = jnp.concatenate([small, flip(small, 0, 1)], axis=0)
    small = jnp.concatenate([small, flip(small, 0, 2)], axis=0)
    b_up_all = jnp.concatenate(
        [
            lax.dynamic_index_in_dim(small, tensor_index ^ n, 0)[:, 384 : 384 + hidden]
            for n in range(GROUP)
        ],
        axis=1,
    )
    mine = lax.dynamic_index_in_dim(small, tensor_index ^ rank, 0, keepdims=False)
    my_random = mine[384 + hidden :].reshape(HEADS, NB, -1).astype(jnp.int32)

    own = rehome(inputs)
    near = jnp.where(here, flip(inputs, 0, 1, stays), flip(own, 0, 1, moves))
    side = side_of(own)
    far = side_of(near)
    rows = (own, near, side, far)
    cotangent, _ = lax.optimization_barrier((cotangent, near))
    grad_top = rehome(cotangent)

    b_key = jnp.zeros_like(b_query)
    b_qkv = insert_zero(pack_columns(mine[:192], b_key, mine[192:384], 0), 0)
    scale = jnp.concatenate([jnp.ones((KV,), jnp.float32), jnp.full((256,), 0.125, jnp.float32)])
    qkv = [((dot_nn(part, w_qkv) + b_qkv) * scale).astype(jnp.bfloat16) for part in rows]

    block = jnp.arange(NB, dtype=jnp.int32)
    block = block ^ (rank * QB)
    fixed = jnp.clip(
        jnp.stack(
            [
                jnp.zeros_like(block),
                jnp.full_like(block, NB - 1),
                block - 1,
                block,
                block + 1,
            ],
            axis=-1,
        ),
        0,
        NB - 1,
    )
    local_random = jnp.take(my_random, block, axis=1)
    table = jnp.concatenate(
        [jnp.broadcast_to(fixed[None], (HEADS, NB, 5)), local_random], axis=-1
    )
    table = (table ^ (rank * QB)).reshape(-1)

    remote, probs = attend_forward((1, 3), rank, table, qkv, None)
    local, probs = attend_forward((0, 2), rank, table, qkv, probs)
    outs = (
        local[0],
        near_of(remote[0]),
        side_of(local[1]),
        flip(remote[1], 1, 1),
    )

    vectors = jnp.stack([b_output, gain_attn, bias_attn, b_down, gain_mlp, bias_mlp])
    layer_out, n1, g, du, dfr, dar, da, do, sums, up_sums = token_block(
        rank, outs, own, grad_top, vectors, b_up_all, rest_all
    )
    grads = (do[0], near_of(do[1]), side_of(do[2]), flip(do[3], 1, 1))
    rest_grad = weight_block(rank, n1, dfr, dar, g, du, outs)
    rest_grad, *grads = lax.optimization_barrier((rest_grad, *grads))
    rest_sum = lax.psum_scatter(
        rest_grad.reshape(GROUP, width, -1), "dp", scatter_dimension=1, tiled=True
    )
    rest_sum = lax.psum_scatter(rest_sum, "tensor", scatter_dimension=0, tiled=False).astype(
        jnp.float32
    )
    shard_up = rest_sum[:, :hidden]
    shard_down = rest_sum[:, hidden : 2 * hidden].T
    shard_output = rest_sum[:, 2 * hidden :].T
    layer_out = rehome(layer_out)

    grad_qkv = attend_backward(table, probs, qkv, grads)

    def input_part(n):
        return dot_nt(grad_qkv[n * QROWS : (n + 1) * QROWS], w_qkv)

    low = jnp.bfloat16
    side_far = side_of(input_part(3).astype(low))
    side_own = side_of(input_part(2).astype(low))
    to_near = (input_part(1) + side_far.astype(jnp.float32)).astype(low)
    base = da + input_part(0) + side_own.astype(jnp.float32)
    near_move = flip(to_near, 0, 1, moves)
    to_near, near_move = lax.optimization_barrier((to_near, near_move))
    near_stay = flip(to_near, 0, 1, stays)
    grad_move = (base + near_move.astype(jnp.float32)).astype(low)
    grad_stay = (base + near_stay.astype(jnp.float32)).astype(low)
    grad_input = jnp.where(here, grad_stay, flip(grad_move, 1, 2, moves))

    all_rows = jnp.concatenate(rows, axis=0)
    grad_w = drop_zero(dot_tn(all_rows, grad_qkv), 1).astype(low)
    for bit in reversed(pair_bits):
        grad_w = halve(flip, (dp_index >> bit) % 2, grad_w, 1 << bit, 0)
    grad_w = halve(flip, half, grad_w, 0, 2)
    shard_query, shard_key, shard_value = unpack_columns(
        rehome(grad_w).astype(jnp.float32), 1
    )

    bias_sum = drop_zero(jnp.sum(grad_qkv.astype(jnp.float32), axis=0), 0)
    bias_query, _, bias_value = unpack_columns(bias_sum, 0)
    bias_pair = jnp.concatenate([bias_query, bias_value])
    groups = jnp.arange(GROUP, dtype=jnp.int32)[:, None]
    bias_pair = jnp.where(groups == rank, bias_pair[None], 0.0)
    sums = jnp.concatenate(
        [
            jnp.sum(sums, axis=1).reshape(-1),
            jnp.sum(up_sums, axis=0),
            bias_pair.reshape(-1),
        ]
    ).reshape(-1, 128)
    sums = sums + side_of(sums)
    for bit in pair_bits:
        sums = sums + flip(sums, 1 << bit, 0)
    for bit in (1, 2):
        sums = sums + flip(sums, 0, bit)
    sums = sums.reshape(-1)
    top = sums[: 6 * width].reshape(6, width)
    grad_b_up = lax.dynamic_slice_in_dim(sums, 6 * width + tensor_index * hidden, hidden, 0)
    bias_pair = lax.dynamic_slice_in_dim(
        sums, 6 * width + GROUP * hidden + tensor_index * 384, 384, 0
    )
    return (
        layer_out,
        grad_input,
        shard_query,
        shard_key,
        shard_value,
        shard_output,
        shard_up,
        shard_down,
        bias_pair[:192],
        bias_pair[192:],
        top[5],
        top[3],
        top[4],
        grad_b_up,
        top[2],
        top[0],
        top[1],
    )


def order_halves(bit, own, other):
    return jnp.where(
        bit == 0,
        jnp.concatenate([own, other], axis=0),
        jnp.concatenate([other, own], axis=0),
    )


def halve(flip, bit, value, d_bits, t_bits):
    rows = value.shape[0] // 2
    keep = lax.dynamic_slice_in_dim(value, bit * rows, rows, 0)
    send = lax.dynamic_slice_in_dim(value, (1 - bit) * rows, rows, 0)
    got = flip(send, d_bits, t_bits)
    return (keep.astype(jnp.float32) + got.astype(jnp.float32)).astype(value.dtype)


def solution(mesh):
    in_specs = (
        P(("dp", "tensor"), None),
        P(("dp", "tensor"), None),
        P("dp", "tensor"),
        P("dp", "tensor"),
        P("dp", "tensor"),
        P("tensor", "dp"),
        P("dp", "tensor"),
        P("tensor", "dp"),
        P("tensor"),
        P("tensor"),
        P(),
        P(),
        P(),
        P("tensor"),
        P(),
        P(),
        P(),
        P("tensor", None, None),
    )
    out_specs = (
        P(("dp", "tensor"), None),
        P(("dp", "tensor"), None),
        P("dp", "tensor"),
        P("dp", "tensor"),
        P("dp", "tensor"),
        P("tensor", "dp"),
        P("dp", "tensor"),
        P("tensor", "dp"),
        P("tensor"),
        P("tensor"),
        P(),
        P(),
        P(),
        P("tensor"),
        P(),
        P(),
        P(),
    )
    body = functools.partial(per_device, mesh.shape["dp"], mesh.shape["tensor"])
    return jax.shard_map(body, mesh=mesh, in_specs=in_specs, out_specs=out_specs, check_vma=False)
```

time: 723 us -> 473 us (0.65)
  blocking collectives: 121 us -> 0 us
  matrix products: 111 us -> 35.1 us
  local copies, waits for them, and re-layouts: 86.9 us -> 18.2 us
  Pallas kernels: 152 us -> 122 us
  waiting for transfers between devices: 163 us -> 193 us
  starting transfers between devices: 30.1 us -> 57.1 us
  other arithmetic: 33.9 us -> 25.4 us
    psum x1 -> x0, blocking collectives: 68.2 us -> none  [per_device(): lax.psum(jnp.where(groups[:, :, 0] == rank, bias_pair[None], 0.0), both)]
    unnamed x1 -> x0, blocking collectives: 52.5 us -> none
    reduce_scatter x2, waiting for transfers between devices: 48.6 us -> 0.02 us  [the longest x1 0.02 us: per_device(): lax.psum_scatter(rest_grad.reshape(GROUP, width, -1), 'dp', scatter_dimen...]
    ppermute x17 -> x33, waiting for transfers between devices: 114 us -> 157 us  [flip(): return lax.ppermute(value, both, pairs)]
    all_gather x2, waiting for transfers between devices: 0.02 us -> 35.3 us  [the longest x1 35.3 us: per_device(): rest = lax.all_gather(rest, 'tensor', axis=0)]
    pallas_call x1, Pallas kernels: 66.4 us -> 35.2 us  [attend_backward(): pl.pallas_call(functools.partial(backward_kernel, steps), grid_spec=pltpu...]
    dot_general x7 -> x4, matrix products: 42.3 us -> 14.6 us  [dot_nn(): return jnp.dot(left, right, preferred_element_type=jnp.float32)]
    ppermute x17 -> x33, starting transfers between devices: 29.9 us -> 57 us  [flip(): return lax.ppermute(value, both, pairs)]
  transfers between devices with their start and end apart: 21 -> 37, of which waited for: 5 -> 14; matrix products, arithmetic and copies ran while one was open for 24% -> 15% of each run, Pallas kernels for 12% -> 17%
where the time goes in v2:
time: 473 us; the launch traced here: 466 us
  waiting for transfers between devices  193 us (41%)
  Pallas kernels  122 us (26%)
  starting transfers between devices  57.1 us (12%)
  matrix products  35.1 us (7%)
  other arithmetic  25.4 us (5%)
  local copies, waits for them, and re-layouts  18.2 us (4%)
  between operations  15.3 us (3%)
    ppermute x33, waiting for transfers between devices, flip(): return lax.ppermute(value, both, pairs)  157 us
    ppermute x33, starting transfers between devices, flip(): return lax.ppermute(value, both, pairs)  57 us
    pallas_call x1, Pallas kernels, token_block(): pl.pallas_call(functools.partial(token_kernel, tile, width, hidden), grid...  40.6 us
    all_gather x1, waiting for transfers between devices, per_device(): rest = lax.all_gather(rest, 'tensor', axis=0)  35.3 us
    pallas_call x1, Pallas kernels, attend_backward(): pl.pallas_call(functools.partial(backward_kernel, steps), grid_spec=pltpu...  35.2 us
    pallas_call x2, Pallas kernels, attend_forward(): pl.pallas_call(functools.partial(forward_kernel, steps, probs is None), g...  26.5 us
    pallas_call x1, Pallas kernels, weight_block(): pl.pallas_call(functools.partial(weight_kernel, width, hidden), grid_spec...  19.6 us
    dot_general x4, matrix products, dot_nn(): return jnp.dot(left, right, preferred_element_type=jnp.float32)  14.6 us
  transfers between devices with their start and end apart: 37, of which 14 were waited for; matrix products, arithmetic and copies ran while one was open for 15% of the time, Pallas kernels for 17%

profile of v2, /device:TPU:1, one launch (start us, length us, event | category | flops | bytes accessed | tf_op | source)
XLA Modules:
  0.0 465.6 jit_solution(3128731791072120568)
XLA Ops:
  8.4 1.7 pad_maximum_fusion.1
  10.2 35.3 %all-gather.6.cloned.1.call-done = bf16[384,1728]{1,0:T(8,128)(2,1)} async-done(((bf16[96,1728]{1,0:T(8,128)(2,1)}), bf16[384,1728]{1,0:T(8,128)(2,1)}) %all-gather.6.cloned.1.call-update) | async-done | bytes 1327120 | tf_op jit(solution)/shard_map/all_gather | solution.py:640
  45.6 4.2 collective-permute-start.2
  49.9 1.8 collective-permute-start.7
  52.7 2.2 collective-permute-start.3
  57.2 27.8 %collective-permute-done.2 = bf16[1024,768]{1,0:T(8,128)(2,1)S(1)} collective-permute-done((bf16[1024,768]{1,0:T(8,128)(2,1)}, bf16[1024,768]{1,0:T(8,128)(2,1)S(1)}, u32[]{:S(2)}, u32[]{:S(2)}) %collective-permute-start.2) | collective-permute-done | bytes 1572896 | tf_op jit(solution)/shard_map/ppermute | solution.py:625
  85.2 3.0 collective-permute-start.8
  88.9 2.4 collective-permute-start.1
  91.3 17.5 %collective-permute-done.4 = bf16[96,576]{0,1:T(8,128)(2,1)S(1)} collective-permute-done((bf16[96,576]{0,1:T(8,128)(2,1)S(1)}, bf16[96,576]{0,1:T(8,128)(2,1)S(1)}, u32[]{:S(2)}, u32[]{:S(2)}) %collective-permute-start.4) | collective-permute-done | bytes 110624 | tf_op jit(solution)/shard_map/ppermute | solution.py:625
  111.4 5.6 %collective-permute-done.5 = bf16[192,576]{0,1:T(8,128)(2,1)S(1)} collective-permute-done((bf16[192,576]{0,1:T(8,128)(2,1)S(1)}, bf16[192,576]{0,1:T(8,128)(2,1)S(1)}, u32[]{:S(2)}, u32[]{:S(2)}) %collective-permute-start.5) | collective-permute-done | bytes 221216 | tf_op jit(solution)/shard_map/ppermute | solution.py:625
  118.7 2.7 broadcast_select_fusion.2
  124.9 2.6 multiply_convert_fusion.3.refs_0_.qkv0
  127.6 2.6 collective-permute-start.14
  130.1 4.0 multiply_convert_fusion.2.refs_1_.qkv1
  134.1 4.0 multiply_convert_fusion.1.refs_2_.qkv2
  138.1 4.0 multiply_convert_fusion.refs_3_.qkv3
  142.1 13.3 %attend_forward.2 = (bf16[2,1024,192]{2,1,0:T(8,128)(2,1)}, bf16[64,3,64,512]{3,2,1,0:T(8,128)(2,1)}) custom-call(s32[1536]{0:T(1024)} %xor.66.table, s32[3]{0:T(128)} %get-tuple-element.155.place, bf16[1024,640]{1,0:T(8,128)(2,1)} %multiply_convert_fusion.3.refs_0_.qkv0, bf16[1024,640]{1,0:T(8,128)(2,1)} %multiply_convert_fusion.2.refs_1_.qkv1, ...), custom_call_target="tpu_custom_call" | custom-call | tf_op jit(solution)/shard_map/attend_forward/pallas_call | solution.py:136
  155.5 13.2 %attend_forward.3 = (bf16[2,1024,192]{2,1,0:T(8,128)(2,1)}, bf16[64,3,64,512]{3,2,1,0:T(8,128)(2,1)}) custom-call(s32[1536]{0:T(1024)} %xor.66.table, s32[3]{0:T(128)} %get-tuple-element.154.place, bf16[1024,640]{1,0:T(8,128)(2,1)} %multiply_convert_fusion.3.refs_0_.qkv0, ...), custom_call_target="tpu_custom_call", output_to_operand_aliasing={{1}: (6, {})} | custom-call | tf_op jit(solution)/shard_map/attend_forward/pallas_call | solution.py:136
  168.7 2.2 slice_bitcast_fusion.5
  170.9 4.2 collective-permute-start.11
  177.4 9.5 %collective-permute-done.11.o1 = bf16[1024,192]{1,0:T(8,128)(2,1)S(1)} collective-permute-done((bf16[1024,192]{1,0:T(8,128)(2,1)S(1)}, bf16[1024,192]{1,0:T(8,128)(2,1)S(1)}, u32[]{:S(2)}, u32[]{:S(2)}) %collective-permute-start.11) | collective-permute-done | bytes 393248 | tf_op jit(solution)/shard_map/ppermute | solution.py:625
  186.9 11.6 %collective-permute-done.13.o3 = bf16[1024,192]{1,0:T(8,128)(2,1)S(1)} collective-permute-done((bf16[1024,192]{1,0:T(8,128)(2,1)S(1)}, bf16[1024,192]{1,0:T(8,128)(2,1)S(1)}, u32[]{:S(2)}, u32[]{:S(2)}) %collective-permute-start.13) | collective-permute-done | bytes 393248 | tf_op jit(solution)/shard_map/ppermute | solution.py:625
  199.3 40.6 %token_block.1 = (bf16[1024,768]{1,0:T(8,128)(2,1)}, bf16[1024,768]{1,0:T(8,128)(2,1)}, bf16[1024,3072]{1,0:T(8,128)(2,1)}, bf16[1024,3072]{1,0:T(8,128)(2,1)}, ...) custom-call(s32[1]{0:T(128)} %bitcast.rank_ref, ...), custom_call_target="tpu_custom_call" | custom-call | tf_op jit(solution)/shard_map/token_block/pallas_call | solution.py:442
  239.9 2.4 slice_bitcast_fusion
  242.3 1.5 collective-permute-start.16
  244.2 19.6 %weight_block.1 = bf16[3072,1728]{1,0:T(8,128)(2,1)} custom-call(s32[1]{0:T(128)} %bitcast.rank_ref, bf16[1024,768]{1,0:T(8,128)(2,1)} %get-tuple-element.46.n1, bf16[1024,768]{1,0:T(8,128)(2,1)} %get-tuple-element.47.dfr, bf16[1024,768]{1,0:T(8,128)(2,1)} %get-tuple-element.48.dar, bf16[1024,3072]{1,0:T(8,128)(2,1)} %get-tuple-element.49.g, ...), custom_call_target="tpu_custom_call" | custom-call | tf_op jit(solution)/shard_map/weight_block/pallas_call | solution.py:519
  263.8 3.4 collective-permute-done.18.do3
  268.4 35.2 %attend_backward.1 = bf16[4096,640]{1,0:T(8,128)(2,1)} custom-call(s32[1536]{0:T(1024)} %xor.66.table, bf16[64,3,64,512]{3,2,1,0:T(8,128)(2,1)} %get-tuple-element.45.p_ref, bf16[1024,640]{1,0:T(8,128)(2,1)} %multiply_convert_fusion.3.refs_0_.qkv0, bf16[1024,640]{1,0:T(8,128)(2,1)} %multiply_convert_fusion.2.refs_1_.qkv1, ...), custom_call_target="tpu_custom_call" | custom-call | tf_op jit(solution)/shard_map/attend_backward/pallas_call | solution.py:249
  303.6 3.4 convert_reduce_fusion
  308.0 3.1 convolution_convert_fusion
  311.2 7.5 %fusion.9 = bf16[768,640]{0,1:T(8,128)(2,1)S(1)} fusion(bf16[4096,640]{1,0:T(8,128)(2,1)S(1)} %bitcast.71, bf16[1024,768]{1,0:T(8,128)(2,1)} %collective-permute-done.10, bf16[1024,768]{1,0:T(8,128)(2,1)} %collective-permute-done.9, bf16[1024,768]{1,0:T(8,128)(2,1)} %broadcast_select_fusion.2, bf16[1024,768]{1,0:T(8,128)(2,1)S(1)} %copy-done.3), kind=kOutput, calls=%fused_computation.25 | convolution fusion | flops 4052189184 | bytes 12517376 | tf_op jit(solution)/shard_map/dot_general | solution.py:33
  320.3 2.6 collective-permute-done.29
  324.1 2.7 add_convert_fusion.2
  326.7 3.5 collective-permute-start.21
  330.2 2.7 convolution_convert_fusion.1
  332.9 1.4 collective-permute-done.30
  335.4 5.3 %collective-permute-start.15 = (bf16[1024,768]{1,0:T(8,128)(2,1)}, bf16[1024,768]{1,0:T(8,128)(2,1)}, u32[]{:S(2)}, u32[]{:S(2)}) collective-permute-start(bf16[1024,768]{1,0:T(8,128)(2,1)} %get-tuple-element.43), channel_id=1, source_target_pairs={{2,4},{3,5},{4,2},{5,3},{10,12},{11,13},{12,10},{13,11},{18,20},{1... | collective-permute-start | bytes 4718600 | tf_op jit(solution)/shard_map/ppermute | solution.py:625
  340.7 16.0 %collective-permute-done.31 = f32[72,128]{1,0:T(8,128)S(1)} collective-permute-done((f32[72,128]{1,0:T(8,128)S(1)}, f32[72,128]{1,0:T(8,128)S(1)}, u32[]{:S(2)}, u32[]{:S(2)}) %collective-permute-start.31) | collective-permute-done | bytes 36896 | tf_op jit(solution)/shard_map/ppermute | solution.py:625
  357.1 4.4 fusion.18
  361.5 6.6 %collective-permute-done.32 = f32[72,128]{1,0:T(8,128)S(1)} collective-permute-done((f32[72,128]{1,0:T(8,128)S(1)}, f32[72,128]{1,0:T(8,128)S(1)}, u32[]{:S(2)}, u32[]{:S(2)}) %collective-permute-start.32) | collective-permute-done | bytes 36896 | tf_op jit(solution)/shard_map/ppermute | solution.py:625
  370.2 6.5 %collective-permute-done.26 = bf16[96,576]{0,1:T(8,128)(2,1)S(1)} collective-permute-done((bf16[96,576]{0,1:T(8,128)(2,1)S(1)}, bf16[96,576]{0,1:T(8,128)(2,1)S(1)}, u32[]{:S(2)}, u32[]{:S(2)}) %collective-permute-start.26) | collective-permute-done | bytes 110624 | tf_op jit(solution)/shard_map/ppermute | solution.py:625
  376.8 12.5 %collective-permute-start.27 = (bf16[96,576]{0,1:T(8,128)(2,1)S(1)}, bf16[96,576]{0,1:T(8,128)(2,1)S(1)}, u32[]{:S(2)}, u32[]{:S(2)}) collective-permute-start(bf16[96,576]{0,1:T(8,128)(2,1)S(1)} %add_convert_fusion.5), channel_id=1, source_target_pairs={{2,4},{3,5},{4,2},{5,3},{10,12},{11,13},{12,10},{13,11},{18,20},{1... | collective-permute-start | bytes 331784 | tf_op jit(solution)/shard_map/ppermute | solution.py:625
  389.4 4.6 add_convert_fusion
  394.0 1.9 collective-permute-start.23
  395.9 1.8 collective-permute-start.22
  401.3 2.9 broadcast_select_fusion
  404.2 47.4 %collective-permute-done.23 = bf16[1024,768]{1,0:T(8,128)(2,1)} collective-permute-done((bf16[1024,768]{1,0:T(8,128)(2,1)}, bf16[1024,768]{1,0:T(8,128)(2,1)}, u32[]{:S(2)}, u32[]{:S(2)}) %collective-permute-start.23) | collective-permute-done | bytes 1572896 | tf_op jit(solution)/shard_map/ppermute | solution.py:625
  451.6 4.4 fusion.8
  (225 shorter events, 31.0 us)
Async XLA Ops:
  7.2 47.7 %copy-start.16 = (s32[3,64,3]{1,2,0:T(4,128)S(1)}, s32[3,64,3]{1,2,0:T(4,128)}, u32[]{:S(2)}) copy-start(s32[3,64,3]{1,2,0:T(4,128)} %param.35) | copy-start | bytes 6916
  7.3 48.0 %copy-start.24 = (f32[192]{0:T(256)S(1)}, f32[192]{0:T(256)}, u32[]{:S(2)}) copy-start(f32[192]{0:T(256)} %param.26) | copy-start | bytes 2308
  7.3 48.0 %copy-start.25 = (f32[192]{0:T(256)S(1)}, f32[192]{0:T(256)}, u32[]{:S(2)}) copy-start(f32[192]{0:T(256)} %param.27) | copy-start | bytes 2308
  7.3 48.0 %copy-start.23 = (f32[768]{0:T(1024)S(1)}, f32[768]{0:T(1024)}, u32[]{:S(2)}) copy-start(f32[768]{0:T(1024)} %param.31) | copy-start | bytes 9220
  7.3 49.1 %copy-start.17 = (f32[768]{0:T(1024)S(1)}, f32[768]{0:T(1024)}, u32[]{:S(2)}) copy-start(f32[768]{0:T(1024)} %param.28) | copy-start | bytes 9220
  7.3 49.0 %copy-start.18 = (f32[768]{0:T(1024)S(1)}, f32[768]{0:T(1024)}, u32[]{:S(2)}) copy-start(f32[768]{0:T(1024)} %param.29) | copy-start | bytes 9220
  7.3 49.1 %copy-start.19 = (f32[768]{0:T(1024)S(1)}, f32[768]{0:T(1024)}, u32[]{:S(2)}) copy-start(f32[768]{0:T(1024)} %param.30) | copy-start | bytes 9220
  7.3 49.1 %copy-start.20 = (f32[768]{0:T(1024)S(1)}, f32[768]{0:T(1024)}, u32[]{:S(2)}) copy-start(f32[768]{0:T(1024)} %param.32) | copy-start | bytes 9220
  7.3 49.1 %copy-start.21 = (f32[768]{0:T(1024)S(1)}, f32[768]{0:T(1024)}, u32[]{:S(2)}) copy-start(f32[768]{0:T(1024)} %param.33) | copy-start | bytes 9220
  7.3 49.1 %copy-start.22 = (f32[768]{0:T(1024)S(1)}, f32[768]{0:T(1024)}, u32[]{:S(2)}) copy-start(f32[768]{0:T(1024)} %param.34) | copy-start | bytes 9220
  7.3 38.2 %all-gather.6.cloned.1.call-start = ((), (), s32[]{:S(2)}) async-start(), calls=%async_computation.5 | async-start | bytes 1720320 | tf_op jit(solution)/shard_map/all_gather | solution.py:640
  10.2 188.3 %all-gather.4.cloned.1.call-start = ((), (), s32[]{:S(2)}) async-start(), calls=%async_computation.2 | async-start | bytes 12386304 | tf_op jit(solution)/shard_map/all_gather | solution.py:641
  45.6 343.7 %reduce-scatter.3.cloned.1.call-start = ((), (), s32[]{:S(2)}) async-start(), calls=%async_computation.3 | async-start | bytes 12386304 | tf_op jit(solution)/shard_map/reduce_scatter | solution.py:715
  45.6 39.4 %collective-permute-start.2 = (bf16[1024,768]{1,0:T(8,128)(2,1)}, bf16[1024,768]{1,0:T(8,128)(2,1)S(1)}, u32[]{:S(2)}, u32[]{:S(2)}) collective-permute-start(bf16[1024,768]{1,0:T(8,128)(2,1)} %param.18), channel_id=1, source_target_pairs={{2,4},{3,5},{4,2},{5,3},{10,12},{11,13},{12,10},{13,11},{18,20},{1... | collective-permute-start | bytes 4718600 | tf_op jit(solution)/shard_map/ppermute | solution.py:625
  49.9 68.8 %collective-permute-start.7 = (bf16[1024,768]{1,0:T(8,128)(2,1)}, bf16[1024,768]{1,0:T(8,128)(2,1)}, u32[]{:S(2)}, u32[]{:S(2)}) collective-permute-start(bf16[1024,768]{1,0:T(8,128)(2,1)} %param.18), channel_id=1, source_target_pairs={{0,1},{1,0},{6,7},{7,6},{8,9},{9,8},{14,15},{15,14},{16,17},{17,16... | collective-permute-start | bytes 4718600 | tf_op jit(solution)/shard_map/ppermute | solution.py:625
  52.7 36.0 %collective-permute-start.3 = (bf16[96,576]{0,1:T(8,128)(2,1)S(1)}, bf16[96,576]{0,1:T(8,128)(2,1)S(1)}, u32[]{:S(2)}, u32[]{:S(2)}) collective-permute-start(bf16[96,576]{0,1:T(8,128)(2,1)S(1)} %constant_dynamic-update-slice_fusion), channel_id=1, source_target_pairs={{2,4},{3,5},{4,2},{5,3},{10,12},{11,13},{12,10},{13,11},{18,20},{1... | collective-permute-start | bytes 331784 | tf_op jit(solution)/shard_map/ppermute | solution.py:625
  55.4 33.5 %collective-permute-start = (f32[1,1728]{1,0:T(1,128)S(1)}, f32[1,1728]{1,0:T(1,128)S(1)}, u32[]{:S(2)}, u32[]{:S(2)}) collective-permute-start(f32[1,1728]{1,0:T(1,128)S(1)} %broadcast_in_dim.50), channel_id=1, source_target_pairs={{0,1},{1,0},{2,3},{3,2},{4,5},{5,4},{6,7},{7,6},{8,9},{9,8},{10,11... | collective-permute-start | bytes 20744 | tf_op jit(solution)/shard_map/ppermute | solution.py:625
  85.2 33.5 %collective-permute-start.8 = (bf16[1024,768]{1,0:T(8,128)(2,1)S(1)}, bf16[1024,768]{1,0:T(8,128)(2,1)}, u32[]{:S(2)}, u32[]{:S(2)}) collective-permute-start(bf16[1024,768]{1,0:T(8,128)(2,1)S(1)} %broadcast_select_fusion.3.x_ref), channel_id=1, source_target_pairs={{2,3},{3,2},{4,5},{5,4},{10,11},{11,10},{12,13},{13,12},{18,19},{1... | collective-permute-start | bytes 4718600 | tf_op jit(solution)/shard_map/ppermute | solution.py:625
  88.8 20.0 %collective-permute-start.4 = (bf16[96,576]{0,1:T(8,128)(2,1)S(1)}, bf16[96,576]{0,1:T(8,128)(2,1)S(1)}, u32[]{:S(2)}, u32[]{:S(2)}) collective-permute-start(bf16[96,576]{0,1:T(8,128)(2,1)S(1)} %broadcast_select_fusion.4), channel_id=1, source_target_pairs={{0,2},{1,3},{2,0},{3,1},{4,6},{5,7},{6,4},{7,5},{8,10},{9,11},{10,... | collective-permute-start | bytes 331784 | tf_op jit(solution)/shard_map/ppermute | solution.py:625
  88.9 21.4 %collective-permute-start.1 = (f32[2,1728]{1,0:T(2,128)S(1)}, f32[2,1728]{1,0:T(2,128)S(1)}, u32[]{:S(2)}, u32[]{:S(2)}) collective-permute-start(f32[2,1728]{1,0:T(2,128)S(1)} %pad_maximum_fusion.6), channel_id=1, source_target_pairs={{0,2},{1,3},{2,0},{3,1},{4,6},{5,7},{6,4},{7,5},{8,10},{9,11},{10,... | collective-permute-start | bytes 41480 | tf_op jit(solution)/shard_map/ppermute | solution.py:625
  109.1 8.0 %collective-permute-start.5 = (bf16[192,576]{0,1:T(8,128)(2,1)S(1)}, bf16[192,576]{0,1:T(8,128)(2,1)S(1)}, u32[]{:S(2)}, u32[]{:S(2)}) collective-permute-start(bf16[192,576]{0,1:T(8,128)(2,1)S(1)} %maximum_select_fusion.2), channel_id=1, source_target_pairs={{0,8},{1,9},{2,10},{3,11},{4,12},{5,13},{6,14},{7,15},{8,0},{9,1},... | collective-permute-start | bytes 663560 | tf_op jit(solution)/shard_map/ppermute | solution.py:625
  117.4 7.2 %collective-permute-start.6 = (bf16[384,576]{0,1:T(8,128)(2,1)S(1)}, bf16[384,576]{0,1:T(8,128)(2,1)S(1)}, u32[]{:S(2)}, u32[]{:S(2)}) collective-permute-start(bf16[384,576]{0,1:T(8,128)(2,1)S(1)} %maximum_select_fusion.1), channel_id=1, source_target_pairs={{0,16},{1,17},{2,18},{3,19},{4,20},{5,21},{6,22},{7,23},{8,24},{9,... | collective-permute-start | bytes 1327112 | tf_op jit(solution)/shard_map/ppermute | solution.py:625
  118.7 15.4 %collective-permute-start.9 = (bf16[1024,768]{1,0:T(8,128)(2,1)S(1)}, bf16[1024,768]{1,0:T(8,128)(2,1)}, u32[]{:S(2)}, u32[]{:S(2)}) collective-permute-start(bf16[1024,768]{1,0:T(8,128)(2,1)S(1)} %broadcast_select_fusion.3.x_ref), channel_id=1, source_target_pairs={{0,4},{1,5},{2,6},{3,7},{4,0},{5,1},{6,2},{7,3},{8,12},{9,13},{10,... | collective-permute-start | bytes 4718600 | tf_op jit(solution)/shard_map/ppermute | solution.py:625
  121.4 16.7 %collective-permute-start.10 = (bf16[1024,768]{1,0:T(8,128)(2,1)}, bf16[1024,768]{1,0:T(8,128)(2,1)}, u32[]{:S(2)}, u32[]{:S(2)}) collective-permute-start(bf16[1024,768]{1,0:T(8,128)(2,1)} %broadcast_select_fusion.2), channel_id=1, source_target_pairs={{0,4},{1,5},{2,6},{3,7},{4,0},{5,1},{6,2},{7,3},{8,12},{9,13},{10,... | collective-permute-start | bytes 4718600 | tf_op jit(solution)/shard_map/ppermute | solution.py:625
  127.6 48.6 %collective-permute-start.14 = (bf16[1024,768]{1,0:T(8,128)(2,1)S(1)}, bf16[1024,768]{1,0:T(8,128)(2,1)S(1)}, u32[]{:S(2)}, u32[]{:S(2)}) collective-permute-start(bf16[1024,768]{1,0:T(8,128)(2,1)S(1)} %copy-done.7), channel_id=1, source_target_pairs={{2,4},{3,5},{4,2},{5,3},{10,12},{11,13},{12,10},{13,11},{18,20},{1... | collective-permute-start | bytes 4718600 | tf_op jit(solution)/shard_map/ppermute | solution.py:625
  170.8 6.6 %collective-permute-start.12 = (bf16[1024,192]{1,0:T(8,128)(2,1)S(1)}, bf16[1024,192]{1,0:T(8,128)(2,1)S(1)}, u32[]{:S(2)}, u32[]{:S(2)}) collective-permute-start(bf16[1024,192]{1,0:T(8,128)(2,1)S(1)} %get-tuple-element.118), channel_id=1, source_target_pairs={{0,4},{1,5},{2,6},{3,7},{4,0},{5,1},{6,2},{7,3},{8,12},{9,13},{10,... | collective-permute-start | bytes 1179656 | tf_op jit(solution)/shard_map/ppermute | solution.py:625
  170.9 16.0 %collective-permute-start.11 = (bf16[1024,192]{1,0:T(8,128)(2,1)S(1)}, bf16[1024,192]{1,0:T(8,128)(2,1)S(1)}, u32[]{:S(2)}, u32[]{:S(2)}) collective-permute-start(bf16[1024,192]{1,0:T(8,128)(2,1)S(1)} %get-tuple-element.117), channel_id=1, source_target_pairs={{0,1},{1,0},{2,3},{3,2},{4,5},{5,4},{6,7},{7,6},{8,9},{9,8},{10,11... | collective-permute-start | bytes 1179656 | tf_op jit(solution)/shard_map/ppermute | solution.py:625
  175.1 23.4 %collective-permute-start.13 = (bf16[1024,192]{1,0:T(8,128)(2,1)S(1)}, bf16[1024,192]{1,0:T(8,128)(2,1)S(1)}, u32[]{:S(2)}, u32[]{:S(2)}) collective-permute-start(bf16[1024,192]{1,0:T(8,128)(2,1)S(1)} %get-tuple-element.116), channel_id=1, source_target_pairs={{0,5},{1,4},{2,7},{3,6},{4,1},{5,0},{6,3},{7,2},{8,13},{9,12},{10,... | collective-permute-start | bytes 1179656 | tf_op jit(solution)/shard_map/ppermute | solution.py:625
  242.3 21.5 %collective-permute-start.16 = (bf16[1024,192]{1,0:T(8,128)(2,1)S(1)}, bf16[1024,192]{1,0:T(8,128)(2,1)S(1)}, u32[]{:S(2)}, u32[]{:S(2)}) collective-permute-start(bf16[1024,192]{1,0:T(8,128)(2,1)S(1)} %get-tuple-element.114), channel_id=1, source_target_pairs={{0,1},{1,0},{2,3},{3,2},{4,5},{5,4},{6,7},{7,6},{8,9},{9,8},{10,11... | collective-permute-start | bytes 1179656 | tf_op jit(solution)/shard_map/ppermute | solution.py:625
  243.8 20.0 %collective-permute-start.17 = (bf16[1024,192]{1,0:T(8,128)(2,1)S(1)}, bf16[1024,192]{1,0:T(8,128)(2,1)S(1)}, u32[]{:S(2)}, u32[]{:S(2)}) collective-permute-start(bf16[1024,192]{1,0:T(8,128)(2,1)S(1)} %get-tuple-element.113), channel_id=1, source_target_pairs={{0,4},{1,5},{2,6},{3,7},{4,0},{5,1},{6,2},{7,3},{8,12},{9,13},{10,... | collective-permute-start | bytes 1179656 | tf_op jit(solution)/shard_map/ppermute | solution.py:625
  243.8 23.4 %collective-permute-start.18 = (bf16[1024,192]{1,0:T(8,128)(2,1)S(1)}, bf16[1024,192]{1,0:T(8,128)(2,1)S(1)}, u32[]{:S(2)}, u32[]{:S(2)}) collective-permute-start(bf16[1024,192]{1,0:T(8,128)(2,1)S(1)} %get-tuple-element.112), channel_id=1, source_target_pairs={{0,5},{1,4},{2,7},{3,6},{4,1},{5,0},{6,3},{7,2},{8,13},{9,12},{10,... | collective-permute-start | bytes 1179656 | tf_op jit(solution)/shard_map/ppermute | solution.py:625
  268.0 188.0 %reduce-scatter.5.cloned.1.call-start = ((), (), s32[]{:S(2)}) async-start(), calls=%async_computation.4 | async-start | bytes 1720320 | tf_op jit(solution)/shard_map/reduce_scatter | solution.py:718
  307.4 11.4 %collective-permute-start.28 = (f32[72,128]{1,0:T(8,128)S(1)}, f32[72,128]{1,0:T(8,128)S(1)}, u32[]{:S(2)}, u32[]{:S(2)}) collective-permute-start(f32[72,128]{1,0:T(8,128)S(1)} %maximum_bitcast_fusion), channel_id=1, source_target_pairs={{0,4},{1,5},{2,6},{3,7},{4,0},{5,1},{6,2},{7,3},{8,12},{9,13},{10,... | collective-permute-start | bytes 110600 | tf_op jit(solution)/shard_map/ppermute | solution.py:625
  311.1 13.0 %collective-permute-start.20 = (bf16[1024,768]{1,0:T(8,128)(2,1)S(1)}, bf16[1024,768]{1,0:T(8,128)(2,1)S(1)}, u32[]{:S(2)}, u32[]{:S(2)}) collective-permute-start(bf16[1024,768]{1,0:T(8,128)(2,1)S(1)} %convolution_convert_fusion), channel_id=1, source_target_pairs={{0,4},{1,5},{2,6},{3,7},{4,0},{5,1},{6,2},{7,3},{8,12},{9,13},{10,... | collective-permute-start | bytes 4718600 | tf_op jit(solution)/shard_map/ppermute | solution.py:625
  318.9 4.1 collective-permute-start.29
  319.4 37.3 %collective-permute-start.24 = (bf16[384,576]{0,1:T(8,128)(2,1)S(1)}, bf16[384,576]{0,1:T(8,128)(2,1)S(1)}, u32[]{:S(2)}, u32[]{:S(2)}) collective-permute-start(bf16[384,576]{0,1:T(8,128)(2,1)S(1)} %fusion.20), channel_id=1, source_target_pairs={{0,16},{1,17},{2,18},{3,19},{4,20},{5,21},{6,22},{7,23},{8,24},{9,... | collective-permute-start | bytes 1327112 | tf_op jit(solution)/shard_map/ppermute | solution.py:625
  323.0 11.3 %collective-permute-start.30 = (f32[72,128]{1,0:T(8,128)S(1)}, f32[72,128]{1,0:T(8,128)S(1)}, u32[]{:S(2)}, u32[]{:S(2)}) collective-permute-start(f32[72,128]{1,0:T(8,128)S(1)} %fusion.38), channel_id=1, source_target_pairs={{0,16},{1,17},{2,18},{3,19},{4,20},{5,21},{6,22},{7,23},{8,24},{9,... | collective-permute-start | bytes 110600 | tf_op jit(solution)/shard_map/ppermute | solution.py:625
  326.7 62.5 %collective-permute-start.21 = (bf16[1024,768]{1,0:T(8,128)(2,1)}, bf16[1024,768]{1,0:T(8,128)(2,1)}, u32[]{:S(2)}, u32[]{:S(2)}) collective-permute-start(bf16[1024,768]{1,0:T(8,128)(2,1)} %add_convert_fusion.2), channel_id=1, source_target_pairs={{2,3},{3,2},{4,5},{5,4},{10,11},{11,10},{12,13},{13,12},{18,19},{1... | collective-permute-start | bytes 4718600 | tf_op jit(solution)/shard_map/ppermute | solution.py:625
  332.9 56.5 %collective-permute-start.19 = (bf16[1024,768]{1,0:T(8,128)(2,1)}, bf16[1024,768]{1,0:T(8,128)(2,1)}, u32[]{:S(2)}, u32[]{:S(2)}) collective-permute-start(bf16[1024,768]{1,0:T(8,128)(2,1)} %convolution_convert_fusion.1), channel_id=1, source_target_pairs={{0,4},{1,5},{2,6},{3,7},{4,0},{5,1},{6,2},{7,3},{8,12},{9,13},{10,... | collective-permute-start | bytes 4718600 | tf_op jit(solution)/shard_map/ppermute | solution.py:625
  334.3 22.4 %collective-permute-start.31 = (f32[72,128]{1,0:T(8,128)S(1)}, f32[72,128]{1,0:T(8,128)S(1)}, u32[]{:S(2)}, u32[]{:S(2)}) collective-permute-start(f32[72,128]{1,0:T(8,128)S(1)} %add.212), channel_id=1, source_target_pairs={{0,1},{1,0},{2,3},{3,2},{4,5},{5,4},{6,7},{7,6},{8,9},{9,8},{10,11... | collective-permute-start | bytes 110600 | tf_op jit(solution)/shard_map/ppermute | solution.py:625
  335.4 65.9 %collective-permute-start.15 = (bf16[1024,768]{1,0:T(8,128)(2,1)}, bf16[1024,768]{1,0:T(8,128)(2,1)}, u32[]{:S(2)}, u32[]{:S(2)}) collective-permute-start(bf16[1024,768]{1,0:T(8,128)(2,1)} %get-tuple-element.43), channel_id=1, source_target_pairs={{2,4},{3,5},{4,2},{5,3},{10,12},{11,13},{12,10},{13,11},{18,20},{1... | collective-permute-start | bytes 4718600 | tf_op jit(solution)/shard_map/ppermute | solution.py:625
  356.7 11.5 %collective-permute-start.32 = (f32[72,128]{1,0:T(8,128)S(1)}, f32[72,128]{1,0:T(8,128)S(1)}, u32[]{:S(2)}, u32[]{:S(2)}) collective-permute-start(f32[72,128]{1,0:T(8,128)S(1)} %add.213), channel_id=1, source_target_pairs={{0,2},{1,3},{2,0},{3,1},{4,6},{5,7},{6,4},{7,5},{8,10},{9,11},{10,... | collective-permute-start | bytes 110600 | tf_op jit(solution)/shard_map/ppermute | solution.py:625
  357.0 11.2 %collective-permute-start.25 = (bf16[192,576]{0,1:T(8,128)(2,1)S(1)}, bf16[192,576]{0,1:T(8,128)(2,1)S(1)}, u32[]{:S(2)}, u32[]{:S(2)}) collective-permute-start(bf16[192,576]{0,1:T(8,128)(2,1)S(1)} %constant_dynamic-slice_fusion.1), channel_id=1, source_target_pairs={{0,8},{1,9},{2,10},{3,11},{4,12},{5,13},{6,14},{7,15},{8,0},{9,1},... | collective-permute-start | bytes 663560 | tf_op jit(solution)/shard_map/ppermute | solution.py:625
  368.5 8.2 %collective-permute-start.26 = (bf16[96,576]{0,1:T(8,128)(2,1)S(1)}, bf16[96,576]{0,1:T(8,128)(2,1)S(1)}, u32[]{:S(2)}, u32[]{:S(2)}) collective-permute-start(bf16[96,576]{0,1:T(8,128)(2,1)S(1)} %constant_dynamic-slice_fusion), channel_id=1, source_target_pairs={{0,2},{1,3},{2,0},{3,1},{4,6},{5,7},{6,4},{7,5},{8,10},{9,11},{10,... | collective-permute-start | bytes 331784 | tf_op jit(solution)/shard_map/ppermute | solution.py:625
  376.8 22.3 %collective-permute-start.27 = (bf16[96,576]{0,1:T(8,128)(2,1)S(1)}, bf16[96,576]{0,1:T(8,128)(2,1)S(1)}, u32[]{:S(2)}, u32[]{:S(2)}) collective-permute-start(bf16[96,576]{0,1:T(8,128)(2,1)S(1)} %add_convert_fusion.5), channel_id=1, source_target_pairs={{2,4},{3,5},{4,2},{5,3},{10,12},{11,13},{12,10},{13,11},{18,20},{1... | collective-permute-start | bytes 331784 | tf_op jit(solution)/shard_map/ppermute | solution.py:625
  394.0 57.6 %collective-permute-start.23 = (bf16[1024,768]{1,0:T(8,128)(2,1)}, bf16[1024,768]{1,0:T(8,128)(2,1)}, u32[]{:S(2)}, u32[]{:S(2)}) collective-permute-start(bf16[1024,768]{1,0:T(8,128)(2,1)} %add_convert_fusion), channel_id=1, source_target_pairs={{2,4},{3,5},{4,2},{5,3},{10,12},{11,13},{12,10},{13,11},{18,20},{1... | collective-permute-start | bytes 4718600 | tf_op jit(solution)/shard_map/ppermute | solution.py:625
  395.9 55.7 %collective-permute-start.22 = (bf16[1024,768]{1,0:T(8,128)(2,1)}, bf16[1024,768]{1,0:T(8,128)(2,1)}, u32[]{:S(2)}, u32[]{:S(2)}) collective-permute-start(bf16[1024,768]{1,0:T(8,128)(2,1)} %add_convert_fusion.2), channel_id=1, source_target_pairs={{0,1},{1,0},{6,7},{7,6},{8,9},{9,8},{14,15},{15,14},{16,17},{17,16... | collective-permute-start | bytes 4718600 | tf_op jit(solution)/shard_map/ppermute | solution.py:625
  401.3 50.3 %copy-start.1 = (f32[1024,768]{1,0:T(8,128)S(1)}, f32[1024,768]{1,0:T(8,128)}, u32[]{:S(2)}) copy-start(f32[1024,768]{1,0:T(8,128)} %fusion.18) | copy-start | bytes 9437188
  (21 other events, 353.8 us)
Sparse Core Ops, SparseCore 0:
  10.3 35.1 all-gather.5
  47.5 69.3 all-gather.3
  267.4 87.3 reduce-scatter.2
  389.5 49.3 reduce-scatter.4

commit v3 on v2

--- a/solution.py
+++ b/solution.py
@@ -69,22 +69,51 @@
     return (first * high, first * low, second)
 
 
-def forward_kernel(steps, fill, table, place, *refs):
-    if fill:
-        qkv0, qkv1, qkv2, qkv3, o_ref, p_ref, qkv_scr, s_scr, sems = refs
+def forward_kernel(steps, count, project, table, place, *refs):
+    step = pl.program_id(0)
+    last = step == pl.num_programs(0) - 1
+    if project:
+        x_refs, (w_ref, add_ref, scale_ref), refs = refs[:4], refs[4:7], refs[7:]
+        o_refs, (p_ref, qkv_hbm), refs = refs[:count], refs[count : count + 2], refs[count + 2 :]
+        qkv_scr, s_scr, o_scr, x_scr, sems = refs
+        out_copy = pltpu.make_async_copy(qkv_scr, qkv_hbm, sems.at[4])
+
+        @pl.when(step == 0)
+        def _project():
+            copies = [
+                pltpu.make_async_copy(src, x_scr.at[pl.ds(n * QROWS, QROWS)], sems.at[n])
+                for n, src in enumerate(x_refs)
+            ]
+            for copy in copies:
+                copy.start()
+            for copy in copies:
+                copy.wait()
+            chunk = 256
+
+            def body(n, carry):
+                rows = pl.ds(pl.multiple_of(n * chunk, chunk), chunk)
+                total = dot_nn(x_scr[rows], w_ref[...]) + add_ref[...]
+                qkv_scr[rows] = (total.astype(jnp.bfloat16).astype(jnp.float32) * scale_ref[...]).astype(
+                    jnp.bfloat16
+                )
+                return carry
+
+            lax.fori_loop(0, LENGTH // chunk, body, 0)
+            out_copy.start()
+
+        @pl.when(last)
+        def _written():
+            out_copy.wait()
+
     else:
-        qkv0, qkv1, qkv2, qkv3, _, o_ref, p_ref, qkv_scr, s_scr, sems = refs
-    step = pl.program_id(0)
-
-    @pl.when(step == 0)
-    def _load():
-        copies = [
-            pltpu.make_async_copy(src, qkv_scr.at[pl.ds(n * QROWS, QROWS)], sems.at[n])
-            for n, src in enumerate((qkv0, qkv1, qkv2, qkv3))
-        ]
-        for copy in copies:
+        qkv_hbm, _ = refs[:2]
+        o_refs, refs = refs[2 : 2 + count], refs[2 + count :]
+        p_ref, qkv_scr, s_scr, o_scr, sems = refs
+
+        @pl.when(step == 0)
+        def _load():
+            copy = pltpu.make_async_copy(qkv_hbm, qkv_scr, sems.at[0])
             copy.start()
-        for copy in copies:
             copy.wait()
 
     low, high = lane_masks(jnp.bfloat16)
@@ -118,45 +147,60 @@
     for sub in range(per):
         rows = slice(sub * BLOCK, (sub + 1) * BLOCK)
         outs = [dot_nn(p_ref[sub, head], keys[sub * HEADS + head]) for head in range(HEADS)]
-        o_ref[0, rows, 0:128] = jnp.where(lane < 64, outs[0], outs[1]).astype(jnp.bfloat16)
-        o_ref[0, rows, 128:192] = outs[2][:, 0:64].astype(jnp.bfloat16)
-
-
-def attend_forward(slots, rank, table, qkv, probs):
+        o_scr[rows, 0:128] = jnp.where(lane < 64, outs[0], outs[1]).astype(jnp.bfloat16)
+        o_scr[rows, 128:192] = outs[2][:, 0:64].astype(jnp.bfloat16)
+    for turn, o_ref in enumerate(o_refs):
+
+        @pl.when(step // steps == turn)
+        def _out(o_ref=o_ref):
+            o_ref[...] = o_scr[...]
+
+
+def attend_forward(slots, rank, table, rows=None, weights=None, qkv=None, probs=None):
     steps = 4
     per = QB // steps
     count = len(slots)
+    project = rows is not None
     any_spec = pl.BlockSpec(memory_space=pl.ANY)
     place = jnp.stack([rank.astype(jnp.int32)] + [jnp.int32(slot) for slot in slots])
-    operands = [table, place, *qkv]
-    alias = {}
-    if probs is not None:
-        alias = {6: 1}
-        operands.append(probs)
+    operands = [table, place] + ([*rows, *weights] if project else [qkv, probs])
+    in_specs = [any_spec] * (4 if project else 2)
+    if project:
+        in_specs += [pl.BlockSpec(each.shape, lambda g, *_: (0, 0)) for each in weights]
+    qkv_out = [jax.ShapeDtypeStruct((LENGTH, QKV), jnp.bfloat16)] * project
+    extra = [pltpu.VMEM((LENGTH, weights[0].shape[0]), jnp.bfloat16)] if project else []
     return pl.pallas_call(
-        functools.partial(forward_kernel, steps, probs is None),
+        functools.partial(forward_kernel, steps, count, project),
         grid_spec=pltpu.PrefetchScalarGridSpec(
             num_scalar_prefetch=2,
             grid=(count * steps,),
-            in_specs=[any_spec] * (4 + len(alias)),
+            in_specs=in_specs,
             out_specs=[
-                pl.BlockSpec((1, per * BLOCK, 192), lambda g, *_: (g // steps, g % steps, 0)),
+                pl.BlockSpec(
+                    (per * BLOCK, 192),
+                    lambda g, *_, turn=turn: (jnp.clip(g - turn * steps, 0, steps - 1), 0),
+                )
+                for turn in range(count)
+            ]
+            + [
                 pl.BlockSpec(
                     (per, HEADS, BLOCK, KEYS),
                     lambda g, t, pos: (pos[1 + g // steps] * steps + g % steps, 0, 0, 0),
                 ),
-            ],
+            ]
+            + [any_spec] * project,
             scratch_shapes=[
                 pltpu.VMEM((LENGTH, QKV), jnp.bfloat16),
                 pltpu.VMEM((per * HEADS, BLOCK, KEYS), jnp.float32),
-                pltpu.SemaphoreType.DMA((4,)),
-            ],
-        ),
-        out_shape=[
-            jax.ShapeDtypeStruct((count, QROWS, 192), jnp.bfloat16),
-            jax.ShapeDtypeStruct((NB, HEADS, BLOCK, KEYS), jnp.bfloat16),
-        ],
-        input_output_aliases=alias,
+                pltpu.VMEM((per * BLOCK, 192), jnp.bfloat16),
+            ]
+            + extra
+            + [pltpu.SemaphoreType.DMA((5,))],
+        ),
+        out_shape=[jax.ShapeDtypeStruct((QROWS, 192), jnp.bfloat16)] * count
+        + [jax.ShapeDtypeStruct((NB, HEADS, BLOCK, KEYS), jnp.bfloat16)]
+        + qkv_out,
+        input_output_aliases={} if project else {3: count},
         compiler_params=pltpu.CompilerParams(
             dimension_semantics=("arbitrary",), vmem_limit_bytes=vmem_limit
         ),
@@ -165,19 +209,41 @@
 
 
 def backward_kernel(
-    steps, table, p_ref, qkv0, qkv1, qkv2, qkv3, do0, do1, do2, do3, out_ref, qkv_scr, do_scr, acc, dp_scr, st_scr, sems
+    steps,
+    table,
+    p_ref,
+    qkv_hbm,
+    do0,
+    do1,
+    do2,
+    do3,
+    w_ref,
+    da_hbm,
+    out_hbm,
+    base_hbm,
+    near_hbm,
+    side_hbm,
+    far_hbm,
+    sum_ref,
+    qkv_scr,
+    do_scr,
+    acc,
+    dp_scr,
+    st_scr,
+    out_ref,
+    da_scr,
+    share_scr,
+    sems,
 ):
     step = pl.program_id(0)
 
     @pl.when(step == 0)
     def _load():
-        copies = [
-            pltpu.make_async_copy(src, qkv_scr.at[pl.ds(n * QROWS, QROWS)], sems.at[n])
-            for n, src in enumerate((qkv0, qkv1, qkv2, qkv3))
-        ] + [
+        copies = [pltpu.make_async_copy(qkv_hbm, qkv_scr, sems.at[0])] + [
             pltpu.make_async_copy(src, do_scr.at[pl.ds(n * QROWS, QROWS)], sems.at[4 + n])
             for n, src in enumerate((do0, do1, do2, do3))
         ]
+        copies.append(pltpu.make_async_copy(da_hbm, da_scr, sems.at[8]))
         for copy in copies:
             copy.start()
         acc[...] = jnp.zeros_like(acc)
@@ -240,35 +306,130 @@
     @pl.when(step == steps - 1)
     def _store():
         out_ref[:, 0:KV] = acc[...].astype(jnp.bfloat16)
-
-
-def attend_backward(table, probs, qkv, grads):
+        total = jnp.zeros((8, QKV), jnp.float32)
+        for row in range(0, LENGTH, 128):
+            total = total + fold_rows(out_ref[row : row + 128].astype(jnp.float32))
+        sum_ref[...] = total
+        done = [pltpu.make_async_copy(out_ref, out_hbm, sems.at[0])]
+        done[0].start()
+        chunk = 256
+
+        def share(n, carry):
+            source = (3 - n // (QROWS // chunk)) * QROWS + (n % (QROWS // chunk)) * chunk
+            rows = pl.ds(pl.multiple_of(source, chunk), chunk)
+            place = pl.ds(pl.multiple_of(n * chunk, chunk), chunk)
+            share_scr[place] = dot_nt(out_ref[rows], w_ref[...]).astype(jnp.bfloat16)
+            return carry
+
+        lax.fori_loop(0, 3 * QROWS // chunk, share, 0)
+        for n, share_hbm in enumerate((far_hbm, side_hbm, near_hbm)):
+            rows = pl.ds(n * QROWS, QROWS)
+            done.append(pltpu.make_async_copy(share_scr.at[rows], share_hbm, sems.at[1 + n]))
+            done[-1].start()
+
+        def base(n, carry):
+            rows = pl.ds(pl.multiple_of(n * chunk, chunk), chunk)
+            da_scr[rows] += dot_nt(out_ref[rows], w_ref[...])
+            return carry
+
+        lax.fori_loop(0, QROWS // chunk, base, 0)
+        done.append(pltpu.make_async_copy(da_scr, base_hbm, sems.at[4]))
+        done[-1].start()
+        for copy in done:
+            copy.wait()
+
+
+def attend_backward(table, probs, qkv, grads, w_qkv, da):
     steps = 16
     per = NB // steps
+    width = w_qkv.shape[0]
     any_spec = pl.BlockSpec(memory_space=pl.ANY)
+    share = jax.ShapeDtypeStruct((QROWS, width), jnp.bfloat16)
     return pl.pallas_call(
         functools.partial(backward_kernel, steps),
         grid_spec=pltpu.PrefetchScalarGridSpec(
             num_scalar_prefetch=1,
             grid=(steps,),
             in_specs=[pl.BlockSpec((per, HEADS, BLOCK, KEYS), lambda g, *_: (g, 0, 0, 0))]
-            + [any_spec] * 8,
-            out_specs=pl.BlockSpec((LENGTH, QKV), lambda g, *_: (0, 0)),
+            + [any_spec] * 5
+            + [pl.BlockSpec((width, QKV), lambda g, *_: (0, 0)), any_spec],
+            out_specs=[any_spec] * 5 + [pl.BlockSpec((8, QKV), lambda g, *_: (0, 0))],
             scratch_shapes=[
                 pltpu.VMEM((LENGTH, QKV), jnp.bfloat16),
                 pltpu.VMEM((LENGTH, 192), jnp.bfloat16),
                 pltpu.VMEM((LENGTH, KV), jnp.float32),
                 pltpu.VMEM((per * HEADS, BLOCK, KEYS), jnp.float32),
                 pltpu.VMEM((per * HEADS, 128, KEYS), jnp.bfloat16),
-                pltpu.SemaphoreType.DMA((8,)),
+                pltpu.VMEM((LENGTH, QKV), jnp.bfloat16),
+                pltpu.VMEM((QROWS, width), jnp.float32),
+                pltpu.VMEM((3 * QROWS, width), jnp.bfloat16),
+                pltpu.SemaphoreType.DMA((9,)),
             ],
         ),
-        out_shape=jax.ShapeDtypeStruct((LENGTH, QKV), jnp.bfloat16),
+        out_shape=[
+            jax.ShapeDtypeStruct((LENGTH, QKV), jnp.bfloat16),
+            jax.ShapeDtypeStruct((QROWS, width), jnp.float32),
+            share,
+            share,
+            share,
+            jax.ShapeDtypeStruct((8, QKV), jnp.float32),
+        ],
         compiler_params=pltpu.CompilerParams(
             dimension_semantics=("arbitrary",), vmem_limit_bytes=vmem_limit
         ),
+        cost_estimate=pl.CostEstimate(
+            flops=40 * 10**9, transcendentals=0, bytes_accessed=25 * 10**6
+        ),
         name="attend_backward",
-    )(table, probs, *qkv, *grads)
+    )(table, probs, qkv, *grads, w_qkv, da)
+
+
+def head_weight_kernel(x0, x1, x2, x3, grad_ref, out_ref, x_scr, acc, sems):
+    slot = pl.program_id(0)
+
+    @pl.when(slot == 0)
+    def _load():
+        copies = [
+            pltpu.make_async_copy(src, x_scr.at[pl.ds(n * QROWS, QROWS)], sems.at[n])
+            for n, src in enumerate((x0, x1, x2, x3))
+        ]
+        for copy in copies:
+            copy.start()
+        acc[...] = jnp.zeros_like(acc)
+        for copy in copies:
+            copy.wait()
+
+    rows = pl.ds(pl.multiple_of(slot * QROWS, QROWS), QROWS)
+    acc[...] += dot_tn(x_scr[rows], grad_ref[...])
+
+    @pl.when(slot == pl.num_programs(0) - 1)
+    def _store():
+        out_ref[:, 0 : KV + 128] = acc[:, 0 : KV + 128].astype(jnp.bfloat16)
+        out_ref[:, KV + 128 : KV + 192] = acc[:, KV + 192 : KV + 256].astype(jnp.bfloat16)
+
+
+def head_weight_block(rows, grad_qkv):
+    width = rows[0].shape[1]
+    any_spec = pl.BlockSpec(memory_space=pl.ANY)
+    return pl.pallas_call(
+        head_weight_kernel,
+        grid=(GROUP,),
+        in_specs=[any_spec] * 4 + [pl.BlockSpec((QROWS, QKV), lambda g: (g, 0))],
+        out_specs=pl.BlockSpec((width, QKV - 64), lambda g: (0, 0)),
+        scratch_shapes=[
+            pltpu.VMEM((LENGTH, width), jnp.bfloat16),
+            pltpu.VMEM((width, QKV), jnp.float32),
+            pltpu.SemaphoreType.DMA((4,)),
+        ],
+        out_shape=jax.ShapeDtypeStruct((width, QKV - 64), jnp.bfloat16),
+        compiler_params=pltpu.CompilerParams(
+            dimension_semantics=("arbitrary",), vmem_limit_bytes=vmem_limit
+        ),
+        cost_estimate=pl.CostEstimate(
+            flops=8 * 10**9, transcendentals=0, bytes_accessed=12 * 10**6
+        ),
+        name="head_weight_block",
+    )(*rows, grad_qkv)
 
 
 def row_mean(values):
@@ -303,15 +464,19 @@
     dfr_ref,
     dar_ref,
     da_ref,
-    do_ref,
-    sum_ref,
-    up_sum_ref,
+    do0,
+    do1,
+    do2,
+    do3,
+    total_ref,
     w_scr,
     acc,
     u_scr,
     slope_scr,
     xhat_scr,
     m1_scr,
+    sum_ref,
+    up_sum_ref,
     sem,
 ):
     step = pl.program_id(0)
@@ -421,8 +586,16 @@
         dar_ref[rows] = down.astype(jnp.bfloat16)
     for n in range(6):
         sum_ref[n] += sums[n]
-    for n in range(parts):
-        do_ref[n] = dot_nn(dar_ref[...], out_weight(n)).astype(jnp.bfloat16)
+    for n, do_ref in enumerate((do0, do1, do2, do3)):
+        do_ref[...] = dot_nn(dar_ref[...], out_weight(n)).astype(jnp.bfloat16)
+
+    @pl.when(step == pl.num_programs(0) - 1)
+    def _totals():
+        for n in range(6):
+            total_ref[:, n * width : (n + 1) * width] = jnp.sum(
+                sum_ref[n], axis=0, keepdims=True
+            )
+        total_ref[:, 6 * width :] = jnp.sum(up_sum_ref[...], axis=0, keepdims=True)
 
 
 def token_block(rank, outs, own, cot, vectors, up_bias, weights):
@@ -446,7 +619,7 @@
             grid=(count // tile,),
             in_specs=[rows_of(head)] * 4
             + [rows_of(width)] * 2
-            + [whole(vectors.shape), whole(up_bias.shape), pl.BlockSpec(memory_space=pl.ANY)],
+            + [whole(vectors.shape), whole(up_bias.shape)] + [pl.BlockSpec(memory_space=pl.ANY)],
             out_specs=[
                 rows_of(width),
                 rows_of(width),
@@ -455,9 +628,11 @@
                 rows_of(width),
                 rows_of(width),
                 rows_of(width),
-                pl.BlockSpec((GROUP, tile, head), lambda g, *_: (0, g, 0)),
-                whole((6, 8, width)),
-                whole((8, total_hidden)),
+                rows_of(head),
+                rows_of(head),
+                rows_of(head),
+                rows_of(head),
+                whole((1, 6 * width + total_hidden)),
             ],
             scratch_shapes=[
                 pltpu.VMEM(weights.shape, low),
@@ -466,6 +641,8 @@
                 pltpu.VMEM((tile, total_hidden), jnp.float32),
                 pltpu.VMEM((tile, width), jnp.float32),
                 pltpu.VMEM((tile, width), jnp.float32),
+                pltpu.VMEM((6, 8, width), jnp.float32),
+                pltpu.VMEM((8, total_hidden), jnp.float32),
                 pltpu.SemaphoreType.DMA,
             ],
         ),
@@ -477,12 +654,17 @@
             jax.ShapeDtypeStruct((count, width), low),
             jax.ShapeDtypeStruct((count, width), low),
             jax.ShapeDtypeStruct((count, width), jnp.float32),
-            jax.ShapeDtypeStruct((GROUP, count, head), low),
-            jax.ShapeDtypeStruct((6, 8, width), jnp.float32),
-            jax.ShapeDtypeStruct((8, total_hidden), jnp.float32),
+            jax.ShapeDtypeStruct((count, head), low),
+            jax.ShapeDtypeStruct((count, head), low),
+            jax.ShapeDtypeStruct((count, head), low),
+            jax.ShapeDtypeStruct((count, head), low),
+            jax.ShapeDtypeStruct((1, 6 * width + total_hidden), jnp.float32),
         ],
         compiler_params=pltpu.CompilerParams(
             dimension_semantics=("arbitrary",), vmem_limit_bytes=vmem_limit
+        ),
+        cost_estimate=pl.CostEstimate(
+            flops=46 * 10**9, transcendentals=0, bytes_accessed=40 * 10**6
         ),
         name="token_block",
     )(rank.astype(jnp.int32).reshape(1), *outs, own, cot, vectors, up_bias, weights)
@@ -497,8 +679,15 @@
         dfr_t[...] = dfr[...].T
         dar_t[...] = dar[...].T
 
-    out_ref[:, 0:hidden] = dot_nn(n1_t[...], du[...]).astype(jnp.bfloat16)
-    out_ref[:, hidden : 2 * hidden] = dot_nn(dfr_t[...], g[...]).astype(jnp.bfloat16)
+    chunk = 256
+
+    def product(n, carry):
+        rows = pl.ds(pl.multiple_of(n * chunk, chunk), chunk)
+        out_ref[rows, 0:hidden] = dot_nn(n1_t[rows], du[...]).astype(jnp.bfloat16)
+        out_ref[rows, hidden : 2 * hidden] = dot_nn(dfr_t[rows], g[...]).astype(jnp.bfloat16)
+        return carry
+
+    lax.fori_loop(0, width // chunk, product, 0)
     for n, piece in enumerate((o0, o1, o2, o3)):
 
         @pl.when(part == rank_ref[0] ^ n)
@@ -530,6 +719,9 @@
         out_shape=jax.ShapeDtypeStruct((GROUP * width, columns), low),
         compiler_params=pltpu.CompilerParams(
             dimension_semantics=("arbitrary",), vmem_limit_bytes=vmem_limit
+        ),
+        cost_estimate=pl.CostEstimate(
+            flops=22 * 10**9, transcendentals=0, bytes_accessed=30 * 10**6
         ),
         name="weight_block",
     )(rank.astype(jnp.int32).reshape(1), n1, dfr, dar, g, du, *outs)
@@ -601,6 +793,7 @@
 ):
     width = inputs.shape[1]
     hidden = b_up.shape[0]
+    low = jnp.bfloat16
     dp_index = lax.axis_index("dp")
     tensor_index = lax.axis_index("tensor")
     core = dp_index % 2
@@ -637,43 +830,50 @@
         return flip(value, 1, 0)
 
     rest = jnp.concatenate([w_up, w_down.T, w_output.T], axis=1)
-    rest = lax.all_gather(rest, "tensor", axis=0)
-    rest_all = lax.all_gather(rest, "dp", axis=1, tiled=True).reshape(GROUP * width, -1)
-
-    packed = rehome(pack_columns(w_query, w_key, w_value, 1))
-    packed = order_halves(half, packed, flip(packed, 0, 2))
+    below = jnp.concatenate(split_three(b_up))
+    below = jnp.pad(below, (0, -below.shape[0] % rest.shape[1])).reshape(-1, rest.shape[1])
+    rest = lax.all_gather(jnp.concatenate([rest, below], axis=0), "tensor", axis=0)
+
+    packed = pack_columns(w_query, w_key, w_value, 1)
+    columns = packed.shape[1]
+    floats = jnp.concatenate([b_query, b_value])
+    small = jnp.concatenate(split_three(floats) + [random_blocks.astype(low).reshape(-1)])
+    small = jnp.pad(small, (0, -small.shape[0] % columns)).reshape(-1, columns)
+    packed = jnp.concatenate([order_halves(core, packed, side_of(packed)), small], axis=0)
+    packed = jnp.where(here, packed, flip(packed, 0, 2, stays))
+    inputs, packed = lax.optimization_barrier((inputs, packed))
+    moved = flip(inputs, 1, 2, moves)
+    near_stay = flip(inputs, 0, 1, stays)
+    small = packed[2 * w_query.shape[0] :].reshape(-1)
+    packed = packed[: 2 * w_query.shape[0]]
     for bit in pair_bits:
         packed = order_halves((dp_index >> bit) % 2, packed, flip(packed, 1 << bit, 0))
     w_qkv = insert_zero(packed, 1)
-
-    small = jnp.concatenate(
-        [b_query, b_value, b_up, random_blocks.astype(jnp.float32).reshape(-1)]
-    )[None]
-    small = jnp.concatenate([small, flip(small, 0, 1)], axis=0)
-    small = jnp.concatenate([small, flip(small, 0, 2)], axis=0)
-    b_up_all = jnp.concatenate(
-        [
-            lax.dynamic_index_in_dim(small, tensor_index ^ n, 0)[:, 384 : 384 + hidden]
-            for n in range(GROUP)
-        ],
-        axis=1,
-    )
-    mine = lax.dynamic_index_in_dim(small, tensor_index ^ rank, 0, keepdims=False)
-    my_random = mine[384 + hidden :].reshape(HEADS, NB, -1).astype(jnp.int32)
-
-    own = rehome(inputs)
-    near = jnp.where(here, flip(inputs, 0, 1, stays), flip(own, 0, 1, moves))
-    side = side_of(own)
-    far = side_of(near)
+    count = floats.shape[0]
+    mine = sum(small[n * count : (n + 1) * count].astype(jnp.float32) for n in range(3))
+    my_random = small[3 * count : 3 * count + random_blocks.size]
+    my_random = my_random.reshape(HEADS, NB, -1).astype(jnp.int32)
+    b_key = jnp.zeros_like(b_query)
+    b_qkv = insert_zero(pack_columns(mine[:192], b_key, mine[192:], 0), 0)
+    scale = jnp.concatenate([jnp.ones((KV,), jnp.float32), jnp.full((256,), 0.125, jnp.float32)])
+
+    moved, rest, w_qkv, b_qkv = lax.optimization_barrier((moved, rest, w_qkv, b_qkv))
+    below = rest[:, w_up.shape[0] :].reshape(GROUP, -1)
+    rest_all = lax.all_gather(
+        rest[:, : w_up.shape[0]], "dp", axis=1, tiled=True
+    ).reshape(GROUP * width, -1)
+    b_up_all = sum(
+        below[:, n * hidden : (n + 1) * hidden].astype(jnp.float32) for n in range(3)
+    ).reshape(1, -1)
+    own = jnp.where(here, inputs, moved)
+    near_move = flip(own, 0, 1, moves)
+
+    near = jnp.where(here, near_stay, near_move)
+    near, own, cotangent = lax.optimization_barrier((near, own, cotangent))
+    side, far = side_of(own), side_of(near)
+    cot_moved = flip(cotangent, 1, 2, moves)
     rows = (own, near, side, far)
-    cotangent, _ = lax.optimization_barrier((cotangent, near))
-    grad_top = rehome(cotangent)
-
-    b_key = jnp.zeros_like(b_query)
-    b_qkv = insert_zero(pack_columns(mine[:192], b_key, mine[192:384], 0), 0)
-    scale = jnp.concatenate([jnp.ones((KV,), jnp.float32), jnp.full((256,), 0.125, jnp.float32)])
-    qkv = [((dot_nn(part, w_qkv) + b_qkv) * scale).astype(jnp.bfloat16) for part in rows]
-
+    grad_top = jnp.where(here, cotangent, cot_moved)
     block = jnp.arange(NB, dtype=jnp.int32)
     block = block ^ (rank * QB)
     fixed = jnp.clip(
@@ -696,22 +896,20 @@
     )
     table = (table ^ (rank * QB)).reshape(-1)
 
-    remote, probs = attend_forward((1, 3), rank, table, qkv, None)
-    local, probs = attend_forward((0, 2), rank, table, qkv, probs)
-    outs = (
-        local[0],
-        near_of(remote[0]),
-        side_of(local[1]),
-        flip(remote[1], 1, 1),
-    )
+    weights = (w_qkv, b_qkv[None], scale[None])
+    out_near, out_far, out_side, probs, qkv = attend_forward((1, 3, 2), rank, table, rows, weights)
+    out_own, probs = attend_forward((0,), rank, table, qkv=qkv, probs=probs)
+    outs = (out_own, near_of(out_near), side_of(out_side), flip(out_far, 1, 1))
 
     vectors = jnp.stack([b_output, gain_attn, bias_attn, b_down, gain_mlp, bias_mlp])
-    layer_out, n1, g, du, dfr, dar, da, do, sums, up_sums = token_block(
+    layer_out, n1, g, du, dfr, dar, da, *do, sums = token_block(
         rank, outs, own, grad_top, vectors, b_up_all, rest_all
     )
     grads = (do[0], near_of(do[1]), side_of(do[2]), flip(do[3], 1, 1))
     rest_grad = weight_block(rank, n1, dfr, dar, g, du, outs)
-    rest_grad, *grads = lax.optimization_barrier((rest_grad, *grads))
+    sums = sums.reshape(-1)
+    sums = sums + flip(sums, 0, 1)
+    rest_grad, sums, *grads = lax.optimization_barrier((rest_grad, sums, *grads))
     rest_sum = lax.psum_scatter(
         rest_grad.reshape(GROUP, width, -1), "dp", scatter_dimension=1, tiled=True
     )
@@ -721,57 +919,58 @@
     shard_up = rest_sum[:, :hidden]
     shard_down = rest_sum[:, hidden : 2 * hidden].T
     shard_output = rest_sum[:, 2 * hidden :].T
-    layer_out = rehome(layer_out)
-
-    grad_qkv = attend_backward(table, probs, qkv, grads)
-
-    def input_part(n):
-        return dot_nt(grad_qkv[n * QROWS : (n + 1) * QROWS], w_qkv)
-
-    low = jnp.bfloat16
-    side_far = side_of(input_part(3).astype(low))
-    side_own = side_of(input_part(2).astype(low))
-    to_near = (input_part(1) + side_far.astype(jnp.float32)).astype(low)
-    base = da + input_part(0) + side_own.astype(jnp.float32)
+    layer_sent = flip(layer_out, 1, 2, moves)
+
+    grad_qkv, base, to_near, to_side, to_far, bias_sum = attend_backward(
+        table, probs, qkv, grads, w_qkv, da
+    )
+    grad_qkv, base, to_near, to_side, to_far, bias_sum, layer_sent = lax.optimization_barrier(
+        (grad_qkv, base, to_near, to_side, to_far, bias_sum, layer_sent)
+    )
+    side_far = side_of(to_far)
+    side_own = side_of(to_side)
+    bias_query, _, bias_value = unpack_columns(drop_zero(jnp.sum(bias_sum, axis=0), 0), 0)
+    sums = jnp.concatenate([sums, bias_query, bias_value])
+    sums = sums + flip(sums, 0, 2)
+    to_near = (to_near.astype(jnp.float32) + side_far.astype(jnp.float32)).astype(low)
+    to_near, sums = lax.optimization_barrier((to_near, sums))
     near_move = flip(to_near, 0, 1, moves)
-    to_near, near_move = lax.optimization_barrier((to_near, near_move))
+    base = base + side_own.astype(jnp.float32)
+    grad_late, to_near = lax.optimization_barrier((grad_qkv, to_near))
+    for bit in pair_bits:
+        sums = sums + flip(sums, 1 << bit, 0)
+    other = side_of(sums)
+    grad_w = head_weight_block(rows, grad_late)
+    to_near, near_move, grad_w, base, sums, other = lax.optimization_barrier(
+        (to_near, near_move, grad_w, base, sums, other)
+    )
+    grad_move = (base + near_move.astype(jnp.float32)).astype(low)
+    grad_move, to_near, grad_w, base = lax.optimization_barrier(
+        (grad_move, to_near, grad_w, base)
+    )
+    grad_moved = flip(grad_move, 1, 2, moves)
     near_stay = flip(to_near, 0, 1, stays)
-    grad_move = (base + near_move.astype(jnp.float32)).astype(low)
     grad_stay = (base + near_stay.astype(jnp.float32)).astype(low)
-    grad_input = jnp.where(here, grad_stay, flip(grad_move, 1, 2, moves))
-
-    all_rows = jnp.concatenate(rows, axis=0)
-    grad_w = drop_zero(dot_tn(all_rows, grad_qkv), 1).astype(low)
+    grad_moved, grad_stay = lax.optimization_barrier((grad_moved, grad_stay))
+    grad_input = jnp.where(here, grad_stay, grad_moved)
+
     for bit in reversed(pair_bits):
         grad_w = halve(flip, (dp_index >> bit) % 2, grad_w, 1 << bit, 0)
-    grad_w = halve(flip, half, grad_w, 0, 2)
-    shard_query, shard_key, shard_value = unpack_columns(
-        rehome(grad_w).astype(jnp.float32), 1
-    )
-
-    bias_sum = drop_zero(jnp.sum(grad_qkv.astype(jnp.float32), axis=0), 0)
-    bias_query, _, bias_value = unpack_columns(bias_sum, 0)
-    bias_pair = jnp.concatenate([bias_query, bias_value])
-    groups = jnp.arange(GROUP, dtype=jnp.int32)[:, None]
-    bias_pair = jnp.where(groups == rank, bias_pair[None], 0.0)
-    sums = jnp.concatenate(
-        [
-            jnp.sum(sums, axis=1).reshape(-1),
-            jnp.sum(up_sums, axis=0),
-            bias_pair.reshape(-1),
-        ]
-    ).reshape(-1, 128)
-    sums = sums + side_of(sums)
-    for bit in pair_bits:
-        sums = sums + flip(sums, 1 << bit, 0)
-    for bit in (1, 2):
-        sums = sums + flip(sums, 0, bit)
-    sums = sums.reshape(-1)
+    grad_w, layer_sent = lax.optimization_barrier((grad_w, layer_sent))
+    layer_out = jnp.where(here, layer_out, layer_sent)
+    grad_w = grad_w.astype(jnp.float32) + flip(grad_w, 0, 2, moves).astype(jnp.float32)
+    rows_each = grad_w.shape[0] // 2
+    grad_w = grad_w.astype(low)
+    keep = lax.dynamic_slice_in_dim(grad_w, core * rows_each, rows_each, 0)
+    send = lax.dynamic_slice_in_dim(grad_w, (1 - core) * rows_each, rows_each, 0)
+    shard = jnp.where(here, keep, side_of(send)).astype(jnp.float32)
+    shard_query, shard_key, shard_value = unpack_columns(shard, 1)
+
+    count = 6 * width + GROUP * hidden
+    bias_pair = jnp.where(here, sums[count:], other[count:])
+    sums = sums + other
     top = sums[: 6 * width].reshape(6, width)
     grad_b_up = lax.dynamic_slice_in_dim(sums, 6 * width + tensor_index * hidden, hidden, 0)
-    bias_pair = lax.dynamic_slice_in_dim(
-        sums, 6 * width + GROUP * hidden + tensor_index * 384, 384, 0
-    )
     return (
         layer_out,
         grad_input,
@@ -801,6 +1000,15 @@
     )
 
 
+def split_three(values):
+    parts = []
+    for _ in range(3):
+        part = lax.reduce_precision(values, 8, 7)
+        parts.append(part.astype(jnp.bfloat16))
+        values = values - part
+    return parts
+
+
 def halve(flip, bit, value, d_bits, t_bits):
     rows = value.shape[0] // 2
     keep = lax.dynamic_slice_in_dim(value, bit * rows, rows, 0)

time: 473 us -> 436 us (0.922); the launches traced: 466 us -> 434 us
  waiting for transfers between devices: 193 us -> 146 us
  matrix products: 35.1 us -> 0 us
  Pallas kernels: 122 us -> 157 us
  other arithmetic: 25.4 us -> 32.8 us
  starting transfers between devices: 57.1 us -> 62.6 us
    all_gather x2, waiting for transfers between devices: 35.3 us -> 0.01 us  [the longest x1 0.01 us: per_device(): lax.all_gather(jnp.concatenate([rest, below], axis=0), 'tensor', axis=0)]
    dot_general x9 -> x0, matrix products: 35.1 us -> none  [the longest x4 14.6 us: dot_nn(): return jnp.dot(left, right, preferred_element_type=jnp.float32)]
    pallas_call x2 -> x3, Pallas kernels: 26.5 us -> 48.7 us  [the longest x2 37.3 us: attend_forward(): pl.pallas_call(functools.partial(forward_kernel, steps, count, project),...]
    ppermute x33 -> x31, waiting for transfers between devices: 157 us -> 146 us  [flip(): return lax.ppermute(value, both, pairs)]
    pallas_call x1, Pallas kernels: 35.2 us -> 46.5 us  [attend_backward(): pl.pallas_call(functools.partial(backward_kernel, steps), grid_spec=pltpu...]
    convert_element_type x3 -> x8, other arithmetic: 0.12 us -> 8 us  [the longest x1 2.93 us: per_device(): (to_near.astype(jnp.float32) + side_far.astype(jnp.float32)).astype(low)]
    ppermute x33 -> x31, starting transfers between devices: 57 us -> 62.5 us  [flip(): return lax.ppermute(value, both, pairs)]
    squeeze x4 -> x0, local copies, waits for them, and re-layouts: 5.29 us -> none  [the longest x1 2.45 us: per_device(): grads = (do[0], near_of(do[1]), side_of(do[2]), flip(do[3], 1, 1))]
  transfers between devices with their start and end apart: 37 -> 35, of which waited for: 14 -> 14; matrix products, arithmetic and copies ran while one was open for 15% -> 9% of each run, Pallas kernels for 17% -> 27%
where the time goes in v3:
time: 436 us; the launch traced here: 434 us
  Pallas kernels  157 us (36%)
  waiting for transfers between devices  146 us (33%)
  starting transfers between devices  62.6 us (14%)
  other arithmetic  32.8 us (8%)
  local copies, waits for them, and re-layouts  21 us (5%)
  between operations  14.6 us (3%)
    ppermute x31, waiting for transfers between devices, flip(): return lax.ppermute(value, both, pairs)  146 us
    ppermute x31, starting transfers between devices, flip(): return lax.ppermute(value, both, pairs)  62.5 us
    pallas_call x1, Pallas kernels, attend_backward(): pl.pallas_call(functools.partial(backward_kernel, steps), grid_spec=pltpu...  46.5 us
    pallas_call x1, Pallas kernels, token_block(): pl.pallas_call(functools.partial(token_kernel, tile, width, hidden), grid...  41 us
    pallas_call x2, Pallas kernels, attend_forward(): pl.pallas_call(functools.partial(forward_kernel, steps, count, project),...  37.3 us
    pallas_call x1, Pallas kernels, weight_block(): pl.pallas_call(functools.partial(weight_kernel, width, hidden), grid_spec...  21.1 us
    pallas_call x1, Pallas kernels, head_weight_block(): pl.pallas_call(head_weight_kernel, grid=(GROUP,), in_specs=[any_spec] * 4...  11.4 us
  transfers between devices with their start and end apart: 35, of which 14 were waited for; matrix products, arithmetic and copies ran while one was open for 9% of the time, Pallas kernels for 27%

profile of v3, /device:TPU:1, one launch (start us, length us, event | category | flops | bytes accessed | tf_op | source)
XLA Modules:
  0.0 434.0 jit_solution(2231441933763891371)
XLA Ops:
  15.4 1.3 collective-permute-start.1
  17.6 9.3 %collective-permute-done.1 = bf16[195,576]{1,0:T(8,128)(2,1)S(1)} collective-permute-done((bf16[195,576]{1,0:T(8,128)(2,1)S(1)}, bf16[195,576]{1,0:T(8,128)(2,1)S(1)}, u32[]{:S(2)}, u32[]{:S(2)}) %collective-permute-start.1) | collective-permute-done | bytes 224672 | tf_op jit(solution)/shard_map/ppermute | solution.py:818
  27.0 3.3 collective-permute-start.3
  30.3 1.3 collective-permute-start.4
  31.7 4.1 collective-permute-done.4
  36.0 1.3 collective-permute-start.5
  37.5 10.0 %collective-permute-done.5 = bf16[384,576]{1,0:T(8,128)(2,1)S(1)} collective-permute-done((bf16[384,576]{1,0:T(8,128)(2,1)S(1)}, bf16[384,576]{1,0:T(8,128)(2,1)S(1)}, u32[]{:S(2)}, u32[]{:S(2)}) %collective-permute-start.5) | collective-permute-done | bytes 442400 | tf_op jit(solution)/shard_map/ppermute | solution.py:818
  48.0 1.2 pad_maximum_fusion.refs_4_.w_ref
  49.2 41.0 %collective-permute-done.3 = bf16[1024,768]{1,0:T(8,128)(2,1)} collective-permute-done((bf16[1024,768]{1,0:T(8,128)(2,1)S(1)}, bf16[1024,768]{1,0:T(8,128)(2,1)}, u32[]{:S(2)}, u32[]{:S(2)}) %collective-permute-start.3) | collective-permute-done | bytes 1572896 | tf_op jit(solution)/shard_map/ppermute | solution.py:818
  90.2 2.5 slice.215
  93.6 1.6 broadcast_select_fusion.4.refs_0_.x_ref.x0
  95.2 2.1 collective-permute-start.6
  97.3 26.4 %collective-permute-done.6 = bf16[1024,768]{1,0:T(8,128)(2,1)S(1)} collective-permute-done((bf16[1024,768]{1,0:T(8,128)(2,1)S(1)}, bf16[1024,768]{1,0:T(8,128)(2,1)S(1)}, u32[]{:S(2)}, u32[]{:S(2)}) %collective-permute-start.6) | collective-permute-done | bytes 1572896 | tf_op jit(solution)/shard_map/ppermute | solution.py:818
  124.6 2.1 collective-permute-start.12
  132.7 28.4 %attend_forward.2 = (bf16[1024,192]{1,0:T(8,128)(2,1)}, bf16[1024,192]{1,0:T(8,128)(2,1)}, bf16[1024,192]{1,0:T(8,128)(2,1)}, bf16[64,3,64,512]{3,2,1,0:T(8,128)(2,1)}, bf16[4096,640]{1,0:T(8,128)(2,1)}) custom-call(s32[1536]{0:T(1024)} %xor.53.table, s32[4]{0:T(128)} %pad_add_fusion.1.place, bf16[1024,768]{1,0:T(8,128)(2,1)} %copy-done, ...), custom_call_target="tpu_custom_call" | custom-call | tf_op jit(solution)/shard_map/attend_forward/pallas_call | solution.py:172
  163.7 8.9 %attend_forward.3 = (bf16[1024,192]{1,0:T(8,128)(2,1)}, bf16[64,3,64,512]{3,2,1,0:T(8,128)(2,1)}) custom-call(s32[1536]{0:T(1024)} %xor.53.table, s32[2]{0:T(128)} %pad_add_fusion.place, bf16[4096,640]{1,0:T(8,128)(2,1)} %get-tuple-element.89.refs_0_.qkv_hbm, bf16[64,3,64,512]{3,2,1,0:T(8,128)(2,1)} %get-tuple-element.90.refs_1_), custom_call_target="tpu_custom_call", output_to_operand_aliasing={{1}: (3, {})} | custom-call | tf_op jit(solution)/shard_map/attend_forward/pallas_call | solution.py:172
  172.7 2.7 broadcast_select_fusion.2.cot_ref
  176.1 10.4 %collective-permute-done.9.o1 = bf16[1024,192]{1,0:T(8,128)(2,1)S(1)} collective-permute-done((bf16[1024,192]{1,0:T(8,128)(2,1)}, bf16[1024,192]{1,0:T(8,128)(2,1)S(1)}, u32[]{:S(2)}, u32[]{:S(2)}) %collective-permute-start.9) | collective-permute-done | bytes 393248 | tf_op jit(solution)/shard_map/ppermute | solution.py:818
  187.3 41.0 %token_block.1 = (bf16[1024,768]{1,0:T(8,128)(2,1)}, bf16[1024,768]{1,0:T(8,128)(2,1)}, bf16[1024,3072]{1,0:T(8,128)(2,1)}, bf16[1024,3072]{1,0:T(8,128)(2,1)}, ...) custom-call(s32[1]{0:T(128)} %bitcast.rank_ref, ...), custom_call_target="tpu_custom_call" | custom-call | flops 46000001024 | bytes 40000000 | tf_op jit(solution)/shard_map/token_block/pallas_call | solution.py:615
  229.1 1.4 collective-permute-start.13
  230.6 1.5 collective-permute-start.15
  233.1 21.1 %weight_block.1 = bf16[3072,1728]{1,0:T(8,128)(2,1)} custom-call(s32[1]{0:T(128)} %bitcast.rank_ref, bf16[1024,768]{1,0:T(8,128)(2,1)} %get-tuple-element.99.n1, bf16[1024,768]{1,0:T(8,128)(2,1)} %get-tuple-element.100.dfr, bf16[1024,768]{1,0:T(8,128)(2,1)} %get-tuple-element.101.dar, bf16[1024,3072]{1,0:T(8,128)(2,1)} %get-tuple-element.102.g, ...), custom_call_target="tpu_custom_call" | custom-call | flops 22000001024 | bytes 30000000 | tf_op jit(solution)/shard_map/weight_block/pallas_call | solution.py:708
  254.2 1.6 collective-permute-done.16.do3
  257.4 2.2 collective-permute-start.17
  259.7 46.5 %attend_backward.1 = (bf16[4096,640]{1,0:T(8,128)(2,1)}, f32[1024,768]{1,0:T(8,128)}, bf16[1024,768]{1,0:T(8,128)(2,1)}, bf16[1024,768]{1,0:T(8,128)(2,1)}, bf16[1024,768]{1,0:T(8,128)(2,1)}, /*index=5*/f32[8,640]{1,0:T(8,128)}) custom-call(s32[1536]{0:T(1024)} %xor.53.table, bf16[64,3,64,512]{3,2,1,0:T(8,128)(2,1)} %get-tuple-element.98.p_ref, ...), custom_call_target="tpu_custom_call" | custom-call | flops 40000000000 | bytes 25000000 | tf_op jit(solution)/shard_map/attend_backward/pallas_call | solution.py:348
  308.9 2.1 collective-permute-start.19
  311.0 1.6 collective-permute-done.19
  312.6 2.9 add_convert_fusion.2
  315.5 3.0 collective-permute-start.20
  318.5 1.3 collective-permute-start.22
  319.8 1.5 collective-permute-done.22
  321.3 1.2 collective-permute-start.23
  322.5 11.4 %head_weight_block.1 = bf16[768,576]{1,0:T(8,128)(2,1)} custom-call(bf16[1024,768]{1,0:T(8,128)(2,1)} %copy-done, bf16[1024,768]{1,0:T(8,128)(2,1)} %copy-done.1, bf16[1024,768]{1,0:T(8,128)(2,1)} %collective-permute-done.7.refs_2_.x2, bf16[1024,768]{1,0:T(8,128)(2,1)} %collective-permute-done.8.refs_3_.x3, bf16[4096,640]{1,0:T(8,128)(2,1)} %get-tuple-element.127.grad_ref), custom_call_target="tpu_custom_call" | custom-call | flops 8000000000 | bytes 12000000 | tf_op jit(solution)/shard_map/head_weight_block/pallas_call | solution.py:414
  333.9 2.5 collective-permute-start.24
  336.5 1.7 convert_add_fusion
  338.2 3.0 add_convert_fusion.1
  342.3 1.8 collective-permute-start.28
  344.2 6.7 %collective-permute-start.27 = (bf16[1024,768]{1,0:T(8,128)(2,1)}, bf16[1024,768]{1,0:T(8,128)(2,1)}, u32[]{:S(2)}, u32[]{:S(2)}) collective-permute-start(bf16[1024,768]{1,0:T(8,128)(2,1)} %add_convert_fusion.1), channel_id=1, source_target_pairs={{2,4},{3,5},{4,2},{5,3},{10,12},{11,13},{12,10},{13,11},{18,20},{1... | collective-permute-start | bytes 4718600 | tf_op jit(solution)/shard_map/ppermute | solution.py:818
  351.6 3.7 collective-permute-done.25
  355.3 1.3 add_convert_fusion.3
  356.6 1.4 collective-permute-start.26
  358.0 5.5 %collective-permute-done.26 = bf16[192,576]{1,0:T(8,128)(2,1)S(1)} collective-permute-done((bf16[192,576]{1,0:T(8,128)(2,1)S(1)}, bf16[192,576]{1,0:T(8,128)(2,1)S(1)}, u32[]{:S(2)}, u32[]{:S(2)}) %collective-permute-start.26) | collective-permute-done | bytes 221216 | tf_op jit(solution)/shard_map/ppermute | solution.py:818
  363.6 4.8 %collective-permute-start.29 = (bf16[192,576]{1,0:T(8,128)(2,1)S(1)}, bf16[192,576]{1,0:T(8,128)(2,1)}, u32[]{:S(2)}, u32[]{:S(2)}) collective-permute-start(bf16[192,576]{1,0:T(8,128)(2,1)S(1)} %add_convert_fusion.5), channel_id=1, source_target_pairs={{2,0},{3,1},{4,6},{5,7},{10,8},{11,9},{12,14},{13,15},{18,16},{19,... | collective-permute-start | bytes 663560 | tf_op jit(solution)/shard_map/ppermute | solution.py:818
  369.1 29.4 %collective-permute-done.29 = bf16[192,576]{1,0:T(8,128)(2,1)} collective-permute-done((bf16[192,576]{1,0:T(8,128)(2,1)S(1)}, bf16[192,576]{1,0:T(8,128)(2,1)}, u32[]{:S(2)}, u32[]{:S(2)}) %collective-permute-start.29) | collective-permute-done | bytes 221216 | tf_op jit(solution)/shard_map/ppermute | solution.py:818
  399.6 15.8 %collective-permute-start.30 = (bf16[96,576]{1,0:T(8,128)(2,1)S(1)}, bf16[96,576]{1,0:T(8,128)(2,1)S(1)}, u32[]{:S(2)}, u32[]{:S(2)}) collective-permute-start(bf16[96,576]{1,0:T(8,128)(2,1)S(1)} %constant_dynamic-slice_fusion), channel_id=1, source_target_pairs={{0,4},{1,5},{2,6},{3,7},{4,0},{5,1},{6,2},{7,3},{8,12},{9,13},{10,... | collective-permute-start | bytes 331784 | tf_op jit(solution)/shard_map/ppermute | solution.py:818
  415.3 2.7 broadcast_select_fusion.1
  420.4 1.7 add_convert_fusion
  422.1 2.7 broadcast_select_fusion
  (184 shorter events, 36.3 us)
Async XLA Ops:
  7.2 9.5 %copy-start.8 = (bf16[768,96]{0,1:T(8,128)(2,1)S(1)}, bf16[768,96]{0,1:T(8,128)(2,1)}, u32[]{:S(2)}) copy-start(bf16[768,96]{0,1:T(8,128)(2,1)} %param.25) | copy-start | bytes 442372
  7.2 9.5 %copy-start.9 = (bf16[96,768]{1,0:T(8,128)(2,1)S(1)}, bf16[96,768]{1,0:T(8,128)(2,1)}, u32[]{:S(2)}) copy-start(bf16[96,768]{1,0:T(8,128)(2,1)} %param.24) | copy-start | bytes 442372
  7.2 83.0 %all-gather.7.cloned.1.call-start = ((), (), s32[]{:S(2)}) async-start(), calls=%async_computation.5 | async-start | bytes 1863680 | tf_op jit(solution)/shard_map/all_gather | solution.py:835
  11.4 3.9 collective-permute-start
  12.4 14.6 %copy-start.3 = (bf16[1024,768]{1,0:T(8,128)(2,1)S(1)}, bf16[1024,768]{1,0:T(8,128)(2,1)}, u32[]{:S(2)}) copy-start(bf16[1024,768]{1,0:T(8,128)(2,1)} %param.18) | copy-start | bytes 4718596
  15.4 11.5 %collective-permute-start.1 = (bf16[195,576]{1,0:T(8,128)(2,1)S(1)}, bf16[195,576]{1,0:T(8,128)(2,1)S(1)}, u32[]{:S(2)}, u32[]{:S(2)}) collective-permute-start(bf16[195,576]{1,0:T(8,128)(2,1)S(1)} %pad_maximum_fusion.1), channel_id=1, source_target_pairs={{0,2},{1,3},{6,4},{7,5},{8,10},{9,11},{14,12},{15,13},{16,18},{17,... | collective-permute-start | bytes 673928 | tf_op jit(solution)/shard_map/ppermute | solution.py:818
  17.5 168.9 %all-gather.5.cloned.1.call-start = ((), (), s32[]{:S(2)}) async-start(), calls=%async_computation.2 | async-start | bytes 12386304 | tf_op jit(solution)/shard_map/all_gather | solution.py:862
  27.0 63.2 %collective-permute-start.3 = (bf16[1024,768]{1,0:T(8,128)(2,1)S(1)}, bf16[1024,768]{1,0:T(8,128)(2,1)}, u32[]{:S(2)}, u32[]{:S(2)}) collective-permute-start(bf16[1024,768]{1,0:T(8,128)(2,1)S(1)} %copy-done.3), channel_id=1, source_target_pairs={{2,4},{3,5},{4,2},{5,3},{10,12},{11,13},{12,10},{13,11},{18,20},{1... | collective-permute-start | bytes 4718600 | tf_op jit(solution)/shard_map/ppermute | solution.py:818
  30.3 5.5 %collective-permute-start.4 = (bf16[192,576]{1,0:T(8,128)(2,1)S(1)}, bf16[192,576]{1,0:T(8,128)(2,1)S(1)}, u32[]{:S(2)}, u32[]{:S(2)}) collective-permute-start(bf16[192,576]{1,0:T(8,128)(2,1)S(1)} %slice.199), channel_id=1, source_target_pairs={{0,8},{1,9},{2,10},{3,11},{4,12},{5,13},{6,14},{7,15},{8,0},{9,1},... | collective-permute-start | bytes 663560 | tf_op jit(solution)/shard_map/ppermute | solution.py:818
  36.0 11.5 %collective-permute-start.5 = (bf16[384,576]{1,0:T(8,128)(2,1)S(1)}, bf16[384,576]{1,0:T(8,128)(2,1)S(1)}, u32[]{:S(2)}, u32[]{:S(2)}) collective-permute-start(bf16[384,576]{1,0:T(8,128)(2,1)S(1)} %maximum_select_fusion.1), channel_id=1, source_target_pairs={{0,16},{1,17},{2,18},{3,19},{4,20},{5,21},{6,22},{7,23},{8,24},{9,... | collective-permute-start | bytes 1327112 | tf_op jit(solution)/shard_map/ppermute | solution.py:818
  92.8 275.7 %reduce-scatter.3.cloned.1.call-start = ((), (), s32[]{:S(2)}) async-start(), calls=%async_computation.3 | async-start | bytes 12386304 | tf_op jit(solution)/shard_map/reduce_scatter | solution.py:913
  92.8 4.5 %collective-permute-start.2 = (bf16[1024,768]{1,0:T(8,128)(2,1)S(1)}, bf16[1024,768]{1,0:T(8,128)(2,1)S(1)}, u32[]{:S(2)}, u32[]{:S(2)}) collective-permute-start(bf16[1024,768]{1,0:T(8,128)(2,1)S(1)} %copy-done.3), channel_id=1, source_target_pairs={{0,1},{1,0},{6,7},{7,6},{8,9},{9,8},{14,15},{15,14},{16,17},{17,16... | collective-permute-start | bytes 4718600 | tf_op jit(solution)/shard_map/ppermute | solution.py:818
  95.2 28.7 %copy-start = (bf16[1024,768]{1,0:T(8,128)(2,1)}, bf16[1024,768]{1,0:T(8,128)(2,1)S(1)}, u32[]{:S(2)}) copy-start(bf16[1024,768]{1,0:T(8,128)(2,1)S(1)} %broadcast_select_fusion.4.refs_0_.x_ref.x0) | copy-start | bytes 4718596
  95.2 29.3 %copy-start.10 = (f32[768]{0:T(1024)S(1)}, f32[768]{0:T(1024)}, u32[]{:S(2)}) copy-start(f32[768]{0:T(1024)} %param.28) | copy-start | bytes 9220
  95.2 29.3 %copy-start.11 = (f32[768]{0:T(1024)S(1)}, f32[768]{0:T(1024)}, u32[]{:S(2)}) copy-start(f32[768]{0:T(1024)} %param.29) | copy-start | bytes 9220
  95.2 29.3 %copy-start.12 = (f32[768]{0:T(1024)S(1)}, f32[768]{0:T(1024)}, u32[]{:S(2)}) copy-start(f32[768]{0:T(1024)} %param.30) | copy-start | bytes 9220
  95.2 29.3 %copy-start.13 = (f32[768]{0:T(1024)S(1)}, f32[768]{0:T(1024)}, u32[]{:S(2)}) copy-start(f32[768]{0:T(1024)} %param.32) | copy-start | bytes 9220
  95.2 29.3 %copy-start.14 = (f32[768]{0:T(1024)S(1)}, f32[768]{0:T(1024)}, u32[]{:S(2)}) copy-start(f32[768]{0:T(1024)} %param.33) | copy-start | bytes 9220
  95.2 29.3 %copy-start.15 = (f32[768]{0:T(1024)S(1)}, f32[768]{0:T(1024)}, u32[]{:S(2)}) copy-start(f32[768]{0:T(1024)} %param.34) | copy-start | bytes 9220
  95.2 28.5 %collective-permute-start.6 = (bf16[1024,768]{1,0:T(8,128)(2,1)S(1)}, bf16[1024,768]{1,0:T(8,128)(2,1)S(1)}, u32[]{:S(2)}, u32[]{:S(2)}) collective-permute-start(bf16[1024,768]{1,0:T(8,128)(2,1)S(1)} %broadcast_select_fusion.4.refs_0_.x_ref.x0), channel_id=1, source_target_pairs={{2,3},{3,2},{4,5},{5,4},{10,11},{11,10},{12,13},{13,12},{18,19},{1... | collective-permute-start | bytes 4718600 | tf_op jit(solution)/shard_map/ppermute | solution.py:818
  123.9 8.4 %collective-permute-start.7 = (bf16[1024,768]{1,0:T(8,128)(2,1)S(1)}, bf16[1024,768]{1,0:T(8,128)(2,1)}, u32[]{:S(2)}, u32[]{:S(2)}) collective-permute-start(bf16[1024,768]{1,0:T(8,128)(2,1)S(1)} %broadcast_select_fusion.4.refs_0_.x_ref.x0), channel_id=1, source_target_pairs={{0,4},{1,5},{2,6},{3,7},{4,0},{5,1},{6,2},{7,3},{8,12},{9,13},{10,... | collective-permute-start | bytes 4718600 | tf_op jit(solution)/shard_map/ppermute | solution.py:818
  124.0 8.8 %collective-permute-start.8 = (bf16[1024,768]{1,0:T(8,128)(2,1)S(1)}, bf16[1024,768]{1,0:T(8,128)(2,1)}, u32[]{:S(2)}, u32[]{:S(2)}) collective-permute-start(bf16[1024,768]{1,0:T(8,128)(2,1)S(1)} %broadcast_select_fusion.3.refs_1_.x1), channel_id=1, source_target_pairs={{0,4},{1,5},{2,6},{3,7},{4,0},{5,1},{6,2},{7,3},{8,12},{9,13},{10,... | collective-permute-start | bytes 4718600 | tf_op jit(solution)/shard_map/ppermute | solution.py:818
  124.6 48.0 %collective-permute-start.12 = (bf16[1024,768]{1,0:T(8,128)(2,1)}, bf16[1024,768]{1,0:T(8,128)(2,1)}, u32[]{:S(2)}, u32[]{:S(2)}) collective-permute-start(bf16[1024,768]{1,0:T(8,128)(2,1)} %param.19), channel_id=1, source_target_pairs={{2,4},{3,5},{4,2},{5,3},{10,12},{11,13},{12,10},{13,11},{18,20},{1... | collective-permute-start | bytes 4718600 | tf_op jit(solution)/shard_map/ppermute | solution.py:818
  161.1 14.3 %collective-permute-start.10 = (bf16[1024,192]{1,0:T(8,128)(2,1)}, bf16[1024,192]{1,0:T(8,128)(2,1)S(1)}, u32[]{:S(2)}, u32[]{:S(2)}) collective-permute-start(bf16[1024,192]{1,0:T(8,128)(2,1)} %get-tuple-element.93), channel_id=1, source_target_pairs={{0,4},{1,5},{2,6},{3,7},{4,0},{5,1},{6,2},{7,3},{8,12},{9,13},{10,... | collective-permute-start | bytes 1179656 | tf_op jit(solution)/shard_map/ppermute | solution.py:818
  161.7 14.4 %collective-permute-start.11 = (bf16[1024,192]{1,0:T(8,128)(2,1)}, bf16[1024,192]{1,0:T(8,128)(2,1)S(1)}, u32[]{:S(2)}, u32[]{:S(2)}) collective-permute-start(bf16[1024,192]{1,0:T(8,128)(2,1)} %get-tuple-element.94), channel_id=1, source_target_pairs={{0,5},{1,4},{2,7},{3,6},{4,1},{5,0},{6,3},{7,2},{8,13},{9,12},{10,... | collective-permute-start | bytes 1179656 | tf_op jit(solution)/shard_map/ppermute | solution.py:818
  162.7 23.8 %collective-permute-start.9 = (bf16[1024,192]{1,0:T(8,128)(2,1)}, bf16[1024,192]{1,0:T(8,128)(2,1)S(1)}, u32[]{:S(2)}, u32[]{:S(2)}) collective-permute-start(bf16[1024,192]{1,0:T(8,128)(2,1)} %get-tuple-element.92), channel_id=1, source_target_pairs={{0,1},{1,0},{2,3},{3,2},{4,5},{5,4},{6,7},{7,6},{8,9},{9,8},{10,11... | collective-permute-start | bytes 1179656 | tf_op jit(solution)/shard_map/ppermute | solution.py:818
  175.4 11.0 %copy-start.16 = (bf16[1024,192]{1,0:T(8,128)(2,1)}, bf16[1024,192]{1,0:T(8,128)(2,1)S(1)}, u32[]{:S(2)}) copy-start(bf16[1024,192]{1,0:T(8,128)(2,1)S(1)} %collective-permute-done.10.o2) | copy-start | bytes 1179652
  176.1 10.4 %copy-start.17 = (bf16[1024,192]{1,0:T(8,128)(2,1)}, bf16[1024,192]{1,0:T(8,128)(2,1)S(1)}, u32[]{:S(2)}) copy-start(bf16[1024,192]{1,0:T(8,128)(2,1)S(1)} %collective-permute-done.11.o3) | copy-start | bytes 1179652
  229.1 25.1 %collective-permute-start.13 = (f32[7680]{0:T(1024)S(1)}, f32[7680]{0:T(1024)S(1)}, u32[]{:S(2)}, u32[]{:S(2)}) collective-permute-start(f32[7680]{0:T(1024)S(1)} %reduce.1), channel_id=1, source_target_pairs={{0,1},{1,0},{2,3},{3,2},{4,5},{5,4},{6,7},{7,6},{8,9},{9,8},{10,11... | collective-permute-start | bytes 92168 | tf_op jit(solution)/shard_map/ppermute | solution.py:818
  230.5 23.7 %collective-permute-start.14 = (bf16[1024,192]{1,0:T(8,128)(2,1)}, bf16[1024,192]{1,0:T(8,128)(2,1)S(1)}, u32[]{:S(2)}, u32[]{:S(2)}) collective-permute-start(bf16[1024,192]{1,0:T(8,128)(2,1)} %get-tuple-element.106), channel_id=1, source_target_pairs={{0,1},{1,0},{2,3},{3,2},{4,5},{5,4},{6,7},{7,6},{8,9},{9,8},{10,11... | collective-permute-start | bytes 1179656 | tf_op jit(solution)/shard_map/ppermute | solution.py:818
  230.6 23.6 %collective-permute-start.15 = (bf16[1024,192]{1,0:T(8,128)(2,1)}, bf16[1024,192]{1,0:T(8,128)(2,1)S(1)}, u32[]{:S(2)}, u32[]{:S(2)}) collective-permute-start(bf16[1024,192]{1,0:T(8,128)(2,1)} %get-tuple-element.107), channel_id=1, source_target_pairs={{0,4},{1,5},{2,6},{3,7},{4,0},{5,1},{6,2},{7,3},{8,12},{9,13},{10,... | collective-permute-start | bytes 1179656 | tf_op jit(solution)/shard_map/ppermute | solution.py:818
  232.2 23.7 %collective-permute-start.16 = (bf16[1024,192]{1,0:T(8,128)(2,1)}, bf16[1024,192]{1,0:T(8,128)(2,1)S(1)}, u32[]{:S(2)}, u32[]{:S(2)}) collective-permute-start(bf16[1024,192]{1,0:T(8,128)(2,1)} %get-tuple-element.108), channel_id=1, source_target_pairs={{0,5},{1,4},{2,7},{3,6},{4,1},{5,0},{6,3},{7,2},{8,13},{9,12},{10,... | collective-permute-start | bytes 1179656 | tf_op jit(solution)/shard_map/ppermute | solution.py:818
  256.6 168.2 %reduce-scatter.5.cloned.1.call-start = ((), (), s32[]{:S(2)}) async-start(), calls=%async_computation.4 | async-start | bytes 1720320 | tf_op jit(solution)/shard_map/reduce_scatter | solution.py:916
  257.4 48.7 %collective-permute-start.17 = (bf16[1024,768]{1,0:T(8,128)(2,1)S(1)}, bf16[1024,768]{1,0:T(8,128)(2,1)S(1)}, u32[]{:S(2)}, u32[]{:S(2)}) collective-permute-start(bf16[1024,768]{1,0:T(8,128)(2,1)S(1)} %copy-done.5), channel_id=1, source_target_pairs={{2,4},{3,5},{4,2},{5,3},{10,12},{11,13},{12,10},{13,11},{18,20},{1... | collective-permute-start | bytes 4718600 | tf_op jit(solution)/shard_map/ppermute | solution.py:818
  307.3 5.3 %collective-permute-start.18 = (bf16[1024,768]{1,0:T(8,128)(2,1)}, bf16[1024,768]{1,0:T(8,128)(2,1)S(1)}, u32[]{:S(2)}, u32[]{:S(2)}) collective-permute-start(bf16[1024,768]{1,0:T(8,128)(2,1)} %get-tuple-element.122), channel_id=1, source_target_pairs={{0,4},{1,5},{2,6},{3,7},{4,0},{5,1},{6,2},{7,3},{8,12},{9,13},{10,... | collective-permute-start | bytes 4718600 | tf_op jit(solution)/shard_map/ppermute | solution.py:818
  308.1 28.4 %collective-permute-start.21 = (bf16[1024,768]{1,0:T(8,128)(2,1)}, bf16[1024,768]{1,0:T(8,128)(2,1)}, u32[]{:S(2)}, u32[]{:S(2)}) collective-permute-start(bf16[1024,768]{1,0:T(8,128)(2,1)} %get-tuple-element.129), channel_id=1, source_target_pairs={{0,4},{1,5},{2,6},{3,7},{4,0},{5,1},{6,2},{7,3},{8,12},{9,13},{10,... | collective-permute-start | bytes 4718600 | tf_op jit(solution)/shard_map/ppermute | solution.py:818
  308.9 3.7 collective-permute-start.19
  315.5 22.7 %collective-permute-start.20 = (bf16[1024,768]{1,0:T(8,128)(2,1)}, bf16[1024,768]{1,0:T(8,128)(2,1)}, u32[]{:S(2)}, u32[]{:S(2)}) collective-permute-start(bf16[1024,768]{1,0:T(8,128)(2,1)} %add_convert_fusion.2), channel_id=1, source_target_pairs={{2,3},{3,2},{4,5},{5,4},{10,11},{11,10},{12,13},{13,12},{18,19},{1... | collective-permute-start | bytes 4718600 | tf_op jit(solution)/shard_map/ppermute | solution.py:818
  318.5 2.8 collective-permute-start.22
  321.3 12.6 %collective-permute-start.23 = (f32[8064]{0:T(1024)S(1)}, f32[8064]{0:T(1024)S(1)}, u32[]{:S(2)}, u32[]{:S(2)}) collective-permute-start(f32[8064]{0:T(1024)S(1)} %add.157), channel_id=1, source_target_pairs={{0,16},{1,17},{2,18},{3,19},{4,20},{5,21},{6,22},{7,23},{8,24},{9,... | collective-permute-start | bytes 96776 | tf_op jit(solution)/shard_map/ppermute | solution.py:818
  322.5 14.0 %copy-start.2 = (f32[1024,768]{1,0:T(8,128)S(1)}, f32[1024,768]{1,0:T(8,128)}, u32[]{:S(2)}) copy-start(f32[1024,768]{1,0:T(8,128)} %get-tuple-element.128) | copy-start | bytes 9437188
  333.9 4.3 collective-permute-start.24
  342.1 13.2 %collective-permute-start.25 = (bf16[384,576]{1,0:T(8,128)(2,1)}, bf16[384,576]{1,0:T(8,128)(2,1)}, u32[]{:S(2)}, u32[]{:S(2)}) collective-permute-start(bf16[384,576]{1,0:T(8,128)(2,1)} %constant_dynamic-slice_fusion.2), channel_id=1, source_target_pairs={{0,16},{1,17},{2,18},{3,19},{4,20},{5,21},{6,22},{7,23},{8,24},{9,... | collective-permute-start | bytes 1327112 | tf_op jit(solution)/shard_map/ppermute | solution.py:818
  342.3 78.0 %collective-permute-start.28 = (bf16[1024,768]{1,0:T(8,128)(2,1)}, bf16[1024,768]{1,0:T(8,128)(2,1)}, u32[]{:S(2)}, u32[]{:S(2)}) collective-permute-start(bf16[1024,768]{1,0:T(8,128)(2,1)} %add_convert_fusion.2), channel_id=1, source_target_pairs={{0,1},{1,0},{6,7},{7,6},{8,9},{9,8},{14,15},{15,14},{16,17},{17,16... | collective-permute-start | bytes 4718600 | tf_op jit(solution)/shard_map/ppermute | solution.py:818
  344.2 78.0 %collective-permute-start.27 = (bf16[1024,768]{1,0:T(8,128)(2,1)}, bf16[1024,768]{1,0:T(8,128)(2,1)}, u32[]{:S(2)}, u32[]{:S(2)}) collective-permute-start(bf16[1024,768]{1,0:T(8,128)(2,1)} %add_convert_fusion.1), channel_id=1, source_target_pairs={{2,4},{3,5},{4,2},{5,3},{10,12},{11,13},{12,10},{13,11},{18,20},{1... | collective-permute-start | bytes 4718600 | tf_op jit(solution)/shard_map/ppermute | solution.py:818
  356.6 6.9 %collective-permute-start.26 = (bf16[192,576]{1,0:T(8,128)(2,1)S(1)}, bf16[192,576]{1,0:T(8,128)(2,1)S(1)}, u32[]{:S(2)}, u32[]{:S(2)}) collective-permute-start(bf16[192,576]{1,0:T(8,128)(2,1)S(1)} %constant_dynamic-slice_fusion.1), channel_id=1, source_target_pairs={{0,8},{1,9},{2,10},{3,11},{4,12},{5,13},{6,14},{7,15},{8,0},{9,1},... | collective-permute-start | bytes 663560 | tf_op jit(solution)/shard_map/ppermute | solution.py:818
  363.6 34.9 %collective-permute-start.29 = (bf16[192,576]{1,0:T(8,128)(2,1)S(1)}, bf16[192,576]{1,0:T(8,128)(2,1)}, u32[]{:S(2)}, u32[]{:S(2)}) collective-permute-start(bf16[192,576]{1,0:T(8,128)(2,1)S(1)} %add_convert_fusion.5), channel_id=1, source_target_pairs={{2,0},{3,1},{4,6},{5,7},{10,8},{11,9},{12,14},{13,15},{18,16},{19,... | collective-permute-start | bytes 663560 | tf_op jit(solution)/shard_map/ppermute | solution.py:818
  399.6 18.5 %collective-permute-start.30 = (bf16[96,576]{1,0:T(8,128)(2,1)S(1)}, bf16[96,576]{1,0:T(8,128)(2,1)S(1)}, u32[]{:S(2)}, u32[]{:S(2)}) collective-permute-start(bf16[96,576]{1,0:T(8,128)(2,1)S(1)} %constant_dynamic-slice_fusion), channel_id=1, source_target_pairs={{0,4},{1,5},{2,6},{3,7},{4,0},{5,1},{6,2},{7,3},{8,12},{9,13},{10,... | collective-permute-start | bytes 331784 | tf_op jit(solution)/shard_map/ppermute | solution.py:818
  (9 other events, 28.5 us)
Sparse Core Ops, SparseCore 0:
  17.7 61.6 all-gather.6
  92.9 64.7 all-gather.4
  256.0 83.5 reduce-scatter.2
  368.6 40.6 reduce-scatter.4

commit v4 on v3

--- a/solution.py
+++ b/solution.py
@@ -88,7 +88,7 @@
                 copy.start()
             for copy in copies:
                 copy.wait()
-            chunk = 256
+            chunk = 512
 
             def body(n, carry):
                 rows = pl.ds(pl.multiple_of(n * chunk, chunk), chunk)
@@ -217,6 +217,10 @@
     do1,
     do2,
     do3,
+    o0,
+    o1,
+    o2,
+    o3,
     w_ref,
     da_hbm,
     out_hbm,
@@ -227,8 +231,8 @@
     sum_ref,
     qkv_scr,
     do_scr,
+    o_scr,
     acc,
-    dp_scr,
     st_scr,
     out_ref,
     da_scr,
@@ -243,6 +247,10 @@
             pltpu.make_async_copy(src, do_scr.at[pl.ds(n * QROWS, QROWS)], sems.at[4 + n])
             for n, src in enumerate((do0, do1, do2, do3))
         ]
+        copies += [
+            pltpu.make_async_copy(src, o_scr.at[pl.ds(n * QROWS, QROWS)], sems.at[9 + n])
+            for n, src in enumerate((o0, o1, o2, o3))
+        ]
         copies.append(pltpu.make_async_copy(da_hbm, da_scr, sems.at[8]))
         for copy in copies:
             copy.start()
@@ -254,7 +262,7 @@
     lane = lax.broadcasted_iota(jnp.int32, (1, 128), 1)
     per = NB // steps
     units = [(sub, head) for sub in range(per) for head in range(HEADS)]
-    keys, right = [], []
+    keys, right, wide_low, wide_high = [], [], low.astype(jnp.float32), high.astype(jnp.float32)
     for sub in range(per):
         local = step * per + sub
         rows = pl.ds(pl.multiple_of(local * BLOCK, BLOCK), BLOCK)
@@ -263,6 +271,13 @@
         )
         g_first = do_scr[rows, 0:128]
         g_second = do_scr[rows, 128:192]
+        first = g_first.astype(jnp.float32) * o_scr[rows, 0:128].astype(jnp.float32)
+        second = g_second.astype(jnp.float32) * o_scr[rows, 128:192].astype(jnp.float32)
+        totals = (
+            jnp.sum(first * wide_low, axis=1, keepdims=True),
+            jnp.sum(first * wide_high, axis=1, keepdims=True),
+            jnp.sum(second, axis=1, keepdims=True),
+        )
         grads = (
             g_first * low,
             g_first * high,
@@ -272,16 +287,10 @@
             n = sub * HEADS + head
             keys.append(gather_keys(table, qkv_scr, head, local))
             right.append(jnp.concatenate([queries[head], grads[head]], axis=0))
-            dp_scr[n] = dot_nt(grads[head], keys[n])
-    totals = []
-    for n, (sub, head) in enumerate(units):
-        weighted = p_ref[sub, head].astype(jnp.float32) * dp_scr[n]
-        dp_scr[n] = weighted
-        totals.append(jnp.sum(weighted, axis=1, keepdims=True))
-    for n, (sub, head) in enumerate(units):
-        probs = p_ref[sub, head]
-        st_scr[n, 0:BLOCK] = (dp_scr[n] - probs.astype(jnp.float32) * totals[n]).astype(jnp.bfloat16)
-        st_scr[n, BLOCK:128] = probs
+            probs = p_ref[sub, head]
+            slopes = probs.astype(jnp.float32) * (dot_nt(grads[head], keys[n]) - totals[head])
+            st_scr[n, 0:BLOCK] = slopes.astype(jnp.bfloat16)
+            st_scr[n, BLOCK:128] = probs
     for sub in range(per):
         local = step * per + sub
         rows = pl.ds(pl.multiple_of(local * BLOCK, BLOCK), BLOCK)
@@ -312,7 +321,7 @@
         sum_ref[...] = total
         done = [pltpu.make_async_copy(out_ref, out_hbm, sems.at[0])]
         done[0].start()
-        chunk = 256
+        chunk = 512
 
         def share(n, carry):
             source = (3 - n // (QROWS // chunk)) * QROWS + (n % (QROWS // chunk)) * chunk
@@ -339,7 +348,7 @@
             copy.wait()
 
 
-def attend_backward(table, probs, qkv, grads, w_qkv, da):
+def attend_backward(table, probs, qkv, grads, outs, w_qkv, da):
     steps = 16
     per = NB // steps
     width = w_qkv.shape[0]
@@ -351,19 +360,19 @@
             num_scalar_prefetch=1,
             grid=(steps,),
             in_specs=[pl.BlockSpec((per, HEADS, BLOCK, KEYS), lambda g, *_: (g, 0, 0, 0))]
-            + [any_spec] * 5
+            + [any_spec] * 9
             + [pl.BlockSpec((width, QKV), lambda g, *_: (0, 0)), any_spec],
             out_specs=[any_spec] * 5 + [pl.BlockSpec((8, QKV), lambda g, *_: (0, 0))],
             scratch_shapes=[
                 pltpu.VMEM((LENGTH, QKV), jnp.bfloat16),
                 pltpu.VMEM((LENGTH, 192), jnp.bfloat16),
+                pltpu.VMEM((LENGTH, 192), jnp.bfloat16),
                 pltpu.VMEM((LENGTH, KV), jnp.float32),
-                pltpu.VMEM((per * HEADS, BLOCK, KEYS), jnp.float32),
                 pltpu.VMEM((per * HEADS, 128, KEYS), jnp.bfloat16),
                 pltpu.VMEM((LENGTH, QKV), jnp.bfloat16),
                 pltpu.VMEM((QROWS, width), jnp.float32),
                 pltpu.VMEM((3 * QROWS, width), jnp.bfloat16),
-                pltpu.SemaphoreType.DMA((9,)),
+                pltpu.SemaphoreType.DMA((13,)),
             ],
         ),
         out_shape=[
@@ -381,7 +390,7 @@
             flops=40 * 10**9, transcendentals=0, bytes_accessed=25 * 10**6
         ),
         name="attend_backward",
-    )(table, probs, qkv, *grads, w_qkv, da)
+    )(table, probs, qkv, *grads, *outs, w_qkv, da)
 
 
 def head_weight_kernel(x0, x1, x2, x3, grad_ref, out_ref, x_scr, acc, sems):
@@ -483,14 +492,21 @@
     parts = GROUP
     small = 32
     cols = 256
+    spans = ((2 * hidden, weights.shape[1] - 2 * hidden), (0, hidden), (hidden, hidden))
+    arrivals = [
+        pltpu.make_async_copy(
+            weights.at[:, pl.ds(*span)], w_scr.at[:, pl.ds(*span)], sem.at[n]
+        )
+        for n, span in enumerate(spans)
+    ]
 
     @pl.when(step == 0)
     def _load():
-        copy = pltpu.make_async_copy(weights, w_scr, sem)
-        copy.start()
+        for copy in arrivals:
+            copy.start()
         sum_ref[...] = jnp.zeros_like(sum_ref)
         up_sum_ref[...] = jnp.zeros_like(up_sum_ref)
-        copy.wait()
+        arrivals[0].wait()
 
     def vector(n):
         return vec_ref[n : n + 1, :]
@@ -518,6 +534,12 @@
         xhat_scr[rows] = xhat
         m1_scr[rows] = normed
         n1_ref[rows] = normed.astype(jnp.bfloat16)
+
+    @pl.when(step == 0)
+    def _arrived():
+        arrivals[1].wait()
+        arrivals[2].wait()
+
     for part in range(parts):
         u_scr[part % 2] = dot_nn(n1_ref[...], w_scr[part_rows(part), 0:hidden])
         for row in range(0, tile, small):
@@ -643,7 +665,7 @@
                 pltpu.VMEM((tile, width), jnp.float32),
                 pltpu.VMEM((6, 8, width), jnp.float32),
                 pltpu.VMEM((8, total_hidden), jnp.float32),
-                pltpu.SemaphoreType.DMA,
+                pltpu.SemaphoreType.DMA((3,)),
             ],
         ),
         out_shape=[
@@ -913,16 +935,10 @@
     rest_sum = lax.psum_scatter(
         rest_grad.reshape(GROUP, width, -1), "dp", scatter_dimension=1, tiled=True
     )
-    rest_sum = lax.psum_scatter(rest_sum, "tensor", scatter_dimension=0, tiled=False).astype(
-        jnp.float32
-    )
-    shard_up = rest_sum[:, :hidden]
-    shard_down = rest_sum[:, hidden : 2 * hidden].T
-    shard_output = rest_sum[:, 2 * hidden :].T
     layer_sent = flip(layer_out, 1, 2, moves)
 
     grad_qkv, base, to_near, to_side, to_far, bias_sum = attend_backward(
-        table, probs, qkv, grads, w_qkv, da
+        table, probs, qkv, grads, (out_own, out_near, out_side, out_far), w_qkv, da
     )
     grad_qkv, base, to_near, to_side, to_far, bias_sum, layer_sent = lax.optimization_barrier(
         (grad_qkv, base, to_near, to_side, to_far, bias_sum, layer_sent)
@@ -934,37 +950,49 @@
     sums = sums + flip(sums, 0, 2)
     to_near = (to_near.astype(jnp.float32) + side_far.astype(jnp.float32)).astype(low)
     to_near, sums = lax.optimization_barrier((to_near, sums))
-    near_move = flip(to_near, 0, 1, moves)
+    near_got = near_of(to_near)
     base = base + side_own.astype(jnp.float32)
     grad_late, to_near = lax.optimization_barrier((grad_qkv, to_near))
     for bit in pair_bits:
         sums = sums + flip(sums, 1 << bit, 0)
     other = side_of(sums)
+    grad_late, sums = lax.optimization_barrier((grad_late, sums))
     grad_w = head_weight_block(rows, grad_late)
-    to_near, near_move, grad_w, base, sums, other = lax.optimization_barrier(
-        (to_near, near_move, grad_w, base, sums, other)
-    )
-    grad_move = (base + near_move.astype(jnp.float32)).astype(low)
-    grad_move, to_near, grad_w, base = lax.optimization_barrier(
-        (grad_move, to_near, grad_w, base)
-    )
-    grad_moved = flip(grad_move, 1, 2, moves)
-    near_stay = flip(to_near, 0, 1, stays)
-    grad_stay = (base + near_stay.astype(jnp.float32)).astype(low)
-    grad_moved, grad_stay = lax.optimization_barrier((grad_moved, grad_stay))
-    grad_input = jnp.where(here, grad_stay, grad_moved)
-
-    for bit in reversed(pair_bits):
+    rest_sum, base, grad_w = lax.optimization_barrier((rest_sum, base, grad_w))
+    rest_sum = lax.psum_scatter(rest_sum, "tensor", scatter_dimension=0, tiled=False).astype(
+        jnp.float32
+    )
+    for bit in reversed(pair_bits[2:]):
         grad_w = halve(flip, (dp_index >> bit) % 2, grad_w, 1 << bit, 0)
-    grad_w, layer_sent = lax.optimization_barrier((grad_w, layer_sent))
-    layer_out = jnp.where(here, layer_out, layer_sent)
-    grad_w = grad_w.astype(jnp.float32) + flip(grad_w, 0, 2, moves).astype(jnp.float32)
+    place = (dp_index // 2) % 4
+    rows_each = grad_w.shape[0] // 4
+    total = lax.dynamic_slice_in_dim(grad_w, place * rows_each, rows_each, 0).astype(jnp.float32)
+    for n in (3, 1, 2):
+        send = lax.dynamic_slice_in_dim(grad_w, (place ^ n) * rows_each, rows_each, 0)
+        total = total + flip(send, 2 * n, 0).astype(jnp.float32)
+    grad_w = total.astype(low)
+    near_got, grad_w, base, sums, other, layer_sent = lax.optimization_barrier(
+        (near_got, grad_w, base, sums, other, layer_sent)
+    )
+    grad_own = (base + near_got.astype(jnp.float32)).astype(low)
+    grad_own, grad_w, layer_sent = lax.optimization_barrier((grad_own, grad_w, layer_sent))
+    grad_moved = flip(grad_own, 1, 2, moves)
+
+    grad_got = flip(grad_w, 0, 2, moves)
+    grad_w = grad_w.astype(jnp.float32) + grad_got.astype(jnp.float32)
     rows_each = grad_w.shape[0] // 2
     grad_w = grad_w.astype(low)
     keep = lax.dynamic_slice_in_dim(grad_w, core * rows_each, rows_each, 0)
     send = lax.dynamic_slice_in_dim(grad_w, (1 - core) * rows_each, rows_each, 0)
-    shard = jnp.where(here, keep, side_of(send)).astype(jnp.float32)
+    side_got = side_of(send)
+    grad_moved, side_got, rest_sum = lax.optimization_barrier((grad_moved, side_got, rest_sum))
+    shard = jnp.where(here, keep, side_got).astype(jnp.float32)
     shard_query, shard_key, shard_value = unpack_columns(shard, 1)
+    shard_up = rest_sum[:, :hidden]
+    shard_down = rest_sum[:, hidden : 2 * hidden].T
+    shard_output = rest_sum[:, 2 * hidden :].T
+    layer_out = jnp.where(here, layer_out, layer_sent)
+    grad_input = jnp.where(here, grad_own, grad_moved)
 
     count = 6 * width + GROUP * hidden
     bias_pair = jnp.where(here, sums[count:], other[count:])

time: 436 us -> 425 us (0.975)
  other arithmetic: 32.8 us -> 28.1 us
    ppermute x31, waiting for transfers between devices: 146 us -> 136 us  [flip(): return lax.ppermute(value, both, pairs)]
    reduce_scatter x1, waiting for transfers between devices: 0.01 us -> 5.75 us  [per_device(): lax.psum_scatter(rest_grad.reshape(GROUP, width, -1), 'dp', scatter_dimen...]
  transfers between devices with their start and end apart: 35 -> 35, of which waited for: 14 -> 17; matrix products, arithmetic and copies ran while one was open for 9% -> 8% of each run, Pallas kernels for 27% -> 27%
where the time goes in v4:
time: 425 us; the launch traced here: 423 us
  Pallas kernels  153 us (36%)
  waiting for transfers between devices  142 us (33%)
  starting transfers between devices  63.6 us (15%)
  other arithmetic  28.1 us (7%)
  local copies, waits for them, and re-layouts  22.2 us (5%)
  between operations  14.6 us (3%)
    ppermute x31, waiting for transfers between devices, flip(): return lax.ppermute(value, both, pairs)  136 us
    ppermute x31, starting transfers between devices, flip(): return lax.ppermute(value, both, pairs)  63.5 us
    pallas_call x1, Pallas kernels, attend_backward(): pl.pallas_call(functools.partial(backward_kernel, steps), grid_spec=pltpu...  44.9 us
    pallas_call x1, Pallas kernels, token_block(): pl.pallas_call(functools.partial(token_kernel, tile, width, hidden), grid...  40.2 us
    pallas_call x2, Pallas kernels, attend_forward(): pl.pallas_call(functools.partial(forward_kernel, steps, count, project),...  35.8 us
    pallas_call x1, Pallas kernels, weight_block(): pl.pallas_call(functools.partial(weight_kernel, width, hidden), grid_spec...  21.2 us
    pallas_call x1, Pallas kernels, head_weight_block(): pl.pallas_call(head_weight_kernel, grid=(GROUP,), in_specs=[any_spec] * 4...  11.1 us
  transfers between devices with their start and end apart: 35, of which 17 were waited for; matrix products, arithmetic and copies ran while one was open for 8% of the time, Pallas kernels for 27%

profile of v4, /device:TPU:1, one launch (start us, length us, event | category | flops | bytes accessed | tf_op | source)
XLA Modules:
  0.0 423.3 jit_solution(15425672357295980968)
XLA Ops:
  15.4 1.3 collective-permute-start.1
  17.6 9.3 %collective-permute-done.1 = bf16[195,576]{1,0:T(8,128)(2,1)S(1)} collective-permute-done((bf16[195,576]{1,0:T(8,128)(2,1)S(1)}, bf16[195,576]{1,0:T(8,128)(2,1)S(1)}, u32[]{:S(2)}, u32[]{:S(2)}) %collective-permute-start.1) | collective-permute-done | bytes 224672 | tf_op jit(solution)/shard_map/ppermute | solution.py:840
  27.0 3.3 collective-permute-start.3
  30.3 1.3 collective-permute-start.4
  31.7 4.1 collective-permute-done.4
  36.0 1.3 collective-permute-start.5
  37.5 10.0 %collective-permute-done.5 = bf16[384,576]{1,0:T(8,128)(2,1)S(1)} collective-permute-done((bf16[384,576]{1,0:T(8,128)(2,1)S(1)}, bf16[384,576]{1,0:T(8,128)(2,1)S(1)}, u32[]{:S(2)}, u32[]{:S(2)}) %collective-permute-start.5) | collective-permute-done | bytes 442400 | tf_op jit(solution)/shard_map/ppermute | solution.py:840
  47.9 1.2 pad_maximum_fusion.refs_4_.w_ref
  49.2 41.0 %collective-permute-done.3 = bf16[1024,768]{1,0:T(8,128)(2,1)} collective-permute-done((bf16[1024,768]{1,0:T(8,128)(2,1)S(1)}, bf16[1024,768]{1,0:T(8,128)(2,1)}, u32[]{:S(2)}, u32[]{:S(2)}) %collective-permute-start.3) | collective-permute-done | bytes 1572896 | tf_op jit(solution)/shard_map/ppermute | solution.py:840
  90.2 2.5 slice.215
  93.6 1.6 broadcast_select_fusion.4.refs_0_.x_ref.x0
  95.3 2.1 collective-permute-start.6
  97.3 26.4 %collective-permute-done.6 = bf16[1024,768]{1,0:T(8,128)(2,1)S(1)} collective-permute-done((bf16[1024,768]{1,0:T(8,128)(2,1)S(1)}, bf16[1024,768]{1,0:T(8,128)(2,1)S(1)}, u32[]{:S(2)}, u32[]{:S(2)}) %collective-permute-start.6) | collective-permute-done | bytes 1572896 | tf_op jit(solution)/shard_map/ppermute | solution.py:840
  124.6 2.1 collective-permute-start.12
  132.7 26.8 %attend_forward.2 = (bf16[1024,192]{1,0:T(8,128)(2,1)}, bf16[1024,192]{1,0:T(8,128)(2,1)}, bf16[1024,192]{1,0:T(8,128)(2,1)}, bf16[64,3,64,512]{3,2,1,0:T(8,128)(2,1)}, bf16[4096,640]{1,0:T(8,128)(2,1)}) custom-call(s32[1536]{0:T(1024)} %xor.62.table, s32[4]{0:T(128)} %pad_add_fusion.1.place, bf16[1024,768]{1,0:T(8,128)(2,1)} %copy-done, ...), custom_call_target="tpu_custom_call" | custom-call | tf_op jit(solution)/shard_map/attend_forward/pallas_call | solution.py:172
  162.2 9.0 %attend_forward.3 = (bf16[1024,192]{1,0:T(8,128)(2,1)}, bf16[64,3,64,512]{3,2,1,0:T(8,128)(2,1)}) custom-call(s32[1536]{0:T(1024)} %xor.62.table, s32[2]{0:T(128)} %pad_add_fusion.place, bf16[4096,640]{1,0:T(8,128)(2,1)} %get-tuple-element.91.refs_0_.qkv_hbm, bf16[64,3,64,512]{3,2,1,0:T(8,128)(2,1)} %get-tuple-element.92.refs_1_), custom_call_target="tpu_custom_call", output_to_operand_aliasing={{1}: (3, {})} | custom-call | tf_op jit(solution)/shard_map/attend_forward/pallas_call | solution.py:172
  171.2 2.7 broadcast_select_fusion.2.cot_ref
  175.1 11.2 %collective-permute-done.9.o1 = bf16[1024,192]{1,0:T(8,128)(2,1)S(1)} collective-permute-done((bf16[1024,192]{1,0:T(8,128)(2,1)}, bf16[1024,192]{1,0:T(8,128)(2,1)S(1)}, u32[]{:S(2)}, u32[]{:S(2)}) %collective-permute-start.9) | collective-permute-done | bytes 393248 | tf_op jit(solution)/shard_map/ppermute | solution.py:840
  187.1 40.2 %token_block.1 = (bf16[1024,768]{1,0:T(8,128)(2,1)}, bf16[1024,768]{1,0:T(8,128)(2,1)}, bf16[1024,3072]{1,0:T(8,128)(2,1)}, bf16[1024,3072]{1,0:T(8,128)(2,1)}, ...) custom-call(s32[1]{0:T(128)} %bitcast.rank_ref, ...), custom_call_target="tpu_custom_call" | custom-call | flops 46000001024 | bytes 40000000 | tf_op jit(solution)/shard_map/token_block/pallas_call | solution.py:637
  228.3 1.5 collective-permute-start.14
  230.8 21.2 %weight_block.1 = bf16[3072,1728]{1,0:T(8,128)(2,1)} custom-call(s32[1]{0:T(128)} %bitcast.rank_ref, bf16[1024,768]{1,0:T(8,128)(2,1)} %get-tuple-element.101.n1, bf16[1024,768]{1,0:T(8,128)(2,1)} %get-tuple-element.102.dfr, bf16[1024,768]{1,0:T(8,128)(2,1)} %get-tuple-element.103.dar, bf16[1024,3072]{1,0:T(8,128)(2,1)} %get-tuple-element.104.g, ...), custom_call_target="tpu_custom_call" | custom-call | flops 22000001024 | bytes 30000000 | tf_op jit(solution)/shard_map/weight_block/pallas_call | solution.py:730
  252.0 1.8 collective-permute-done.16.do3
  255.4 2.9 collective-permute-start.17
  258.3 44.9 %attend_backward.1 = (bf16[4096,640]{1,0:T(8,128)(2,1)}, f32[1024,768]{1,0:T(8,128)}, bf16[1024,768]{1,0:T(8,128)(2,1)}, bf16[1024,768]{1,0:T(8,128)(2,1)}, bf16[1024,768]{1,0:T(8,128)(2,1)}, /*index=5*/f32[8,640]{1,0:T(8,128)}) custom-call(s32[1536]{0:T(1024)} %xor.62.table, bf16[64,3,64,512]{3,2,1,0:T(8,128)(2,1)} %get-tuple-element.100.p_ref, ...), custom_call_target="tpu_custom_call" | custom-call | flops 40000000000 | bytes 25000000 | tf_op jit(solution)/shard_map/attend_backward/pallas_call | solution.py:357
  303.3 1.2 copy-done.7
  305.9 1.5 collective-permute-start.19
  307.4 3.4 collective-permute-done.19
  310.8 3.1 add_convert_fusion.1
  313.9 1.2 collective-permute-start.22
  315.1 1.5 collective-permute-done.22
  316.7 1.2 collective-permute-start.23
  317.9 2.3 convert_add_fusion
  320.2 11.1 %head_weight_block.1 = bf16[768,576]{1,0:T(8,128)(2,1)} custom-call(bf16[1024,768]{1,0:T(8,128)(2,1)} %copy-done, bf16[1024,768]{1,0:T(8,128)(2,1)} %copy-done.1, bf16[1024,768]{1,0:T(8,128)(2,1)} %collective-permute-done.7.refs_2_.x2, bf16[1024,768]{1,0:T(8,128)(2,1)} %collective-permute-done.8.refs_3_.x3, bf16[4096,640]{1,0:T(8,128)(2,1)} %get-tuple-element.133.grad_ref), custom_call_target="tpu_custom_call" | custom-call | flops 8000000000 | bytes 12000000 | tf_op jit(solution)/shard_map/head_weight_block/pallas_call | solution.py:423
  331.3 5.7 %reduce-scatter.3.cloned.1.call-done = bf16[4,96,1728]{2,1,0:T(8,128)(2,1)} async-done(((bf16[4,768,1728]{2,1,0:T(8,128)(2,1)}), bf16[4,96,1728]{2,1,0:T(8,128)(2,1)}) %reduce-scatter.3.cloned.1.call-update) | async-done | bytes 1327120 | tf_op jit(solution)/shard_map/reduce_scatter | solution.py:935
  337.1 2.0 constant_dynamic-slice_fusion.3
  339.2 1.3 collective-permute-start.24
  341.8 1.5 collective-permute-start.27
  343.3 3.9 collective-permute-done.24
  347.3 4.9 %collective-permute-done.25 = bf16[192,576]{1,0:T(8,128)(2,1)} collective-permute-done((bf16[192,576]{1,0:T(8,128)(2,1)}, bf16[192,576]{1,0:T(8,128)(2,1)}, u32[]{:S(2)}, u32[]{:S(2)}) %collective-permute-start.25) | collective-permute-done | bytes 221216 | tf_op jit(solution)/shard_map/ppermute | solution.py:840
  352.2 1.3 collective-permute-done.26
  353.5 1.4 add_convert_fusion.3
  355.2 3.0 add_convert_fusion
  358.2 4.0 collective-permute-start.29
  362.2 9.3 %collective-permute-start.28 = (bf16[1024,768]{1,0:T(8,128)(2,1)}, bf16[1024,768]{1,0:T(8,128)(2,1)S(1)}, u32[]{:S(2)}, u32[]{:S(2)}) collective-permute-start(bf16[1024,768]{1,0:T(8,128)(2,1)} %add_convert_fusion), channel_id=1, source_target_pairs={{2,4},{3,5},{4,2},{5,3},{10,12},{11,13},{12,10},{13,11},{18,20},{1... | collective-permute-start | bytes 4718600 | tf_op jit(solution)/shard_map/ppermute | solution.py:840
  372.2 1.3 broadcast_select_fusion.1
  374.2 21.3 %collective-permute-start.30 = (bf16[96,576]{1,0:T(8,128)(2,1)S(1)}, bf16[96,576]{1,0:T(8,128)(2,1)S(1)}, u32[]{:S(2)}, u32[]{:S(2)}) collective-permute-start(bf16[96,576]{1,0:T(8,128)(2,1)S(1)} %constant_dynamic-slice_fusion), channel_id=1, source_target_pairs={{0,4},{1,5},{2,6},{3,7},{4,0},{5,1},{6,2},{7,3},{8,12},{9,13},{10,... | collective-permute-start | bytes 331784 | tf_op jit(solution)/shard_map/ppermute | solution.py:840
  396.6 15.0 %collective-permute-done.28 = bf16[1024,768]{1,0:T(8,128)(2,1)S(1)} collective-permute-done((bf16[1024,768]{1,0:T(8,128)(2,1)}, bf16[1024,768]{1,0:T(8,128)(2,1)S(1)}, u32[]{:S(2)}, u32[]{:S(2)}) %collective-permute-start.28) | collective-permute-done | bytes 1572896 | tf_op jit(solution)/shard_map/ppermute | solution.py:840
  412.6 1.3 broadcast_select_fusion
  (183 shorter events, 35.1 us)
Async XLA Ops:
  7.2 9.5 %copy-start.9 = (bf16[768,96]{0,1:T(8,128)(2,1)S(1)}, bf16[768,96]{0,1:T(8,128)(2,1)}, u32[]{:S(2)}) copy-start(bf16[768,96]{0,1:T(8,128)(2,1)} %param.25) | copy-start | bytes 442372
  7.2 83.0 %all-gather.7.cloned.1.call-start = ((), (), s32[]{:S(2)}) async-start(), calls=%async_computation.5 | async-start | bytes 1863680 | tf_op jit(solution)/shard_map/all_gather | solution.py:857
  11.4 3.9 collective-permute-start
  12.4 14.6 %copy-start.3 = (bf16[1024,768]{1,0:T(8,128)(2,1)S(1)}, bf16[1024,768]{1,0:T(8,128)(2,1)}, u32[]{:S(2)}) copy-start(bf16[1024,768]{1,0:T(8,128)(2,1)} %param.18) | copy-start | bytes 4718596
  15.4 11.5 %collective-permute-start.1 = (bf16[195,576]{1,0:T(8,128)(2,1)S(1)}, bf16[195,576]{1,0:T(8,128)(2,1)S(1)}, u32[]{:S(2)}, u32[]{:S(2)}) collective-permute-start(bf16[195,576]{1,0:T(8,128)(2,1)S(1)} %pad_maximum_fusion.1), channel_id=1, source_target_pairs={{0,2},{1,3},{6,4},{7,5},{8,10},{9,11},{14,12},{15,13},{16,18},{17,... | collective-permute-start | bytes 673928 | tf_op jit(solution)/shard_map/ppermute | solution.py:840
  17.5 168.8 %all-gather.5.cloned.1.call-start = ((), (), s32[]{:S(2)}) async-start(), calls=%async_computation.2 | async-start | bytes 12386304 | tf_op jit(solution)/shard_map/all_gather | solution.py:884
  27.0 63.2 %collective-permute-start.3 = (bf16[1024,768]{1,0:T(8,128)(2,1)S(1)}, bf16[1024,768]{1,0:T(8,128)(2,1)}, u32[]{:S(2)}, u32[]{:S(2)}) collective-permute-start(bf16[1024,768]{1,0:T(8,128)(2,1)S(1)} %copy-done.3), channel_id=1, source_target_pairs={{2,4},{3,5},{4,2},{5,3},{10,12},{11,13},{12,10},{13,11},{18,20},{1... | collective-permute-start | bytes 4718600 | tf_op jit(solution)/shard_map/ppermute | solution.py:840
  30.3 5.5 %collective-permute-start.4 = (bf16[192,576]{1,0:T(8,128)(2,1)S(1)}, bf16[192,576]{1,0:T(8,128)(2,1)S(1)}, u32[]{:S(2)}, u32[]{:S(2)}) collective-permute-start(bf16[192,576]{1,0:T(8,128)(2,1)S(1)} %slice.199), channel_id=1, source_target_pairs={{0,8},{1,9},{2,10},{3,11},{4,12},{5,13},{6,14},{7,15},{8,0},{9,1},... | collective-permute-start | bytes 663560 | tf_op jit(solution)/shard_map/ppermute | solution.py:840
  36.0 11.5 %collective-permute-start.5 = (bf16[384,576]{1,0:T(8,128)(2,1)S(1)}, bf16[384,576]{1,0:T(8,128)(2,1)S(1)}, u32[]{:S(2)}, u32[]{:S(2)}) collective-permute-start(bf16[384,576]{1,0:T(8,128)(2,1)S(1)} %maximum_select_fusion.1), channel_id=1, source_target_pairs={{0,16},{1,17},{2,18},{3,19},{4,20},{5,21},{6,22},{7,23},{8,24},{9,... | collective-permute-start | bytes 1327112 | tf_op jit(solution)/shard_map/ppermute | solution.py:840
  92.8 244.3 %reduce-scatter.3.cloned.1.call-start = ((), (), s32[]{:S(2)}) async-start(), calls=%async_computation.3 | async-start | bytes 12386304 | tf_op jit(solution)/shard_map/reduce_scatter | solution.py:935
  92.8 4.5 %collective-permute-start.2 = (bf16[1024,768]{1,0:T(8,128)(2,1)S(1)}, bf16[1024,768]{1,0:T(8,128)(2,1)S(1)}, u32[]{:S(2)}, u32[]{:S(2)}) collective-permute-start(bf16[1024,768]{1,0:T(8,128)(2,1)S(1)} %copy-done.3), channel_id=1, source_target_pairs={{0,1},{1,0},{6,7},{7,6},{8,9},{9,8},{14,15},{15,14},{16,17},{17,16... | collective-permute-start | bytes 4718600 | tf_op jit(solution)/shard_map/ppermute | solution.py:840
  95.2 28.7 %copy-start = (bf16[1024,768]{1,0:T(8,128)(2,1)}, bf16[1024,768]{1,0:T(8,128)(2,1)S(1)}, u32[]{:S(2)}) copy-start(bf16[1024,768]{1,0:T(8,128)(2,1)S(1)} %broadcast_select_fusion.4.refs_0_.x_ref.x0) | copy-start | bytes 4718596
  95.2 29.3 %copy-start.11 = (f32[768]{0:T(1024)S(1)}, f32[768]{0:T(1024)}, u32[]{:S(2)}) copy-start(f32[768]{0:T(1024)} %param.28) | copy-start | bytes 9220
  95.2 29.3 %copy-start.12 = (f32[768]{0:T(1024)S(1)}, f32[768]{0:T(1024)}, u32[]{:S(2)}) copy-start(f32[768]{0:T(1024)} %param.29) | copy-start | bytes 9220
  95.2 29.3 %copy-start.13 = (f32[768]{0:T(1024)S(1)}, f32[768]{0:T(1024)}, u32[]{:S(2)}) copy-start(f32[768]{0:T(1024)} %param.30) | copy-start | bytes 9220
  95.2 29.3 %copy-start.14 = (f32[768]{0:T(1024)S(1)}, f32[768]{0:T(1024)}, u32[]{:S(2)}) copy-start(f32[768]{0:T(1024)} %param.32) | copy-start | bytes 9220
  95.2 29.3 %copy-start.15 = (f32[768]{0:T(1024)S(1)}, f32[768]{0:T(1024)}, u32[]{:S(2)}) copy-start(f32[768]{0:T(1024)} %param.33) | copy-start | bytes 9220
  95.2 29.3 %copy-start.16 = (f32[768]{0:T(1024)S(1)}, f32[768]{0:T(1024)}, u32[]{:S(2)}) copy-start(f32[768]{0:T(1024)} %param.34) | copy-start | bytes 9220
  95.3 28.5 %collective-permute-start.6 = (bf16[1024,768]{1,0:T(8,128)(2,1)S(1)}, bf16[1024,768]{1,0:T(8,128)(2,1)S(1)}, u32[]{:S(2)}, u32[]{:S(2)}) collective-permute-start(bf16[1024,768]{1,0:T(8,128)(2,1)S(1)} %broadcast_select_fusion.4.refs_0_.x_ref.x0), channel_id=1, source_target_pairs={{2,3},{3,2},{4,5},{5,4},{10,11},{11,10},{12,13},{13,12},{18,19},{1... | collective-permute-start | bytes 4718600 | tf_op jit(solution)/shard_map/ppermute | solution.py:840
  123.9 8.4 %collective-permute-start.7 = (bf16[1024,768]{1,0:T(8,128)(2,1)S(1)}, bf16[1024,768]{1,0:T(8,128)(2,1)}, u32[]{:S(2)}, u32[]{:S(2)}) collective-permute-start(bf16[1024,768]{1,0:T(8,128)(2,1)S(1)} %broadcast_select_fusion.4.refs_0_.x_ref.x0), channel_id=1, source_target_pairs={{0,4},{1,5},{2,6},{3,7},{4,0},{5,1},{6,2},{7,3},{8,12},{9,13},{10,... | collective-permute-start | bytes 4718600 | tf_op jit(solution)/shard_map/ppermute | solution.py:840
  124.0 8.8 %collective-permute-start.8 = (bf16[1024,768]{1,0:T(8,128)(2,1)S(1)}, bf16[1024,768]{1,0:T(8,128)(2,1)}, u32[]{:S(2)}, u32[]{:S(2)}) collective-permute-start(bf16[1024,768]{1,0:T(8,128)(2,1)S(1)} %broadcast_select_fusion.3.refs_1_.x1), channel_id=1, source_target_pairs={{0,4},{1,5},{2,6},{3,7},{4,0},{5,1},{6,2},{7,3},{8,12},{9,13},{10,... | collective-permute-start | bytes 4718600 | tf_op jit(solution)/shard_map/ppermute | solution.py:840
  124.6 46.5 %collective-permute-start.12 = (bf16[1024,768]{1,0:T(8,128)(2,1)}, bf16[1024,768]{1,0:T(8,128)(2,1)}, u32[]{:S(2)}, u32[]{:S(2)}) collective-permute-start(bf16[1024,768]{1,0:T(8,128)(2,1)} %param.19), channel_id=1, source_target_pairs={{2,4},{3,5},{4,2},{5,3},{10,12},{11,13},{12,10},{13,11},{18,20},{1... | collective-permute-start | bytes 4718600 | tf_op jit(solution)/shard_map/ppermute | solution.py:840
  159.6 14.3 %collective-permute-start.10 = (bf16[1024,192]{1,0:T(8,128)(2,1)}, bf16[1024,192]{1,0:T(8,128)(2,1)S(1)}, u32[]{:S(2)}, u32[]{:S(2)}) collective-permute-start(bf16[1024,192]{1,0:T(8,128)(2,1)} %get-tuple-element.95.o2), channel_id=1, source_target_pairs={{0,4},{1,5},{2,6},{3,7},{4,0},{5,1},{6,2},{7,3},{8,12},{9,13},{10,... | collective-permute-start | bytes 1179656 | tf_op jit(solution)/shard_map/ppermute | solution.py:840
  160.1 14.9 %collective-permute-start.11 = (bf16[1024,192]{1,0:T(8,128)(2,1)}, bf16[1024,192]{1,0:T(8,128)(2,1)S(1)}, u32[]{:S(2)}, u32[]{:S(2)}) collective-permute-start(bf16[1024,192]{1,0:T(8,128)(2,1)} %get-tuple-element.96.o3), channel_id=1, source_target_pairs={{0,5},{1,4},{2,7},{3,6},{4,1},{5,0},{6,3},{7,2},{8,13},{9,12},{10,... | collective-permute-start | bytes 1179656 | tf_op jit(solution)/shard_map/ppermute | solution.py:840
  161.1 25.1 %collective-permute-start.9 = (bf16[1024,192]{1,0:T(8,128)(2,1)}, bf16[1024,192]{1,0:T(8,128)(2,1)S(1)}, u32[]{:S(2)}, u32[]{:S(2)}) collective-permute-start(bf16[1024,192]{1,0:T(8,128)(2,1)} %get-tuple-element.94.o1), channel_id=1, source_target_pairs={{0,1},{1,0},{2,3},{3,2},{4,5},{5,4},{6,7},{7,6},{8,9},{9,8},{10,11... | collective-permute-start | bytes 1179656 | tf_op jit(solution)/shard_map/ppermute | solution.py:840
  173.9 12.4 %copy-start.17 = (bf16[1024,192]{1,0:T(8,128)(2,1)}, bf16[1024,192]{1,0:T(8,128)(2,1)S(1)}, u32[]{:S(2)}) copy-start(bf16[1024,192]{1,0:T(8,128)(2,1)S(1)} %collective-permute-done.10.o2) | copy-start | bytes 1179652
  175.1 11.2 %copy-start.18 = (bf16[1024,192]{1,0:T(8,128)(2,1)}, bf16[1024,192]{1,0:T(8,128)(2,1)S(1)}, u32[]{:S(2)}) copy-start(bf16[1024,192]{1,0:T(8,128)(2,1)S(1)} %collective-permute-done.11.o3) | copy-start | bytes 1179652
  228.2 23.8 %collective-permute-start.13 = (f32[7680]{0:T(1024)S(1)}, f32[7680]{0:T(1024)S(1)}, u32[]{:S(2)}, u32[]{:S(2)}) collective-permute-start(f32[7680]{0:T(1024)S(1)} %reduce.1), channel_id=1, source_target_pairs={{0,1},{1,0},{2,3},{3,2},{4,5},{5,4},{6,7},{7,6},{8,9},{9,8},{10,11... | collective-permute-start | bytes 92168 | tf_op jit(solution)/shard_map/ppermute | solution.py:840
  228.3 23.8 %collective-permute-start.14 = (bf16[1024,192]{1,0:T(8,128)(2,1)}, bf16[1024,192]{1,0:T(8,128)(2,1)S(1)}, u32[]{:S(2)}, u32[]{:S(2)}) collective-permute-start(bf16[1024,192]{1,0:T(8,128)(2,1)} %get-tuple-element.108), channel_id=1, source_target_pairs={{0,1},{1,0},{2,3},{3,2},{4,5},{5,4},{6,7},{7,6},{8,9},{9,8},{10,11... | collective-permute-start | bytes 1179656 | tf_op jit(solution)/shard_map/ppermute | solution.py:840
  229.7 22.3 %collective-permute-start.15 = (bf16[1024,192]{1,0:T(8,128)(2,1)}, bf16[1024,192]{1,0:T(8,128)(2,1)S(1)}, u32[]{:S(2)}, u32[]{:S(2)}) collective-permute-start(bf16[1024,192]{1,0:T(8,128)(2,1)} %get-tuple-element.109), channel_id=1, source_target_pairs={{0,4},{1,5},{2,6},{3,7},{4,0},{5,1},{6,2},{7,3},{8,12},{9,13},{10,... | collective-permute-start | bytes 1179656 | tf_op jit(solution)/shard_map/ppermute | solution.py:840
  230.7 23.1 %collective-permute-start.16 = (bf16[1024,192]{1,0:T(8,128)(2,1)}, bf16[1024,192]{1,0:T(8,128)(2,1)S(1)}, u32[]{:S(2)}, u32[]{:S(2)}) collective-permute-start(bf16[1024,192]{1,0:T(8,128)(2,1)} %get-tuple-element.110), channel_id=1, source_target_pairs={{0,5},{1,4},{2,7},{3,6},{4,1},{5,0},{6,3},{7,2},{8,13},{9,12},{10,... | collective-permute-start | bytes 1179656 | tf_op jit(solution)/shard_map/ppermute | solution.py:840
  254.6 140.9 %reduce-scatter.5.cloned.1.call-start = ((), (), s32[]{:S(2)}) async-start(), calls=%async_computation.4 | async-start | bytes 1720320 | tf_op jit(solution)/shard_map/reduce_scatter | solution.py:962
  255.4 47.8 %collective-permute-start.17 = (bf16[1024,768]{1,0:T(8,128)(2,1)S(1)}, bf16[1024,768]{1,0:T(8,128)(2,1)S(1)}, u32[]{:S(2)}, u32[]{:S(2)}) collective-permute-start(bf16[1024,768]{1,0:T(8,128)(2,1)S(1)} %copy-done.5), channel_id=1, source_target_pairs={{2,4},{3,5},{4,2},{5,3},{10,12},{11,13},{12,10},{13,11},{18,20},{1... | collective-permute-start | bytes 4718600 | tf_op jit(solution)/shard_map/ppermute | solution.py:840
  304.4 6.3 %collective-permute-start.18 = (bf16[1024,768]{1,0:T(8,128)(2,1)}, bf16[1024,768]{1,0:T(8,128)(2,1)S(1)}, u32[]{:S(2)}, u32[]{:S(2)}) collective-permute-start(bf16[1024,768]{1,0:T(8,128)(2,1)} %get-tuple-element.123), channel_id=1, source_target_pairs={{0,4},{1,5},{2,6},{3,7},{4,0},{5,1},{6,2},{7,3},{8,12},{9,13},{10,... | collective-permute-start | bytes 4718600 | tf_op jit(solution)/shard_map/ppermute | solution.py:840
  304.4 13.5 %collective-permute-start.21 = (bf16[1024,768]{1,0:T(8,128)(2,1)}, bf16[1024,768]{1,0:T(8,128)(2,1)}, u32[]{:S(2)}, u32[]{:S(2)}) collective-permute-start(bf16[1024,768]{1,0:T(8,128)(2,1)} %get-tuple-element.129), channel_id=1, source_target_pairs={{0,4},{1,5},{2,6},{3,7},{4,0},{5,1},{6,2},{7,3},{8,12},{9,13},{10,... | collective-permute-start | bytes 4718600 | tf_op jit(solution)/shard_map/ppermute | solution.py:840
  305.9 4.8 %collective-permute-start.19 = (f32[8064]{0:T(1024)S(1)}, f32[8064]{0:T(1024)S(1)}, u32[]{:S(2)}, u32[]{:S(2)}) collective-permute-start(f32[8064]{0:T(1024)S(1)} %concatenate.89), channel_id=1, source_target_pairs={{0,2},{1,3},{2,0},{3,1},{4,6},{5,7},{6,4},{7,5},{8,10},{9,11},{10,... | collective-permute-start | bytes 96776 | tf_op jit(solution)/shard_map/ppermute | solution.py:840
  313.9 2.8 collective-permute-start.22
  315.1 40.1 %collective-permute-start.20 = (bf16[1024,768]{1,0:T(8,128)(2,1)}, bf16[1024,768]{1,0:T(8,128)(2,1)}, u32[]{:S(2)}, u32[]{:S(2)}) collective-permute-start(bf16[1024,768]{1,0:T(8,128)(2,1)} %add_convert_fusion.1), channel_id=1, source_target_pairs={{0,1},{1,0},{2,3},{3,2},{4,5},{5,4},{6,7},{7,6},{8,9},{9,8},{10,11... | collective-permute-start | bytes 4718600 | tf_op jit(solution)/shard_map/ppermute | solution.py:840
  316.7 3.5 collective-permute-start.23
  339.2 8.1 %collective-permute-start.24 = (bf16[192,576]{1,0:T(8,128)(2,1)}, bf16[192,576]{1,0:T(8,128)(2,1)}, u32[]{:S(2)}, u32[]{:S(2)}) collective-permute-start(bf16[192,576]{1,0:T(8,128)(2,1)} %get-tuple-element.202), channel_id=1, source_target_pairs={{0,24},{1,25},{2,26},{3,27},{4,28},{5,29},{6,30},{7,31},{8,16},{9,... | collective-permute-start | bytes 663560 | tf_op jit(solution)/shard_map/ppermute | solution.py:840
  340.4 11.7 %collective-permute-start.25 = (bf16[192,576]{1,0:T(8,128)(2,1)}, bf16[192,576]{1,0:T(8,128)(2,1)}, u32[]{:S(2)}, u32[]{:S(2)}) collective-permute-start(bf16[192,576]{1,0:T(8,128)(2,1)} %get-tuple-element.204), channel_id=1, source_target_pairs={{0,8},{1,9},{2,10},{3,11},{4,12},{5,13},{6,14},{7,15},{8,0},{9,1},... | collective-permute-start | bytes 663560 | tf_op jit(solution)/shard_map/ppermute | solution.py:840
  341.2 12.3 %collective-permute-start.26 = (bf16[192,576]{1,0:T(8,128)(2,1)S(1)}, bf16[192,576]{1,0:T(8,128)(2,1)}, u32[]{:S(2)}, u32[]{:S(2)}) collective-permute-start(bf16[192,576]{1,0:T(8,128)(2,1)S(1)} %get-tuple-element.203), channel_id=1, source_target_pairs={{0,16},{1,17},{2,18},{3,19},{4,20},{5,21},{6,22},{7,23},{8,24},{9,... | collective-permute-start | bytes 663560 | tf_op jit(solution)/shard_map/ppermute | solution.py:840
  341.8 13.2 %collective-permute-start.27 = (f32[8064]{0:T(1024)S(1)}, f32[8064]{0:T(1024)S(1)}, u32[]{:S(2)}, u32[]{:S(2)}) collective-permute-start(f32[8064]{0:T(1024)S(1)} %add.160), channel_id=1, source_target_pairs={{0,4},{1,5},{2,6},{3,7},{4,0},{5,1},{6,2},{7,3},{8,12},{9,13},{10,... | collective-permute-start | bytes 96776 | tf_op jit(solution)/shard_map/ppermute | solution.py:840
  355.0 17.2 %copy-start.6 = (bf16[1024,768]{1,0:T(8,128)(2,1)S(1)}, bf16[1024,768]{1,0:T(8,128)(2,1)}, u32[]{:S(2)}) copy-start(bf16[1024,768]{1,0:T(8,128)(2,1)} %get-tuple-element.99) | copy-start | bytes 4718596
  355.0 17.2 %copy-start.8 = (bf16[1024,768]{1,0:T(8,128)(2,1)S(1)}, bf16[1024,768]{1,0:T(8,128)(2,1)}, u32[]{:S(2)}) copy-start(bf16[1024,768]{1,0:T(8,128)(2,1)} %copy-done.7) | copy-start | bytes 4718596
  358.2 15.9 %collective-permute-start.29 = (bf16[192,576]{1,0:T(8,128)(2,1)S(1)}, bf16[192,576]{1,0:T(8,128)(2,1)S(1)}, u32[]{:S(2)}, u32[]{:S(2)}) collective-permute-start(bf16[192,576]{1,0:T(8,128)(2,1)S(1)} %add_convert_fusion.3), channel_id=1, source_target_pairs={{2,0},{3,1},{4,6},{5,7},{10,8},{11,9},{12,14},{13,15},{18,16},{19,... | collective-permute-start | bytes 663560 | tf_op jit(solution)/shard_map/ppermute | solution.py:840
  362.2 49.3 %collective-permute-start.28 = (bf16[1024,768]{1,0:T(8,128)(2,1)}, bf16[1024,768]{1,0:T(8,128)(2,1)S(1)}, u32[]{:S(2)}, u32[]{:S(2)}) collective-permute-start(bf16[1024,768]{1,0:T(8,128)(2,1)} %add_convert_fusion), channel_id=1, source_target_pairs={{2,4},{3,5},{4,2},{5,3},{10,12},{11,13},{12,10},{13,11},{18,20},{1... | collective-permute-start | bytes 4718600 | tf_op jit(solution)/shard_map/ppermute | solution.py:840
  374.2 22.3 %collective-permute-start.30 = (bf16[96,576]{1,0:T(8,128)(2,1)S(1)}, bf16[96,576]{1,0:T(8,128)(2,1)S(1)}, u32[]{:S(2)}, u32[]{:S(2)}) collective-permute-start(bf16[96,576]{1,0:T(8,128)(2,1)S(1)} %constant_dynamic-slice_fusion), channel_id=1, source_target_pairs={{0,4},{1,5},{2,6},{3,7},{4,0},{5,1},{6,2},{7,3},{8,12},{9,13},{10,... | collective-permute-start | bytes 331784 | tf_op jit(solution)/shard_map/ppermute | solution.py:840
  (10 other events, 42.6 us)
Sparse Core Ops, SparseCore 0:
  17.7 61.6 all-gather.6
  92.9 64.7 all-gather.4
  254.0 83.0 reduce-scatter.2
  339.2 37.1 reduce-scatter.4

commit v5 on v4

--- a/solution.py
+++ b/solution.py
@@ -854,7 +854,7 @@
     rest = jnp.concatenate([w_up, w_down.T, w_output.T], axis=1)
     below = jnp.concatenate(split_three(b_up))
     below = jnp.pad(below, (0, -below.shape[0] % rest.shape[1])).reshape(-1, rest.shape[1])
-    rest = lax.all_gather(jnp.concatenate([rest, below], axis=0), "tensor", axis=0)
+    rest = jnp.concatenate([rest, below], axis=0)
 
     packed = pack_columns(w_query, w_key, w_value, 1)
     columns = packed.shape[1]
@@ -862,10 +862,18 @@
     small = jnp.concatenate(split_three(floats) + [random_blocks.astype(low).reshape(-1)])
     small = jnp.pad(small, (0, -small.shape[0] % columns)).reshape(-1, columns)
     packed = jnp.concatenate([order_halves(core, packed, side_of(packed)), small], axis=0)
-    packed = jnp.where(here, packed, flip(packed, 0, 2, stays))
-    inputs, packed = lax.optimization_barrier((inputs, packed))
+    packed_got = flip(packed, 0, 2, stays)
+
     moved = flip(inputs, 1, 2, moves)
     near_stay = flip(inputs, 0, 1, stays)
+    moved, near_stay, packed_got, rest = lax.optimization_barrier(
+        (moved, near_stay, packed_got, rest)
+    )
+    own = jnp.where(here, inputs, moved)
+    near_move = flip(own, 0, 1, moves)
+    own, packed_got = lax.optimization_barrier((own, packed_got))
+    rest = lax.all_gather(rest, "tensor", axis=0)
+    packed = jnp.where(here, packed, packed_got)
     small = packed[2 * w_query.shape[0] :].reshape(-1)
     packed = packed[: 2 * w_query.shape[0]]
     for bit in pair_bits:
@@ -878,8 +886,13 @@
     b_key = jnp.zeros_like(b_query)
     b_qkv = insert_zero(pack_columns(mine[:192], b_key, mine[192:], 0), 0)
     scale = jnp.concatenate([jnp.ones((KV,), jnp.float32), jnp.full((256,), 0.125, jnp.float32)])
-
-    moved, rest, w_qkv, b_qkv = lax.optimization_barrier((moved, rest, w_qkv, b_qkv))
+    near = jnp.where(here, near_stay, near_move)
+    near, own, cotangent, w_qkv, b_qkv = lax.optimization_barrier(
+        (near, own, cotangent, w_qkv, b_qkv)
+    )
+    side, far = side_of(own), side_of(near)
+    cot_moved = flip(cotangent, 1, 2, moves)
+    side, far, rest = lax.optimization_barrier((side, far, rest))
     below = rest[:, w_up.shape[0] :].reshape(GROUP, -1)
     rest_all = lax.all_gather(
         rest[:, : w_up.shape[0]], "dp", axis=1, tiled=True
@@ -887,13 +900,6 @@
     b_up_all = sum(
         below[:, n * hidden : (n + 1) * hidden].astype(jnp.float32) for n in range(3)
     ).reshape(1, -1)
-    own = jnp.where(here, inputs, moved)
-    near_move = flip(own, 0, 1, moves)
-
-    near = jnp.where(here, near_stay, near_move)
-    near, own, cotangent = lax.optimization_barrier((near, own, cotangent))
-    side, far = side_of(own), side_of(near)
-    cot_moved = flip(cotangent, 1, 2, moves)
     rows = (own, near, side, far)
     grad_top = jnp.where(here, cotangent, cot_moved)
     block = jnp.arange(NB, dtype=jnp.int32)

time: 425 us -> 410 us (0.965)
  waiting for transfers between devices: 142 us -> 121 us
  starting transfers between devices: 63.6 us -> 70.5 us
    ppermute x31, waiting for transfers between devices: 136 us -> 88.8 us  [flip(): return lax.ppermute(value, both, pairs)]
    all_gather x1, waiting for transfers between devices: 0.01 us -> 22 us  [per_device(): rest = lax.all_gather(rest, 'tensor', axis=0)]
    ppermute x31, starting transfers between devices: 63.5 us -> 70.3 us  [flip(): return lax.ppermute(value, both, pairs)]
    all_gather x1, waiting for transfers between devices: 0.01 us -> 4.36 us  [per_device(): lax.all_gather(rest[:, :w_up.shape[0]], 'dp', axis=1, tiled=True)]
  transfers between devices with their start and end apart: 35 -> 35, of which waited for: 17 -> 20; matrix products, arithmetic and copies ran while one was open for 8% -> 9% of each run, Pallas kernels for 27% -> 28%
where the time goes in v5:
time: 410 us; the launch traced here: 409 us
  Pallas kernels  153 us (37%)
  waiting for transfers between devices  121 us (30%)
  starting transfers between devices  70.5 us (17%)
  other arithmetic  27.9 us (7%)
  local copies, waits for them, and re-layouts  21.5 us (5%)
  between operations  14.6 us (4%)
    ppermute x31, waiting for transfers between devices, flip(): return lax.ppermute(value, both, pairs)  88.8 us
    ppermute x31, starting transfers between devices, flip(): return lax.ppermute(value, both, pairs)  70.3 us
    pallas_call x1, Pallas kernels, attend_backward(): pl.pallas_call(functools.partial(backward_kernel, steps), grid_spec=pltpu...  45 us
    pallas_call x1, Pallas kernels, token_block(): pl.pallas_call(functools.partial(token_kernel, tile, width, hidden), grid...  40.2 us
    pallas_call x2, Pallas kernels, attend_forward(): pl.pallas_call(functools.partial(forward_kernel, steps, count, project),...  36 us
    all_gather x1, waiting for transfers between devices, per_device(): rest = lax.all_gather(rest, 'tensor', axis=0)  22 us
    pallas_call x1, Pallas kernels, weight_block(): pl.pallas_call(functools.partial(weight_kernel, width, hidden), grid_spec...  21 us
    pallas_call x1, Pallas kernels, head_weight_block(): pl.pallas_call(head_weight_kernel, grid=(GROUP,), in_specs=[any_spec] * 4...  11.1 us
  transfers between devices with their start and end apart: 35, of which 20 were waited for; matrix products, arithmetic and copies ran while one was open for 9% of the time, Pallas kernels for 28%

profile of v5, /device:TPU:1, one launch (start us, length us, event | category | flops | bytes accessed | tf_op | source)
XLA Modules:
  0.0 408.7 jit_solution(17524082635760820865)
XLA Ops:
  7.3 5.7 %collective-permute-start.1 = (bf16[1024,768]{1,0:T(8,128)(2,1)}, bf16[1024,768]{1,0:T(8,128)(2,1)}, u32[]{:S(2)}, u32[]{:S(2)}) collective-permute-start(bf16[1024,768]{1,0:T(8,128)(2,1)} %param.18), channel_id=1, source_target_pairs={{2,4},{3,5},{4,2},{5,3},{10,12},{11,13},{12,10},{13,11},{18,20},{1... | collective-permute-start | bytes 4718600 | tf_op jit(solution)/shard_map/ppermute | solution.py:840
  13.0 1.9 collective-permute-start.2
  22.8 1.3 collective-permute-start.3
  24.9 14.2 %collective-permute-done.3 = bf16[195,576]{1,0:T(8,128)(2,1)S(1)} collective-permute-done((bf16[195,576]{1,0:T(8,128)(2,1)S(1)}, bf16[195,576]{1,0:T(8,128)(2,1)S(1)}, u32[]{:S(2)}, u32[]{:S(2)}) %collective-permute-start.3) | collective-permute-done | bytes 224672 | tf_op jit(solution)/shard_map/ppermute | solution.py:840
  39.1 14.6 %collective-permute-done.1 = bf16[1024,768]{1,0:T(8,128)(2,1)} collective-permute-done((bf16[1024,768]{1,0:T(8,128)(2,1)}, bf16[1024,768]{1,0:T(8,128)(2,1)}, u32[]{:S(2)}, u32[]{:S(2)}) %collective-permute-start.1) | collective-permute-done | bytes 1572896 | tf_op jit(solution)/shard_map/ppermute | solution.py:840
  53.8 1.6 broadcast_select_fusion.4.refs_0_.x_ref.x0
  55.3 2.4 collective-permute-start.4
  57.9 1.3 collective-permute-start.5
  59.2 4.0 collective-permute-done.5
  63.4 1.3 collective-permute-start.6
  65.0 7.6 %collective-permute-done.6 = bf16[384,576]{1,0:T(8,128)(2,1)S(1)} collective-permute-done((bf16[384,576]{1,0:T(8,128)(2,1)S(1)}, bf16[384,576]{1,0:T(8,128)(2,1)S(1)}, u32[]{:S(2)}, u32[]{:S(2)}) %collective-permute-start.6) | collective-permute-done | bytes 442400 | tf_op jit(solution)/shard_map/ppermute | solution.py:840
  74.3 2.4 collective-permute-done.4
  76.7 1.6 broadcast_select_fusion.3.refs_1_.x1
  78.9 22.0 %all-gather.7.cloned.1.call-done = bf16[4,98,1728]{2,1,0:T(8,128)(2,1)} async-done(((bf16[1,98,1728]{2,1,0:T(8,128)(2,1)}), bf16[4,98,1728]{2,1,0:T(8,128)(2,1)}) %all-gather.7.cloned.1.call-update) | async-done | bytes 1354768 | tf_op jit(solution)/shard_map/all_gather | solution.py:875
  100.9 2.6 slice.215
  103.8 5.4 %collective-permute-start.12 = (bf16[1024,768]{1,0:T(8,128)(2,1)S(1)}, bf16[1024,768]{1,0:T(8,128)(2,1)S(1)}, u32[]{:S(2)}, u32[]{:S(2)}) collective-permute-start(bf16[1024,768]{1,0:T(8,128)(2,1)S(1)} %copy-done.4), channel_id=1, source_target_pairs={{2,4},{3,5},{4,2},{5,3},{10,12},{11,13},{12,10},{13,11},{18,20},{1... | collective-permute-start | bytes 4718600 | tf_op jit(solution)/shard_map/ppermute | solution.py:840
  114.7 27.1 %attend_forward.2 = (bf16[1024,192]{1,0:T(8,128)(2,1)}, bf16[1024,192]{1,0:T(8,128)(2,1)}, bf16[1024,192]{1,0:T(8,128)(2,1)}, bf16[64,3,64,512]{3,2,1,0:T(8,128)(2,1)}, bf16[4096,640]{1,0:T(8,128)(2,1)}) custom-call(s32[1536]{0:T(1024)} %xor.62.table, s32[4]{0:T(128)} %pad_add_fusion.1.place, bf16[1024,768]{1,0:T(8,128)(2,1)} %copy-done, ...), custom_call_target="tpu_custom_call" | custom-call | tf_op jit(solution)/shard_map/attend_forward/pallas_call | solution.py:172
  141.9 2.0 collective-permute-start.11
  144.6 8.8 %attend_forward.3 = (bf16[1024,192]{1,0:T(8,128)(2,1)}, bf16[64,3,64,512]{3,2,1,0:T(8,128)(2,1)}) custom-call(s32[1536]{0:T(1024)} %xor.62.table, s32[2]{0:T(128)} %pad_add_fusion.place, bf16[4096,640]{1,0:T(8,128)(2,1)} %get-tuple-element.101.refs_0_.qkv_hbm, bf16[64,3,64,512]{3,2,1,0:T(8,128)(2,1)} %get-tuple-element.102.refs_1_), custom_call_target="tpu_custom_call", output_to_operand_aliasing={{1}: (3, {})} | custom-call | tf_op jit(solution)/shard_map/attend_forward/pallas_call | solution.py:172
  153.5 1.3 broadcast_select_fusion.2.cot_ref
  154.8 2.1 collective-permute-done.11.o3
  156.9 10.5 %collective-permute-done.9.o1 = bf16[1024,192]{1,0:T(8,128)(2,1)} collective-permute-done((bf16[1024,192]{1,0:T(8,128)(2,1)}, bf16[1024,192]{1,0:T(8,128)(2,1)}, u32[]{:S(2)}, u32[]{:S(2)}) %collective-permute-start.9) | collective-permute-done | bytes 393248 | tf_op jit(solution)/shard_map/ppermute | solution.py:840
  167.4 4.4 %all-gather.5.cloned.1.call-done = bf16[4,768,1728]{2,1,0:T(8,128)(2,1)} async-done(((bf16[4,96,1728]{2,1,0:T(8,128)(2,1)}), bf16[4,768,1728]{2,1,0:T(8,128)(2,1)}) %all-gather.5.cloned.1.call-update) | async-done | bytes 10616848 | tf_op jit(solution)/shard_map/all_gather | solution.py:897
  171.7 40.2 %token_block.1 = (bf16[1024,768]{1,0:T(8,128)(2,1)}, bf16[1024,768]{1,0:T(8,128)(2,1)}, bf16[1024,3072]{1,0:T(8,128)(2,1)}, bf16[1024,3072]{1,0:T(8,128)(2,1)}, ...) custom-call(s32[1]{0:T(128)} %bitcast.rank_ref, ...), custom_call_target="tpu_custom_call" | custom-call | flops 46000001024 | bytes 40000000 | tf_op jit(solution)/shard_map/token_block/pallas_call | solution.py:637
  212.8 1.3 collective-permute-start.13
  216.2 21.0 %weight_block.1 = bf16[3072,1728]{1,0:T(8,128)(2,1)} custom-call(s32[1]{0:T(128)} %bitcast.rank_ref, bf16[1024,768]{1,0:T(8,128)(2,1)} %get-tuple-element.111.n1, bf16[1024,768]{1,0:T(8,128)(2,1)} %get-tuple-element.112.dfr, bf16[1024,768]{1,0:T(8,128)(2,1)} %get-tuple-element.113.dar, bf16[1024,3072]{1,0:T(8,128)(2,1)} %get-tuple-element.114.g, ...), custom_call_target="tpu_custom_call" | custom-call | flops 22000001024 | bytes 30000000 | tf_op jit(solution)/shard_map/weight_block/pallas_call | solution.py:730
  237.3 1.8 collective-permute-done.16.do3
  240.8 3.6 collective-permute-start.17
  244.4 45.0 %attend_backward.1 = (bf16[4096,640]{1,0:T(8,128)(2,1)}, f32[1024,768]{1,0:T(8,128)}, bf16[1024,768]{1,0:T(8,128)(2,1)}, bf16[1024,768]{1,0:T(8,128)(2,1)}, bf16[1024,768]{1,0:T(8,128)(2,1)}, /*index=5*/f32[8,640]{1,0:T(8,128)}) custom-call(s32[1536]{0:T(1024)} %xor.62.table, bf16[64,3,64,512]{3,2,1,0:T(8,128)(2,1)} %get-tuple-element.110.p_ref, ...), custom_call_target="tpu_custom_call" | custom-call | flops 40000000000 | bytes 25000000 | tf_op jit(solution)/shard_map/attend_backward/pallas_call | solution.py:357
  292.8 3.0 collective-permute-done.19
  296.4 3.3 add_convert_fusion.1
  303.1 2.2 convert_add_fusion
  305.6 11.1 %head_weight_block.1 = bf16[768,576]{1,0:T(8,128)(2,1)} custom-call(bf16[1024,768]{1,0:T(8,128)(2,1)} %copy-done, bf16[1024,768]{1,0:T(8,128)(2,1)} %copy-done.1, bf16[1024,768]{1,0:T(8,128)(2,1)} %collective-permute-done.7.refs_2_.x2, bf16[1024,768]{1,0:T(8,128)(2,1)} %collective-permute-done.8.refs_3_.x3, bf16[4096,640]{1,0:T(8,128)(2,1)} %get-tuple-element.143.grad_ref), custom_call_target="tpu_custom_call" | custom-call | flops 8000000000 | bytes 12000000 | tf_op jit(solution)/shard_map/head_weight_block/pallas_call | solution.py:423
  316.8 5.7 %reduce-scatter.3.cloned.1.call-done = bf16[4,96,1728]{2,1,0:T(8,128)(2,1)} async-done(((bf16[4,768,1728]{2,1,0:T(8,128)(2,1)}), bf16[4,96,1728]{2,1,0:T(8,128)(2,1)}) %reduce-scatter.3.cloned.1.call-update) | async-done | bytes 1327120 | tf_op jit(solution)/shard_map/reduce_scatter | solution.py:941
  322.6 2.0 constant_dynamic-slice_fusion.3
  327.2 1.5 collective-permute-start.27
  328.8 3.9 collective-permute-done.24
  332.7 4.9 %collective-permute-done.25 = bf16[192,576]{1,0:T(8,128)(2,1)} collective-permute-done((bf16[192,576]{1,0:T(8,128)(2,1)}, bf16[192,576]{1,0:T(8,128)(2,1)}, u32[]{:S(2)}, u32[]{:S(2)}) %collective-permute-start.25) | collective-permute-done | bytes 221216 | tf_op jit(solution)/shard_map/ppermute | solution.py:840
  337.6 1.4 collective-permute-done.26
  338.9 1.4 add_convert_fusion.3
  340.4 1.8 collective-permute-done.20
  342.2 2.9 add_convert_fusion
  345.1 2.6 collective-permute-start.29
  347.7 10.4 %collective-permute-start.28 = (bf16[1024,768]{1,0:T(8,128)(2,1)}, bf16[1024,768]{1,0:T(8,128)(2,1)S(1)}, u32[]{:S(2)}, u32[]{:S(2)}) collective-permute-start(bf16[1024,768]{1,0:T(8,128)(2,1)} %add_convert_fusion), channel_id=1, source_target_pairs={{2,4},{3,5},{4,2},{5,3},{10,12},{11,13},{12,10},{13,11},{18,20},{1... | collective-permute-start | bytes 4718600 | tf_op jit(solution)/shard_map/ppermute | solution.py:840
  358.8 1.3 broadcast_select_fusion.1
  360.8 20.1 %collective-permute-start.30 = (bf16[96,576]{1,0:T(8,128)(2,1)S(1)}, bf16[96,576]{1,0:T(8,128)(2,1)S(1)}, u32[]{:S(2)}, u32[]{:S(2)}) collective-permute-start(bf16[96,576]{1,0:T(8,128)(2,1)S(1)} %constant_dynamic-slice_fusion), channel_id=1, source_target_pairs={{0,4},{1,5},{2,6},{3,7},{4,0},{5,1},{6,2},{7,3},{8,12},{9,13},{10,... | collective-permute-start | bytes 331784 | tf_op jit(solution)/shard_map/ppermute | solution.py:840
  382.0 15.0 %collective-permute-done.28 = bf16[1024,768]{1,0:T(8,128)(2,1)S(1)} collective-permute-done((bf16[1024,768]{1,0:T(8,128)(2,1)}, bf16[1024,768]{1,0:T(8,128)(2,1)S(1)}, u32[]{:S(2)}, u32[]{:S(2)}) %collective-permute-start.28) | collective-permute-done | bytes 1572896 | tf_op jit(solution)/shard_map/ppermute | solution.py:840
  398.0 1.3 broadcast_select_fusion
  (177 shorter events, 39.3 us)
Async XLA Ops:
  7.2 46.6 %copy-start.3 = (bf16[1024,768]{1,0:T(8,128)(2,1)S(1)}, bf16[1024,768]{1,0:T(8,128)(2,1)}, u32[]{:S(2)}) copy-start(bf16[1024,768]{1,0:T(8,128)(2,1)} %param.18) | copy-start | bytes 4718596
  7.2 16.9 %copy-start.9 = (bf16[768,96]{0,1:T(8,128)(2,1)S(1)}, bf16[768,96]{0,1:T(8,128)(2,1)}, u32[]{:S(2)}) copy-start(bf16[768,96]{0,1:T(8,128)(2,1)} %param.25) | copy-start | bytes 442372
  7.2 16.9 %copy-start.10 = (bf16[96,768]{1,0:T(8,128)(2,1)S(1)}, bf16[96,768]{1,0:T(8,128)(2,1)}, u32[]{:S(2)}) copy-start(bf16[96,768]{1,0:T(8,128)(2,1)} %param.24) | copy-start | bytes 442372
  7.2 93.7 %all-gather.7.cloned.1.call-start = ((), (), s32[]{:S(2)}) async-start(), calls=%async_computation.5 | async-start | bytes 1863680 | tf_op jit(solution)/shard_map/all_gather | solution.py:875
  7.3 46.5 %collective-permute-start.1 = (bf16[1024,768]{1,0:T(8,128)(2,1)}, bf16[1024,768]{1,0:T(8,128)(2,1)}, u32[]{:S(2)}, u32[]{:S(2)}) collective-permute-start(bf16[1024,768]{1,0:T(8,128)(2,1)} %param.18), channel_id=1, source_target_pairs={{2,4},{3,5},{4,2},{5,3},{10,12},{11,13},{12,10},{13,11},{18,20},{1... | collective-permute-start | bytes 4718600 | tf_op jit(solution)/shard_map/ppermute | solution.py:840
  13.0 40.7 %collective-permute-start.2 = (bf16[1024,768]{1,0:T(8,128)(2,1)}, bf16[1024,768]{1,0:T(8,128)(2,1)}, u32[]{:S(2)}, u32[]{:S(2)}) collective-permute-start(bf16[1024,768]{1,0:T(8,128)(2,1)} %param.18), channel_id=1, source_target_pairs={{0,1},{1,0},{6,7},{7,6},{8,9},{9,8},{14,15},{15,14},{16,17},{17,16... | collective-permute-start | bytes 4718600 | tf_op jit(solution)/shard_map/ppermute | solution.py:840
  19.0 3.7 collective-permute-start
  22.8 16.3 %collective-permute-start.3 = (bf16[195,576]{1,0:T(8,128)(2,1)S(1)}, bf16[195,576]{1,0:T(8,128)(2,1)S(1)}, u32[]{:S(2)}, u32[]{:S(2)}) collective-permute-start(bf16[195,576]{1,0:T(8,128)(2,1)S(1)} %pad_maximum_fusion.2), channel_id=1, source_target_pairs={{0,2},{1,3},{6,4},{7,5},{8,10},{9,11},{14,12},{15,13},{16,18},{17,... | collective-permute-start | bytes 673928 | tf_op jit(solution)/shard_map/ppermute | solution.py:840
  55.3 22.9 %copy-start = (bf16[1024,768]{1,0:T(8,128)(2,1)}, bf16[1024,768]{1,0:T(8,128)(2,1)S(1)}, u32[]{:S(2)}) copy-start(bf16[1024,768]{1,0:T(8,128)(2,1)S(1)} %broadcast_select_fusion.4.refs_0_.x_ref.x0) | copy-start | bytes 4718596
  55.3 21.3 %collective-permute-start.4 = (bf16[1024,768]{1,0:T(8,128)(2,1)S(1)}, bf16[1024,768]{1,0:T(8,128)(2,1)}, u32[]{:S(2)}, u32[]{:S(2)}) collective-permute-start(bf16[1024,768]{1,0:T(8,128)(2,1)S(1)} %broadcast_select_fusion.4.refs_0_.x_ref.x0), channel_id=1, source_target_pairs={{2,3},{3,2},{4,5},{5,4},{10,11},{11,10},{12,13},{13,12},{18,19},{1... | collective-permute-start | bytes 4718600 | tf_op jit(solution)/shard_map/ppermute | solution.py:840
  57.9 5.4 %collective-permute-start.5 = (bf16[192,576]{1,0:T(8,128)(2,1)S(1)}, bf16[192,576]{1,0:T(8,128)(2,1)S(1)}, u32[]{:S(2)}, u32[]{:S(2)}) collective-permute-start(bf16[192,576]{1,0:T(8,128)(2,1)S(1)} %slice.244), channel_id=1, source_target_pairs={{0,8},{1,9},{2,10},{3,11},{4,12},{5,13},{6,14},{7,15},{8,0},{9,1},... | collective-permute-start | bytes 663560 | tf_op jit(solution)/shard_map/ppermute | solution.py:840
  63.4 9.2 %collective-permute-start.6 = (bf16[384,576]{1,0:T(8,128)(2,1)S(1)}, bf16[384,576]{1,0:T(8,128)(2,1)S(1)}, u32[]{:S(2)}, u32[]{:S(2)}) collective-permute-start(bf16[384,576]{1,0:T(8,128)(2,1)S(1)} %maximum_select_fusion.1), channel_id=1, source_target_pairs={{0,16},{1,17},{2,18},{3,19},{4,20},{5,21},{6,22},{7,23},{8,24},{9,... | collective-permute-start | bytes 1327112 | tf_op jit(solution)/shard_map/ppermute | solution.py:840
  64.8 107.0 %all-gather.5.cloned.1.call-start = ((), (), s32[]{:S(2)}) async-start(), calls=%async_computation.2 | async-start | bytes 12386304 | tf_op jit(solution)/shard_map/all_gather | solution.py:897
  78.2 25.3 %copy-start.1 = (bf16[1024,768]{1,0:T(8,128)(2,1)}, bf16[1024,768]{1,0:T(8,128)(2,1)S(1)}, u32[]{:S(2)}) copy-start(bf16[1024,768]{1,0:T(8,128)(2,1)S(1)} %broadcast_select_fusion.3.refs_1_.x1) | copy-start | bytes 4718596
  78.3 25.4 %copy-start.11 = (f32[768]{0:T(1024)S(1)}, f32[768]{0:T(1024)}, u32[]{:S(2)}) copy-start(f32[768]{0:T(1024)} %param.28) | copy-start | bytes 9220
  78.3 25.4 %copy-start.12 = (f32[768]{0:T(1024)S(1)}, f32[768]{0:T(1024)}, u32[]{:S(2)}) copy-start(f32[768]{0:T(1024)} %param.29) | copy-start | bytes 9220
  78.3 25.4 %copy-start.13 = (f32[768]{0:T(1024)S(1)}, f32[768]{0:T(1024)}, u32[]{:S(2)}) copy-start(f32[768]{0:T(1024)} %param.30) | copy-start | bytes 9220
  78.3 25.4 %copy-start.14 = (f32[768]{0:T(1024)S(1)}, f32[768]{0:T(1024)}, u32[]{:S(2)}) copy-start(f32[768]{0:T(1024)} %param.32) | copy-start | bytes 9220
  78.3 25.4 %copy-start.15 = (f32[768]{0:T(1024)S(1)}, f32[768]{0:T(1024)}, u32[]{:S(2)}) copy-start(f32[768]{0:T(1024)} %param.33) | copy-start | bytes 9220
  78.3 25.4 %copy-start.16 = (f32[768]{0:T(1024)S(1)}, f32[768]{0:T(1024)}, u32[]{:S(2)}) copy-start(f32[768]{0:T(1024)} %param.34) | copy-start | bytes 9220
  78.3 22.6 %collective-permute-start.7 = (bf16[1024,768]{1,0:T(8,128)(2,1)S(1)}, bf16[1024,768]{1,0:T(8,128)(2,1)}, u32[]{:S(2)}, u32[]{:S(2)}) collective-permute-start(bf16[1024,768]{1,0:T(8,128)(2,1)S(1)} %broadcast_select_fusion.4.refs_0_.x_ref.x0), channel_id=1, source_target_pairs={{0,4},{1,5},{2,6},{3,7},{4,0},{5,1},{6,2},{7,3},{8,12},{9,13},{10,... | collective-permute-start | bytes 4718600 | tf_op jit(solution)/shard_map/ppermute | solution.py:840
  78.4 22.5 %collective-permute-start.8 = (bf16[1024,768]{1,0:T(8,128)(2,1)S(1)}, bf16[1024,768]{1,0:T(8,128)(2,1)}, u32[]{:S(2)}, u32[]{:S(2)}) collective-permute-start(bf16[1024,768]{1,0:T(8,128)(2,1)S(1)} %broadcast_select_fusion.3.refs_1_.x1), channel_id=1, source_target_pairs={{0,4},{1,5},{2,6},{3,7},{4,0},{5,1},{6,2},{7,3},{8,12},{9,13},{10,... | collective-permute-start | bytes 4718600 | tf_op jit(solution)/shard_map/ppermute | solution.py:840
  103.6 218.9 %reduce-scatter.3.cloned.1.call-start = ((), (), s32[]{:S(2)}) async-start(), calls=%async_computation.3 | async-start | bytes 12386304 | tf_op jit(solution)/shard_map/reduce_scatter | solution.py:941
  103.8 49.7 %collective-permute-start.12 = (bf16[1024,768]{1,0:T(8,128)(2,1)S(1)}, bf16[1024,768]{1,0:T(8,128)(2,1)S(1)}, u32[]{:S(2)}, u32[]{:S(2)}) collective-permute-start(bf16[1024,768]{1,0:T(8,128)(2,1)S(1)} %copy-done.4), channel_id=1, source_target_pairs={{2,4},{3,5},{4,2},{5,3},{10,12},{11,13},{12,10},{13,11},{18,20},{1... | collective-permute-start | bytes 4718600 | tf_op jit(solution)/shard_map/ppermute | solution.py:840
  141.8 13.0 %collective-permute-start.10 = (bf16[1024,192]{1,0:T(8,128)(2,1)}, bf16[1024,192]{1,0:T(8,128)(2,1)}, u32[]{:S(2)}, u32[]{:S(2)}) collective-permute-start(bf16[1024,192]{1,0:T(8,128)(2,1)} %get-tuple-element.105.o2), channel_id=1, source_target_pairs={{0,4},{1,5},{2,6},{3,7},{4,0},{5,1},{6,2},{7,3},{8,12},{9,13},{10,... | collective-permute-start | bytes 1179656 | tf_op jit(solution)/shard_map/ppermute | solution.py:840
  141.9 15.0 %collective-permute-start.11 = (bf16[1024,192]{1,0:T(8,128)(2,1)}, bf16[1024,192]{1,0:T(8,128)(2,1)}, u32[]{:S(2)}, u32[]{:S(2)}) collective-permute-start(bf16[1024,192]{1,0:T(8,128)(2,1)} %get-tuple-element.106.o3), channel_id=1, source_target_pairs={{0,5},{1,4},{2,7},{3,6},{4,1},{5,0},{6,3},{7,2},{8,13},{9,12},{10,... | collective-permute-start | bytes 1179656 | tf_op jit(solution)/shard_map/ppermute | solution.py:840
  143.9 23.5 %collective-permute-start.9 = (bf16[1024,192]{1,0:T(8,128)(2,1)}, bf16[1024,192]{1,0:T(8,128)(2,1)}, u32[]{:S(2)}, u32[]{:S(2)}) collective-permute-start(bf16[1024,192]{1,0:T(8,128)(2,1)} %get-tuple-element.104.o1), channel_id=1, source_target_pairs={{0,1},{1,0},{2,3},{3,2},{4,5},{5,4},{6,7},{7,6},{8,9},{9,8},{10,11... | collective-permute-start | bytes 1179656 | tf_op jit(solution)/shard_map/ppermute | solution.py:840
  212.8 24.5 %collective-permute-start.13 = (f32[7680]{0:T(1024)S(1)}, f32[7680]{0:T(1024)S(1)}, u32[]{:S(2)}, u32[]{:S(2)}) collective-permute-start(f32[7680]{0:T(1024)S(1)} %reduce.1), channel_id=1, source_target_pairs={{0,1},{1,0},{2,3},{3,2},{4,5},{5,4},{6,7},{7,6},{8,9},{9,8},{10,11... | collective-permute-start | bytes 92168 | tf_op jit(solution)/shard_map/ppermute | solution.py:840
  214.1 23.2 %collective-permute-start.14 = (bf16[1024,192]{1,0:T(8,128)(2,1)}, bf16[1024,192]{1,0:T(8,128)(2,1)S(1)}, u32[]{:S(2)}, u32[]{:S(2)}) collective-permute-start(bf16[1024,192]{1,0:T(8,128)(2,1)} %get-tuple-element.118), channel_id=1, source_target_pairs={{0,1},{1,0},{2,3},{3,2},{4,5},{5,4},{6,7},{7,6},{8,9},{9,8},{10,11... | collective-permute-start | bytes 1179656 | tf_op jit(solution)/shard_map/ppermute | solution.py:840
  214.3 23.0 %collective-permute-start.15 = (bf16[1024,192]{1,0:T(8,128)(2,1)}, bf16[1024,192]{1,0:T(8,128)(2,1)S(1)}, u32[]{:S(2)}, u32[]{:S(2)}) collective-permute-start(bf16[1024,192]{1,0:T(8,128)(2,1)} %get-tuple-element.119), channel_id=1, source_target_pairs={{0,4},{1,5},{2,6},{3,7},{4,0},{5,1},{6,2},{7,3},{8,12},{9,13},{10,... | collective-permute-start | bytes 1179656 | tf_op jit(solution)/shard_map/ppermute | solution.py:840
  215.1 24.0 %collective-permute-start.16 = (bf16[1024,192]{1,0:T(8,128)(2,1)}, bf16[1024,192]{1,0:T(8,128)(2,1)S(1)}, u32[]{:S(2)}, u32[]{:S(2)}) collective-permute-start(bf16[1024,192]{1,0:T(8,128)(2,1)} %get-tuple-element.120), channel_id=1, source_target_pairs={{0,5},{1,4},{2,7},{3,6},{4,1},{5,0},{6,3},{7,2},{8,13},{9,12},{10,... | collective-permute-start | bytes 1179656 | tf_op jit(solution)/shard_map/ppermute | solution.py:840
  240.0 141.0 %reduce-scatter.5.cloned.1.call-start = ((), (), s32[]{:S(2)}) async-start(), calls=%async_computation.4 | async-start | bytes 1720320 | tf_op jit(solution)/shard_map/reduce_scatter | solution.py:968
  240.8 48.6 %collective-permute-start.17 = (bf16[1024,768]{1,0:T(8,128)(2,1)S(1)}, bf16[1024,768]{1,0:T(8,128)(2,1)S(1)}, u32[]{:S(2)}, u32[]{:S(2)}) collective-permute-start(bf16[1024,768]{1,0:T(8,128)(2,1)S(1)} %copy-done.5), channel_id=1, source_target_pairs={{2,4},{3,5},{4,2},{5,3},{10,12},{11,13},{12,10},{13,11},{18,20},{1... | collective-permute-start | bytes 4718600 | tf_op jit(solution)/shard_map/ppermute | solution.py:840
  290.6 5.8 %collective-permute-start.18 = (bf16[1024,768]{1,0:T(8,128)(2,1)}, bf16[1024,768]{1,0:T(8,128)(2,1)S(1)}, u32[]{:S(2)}, u32[]{:S(2)}) collective-permute-start(bf16[1024,768]{1,0:T(8,128)(2,1)} %get-tuple-element.133), channel_id=1, source_target_pairs={{0,4},{1,5},{2,6},{3,7},{4,0},{5,1},{6,2},{7,3},{8,12},{9,13},{10,... | collective-permute-start | bytes 4718600 | tf_op jit(solution)/shard_map/ppermute | solution.py:840
  290.6 12.5 %collective-permute-start.21 = (bf16[1024,768]{1,0:T(8,128)(2,1)}, bf16[1024,768]{1,0:T(8,128)(2,1)}, u32[]{:S(2)}, u32[]{:S(2)}) collective-permute-start(bf16[1024,768]{1,0:T(8,128)(2,1)} %get-tuple-element.139), channel_id=1, source_target_pairs={{0,4},{1,5},{2,6},{3,7},{4,0},{5,1},{6,2},{7,3},{8,12},{9,13},{10,... | collective-permute-start | bytes 4718600 | tf_op jit(solution)/shard_map/ppermute | solution.py:840
  292.1 3.7 collective-permute-start.19
  299.7 2.8 collective-permute-start.22
  300.7 41.5 %collective-permute-start.20 = (bf16[1024,768]{1,0:T(8,128)(2,1)}, bf16[1024,768]{1,0:T(8,128)(2,1)}, u32[]{:S(2)}, u32[]{:S(2)}) collective-permute-start(bf16[1024,768]{1,0:T(8,128)(2,1)} %add_convert_fusion.1), channel_id=1, source_target_pairs={{0,1},{1,0},{2,3},{3,2},{4,5},{5,4},{6,7},{7,6},{8,9},{9,8},{10,11... | collective-permute-start | bytes 4718600 | tf_op jit(solution)/shard_map/ppermute | solution.py:840
  302.5 3.2 collective-permute-start.23
  324.6 8.1 %collective-permute-start.24 = (bf16[192,576]{1,0:T(8,128)(2,1)}, bf16[192,576]{1,0:T(8,128)(2,1)}, u32[]{:S(2)}, u32[]{:S(2)}) collective-permute-start(bf16[192,576]{1,0:T(8,128)(2,1)} %get-tuple-element.212), channel_id=1, source_target_pairs={{0,24},{1,25},{2,26},{3,27},{4,28},{5,29},{6,30},{7,31},{8,16},{9,... | collective-permute-start | bytes 663560 | tf_op jit(solution)/shard_map/ppermute | solution.py:840
  325.8 11.8 %collective-permute-start.25 = (bf16[192,576]{1,0:T(8,128)(2,1)}, bf16[192,576]{1,0:T(8,128)(2,1)}, u32[]{:S(2)}, u32[]{:S(2)}) collective-permute-start(bf16[192,576]{1,0:T(8,128)(2,1)} %get-tuple-element.214), channel_id=1, source_target_pairs={{0,8},{1,9},{2,10},{3,11},{4,12},{5,13},{6,14},{7,15},{8,0},{9,1},... | collective-permute-start | bytes 663560 | tf_op jit(solution)/shard_map/ppermute | solution.py:840
  326.6 12.3 %collective-permute-start.26 = (bf16[192,576]{1,0:T(8,128)(2,1)S(1)}, bf16[192,576]{1,0:T(8,128)(2,1)}, u32[]{:S(2)}, u32[]{:S(2)}) collective-permute-start(bf16[192,576]{1,0:T(8,128)(2,1)S(1)} %get-tuple-element.213), channel_id=1, source_target_pairs={{0,16},{1,17},{2,18},{3,19},{4,20},{5,21},{6,22},{7,23},{8,24},{9,... | collective-permute-start | bytes 663560 | tf_op jit(solution)/shard_map/ppermute | solution.py:840
  327.2 13.2 %collective-permute-start.27 = (f32[8064]{0:T(1024)S(1)}, f32[8064]{0:T(1024)S(1)}, u32[]{:S(2)}, u32[]{:S(2)}) collective-permute-start(f32[8064]{0:T(1024)S(1)} %add.160), channel_id=1, source_target_pairs={{0,4},{1,5},{2,6},{3,7},{4,0},{5,1},{6,2},{7,3},{8,12},{9,13},{10,... | collective-permute-start | bytes 96776 | tf_op jit(solution)/shard_map/ppermute | solution.py:840
  340.4 18.4 %copy-start.6 = (bf16[1024,768]{1,0:T(8,128)(2,1)S(1)}, bf16[1024,768]{1,0:T(8,128)(2,1)}, u32[]{:S(2)}) copy-start(bf16[1024,768]{1,0:T(8,128)(2,1)} %get-tuple-element.109) | copy-start | bytes 4718596
  340.4 18.4 %copy-start.8 = (bf16[1024,768]{1,0:T(8,128)(2,1)S(1)}, bf16[1024,768]{1,0:T(8,128)(2,1)}, u32[]{:S(2)}) copy-start(bf16[1024,768]{1,0:T(8,128)(2,1)} %copy-done.7) | copy-start | bytes 4718596
  345.1 15.7 %collective-permute-start.29 = (bf16[192,576]{1,0:T(8,128)(2,1)S(1)}, bf16[192,576]{1,0:T(8,128)(2,1)S(1)}, u32[]{:S(2)}, u32[]{:S(2)}) collective-permute-start(bf16[192,576]{1,0:T(8,128)(2,1)S(1)} %add_convert_fusion.3), channel_id=1, source_target_pairs={{2,0},{3,1},{4,6},{5,7},{10,8},{11,9},{12,14},{13,15},{18,16},{19,... | collective-permute-start | bytes 663560 | tf_op jit(solution)/shard_map/ppermute | solution.py:840
  347.7 49.2 %collective-permute-start.28 = (bf16[1024,768]{1,0:T(8,128)(2,1)}, bf16[1024,768]{1,0:T(8,128)(2,1)S(1)}, u32[]{:S(2)}, u32[]{:S(2)}) collective-permute-start(bf16[1024,768]{1,0:T(8,128)(2,1)} %add_convert_fusion), channel_id=1, source_target_pairs={{2,4},{3,5},{4,2},{5,3},{10,12},{11,13},{12,10},{13,11},{18,20},{1... | collective-permute-start | bytes 4718600 | tf_op jit(solution)/shard_map/ppermute | solution.py:840
  360.8 21.1 %collective-permute-start.30 = (bf16[96,576]{1,0:T(8,128)(2,1)S(1)}, bf16[96,576]{1,0:T(8,128)(2,1)S(1)}, u32[]{:S(2)}, u32[]{:S(2)}) collective-permute-start(bf16[96,576]{1,0:T(8,128)(2,1)S(1)} %constant_dynamic-slice_fusion), channel_id=1, source_target_pairs={{0,4},{1,5},{2,6},{3,7},{4,0},{5,1},{6,2},{7,3},{8,12},{9,13},{10,... | collective-permute-start | bytes 331784 | tf_op jit(solution)/shard_map/ppermute | solution.py:840
  (7 other events, 17.6 us)
Sparse Core Ops, SparseCore 0:
  64.9 35.9 all-gather.6
  103.7 67.9 all-gather.4
  239.3 83.1 reduce-scatter.2
  324.6 38.4 reduce-scatter.4

commit v6 on v5

--- a/solution.py
+++ b/solution.py
@@ -887,12 +887,11 @@
     b_qkv = insert_zero(pack_columns(mine[:192], b_key, mine[192:], 0), 0)
     scale = jnp.concatenate([jnp.ones((KV,), jnp.float32), jnp.full((256,), 0.125, jnp.float32)])
     near = jnp.where(here, near_stay, near_move)
-    near, own, cotangent, w_qkv, b_qkv = lax.optimization_barrier(
-        (near, own, cotangent, w_qkv, b_qkv)
+    near, own, cotangent, w_qkv, b_qkv, rest = lax.optimization_barrier(
+        (near, own, cotangent, w_qkv, b_qkv, rest)
     )
     side, far = side_of(own), side_of(near)
     cot_moved = flip(cotangent, 1, 2, moves)
-    side, far, rest = lax.optimization_barrier((side, far, rest))
     below = rest[:, w_up.shape[0] :].reshape(GROUP, -1)
     rest_all = lax.all_gather(
         rest[:, : w_up.shape[0]], "dp", axis=1, tiled=True

time: 410 us -> 413 us (level)
  other arithmetic: 27.9 us -> 32.3 us
    all_gather x1, waiting for transfers between devices: 22 us -> 0.02 us  [per_device(): rest = lax.all_gather(rest, 'tensor', axis=0)]
    ppermute x31, waiting for transfers between devices: 88.8 us -> 109 us  [flip(): return lax.ppermute(value, both, pairs)]
  transfers between devices with their start and end apart: 35 -> 35, of which waited for: 20 -> 19; matrix products, arithmetic and copies ran while one was open for 9% -> 10% of each run, Pallas kernels for 28% -> 27%
where the time goes in v6:
time: 413 us; the launch traced here: 412 us
  Pallas kernels  153 us (37%)
  waiting for transfers between devices  118 us (29%)
  starting transfers between devices  69.9 us (17%)
  other arithmetic  32.3 us (8%)
  local copies, waits for them, and re-layouts  23.7 us (6%)
  between operations  14.6 us (4%)
    ppermute x31, waiting for transfers between devices, flip(): return lax.ppermute(value, both, pairs)  109 us
    ppermute x31, starting transfers between devices, flip(): return lax.ppermute(value, both, pairs)  69.8 us
    pallas_call x1, Pallas kernels, attend_backward(): pl.pallas_call(functools.partial(backward_kernel, steps), grid_spec=pltpu...  45 us
    pallas_call x1, Pallas kernels, token_block(): pl.pallas_call(functools.partial(token_kernel, tile, width, hidden), grid...  40.2 us
    pallas_call x2, Pallas kernels, attend_forward(): pl.pallas_call(functools.partial(forward_kernel, steps, count, project),...  36 us
    pallas_call x1, Pallas kernels, weight_block(): pl.pallas_call(functools.partial(weight_kernel, width, hidden), grid_spec...  21 us
    pallas_call x1, Pallas kernels, head_weight_block(): pl.pallas_call(head_weight_kernel, grid=(GROUP,), in_specs=[any_spec] * 4...  11.1 us
  transfers between devices with their start and end apart: 35, of which 19 were waited for; matrix products, arithmetic and copies ran while one was open for 10% of the time, Pallas kernels for 27%

profile of v6, /device:TPU:1, one launch (start us, length us, event | category | flops | bytes accessed | tf_op | source)
XLA Modules:
  0.0 411.8 jit_solution(8662976137414544331)
XLA Ops:
  7.2 5.7 %collective-permute-start.1 = (bf16[1024,768]{1,0:T(8,128)(2,1)}, bf16[1024,768]{1,0:T(8,128)(2,1)}, u32[]{:S(2)}, u32[]{:S(2)}) collective-permute-start(bf16[1024,768]{1,0:T(8,128)(2,1)} %param.18), channel_id=1, source_target_pairs={{2,4},{3,5},{4,2},{5,3},{10,12},{11,13},{12,10},{13,11},{18,20},{1... | collective-permute-start | bytes 4718600 | tf_op jit(solution)/shard_map/ppermute | solution.py:840
  21.2 1.5 copy.46
  23.7 1.3 collective-permute-start.3
  25.0 1.8 pad_maximum_fusion.1
  26.8 13.2 %collective-permute-done.3 = bf16[195,576]{1,0:T(8,128)(2,1)S(1)} collective-permute-done((bf16[195,576]{1,0:T(8,128)(2,1)S(1)}, bf16[195,576]{1,0:T(8,128)(2,1)S(1)}, u32[]{:S(2)}, u32[]{:S(2)}) %collective-permute-start.3) | collective-permute-done | bytes 224672 | tf_op jit(solution)/shard_map/ppermute | solution.py:840
  40.1 13.7 %collective-permute-done.1 = bf16[1024,768]{1,0:T(8,128)(2,1)} collective-permute-done((bf16[1024,768]{1,0:T(8,128)(2,1)}, bf16[1024,768]{1,0:T(8,128)(2,1)}, u32[]{:S(2)}, u32[]{:S(2)}) %collective-permute-start.1) | collective-permute-done | bytes 1572896 | tf_op jit(solution)/shard_map/ppermute | solution.py:840
  54.9 1.6 broadcast_select_fusion.4.refs_0_.x_ref.x0
  56.5 2.4 collective-permute-start.4
  59.1 1.3 collective-permute-start.5
  60.4 4.0 collective-permute-done.5
  64.6 1.3 collective-permute-start.6
  66.1 8.8 %collective-permute-done.6 = bf16[384,576]{1,0:T(8,128)(2,1)S(1)} collective-permute-done((bf16[384,576]{1,0:T(8,128)(2,1)S(1)}, bf16[384,576]{1,0:T(8,128)(2,1)S(1)}, u32[]{:S(2)}, u32[]{:S(2)}) %collective-permute-start.6) | collective-permute-done | bytes 442400 | tf_op jit(solution)/shard_map/ppermute | solution.py:840
  75.4 1.2 pad_maximum_fusion.refs_4_.w_ref
  76.6 25.2 %collective-permute-done.4 = bf16[1024,768]{1,0:T(8,128)(2,1)} collective-permute-done((bf16[1024,768]{1,0:T(8,128)(2,1)S(1)}, bf16[1024,768]{1,0:T(8,128)(2,1)}, u32[]{:S(2)}, u32[]{:S(2)}) %collective-permute-start.4) | collective-permute-done | bytes 1572896 | tf_op jit(solution)/shard_map/ppermute | solution.py:840
  101.8 1.6 broadcast_select_fusion.3.refs_1_.x1
  103.5 3.1 slice.215
  107.4 5.4 %collective-permute-start.12 = (bf16[1024,768]{1,0:T(8,128)(2,1)}, bf16[1024,768]{1,0:T(8,128)(2,1)}, u32[]{:S(2)}, u32[]{:S(2)}) collective-permute-start(bf16[1024,768]{1,0:T(8,128)(2,1)} %param.19), channel_id=1, source_target_pairs={{2,4},{3,5},{4,2},{5,3},{10,12},{11,13},{12,10},{13,11},{18,20},{1... | collective-permute-start | bytes 4718600 | tf_op jit(solution)/shard_map/ppermute | solution.py:840
  119.0 26.8 %attend_forward.2 = (bf16[1024,192]{1,0:T(8,128)(2,1)}, bf16[1024,192]{1,0:T(8,128)(2,1)}, bf16[1024,192]{1,0:T(8,128)(2,1)}, bf16[64,3,64,512]{3,2,1,0:T(8,128)(2,1)}, bf16[4096,640]{1,0:T(8,128)(2,1)}) custom-call(s32[1536]{0:T(1024)} %xor.62.table, s32[4]{0:T(128)} %pad_add_fusion.1.place, bf16[1024,768]{1,0:T(8,128)(2,1)} %copy-done, ...), custom_call_target="tpu_custom_call" | custom-call | tf_op jit(solution)/shard_map/attend_forward/pallas_call | solution.py:172
  146.0 2.1 collective-permute-start.11
  148.7 9.1 %attend_forward.3 = (bf16[1024,192]{1,0:T(8,128)(2,1)}, bf16[64,3,64,512]{3,2,1,0:T(8,128)(2,1)}) custom-call(s32[1536]{0:T(1024)} %xor.62.table, s32[2]{0:T(128)} %pad_add_fusion.place, bf16[4096,640]{1,0:T(8,128)(2,1)} %get-tuple-element.97.refs_0_.qkv_hbm, bf16[64,3,64,512]{3,2,1,0:T(8,128)(2,1)} %get-tuple-element.98.refs_1_), custom_call_target="tpu_custom_call", output_to_operand_aliasing={{1}: (3, {})} | custom-call | tf_op jit(solution)/shard_map/attend_forward/pallas_call | solution.py:172
  157.9 2.9 broadcast_select_fusion.2.cot_ref
  161.1 10.2 %collective-permute-done.9.o1 = bf16[1024,192]{1,0:T(8,128)(2,1)S(1)} collective-permute-done((bf16[1024,192]{1,0:T(8,128)(2,1)}, bf16[1024,192]{1,0:T(8,128)(2,1)S(1)}, u32[]{:S(2)}, u32[]{:S(2)}) %collective-permute-start.9) | collective-permute-done | bytes 393248 | tf_op jit(solution)/shard_map/ppermute | solution.py:840
  171.4 3.4 all-gather.5.cloned.1.call-done
  174.8 40.2 %token_block.1 = (bf16[1024,768]{1,0:T(8,128)(2,1)}, bf16[1024,768]{1,0:T(8,128)(2,1)}, bf16[1024,3072]{1,0:T(8,128)(2,1)}, bf16[1024,3072]{1,0:T(8,128)(2,1)}, ...) custom-call(s32[1]{0:T(128)} %bitcast.rank_ref, ...), custom_call_target="tpu_custom_call" | custom-call | flops 46000001024 | bytes 40000000 | tf_op jit(solution)/shard_map/token_block/pallas_call | solution.py:637
  215.9 1.3 collective-permute-start.13
  219.3 21.0 %weight_block.1 = bf16[3072,1728]{1,0:T(8,128)(2,1)} custom-call(s32[1]{0:T(128)} %bitcast.rank_ref, bf16[1024,768]{1,0:T(8,128)(2,1)} %get-tuple-element.107.n1, bf16[1024,768]{1,0:T(8,128)(2,1)} %get-tuple-element.108.dfr, bf16[1024,768]{1,0:T(8,128)(2,1)} %get-tuple-element.109.dar, bf16[1024,3072]{1,0:T(8,128)(2,1)} %get-tuple-element.110.g, ...), custom_call_target="tpu_custom_call" | custom-call | flops 22000001024 | bytes 30000000 | tf_op jit(solution)/shard_map/weight_block/pallas_call | solution.py:730
  240.4 1.9 collective-permute-done.16.do3
  243.8 3.6 collective-permute-start.17
  247.5 45.0 %attend_backward.1 = (bf16[4096,640]{1,0:T(8,128)(2,1)}, f32[1024,768]{1,0:T(8,128)}, bf16[1024,768]{1,0:T(8,128)(2,1)}, bf16[1024,768]{1,0:T(8,128)(2,1)}, bf16[1024,768]{1,0:T(8,128)(2,1)}, /*index=5*/f32[8,640]{1,0:T(8,128)}) custom-call(s32[1536]{0:T(1024)} %xor.62.table, bf16[64,3,64,512]{3,2,1,0:T(8,128)(2,1)} %get-tuple-element.106.p_ref, ...), custom_call_target="tpu_custom_call" | custom-call | flops 40000000000 | bytes 25000000 | tf_op jit(solution)/shard_map/attend_backward/pallas_call | solution.py:357
  295.9 2.9 collective-permute-done.19
  299.5 3.3 add_convert_fusion.1
  306.2 2.2 convert_add_fusion
  308.7 11.1 %head_weight_block.1 = bf16[768,576]{1,0:T(8,128)(2,1)} custom-call(bf16[1024,768]{1,0:T(8,128)(2,1)} %copy-done, bf16[1024,768]{1,0:T(8,128)(2,1)} %copy-done.1, bf16[1024,768]{1,0:T(8,128)(2,1)} %collective-permute-done.7.refs_2_.x2, bf16[1024,768]{1,0:T(8,128)(2,1)} %collective-permute-done.8.refs_3_.x3, bf16[4096,640]{1,0:T(8,128)(2,1)} %get-tuple-element.139.grad_ref), custom_call_target="tpu_custom_call" | custom-call | flops 8000000000 | bytes 12000000 | tf_op jit(solution)/shard_map/head_weight_block/pallas_call | solution.py:423
  319.8 5.7 %reduce-scatter.3.cloned.1.call-done = bf16[4,96,1728]{2,1,0:T(8,128)(2,1)} async-done(((bf16[4,768,1728]{2,1,0:T(8,128)(2,1)}), bf16[4,96,1728]{2,1,0:T(8,128)(2,1)}) %reduce-scatter.3.cloned.1.call-update) | async-done | bytes 1327120 | tf_op jit(solution)/shard_map/reduce_scatter | solution.py:940
  325.6 2.0 constant_dynamic-slice_fusion.3
  330.3 1.5 collective-permute-start.27
  331.8 3.9 collective-permute-done.24
  335.7 5.0 %collective-permute-done.25 = bf16[192,576]{1,0:T(8,128)(2,1)} collective-permute-done((bf16[192,576]{1,0:T(8,128)(2,1)}, bf16[192,576]{1,0:T(8,128)(2,1)}, u32[]{:S(2)}, u32[]{:S(2)}) %collective-permute-start.25) | collective-permute-done | bytes 221216 | tf_op jit(solution)/shard_map/ppermute | solution.py:840
  340.7 1.3 collective-permute-done.26
  342.0 1.4 add_convert_fusion.3
  343.5 1.9 collective-permute-done.20
  345.3 2.9 add_convert_fusion
  348.2 2.5 collective-permute-start.29
  350.8 10.4 %collective-permute-start.28 = (bf16[1024,768]{1,0:T(8,128)(2,1)}, bf16[1024,768]{1,0:T(8,128)(2,1)S(1)}, u32[]{:S(2)}, u32[]{:S(2)}) collective-permute-start(bf16[1024,768]{1,0:T(8,128)(2,1)} %add_convert_fusion), channel_id=1, source_target_pairs={{2,4},{3,5},{4,2},{5,3},{10,12},{11,13},{12,10},{13,11},{18,20},{1... | collective-permute-start | bytes 4718600 | tf_op jit(solution)/shard_map/ppermute | solution.py:840
  361.9 1.3 broadcast_select_fusion.1
  363.9 20.1 %collective-permute-start.30 = (bf16[96,576]{1,0:T(8,128)(2,1)S(1)}, bf16[96,576]{1,0:T(8,128)(2,1)S(1)}, u32[]{:S(2)}, u32[]{:S(2)}) collective-permute-start(bf16[96,576]{1,0:T(8,128)(2,1)S(1)} %constant_dynamic-slice_fusion), channel_id=1, source_target_pairs={{0,4},{1,5},{2,6},{3,7},{4,0},{5,1},{6,2},{7,3},{8,12},{9,13},{10,... | collective-permute-start | bytes 331784 | tf_op jit(solution)/shard_map/ppermute | solution.py:840
  385.1 15.0 %collective-permute-done.28 = bf16[1024,768]{1,0:T(8,128)(2,1)S(1)} collective-permute-done((bf16[1024,768]{1,0:T(8,128)(2,1)}, bf16[1024,768]{1,0:T(8,128)(2,1)S(1)}, u32[]{:S(2)}, u32[]{:S(2)}) %collective-permute-start.28) | collective-permute-done | bytes 1572896 | tf_op jit(solution)/shard_map/ppermute | solution.py:840
  401.1 1.3 broadcast_select_fusion
  (189 shorter events, 40.8 us)
Async XLA Ops:
  7.2 47.7 %copy-start.3 = (bf16[1024,768]{1,0:T(8,128)(2,1)S(1)}, bf16[1024,768]{1,0:T(8,128)(2,1)}, u32[]{:S(2)}) copy-start(bf16[1024,768]{1,0:T(8,128)(2,1)} %param.18) | copy-start | bytes 4718596
  7.2 96.3 %all-gather.7.cloned.1.call-start = ((), (), s32[]{:S(2)}) async-start(), calls=%async_computation.5 | async-start | bytes 1863680 | tf_op jit(solution)/shard_map/all_gather | solution.py:875
  7.2 46.5 %collective-permute-start.1 = (bf16[1024,768]{1,0:T(8,128)(2,1)}, bf16[1024,768]{1,0:T(8,128)(2,1)}, u32[]{:S(2)}, u32[]{:S(2)}) collective-permute-start(bf16[1024,768]{1,0:T(8,128)(2,1)} %param.18), channel_id=1, source_target_pairs={{2,4},{3,5},{4,2},{5,3},{10,12},{11,13},{12,10},{13,11},{18,20},{1... | collective-permute-start | bytes 4718600 | tf_op jit(solution)/shard_map/ppermute | solution.py:840
  13.0 40.7 %collective-permute-start.2 = (bf16[1024,768]{1,0:T(8,128)(2,1)}, bf16[1024,768]{1,0:T(8,128)(2,1)S(1)}, u32[]{:S(2)}, u32[]{:S(2)}) collective-permute-start(bf16[1024,768]{1,0:T(8,128)(2,1)} %param.18), channel_id=1, source_target_pairs={{0,1},{1,0},{6,7},{7,6},{8,9},{9,8},{14,15},{15,14},{16,17},{17,16... | collective-permute-start | bytes 4718600 | tf_op jit(solution)/shard_map/ppermute | solution.py:840
  17.9 4.8 %collective-permute-start = (bf16[96,576]{1,0:T(8,128)(2,1)S(1)}, bf16[96,576]{1,0:T(8,128)(2,1)}, u32[]{:S(2)}, u32[]{:S(2)}) collective-permute-start(bf16[96,576]{1,0:T(8,128)(2,1)S(1)} %concatenate.72), channel_id=1, source_target_pairs={{0,4},{1,5},{2,6},{3,7},{4,0},{5,1},{6,2},{7,3},{8,12},{9,13},{10,... | collective-permute-start | bytes 331784 | tf_op jit(solution)/shard_map/ppermute | solution.py:840
  23.7 16.3 %collective-permute-start.3 = (bf16[195,576]{1,0:T(8,128)(2,1)S(1)}, bf16[195,576]{1,0:T(8,128)(2,1)S(1)}, u32[]{:S(2)}, u32[]{:S(2)}) collective-permute-start(bf16[195,576]{1,0:T(8,128)(2,1)S(1)} %pad_maximum_fusion.2), channel_id=1, source_target_pairs={{0,2},{1,3},{6,4},{7,5},{8,10},{9,11},{14,12},{15,13},{16,18},{17,... | collective-permute-start | bytes 673928 | tf_op jit(solution)/shard_map/ppermute | solution.py:840
  40.0 13.7 %copy-start.12 = (bf16[195,576]{1,0:T(8,128)(2,1)}, bf16[195,576]{1,0:T(8,128)(2,1)S(1)}, u32[]{:S(2)}) copy-start(bf16[195,576]{1,0:T(8,128)(2,1)S(1)} %collective-permute-done.3) | copy-start | bytes 673924
  54.9 119.9 %all-gather.5.cloned.1.call-start = ((), (), s32[]{:S(2)}) async-start(), calls=%async_computation.2 | async-start | bytes 12386304 | tf_op jit(solution)/shard_map/all_gather | solution.py:896
  54.9 4.0 copy-start.13
  56.5 50.2 %copy-start = (bf16[1024,768]{1,0:T(8,128)(2,1)}, bf16[1024,768]{1,0:T(8,128)(2,1)S(1)}, u32[]{:S(2)}) copy-start(bf16[1024,768]{1,0:T(8,128)(2,1)S(1)} %broadcast_select_fusion.4.refs_0_.x_ref.x0) | copy-start | bytes 4718596
  56.5 45.2 %collective-permute-start.4 = (bf16[1024,768]{1,0:T(8,128)(2,1)S(1)}, bf16[1024,768]{1,0:T(8,128)(2,1)}, u32[]{:S(2)}, u32[]{:S(2)}) collective-permute-start(bf16[1024,768]{1,0:T(8,128)(2,1)S(1)} %broadcast_select_fusion.4.refs_0_.x_ref.x0), channel_id=1, source_target_pairs={{2,3},{3,2},{4,5},{5,4},{10,11},{11,10},{12,13},{13,12},{18,19},{1... | collective-permute-start | bytes 4718600 | tf_op jit(solution)/shard_map/ppermute | solution.py:840
  59.1 5.4 %collective-permute-start.5 = (bf16[192,576]{1,0:T(8,128)(2,1)S(1)}, bf16[192,576]{1,0:T(8,128)(2,1)S(1)}, u32[]{:S(2)}, u32[]{:S(2)}) collective-permute-start(bf16[192,576]{1,0:T(8,128)(2,1)S(1)} %slice.244), channel_id=1, source_target_pairs={{0,8},{1,9},{2,10},{3,11},{4,12},{5,13},{6,14},{7,15},{8,0},{9,1},... | collective-permute-start | bytes 663560 | tf_op jit(solution)/shard_map/ppermute | solution.py:840
  64.6 10.3 %collective-permute-start.6 = (bf16[384,576]{1,0:T(8,128)(2,1)S(1)}, bf16[384,576]{1,0:T(8,128)(2,1)S(1)}, u32[]{:S(2)}, u32[]{:S(2)}) collective-permute-start(bf16[384,576]{1,0:T(8,128)(2,1)S(1)} %maximum_select_fusion.1), channel_id=1, source_target_pairs={{0,16},{1,17},{2,18},{3,19},{4,20},{5,21},{6,22},{7,23},{8,24},{9,... | collective-permute-start | bytes 1327112 | tf_op jit(solution)/shard_map/ppermute | solution.py:840
  75.3 26.4 %copy-start.10 = (bf16[1024,768]{1,0:T(8,128)(2,1)S(1)}, bf16[1024,768]{1,0:T(8,128)(2,1)}, u32[]{:S(2)}) copy-start(bf16[1024,768]{1,0:T(8,128)(2,1)} %copy-done.9) | copy-start | bytes 4718596
  103.4 3.9 copy-start.18
  103.4 3.9 copy-start.19
  106.6 218.9 %reduce-scatter.3.cloned.1.call-start = ((), (), s32[]{:S(2)}) async-start(), calls=%async_computation.3 | async-start | bytes 12386304 | tf_op jit(solution)/shard_map/reduce_scatter | solution.py:940
  106.7 12.4 %collective-permute-start.7 = (bf16[1024,768]{1,0:T(8,128)(2,1)S(1)}, bf16[1024,768]{1,0:T(8,128)(2,1)}, u32[]{:S(2)}, u32[]{:S(2)}) collective-permute-start(bf16[1024,768]{1,0:T(8,128)(2,1)S(1)} %broadcast_select_fusion.4.refs_0_.x_ref.x0), channel_id=1, source_target_pairs={{0,4},{1,5},{2,6},{3,7},{4,0},{5,1},{6,2},{7,3},{8,12},{9,13},{10,... | collective-permute-start | bytes 4718600 | tf_op jit(solution)/shard_map/ppermute | solution.py:840
  106.8 12.3 %collective-permute-start.8 = (bf16[1024,768]{1,0:T(8,128)(2,1)S(1)}, bf16[1024,768]{1,0:T(8,128)(2,1)}, u32[]{:S(2)}, u32[]{:S(2)}) collective-permute-start(bf16[1024,768]{1,0:T(8,128)(2,1)S(1)} %broadcast_select_fusion.3.refs_1_.x1), channel_id=1, source_target_pairs={{0,4},{1,5},{2,6},{3,7},{4,0},{5,1},{6,2},{7,3},{8,12},{9,13},{10,... | collective-permute-start | bytes 4718600 | tf_op jit(solution)/shard_map/ppermute | solution.py:840
  107.4 50.5 %collective-permute-start.12 = (bf16[1024,768]{1,0:T(8,128)(2,1)}, bf16[1024,768]{1,0:T(8,128)(2,1)}, u32[]{:S(2)}, u32[]{:S(2)}) collective-permute-start(bf16[1024,768]{1,0:T(8,128)(2,1)} %param.19), channel_id=1, source_target_pairs={{2,4},{3,5},{4,2},{5,3},{10,12},{11,13},{12,10},{13,11},{18,20},{1... | collective-permute-start | bytes 4718600 | tf_op jit(solution)/shard_map/ppermute | solution.py:840
  145.9 14.8 %collective-permute-start.10 = (bf16[1024,192]{1,0:T(8,128)(2,1)}, bf16[1024,192]{1,0:T(8,128)(2,1)S(1)}, u32[]{:S(2)}, u32[]{:S(2)}) collective-permute-start(bf16[1024,192]{1,0:T(8,128)(2,1)} %get-tuple-element.101.o2), channel_id=1, source_target_pairs={{0,4},{1,5},{2,6},{3,7},{4,0},{5,1},{6,2},{7,3},{8,12},{9,13},{10,... | collective-permute-start | bytes 1179656 | tf_op jit(solution)/shard_map/ppermute | solution.py:840
  146.0 15.1 %collective-permute-start.11 = (bf16[1024,192]{1,0:T(8,128)(2,1)}, bf16[1024,192]{1,0:T(8,128)(2,1)S(1)}, u32[]{:S(2)}, u32[]{:S(2)}) collective-permute-start(bf16[1024,192]{1,0:T(8,128)(2,1)} %get-tuple-element.102.o3), channel_id=1, source_target_pairs={{0,5},{1,4},{2,7},{3,6},{4,1},{5,0},{6,3},{7,2},{8,13},{9,12},{10,... | collective-permute-start | bytes 1179656 | tf_op jit(solution)/shard_map/ppermute | solution.py:840
  148.1 23.3 %collective-permute-start.9 = (bf16[1024,192]{1,0:T(8,128)(2,1)}, bf16[1024,192]{1,0:T(8,128)(2,1)S(1)}, u32[]{:S(2)}, u32[]{:S(2)}) collective-permute-start(bf16[1024,192]{1,0:T(8,128)(2,1)} %get-tuple-element.100.o1), channel_id=1, source_target_pairs={{0,1},{1,0},{2,3},{3,2},{4,5},{5,4},{6,7},{7,6},{8,9},{9,8},{10,11... | collective-permute-start | bytes 1179656 | tf_op jit(solution)/shard_map/ppermute | solution.py:840
  148.7 9.1 %copy-start.4 = (bf16[1024,768]{1,0:T(8,128)(2,1)S(1)}, bf16[1024,768]{1,0:T(8,128)(2,1)}, u32[]{:S(2)}) copy-start(bf16[1024,768]{1,0:T(8,128)(2,1)} %param.19) | copy-start | bytes 4718596
  160.7 14.0 %copy-start.20 = (bf16[1024,192]{1,0:T(8,128)(2,1)}, bf16[1024,192]{1,0:T(8,128)(2,1)S(1)}, u32[]{:S(2)}) copy-start(bf16[1024,192]{1,0:T(8,128)(2,1)S(1)} %collective-permute-done.10.o2) | copy-start | bytes 1179652
  161.1 13.7 %copy-start.21 = (bf16[1024,192]{1,0:T(8,128)(2,1)}, bf16[1024,192]{1,0:T(8,128)(2,1)S(1)}, u32[]{:S(2)}) copy-start(bf16[1024,192]{1,0:T(8,128)(2,1)S(1)} %collective-permute-done.11.o3) | copy-start | bytes 1179652
  215.9 24.5 %collective-permute-start.13 = (f32[7680]{0:T(1024)S(1)}, f32[7680]{0:T(1024)S(1)}, u32[]{:S(2)}, u32[]{:S(2)}) collective-permute-start(f32[7680]{0:T(1024)S(1)} %reduce.1), channel_id=1, source_target_pairs={{0,1},{1,0},{2,3},{3,2},{4,5},{5,4},{6,7},{7,6},{8,9},{9,8},{10,11... | collective-permute-start | bytes 92168 | tf_op jit(solution)/shard_map/ppermute | solution.py:840
  217.1 23.2 %collective-permute-start.14 = (bf16[1024,192]{1,0:T(8,128)(2,1)}, bf16[1024,192]{1,0:T(8,128)(2,1)S(1)}, u32[]{:S(2)}, u32[]{:S(2)}) collective-permute-start(bf16[1024,192]{1,0:T(8,128)(2,1)} %get-tuple-element.114), channel_id=1, source_target_pairs={{0,1},{1,0},{2,3},{3,2},{4,5},{5,4},{6,7},{7,6},{8,9},{9,8},{10,11... | collective-permute-start | bytes 1179656 | tf_op jit(solution)/shard_map/ppermute | solution.py:840
  217.4 23.0 %collective-permute-start.15 = (bf16[1024,192]{1,0:T(8,128)(2,1)}, bf16[1024,192]{1,0:T(8,128)(2,1)S(1)}, u32[]{:S(2)}, u32[]{:S(2)}) collective-permute-start(bf16[1024,192]{1,0:T(8,128)(2,1)} %get-tuple-element.115), channel_id=1, source_target_pairs={{0,4},{1,5},{2,6},{3,7},{4,0},{5,1},{6,2},{7,3},{8,12},{9,13},{10,... | collective-permute-start | bytes 1179656 | tf_op jit(solution)/shard_map/ppermute | solution.py:840
  218.2 24.0 %collective-permute-start.16 = (bf16[1024,192]{1,0:T(8,128)(2,1)}, bf16[1024,192]{1,0:T(8,128)(2,1)S(1)}, u32[]{:S(2)}, u32[]{:S(2)}) collective-permute-start(bf16[1024,192]{1,0:T(8,128)(2,1)} %get-tuple-element.116), channel_id=1, source_target_pairs={{0,5},{1,4},{2,7},{3,6},{4,1},{5,0},{6,3},{7,2},{8,13},{9,12},{10,... | collective-permute-start | bytes 1179656 | tf_op jit(solution)/shard_map/ppermute | solution.py:840
  243.0 141.0 %reduce-scatter.5.cloned.1.call-start = ((), (), s32[]{:S(2)}) async-start(), calls=%async_computation.4 | async-start | bytes 1720320 | tf_op jit(solution)/shard_map/reduce_scatter | solution.py:967
  243.8 48.6 %collective-permute-start.17 = (bf16[1024,768]{1,0:T(8,128)(2,1)S(1)}, bf16[1024,768]{1,0:T(8,128)(2,1)S(1)}, u32[]{:S(2)}, u32[]{:S(2)}) collective-permute-start(bf16[1024,768]{1,0:T(8,128)(2,1)S(1)} %copy-done.5), channel_id=1, source_target_pairs={{2,4},{3,5},{4,2},{5,3},{10,12},{11,13},{12,10},{13,11},{18,20},{1... | collective-permute-start | bytes 4718600 | tf_op jit(solution)/shard_map/ppermute | solution.py:840
  293.6 5.8 %collective-permute-start.18 = (bf16[1024,768]{1,0:T(8,128)(2,1)}, bf16[1024,768]{1,0:T(8,128)(2,1)S(1)}, u32[]{:S(2)}, u32[]{:S(2)}) collective-permute-start(bf16[1024,768]{1,0:T(8,128)(2,1)} %get-tuple-element.129), channel_id=1, source_target_pairs={{0,4},{1,5},{2,6},{3,7},{4,0},{5,1},{6,2},{7,3},{8,12},{9,13},{10,... | collective-permute-start | bytes 4718600 | tf_op jit(solution)/shard_map/ppermute | solution.py:840
  293.6 12.6 %collective-permute-start.21 = (bf16[1024,768]{1,0:T(8,128)(2,1)}, bf16[1024,768]{1,0:T(8,128)(2,1)}, u32[]{:S(2)}, u32[]{:S(2)}) collective-permute-start(bf16[1024,768]{1,0:T(8,128)(2,1)} %get-tuple-element.135), channel_id=1, source_target_pairs={{0,4},{1,5},{2,6},{3,7},{4,0},{5,1},{6,2},{7,3},{8,12},{9,13},{10,... | collective-permute-start | bytes 4718600 | tf_op jit(solution)/shard_map/ppermute | solution.py:840
  295.1 3.7 collective-permute-start.19
  298.8 7.4 %copy-start.2 = (f32[1024,768]{1,0:T(8,128)S(1)}, f32[1024,768]{1,0:T(8,128)}, u32[]{:S(2)}) copy-start(f32[1024,768]{1,0:T(8,128)} %get-tuple-element.134) | copy-start | bytes 9437188
  302.7 2.8 collective-permute-start.22
  303.7 41.6 %collective-permute-start.20 = (bf16[1024,768]{1,0:T(8,128)(2,1)}, bf16[1024,768]{1,0:T(8,128)(2,1)}, u32[]{:S(2)}, u32[]{:S(2)}) collective-permute-start(bf16[1024,768]{1,0:T(8,128)(2,1)} %add_convert_fusion.1), channel_id=1, source_target_pairs={{0,1},{1,0},{2,3},{3,2},{4,5},{5,4},{6,7},{7,6},{8,9},{9,8},{10,11... | collective-permute-start | bytes 4718600 | tf_op jit(solution)/shard_map/ppermute | solution.py:840
  305.5 3.2 collective-permute-start.23
  327.6 8.1 %collective-permute-start.24 = (bf16[192,576]{1,0:T(8,128)(2,1)}, bf16[192,576]{1,0:T(8,128)(2,1)}, u32[]{:S(2)}, u32[]{:S(2)}) collective-permute-start(bf16[192,576]{1,0:T(8,128)(2,1)} %get-tuple-element.208), channel_id=1, source_target_pairs={{0,24},{1,25},{2,26},{3,27},{4,28},{5,29},{6,30},{7,31},{8,16},{9,... | collective-permute-start | bytes 663560 | tf_op jit(solution)/shard_map/ppermute | solution.py:840
  328.8 11.9 %collective-permute-start.25 = (bf16[192,576]{1,0:T(8,128)(2,1)}, bf16[192,576]{1,0:T(8,128)(2,1)}, u32[]{:S(2)}, u32[]{:S(2)}) collective-permute-start(bf16[192,576]{1,0:T(8,128)(2,1)} %get-tuple-element.210), channel_id=1, source_target_pairs={{0,8},{1,9},{2,10},{3,11},{4,12},{5,13},{6,14},{7,15},{8,0},{9,1},... | collective-permute-start | bytes 663560 | tf_op jit(solution)/shard_map/ppermute | solution.py:840
  329.7 12.3 %collective-permute-start.26 = (bf16[192,576]{1,0:T(8,128)(2,1)S(1)}, bf16[192,576]{1,0:T(8,128)(2,1)}, u32[]{:S(2)}, u32[]{:S(2)}) collective-permute-start(bf16[192,576]{1,0:T(8,128)(2,1)S(1)} %get-tuple-element.209), channel_id=1, source_target_pairs={{0,16},{1,17},{2,18},{3,19},{4,20},{5,21},{6,22},{7,23},{8,24},{9,... | collective-permute-start | bytes 663560 | tf_op jit(solution)/shard_map/ppermute | solution.py:840
  330.3 13.2 %collective-permute-start.27 = (f32[8064]{0:T(1024)S(1)}, f32[8064]{0:T(1024)S(1)}, u32[]{:S(2)}, u32[]{:S(2)}) collective-permute-start(f32[8064]{0:T(1024)S(1)} %add.160), channel_id=1, source_target_pairs={{0,4},{1,5},{2,6},{3,7},{4,0},{5,1},{6,2},{7,3},{8,12},{9,13},{10,... | collective-permute-start | bytes 96776 | tf_op jit(solution)/shard_map/ppermute | solution.py:840
  343.4 18.4 %copy-start.6 = (bf16[1024,768]{1,0:T(8,128)(2,1)S(1)}, bf16[1024,768]{1,0:T(8,128)(2,1)}, u32[]{:S(2)}) copy-start(bf16[1024,768]{1,0:T(8,128)(2,1)} %get-tuple-element.105) | copy-start | bytes 4718596
  343.4 18.4 %copy-start.8 = (bf16[1024,768]{1,0:T(8,128)(2,1)S(1)}, bf16[1024,768]{1,0:T(8,128)(2,1)}, u32[]{:S(2)}) copy-start(bf16[1024,768]{1,0:T(8,128)(2,1)} %copy-done.7) | copy-start | bytes 4718596
  348.2 15.6 %collective-permute-start.29 = (bf16[192,576]{1,0:T(8,128)(2,1)S(1)}, bf16[192,576]{1,0:T(8,128)(2,1)S(1)}, u32[]{:S(2)}, u32[]{:S(2)}) collective-permute-start(bf16[192,576]{1,0:T(8,128)(2,1)S(1)} %add_convert_fusion.3), channel_id=1, source_target_pairs={{2,0},{3,1},{4,6},{5,7},{10,8},{11,9},{12,14},{13,15},{18,16},{19,... | collective-permute-start | bytes 663560 | tf_op jit(solution)/shard_map/ppermute | solution.py:840
  350.8 49.3 %collective-permute-start.28 = (bf16[1024,768]{1,0:T(8,128)(2,1)}, bf16[1024,768]{1,0:T(8,128)(2,1)S(1)}, u32[]{:S(2)}, u32[]{:S(2)}) collective-permute-start(bf16[1024,768]{1,0:T(8,128)(2,1)} %add_convert_fusion), channel_id=1, source_target_pairs={{2,4},{3,5},{4,2},{5,3},{10,12},{11,13},{12,10},{13,11},{18,20},{1... | collective-permute-start | bytes 4718600 | tf_op jit(solution)/shard_map/ppermute | solution.py:840
  363.9 21.1 %collective-permute-start.30 = (bf16[96,576]{1,0:T(8,128)(2,1)S(1)}, bf16[96,576]{1,0:T(8,128)(2,1)S(1)}, u32[]{:S(2)}, u32[]{:S(2)}) collective-permute-start(bf16[96,576]{1,0:T(8,128)(2,1)S(1)} %constant_dynamic-slice_fusion), channel_id=1, source_target_pairs={{0,4},{1,5},{2,6},{3,7},{4,0},{5,1},{6,2},{7,3},{8,12},{9,13},{10,... | collective-permute-start | bytes 331784 | tf_op jit(solution)/shard_map/ppermute | solution.py:840
  (13 other events, 32.4 us)
Sparse Core Ops, SparseCore 0:
  53.9 45.4 all-gather.6
  106.7 67.9 all-gather.4
  242.4 83.1 reduce-scatter.2
  327.7 38.5 reduce-scatter.4

commit v7 on v5

--- a/solution.py
+++ b/solution.py
@@ -251,9 +251,9 @@
             pltpu.make_async_copy(src, o_scr.at[pl.ds(n * QROWS, QROWS)], sems.at[9 + n])
             for n, src in enumerate((o0, o1, o2, o3))
         ]
-        copies.append(pltpu.make_async_copy(da_hbm, da_scr, sems.at[8]))
         for copy in copies:
             copy.start()
+        pltpu.make_async_copy(da_hbm, da_scr, sems.at[8]).start()
         acc[...] = jnp.zeros_like(acc)
         for copy in copies:
             copy.wait()
@@ -319,6 +319,7 @@
         for row in range(0, LENGTH, 128):
             total = total + fold_rows(out_ref[row : row + 128].astype(jnp.float32))
         sum_ref[...] = total
+        pltpu.make_async_copy(da_hbm, da_scr, sems.at[8]).wait()
         done = [pltpu.make_async_copy(out_ref, out_hbm, sems.at[0])]
         done[0].start()
         chunk = 512
@@ -349,7 +350,7 @@
 
 
 def attend_backward(table, probs, qkv, grads, outs, w_qkv, da):
-    steps = 16
+    steps = 8
     per = NB // steps
     width = w_qkv.shape[0]
     any_spec = pl.BlockSpec(memory_space=pl.ANY)
@@ -701,7 +702,7 @@
         dfr_t[...] = dfr[...].T
         dar_t[...] = dar[...].T
 
-    chunk = 256
+    chunk = 384
 
     def product(n, carry):
         rows = pl.ds(pl.multiple_of(n * chunk, chunk), chunk)

time: 410 us -> 408 us (level)
  transfers between devices with their start and end apart: 35 -> 35, of which waited for: 20 -> 20; matrix products, arithmetic and copies ran while one was open for 9% -> 9% of each run, Pallas kernels for 28% -> 27%
where the time goes in v7:
time: 408 us; the launch traced here: 406 us
  Pallas kernels  151 us (37%)
  waiting for transfers between devices  123 us (30%)
  starting transfers between devices  69 us (17%)
  other arithmetic  27.9 us (7%)
  local copies, waits for them, and re-layouts  21.5 us (5%)
  between operations  14.6 us (4%)
    ppermute x31, waiting for transfers between devices, flip(): return lax.ppermute(value, both, pairs)  89 us
    ppermute x31, starting transfers between devices, flip(): return lax.ppermute(value, both, pairs)  68.9 us
    pallas_call x1, Pallas kernels, attend_backward(): pl.pallas_call(functools.partial(backward_kernel, steps), grid_spec=pltpu...  42.7 us
    pallas_call x1, Pallas kernels, token_block(): pl.pallas_call(functools.partial(token_kernel, tile, width, hidden), grid...  40.2 us
    pallas_call x2, Pallas kernels, attend_forward(): pl.pallas_call(functools.partial(forward_kernel, steps, count, project),...  36 us
    all_gather x1, waiting for transfers between devices, per_device(): rest = lax.all_gather(rest, 'tensor', axis=0)  22 us
    pallas_call x1, Pallas kernels, weight_block(): pl.pallas_call(functools.partial(weight_kernel, width, hidden), grid_spec...  20.4 us
    pallas_call x1, Pallas kernels, head_weight_block(): pl.pallas_call(head_weight_kernel, grid=(GROUP,), in_specs=[any_spec] * 4...  11.5 us
  transfers between devices with their start and end apart: 35, of which 20 were waited for; matrix products, arithmetic and copies ran while one was open for 9% of the time, Pallas kernels for 27%

profile of v7, /device:TPU:1, one launch (start us, length us, event | category | flops | bytes accessed | tf_op | source)
XLA Modules:
  0.0 406.4 jit_solution(15346423464646403405)
XLA Ops:
  7.3 5.7 %collective-permute-start.1 = (bf16[1024,768]{1,0:T(8,128)(2,1)}, bf16[1024,768]{1,0:T(8,128)(2,1)}, u32[]{:S(2)}, u32[]{:S(2)}) collective-permute-start(bf16[1024,768]{1,0:T(8,128)(2,1)} %param.18), channel_id=1, source_target_pairs={{2,4},{3,5},{4,2},{5,3},{10,12},{11,13},{12,10},{13,11},{18,20},{1... | collective-permute-start | bytes 4718600 | tf_op jit(solution)/shard_map/ppermute | solution.py:841
  13.0 1.9 collective-permute-start.2
  22.8 1.3 collective-permute-start.3
  24.9 14.2 %collective-permute-done.3 = bf16[195,576]{1,0:T(8,128)(2,1)S(1)} collective-permute-done((bf16[195,576]{1,0:T(8,128)(2,1)S(1)}, bf16[195,576]{1,0:T(8,128)(2,1)S(1)}, u32[]{:S(2)}, u32[]{:S(2)}) %collective-permute-start.3) | collective-permute-done | bytes 224672 | tf_op jit(solution)/shard_map/ppermute | solution.py:841
  39.1 14.6 %collective-permute-done.1 = bf16[1024,768]{1,0:T(8,128)(2,1)} collective-permute-done((bf16[1024,768]{1,0:T(8,128)(2,1)}, bf16[1024,768]{1,0:T(8,128)(2,1)}, u32[]{:S(2)}, u32[]{:S(2)}) %collective-permute-start.1) | collective-permute-done | bytes 1572896 | tf_op jit(solution)/shard_map/ppermute | solution.py:841
  53.8 1.6 broadcast_select_fusion.4.refs_0_.x_ref.x0
  55.3 2.4 collective-permute-start.4
  57.9 1.3 collective-permute-start.5
  59.2 4.0 collective-permute-done.5
  63.4 1.3 collective-permute-start.6
  65.0 7.6 %collective-permute-done.6 = bf16[384,576]{1,0:T(8,128)(2,1)S(1)} collective-permute-done((bf16[384,576]{1,0:T(8,128)(2,1)S(1)}, bf16[384,576]{1,0:T(8,128)(2,1)S(1)}, u32[]{:S(2)}, u32[]{:S(2)}) %collective-permute-start.6) | collective-permute-done | bytes 442400 | tf_op jit(solution)/shard_map/ppermute | solution.py:841
  73.1 1.2 pad_maximum_fusion.refs_4_.w_ref
  74.3 2.4 collective-permute-done.4
  76.7 1.6 broadcast_select_fusion.3.refs_1_.x1
  78.9 22.0 %all-gather.7.cloned.1.call-done = bf16[4,98,1728]{2,1,0:T(8,128)(2,1)} async-done(((bf16[1,98,1728]{2,1,0:T(8,128)(2,1)}), bf16[4,98,1728]{2,1,0:T(8,128)(2,1)}) %all-gather.7.cloned.1.call-update) | async-done | bytes 1354768 | tf_op jit(solution)/shard_map/all_gather | solution.py:876
  100.9 2.6 slice.215
  103.8 5.4 %collective-permute-start.12 = (bf16[1024,768]{1,0:T(8,128)(2,1)S(1)}, bf16[1024,768]{1,0:T(8,128)(2,1)S(1)}, u32[]{:S(2)}, u32[]{:S(2)}) collective-permute-start(bf16[1024,768]{1,0:T(8,128)(2,1)S(1)} %copy-done.4), channel_id=1, source_target_pairs={{2,4},{3,5},{4,2},{5,3},{10,12},{11,13},{12,10},{13,11},{18,20},{1... | collective-permute-start | bytes 4718600 | tf_op jit(solution)/shard_map/ppermute | solution.py:841
  114.7 27.1 %attend_forward.2 = (bf16[1024,192]{1,0:T(8,128)(2,1)}, bf16[1024,192]{1,0:T(8,128)(2,1)}, bf16[1024,192]{1,0:T(8,128)(2,1)}, bf16[64,3,64,512]{3,2,1,0:T(8,128)(2,1)}, bf16[4096,640]{1,0:T(8,128)(2,1)}) custom-call(s32[1536]{0:T(1024)} %xor.62.table, s32[4]{0:T(128)} %pad_add_fusion.1.place, bf16[1024,768]{1,0:T(8,128)(2,1)} %copy-done, ...), custom_call_target="tpu_custom_call" | custom-call | tf_op jit(solution)/shard_map/attend_forward/pallas_call | solution.py:172
  141.9 2.0 collective-permute-start.11
  144.6 8.8 %attend_forward.3 = (bf16[1024,192]{1,0:T(8,128)(2,1)}, bf16[64,3,64,512]{3,2,1,0:T(8,128)(2,1)}) custom-call(s32[1536]{0:T(1024)} %xor.62.table, s32[2]{0:T(128)} %pad_add_fusion.place, bf16[4096,640]{1,0:T(8,128)(2,1)} %get-tuple-element.101.refs_0_.qkv_hbm, bf16[64,3,64,512]{3,2,1,0:T(8,128)(2,1)} %get-tuple-element.102.refs_1_), custom_call_target="tpu_custom_call", output_to_operand_aliasing={{1}: (3, {})} | custom-call | tf_op jit(solution)/shard_map/attend_forward/pallas_call | solution.py:172
  153.5 1.3 broadcast_select_fusion.2.cot_ref
  154.8 2.1 collective-permute-done.11.o3
  156.9 10.5 %collective-permute-done.9.o1 = bf16[1024,192]{1,0:T(8,128)(2,1)} collective-permute-done((bf16[1024,192]{1,0:T(8,128)(2,1)}, bf16[1024,192]{1,0:T(8,128)(2,1)}, u32[]{:S(2)}, u32[]{:S(2)}) %collective-permute-start.9) | collective-permute-done | bytes 393248 | tf_op jit(solution)/shard_map/ppermute | solution.py:841
  167.4 4.4 %all-gather.5.cloned.1.call-done = bf16[4,768,1728]{2,1,0:T(8,128)(2,1)} async-done(((bf16[4,96,1728]{2,1,0:T(8,128)(2,1)}), bf16[4,768,1728]{2,1,0:T(8,128)(2,1)}) %all-gather.5.cloned.1.call-update) | async-done | bytes 10616848 | tf_op jit(solution)/shard_map/all_gather | solution.py:898
  171.7 40.2 %token_block.1 = (bf16[1024,768]{1,0:T(8,128)(2,1)}, bf16[1024,768]{1,0:T(8,128)(2,1)}, bf16[1024,3072]{1,0:T(8,128)(2,1)}, bf16[1024,3072]{1,0:T(8,128)(2,1)}, ...) custom-call(s32[1]{0:T(128)} %bitcast.rank_ref, ...), custom_call_target="tpu_custom_call" | custom-call | flops 46000001024 | bytes 40000000 | tf_op jit(solution)/shard_map/token_block/pallas_call | solution.py:638
  212.8 1.3 collective-permute-start.13
  216.2 20.4 %weight_block.1 = bf16[3072,1728]{1,0:T(8,128)(2,1)} custom-call(s32[1]{0:T(128)} %bitcast.rank_ref, bf16[1024,768]{1,0:T(8,128)(2,1)} %get-tuple-element.111.n1, bf16[1024,768]{1,0:T(8,128)(2,1)} %get-tuple-element.112.dfr, bf16[1024,768]{1,0:T(8,128)(2,1)} %get-tuple-element.113.dar, bf16[1024,3072]{1,0:T(8,128)(2,1)} %get-tuple-element.114.g, ...), custom_call_target="tpu_custom_call" | custom-call | flops 22000001024 | bytes 30000000 | tf_op jit(solution)/shard_map/weight_block/pallas_call | solution.py:731
  236.6 2.5 collective-permute-done.16.do3
  240.8 3.6 collective-permute-start.17
  244.4 42.7 %attend_backward.1 = (bf16[4096,640]{1,0:T(8,128)(2,1)}, f32[1024,768]{1,0:T(8,128)}, bf16[1024,768]{1,0:T(8,128)(2,1)}, bf16[1024,768]{1,0:T(8,128)(2,1)}, bf16[1024,768]{1,0:T(8,128)(2,1)}, /*index=5*/f32[8,640]{1,0:T(8,128)}) custom-call(s32[1536]{0:T(1024)} %xor.62.table, bf16[64,3,64,512]{3,2,1,0:T(8,128)(2,1)} %get-tuple-element.110.p_ref, ...), custom_call_target="tpu_custom_call" | custom-call | flops 40000000000 | bytes 25000000 | tf_op jit(solution)/shard_map/attend_backward/pallas_call | solution.py:358
  287.1 1.2 copy-done.7
  290.6 2.9 collective-permute-done.19
  294.1 3.4 add_convert_fusion.1
  300.9 1.8 convert_add_fusion
  303.4 11.5 %head_weight_block.1 = bf16[768,576]{1,0:T(8,128)(2,1)} custom-call(bf16[1024,768]{1,0:T(8,128)(2,1)} %copy-done, bf16[1024,768]{1,0:T(8,128)(2,1)} %copy-done.1, bf16[1024,768]{1,0:T(8,128)(2,1)} %collective-permute-done.7.refs_2_.x2, bf16[1024,768]{1,0:T(8,128)(2,1)} %collective-permute-done.8.refs_3_.x3, bf16[4096,640]{1,0:T(8,128)(2,1)} %get-tuple-element.143.grad_ref), custom_call_target="tpu_custom_call" | custom-call | flops 8000000000 | bytes 12000000 | tf_op jit(solution)/shard_map/head_weight_block/pallas_call | solution.py:424
  315.0 7.3 %reduce-scatter.3.cloned.1.call-done = bf16[4,96,1728]{2,1,0:T(8,128)(2,1)} async-done(((bf16[4,768,1728]{2,1,0:T(8,128)(2,1)}), bf16[4,96,1728]{2,1,0:T(8,128)(2,1)}) %reduce-scatter.3.cloned.1.call-update) | async-done | bytes 1327120 | tf_op jit(solution)/shard_map/reduce_scatter | solution.py:942
  322.3 2.0 constant_dynamic-slice_fusion.3
  327.0 1.5 collective-permute-start.27
  328.5 3.9 collective-permute-done.24
  332.4 5.2 %collective-permute-done.25 = bf16[192,576]{1,0:T(8,128)(2,1)} collective-permute-done((bf16[192,576]{1,0:T(8,128)(2,1)}, bf16[192,576]{1,0:T(8,128)(2,1)}, u32[]{:S(2)}, u32[]{:S(2)}) %collective-permute-start.25) | collective-permute-done | bytes 221216 | tf_op jit(solution)/shard_map/ppermute | solution.py:841
  338.7 1.5 add_convert_fusion.3
  340.2 3.1 add_convert_fusion
  343.3 4.0 collective-permute-start.29
  347.3 5.2 %collective-permute-start.28 = (bf16[1024,768]{1,0:T(8,128)(2,1)}, bf16[1024,768]{1,0:T(8,128)(2,1)S(1)}, u32[]{:S(2)}, u32[]{:S(2)}) collective-permute-start(bf16[1024,768]{1,0:T(8,128)(2,1)} %add_convert_fusion), channel_id=1, source_target_pairs={{2,4},{3,5},{4,2},{5,3},{10,12},{11,13},{12,10},{13,11},{18,20},{1... | collective-permute-start | bytes 4718600 | tf_op jit(solution)/shard_map/ppermute | solution.py:841
  353.3 1.3 broadcast_select_fusion.1
  356.0 22.6 %collective-permute-start.30 = (bf16[96,576]{1,0:T(8,128)(2,1)S(1)}, bf16[96,576]{1,0:T(8,128)(2,1)S(1)}, u32[]{:S(2)}, u32[]{:S(2)}) collective-permute-start(bf16[96,576]{1,0:T(8,128)(2,1)S(1)} %constant_dynamic-slice_fusion), channel_id=1, source_target_pairs={{0,4},{1,5},{2,6},{3,7},{4,0},{5,1},{6,2},{7,3},{8,12},{9,13},{10,... | collective-permute-start | bytes 331784 | tf_op jit(solution)/shard_map/ppermute | solution.py:841
  379.6 15.0 %collective-permute-done.28 = bf16[1024,768]{1,0:T(8,128)(2,1)S(1)} collective-permute-done((bf16[1024,768]{1,0:T(8,128)(2,1)}, bf16[1024,768]{1,0:T(8,128)(2,1)S(1)}, u32[]{:S(2)}, u32[]{:S(2)}) %collective-permute-start.28) | collective-permute-done | bytes 1572896 | tf_op jit(solution)/shard_map/ppermute | solution.py:841
  395.6 1.3 broadcast_select_fusion
  (177 shorter events, 39.1 us)
Async XLA Ops:
  7.2 46.6 %copy-start.3 = (bf16[1024,768]{1,0:T(8,128)(2,1)S(1)}, bf16[1024,768]{1,0:T(8,128)(2,1)}, u32[]{:S(2)}) copy-start(bf16[1024,768]{1,0:T(8,128)(2,1)} %param.18) | copy-start | bytes 4718596
  7.2 16.9 %copy-start.9 = (bf16[768,96]{0,1:T(8,128)(2,1)S(1)}, bf16[768,96]{0,1:T(8,128)(2,1)}, u32[]{:S(2)}) copy-start(bf16[768,96]{0,1:T(8,128)(2,1)} %param.25) | copy-start | bytes 442372
  7.2 16.9 %copy-start.10 = (bf16[96,768]{1,0:T(8,128)(2,1)S(1)}, bf16[96,768]{1,0:T(8,128)(2,1)}, u32[]{:S(2)}) copy-start(bf16[96,768]{1,0:T(8,128)(2,1)} %param.24) | copy-start | bytes 442372
  7.2 93.7 %all-gather.7.cloned.1.call-start = ((), (), s32[]{:S(2)}) async-start(), calls=%async_computation.5 | async-start | bytes 1863680 | tf_op jit(solution)/shard_map/all_gather | solution.py:876
  7.3 46.5 %collective-permute-start.1 = (bf16[1024,768]{1,0:T(8,128)(2,1)}, bf16[1024,768]{1,0:T(8,128)(2,1)}, u32[]{:S(2)}, u32[]{:S(2)}) collective-permute-start(bf16[1024,768]{1,0:T(8,128)(2,1)} %param.18), channel_id=1, source_target_pairs={{2,4},{3,5},{4,2},{5,3},{10,12},{11,13},{12,10},{13,11},{18,20},{1... | collective-permute-start | bytes 4718600 | tf_op jit(solution)/shard_map/ppermute | solution.py:841
  13.0 40.7 %collective-permute-start.2 = (bf16[1024,768]{1,0:T(8,128)(2,1)}, bf16[1024,768]{1,0:T(8,128)(2,1)}, u32[]{:S(2)}, u32[]{:S(2)}) collective-permute-start(bf16[1024,768]{1,0:T(8,128)(2,1)} %param.18), channel_id=1, source_target_pairs={{0,1},{1,0},{6,7},{7,6},{8,9},{9,8},{14,15},{15,14},{16,17},{17,16... | collective-permute-start | bytes 4718600 | tf_op jit(solution)/shard_map/ppermute | solution.py:841
  19.0 3.7 collective-permute-start
  22.8 16.3 %collective-permute-start.3 = (bf16[195,576]{1,0:T(8,128)(2,1)S(1)}, bf16[195,576]{1,0:T(8,128)(2,1)S(1)}, u32[]{:S(2)}, u32[]{:S(2)}) collective-permute-start(bf16[195,576]{1,0:T(8,128)(2,1)S(1)} %pad_maximum_fusion.2), channel_id=1, source_target_pairs={{0,2},{1,3},{6,4},{7,5},{8,10},{9,11},{14,12},{15,13},{16,18},{17,... | collective-permute-start | bytes 673928 | tf_op jit(solution)/shard_map/ppermute | solution.py:841
  55.3 22.9 %copy-start = (bf16[1024,768]{1,0:T(8,128)(2,1)}, bf16[1024,768]{1,0:T(8,128)(2,1)S(1)}, u32[]{:S(2)}) copy-start(bf16[1024,768]{1,0:T(8,128)(2,1)S(1)} %broadcast_select_fusion.4.refs_0_.x_ref.x0) | copy-start | bytes 4718596
  55.3 21.3 %collective-permute-start.4 = (bf16[1024,768]{1,0:T(8,128)(2,1)S(1)}, bf16[1024,768]{1,0:T(8,128)(2,1)}, u32[]{:S(2)}, u32[]{:S(2)}) collective-permute-start(bf16[1024,768]{1,0:T(8,128)(2,1)S(1)} %broadcast_select_fusion.4.refs_0_.x_ref.x0), channel_id=1, source_target_pairs={{2,3},{3,2},{4,5},{5,4},{10,11},{11,10},{12,13},{13,12},{18,19},{1... | collective-permute-start | bytes 4718600 | tf_op jit(solution)/shard_map/ppermute | solution.py:841
  57.9 5.4 %collective-permute-start.5 = (bf16[192,576]{1,0:T(8,128)(2,1)S(1)}, bf16[192,576]{1,0:T(8,128)(2,1)S(1)}, u32[]{:S(2)}, u32[]{:S(2)}) collective-permute-start(bf16[192,576]{1,0:T(8,128)(2,1)S(1)} %slice.244), channel_id=1, source_target_pairs={{0,8},{1,9},{2,10},{3,11},{4,12},{5,13},{6,14},{7,15},{8,0},{9,1},... | collective-permute-start | bytes 663560 | tf_op jit(solution)/shard_map/ppermute | solution.py:841
  63.4 9.2 %collective-permute-start.6 = (bf16[384,576]{1,0:T(8,128)(2,1)S(1)}, bf16[384,576]{1,0:T(8,128)(2,1)S(1)}, u32[]{:S(2)}, u32[]{:S(2)}) collective-permute-start(bf16[384,576]{1,0:T(8,128)(2,1)S(1)} %maximum_select_fusion.1), channel_id=1, source_target_pairs={{0,16},{1,17},{2,18},{3,19},{4,20},{5,21},{6,22},{7,23},{8,24},{9,... | collective-permute-start | bytes 1327112 | tf_op jit(solution)/shard_map/ppermute | solution.py:841
  64.8 107.0 %all-gather.5.cloned.1.call-start = ((), (), s32[]{:S(2)}) async-start(), calls=%async_computation.2 | async-start | bytes 12386304 | tf_op jit(solution)/shard_map/all_gather | solution.py:898
  78.2 25.3 %copy-start.1 = (bf16[1024,768]{1,0:T(8,128)(2,1)}, bf16[1024,768]{1,0:T(8,128)(2,1)S(1)}, u32[]{:S(2)}) copy-start(bf16[1024,768]{1,0:T(8,128)(2,1)S(1)} %broadcast_select_fusion.3.refs_1_.x1) | copy-start | bytes 4718596
  78.3 25.4 %copy-start.11 = (f32[768]{0:T(1024)S(1)}, f32[768]{0:T(1024)}, u32[]{:S(2)}) copy-start(f32[768]{0:T(1024)} %param.28) | copy-start | bytes 9220
  78.3 25.4 %copy-start.12 = (f32[768]{0:T(1024)S(1)}, f32[768]{0:T(1024)}, u32[]{:S(2)}) copy-start(f32[768]{0:T(1024)} %param.29) | copy-start | bytes 9220
  78.3 25.4 %copy-start.13 = (f32[768]{0:T(1024)S(1)}, f32[768]{0:T(1024)}, u32[]{:S(2)}) copy-start(f32[768]{0:T(1024)} %param.30) | copy-start | bytes 9220
  78.3 25.4 %copy-start.14 = (f32[768]{0:T(1024)S(1)}, f32[768]{0:T(1024)}, u32[]{:S(2)}) copy-start(f32[768]{0:T(1024)} %param.32) | copy-start | bytes 9220
  78.3 25.4 %copy-start.15 = (f32[768]{0:T(1024)S(1)}, f32[768]{0:T(1024)}, u32[]{:S(2)}) copy-start(f32[768]{0:T(1024)} %param.33) | copy-start | bytes 9220
  78.3 25.4 %copy-start.16 = (f32[768]{0:T(1024)S(1)}, f32[768]{0:T(1024)}, u32[]{:S(2)}) copy-start(f32[768]{0:T(1024)} %param.34) | copy-start | bytes 9220
  78.3 22.6 %collective-permute-start.7 = (bf16[1024,768]{1,0:T(8,128)(2,1)S(1)}, bf16[1024,768]{1,0:T(8,128)(2,1)}, u32[]{:S(2)}, u32[]{:S(2)}) collective-permute-start(bf16[1024,768]{1,0:T(8,128)(2,1)S(1)} %broadcast_select_fusion.4.refs_0_.x_ref.x0), channel_id=1, source_target_pairs={{0,4},{1,5},{2,6},{3,7},{4,0},{5,1},{6,2},{7,3},{8,12},{9,13},{10,... | collective-permute-start | bytes 4718600 | tf_op jit(solution)/shard_map/ppermute | solution.py:841
  78.4 22.5 %collective-permute-start.8 = (bf16[1024,768]{1,0:T(8,128)(2,1)S(1)}, bf16[1024,768]{1,0:T(8,128)(2,1)}, u32[]{:S(2)}, u32[]{:S(2)}) collective-permute-start(bf16[1024,768]{1,0:T(8,128)(2,1)S(1)} %broadcast_select_fusion.3.refs_1_.x1), channel_id=1, source_target_pairs={{0,4},{1,5},{2,6},{3,7},{4,0},{5,1},{6,2},{7,3},{8,12},{9,13},{10,... | collective-permute-start | bytes 4718600 | tf_op jit(solution)/shard_map/ppermute | solution.py:841
  103.6 218.7 %reduce-scatter.3.cloned.1.call-start = ((), (), s32[]{:S(2)}) async-start(), calls=%async_computation.3 | async-start | bytes 12386304 | tf_op jit(solution)/shard_map/reduce_scatter | solution.py:942
  103.8 49.7 %collective-permute-start.12 = (bf16[1024,768]{1,0:T(8,128)(2,1)S(1)}, bf16[1024,768]{1,0:T(8,128)(2,1)S(1)}, u32[]{:S(2)}, u32[]{:S(2)}) collective-permute-start(bf16[1024,768]{1,0:T(8,128)(2,1)S(1)} %copy-done.4), channel_id=1, source_target_pairs={{2,4},{3,5},{4,2},{5,3},{10,12},{11,13},{12,10},{13,11},{18,20},{1... | collective-permute-start | bytes 4718600 | tf_op jit(solution)/shard_map/ppermute | solution.py:841
  141.8 13.0 %collective-permute-start.10 = (bf16[1024,192]{1,0:T(8,128)(2,1)}, bf16[1024,192]{1,0:T(8,128)(2,1)}, u32[]{:S(2)}, u32[]{:S(2)}) collective-permute-start(bf16[1024,192]{1,0:T(8,128)(2,1)} %get-tuple-element.105.o2), channel_id=1, source_target_pairs={{0,4},{1,5},{2,6},{3,7},{4,0},{5,1},{6,2},{7,3},{8,12},{9,13},{10,... | collective-permute-start | bytes 1179656 | tf_op jit(solution)/shard_map/ppermute | solution.py:841
  141.9 15.0 %collective-permute-start.11 = (bf16[1024,192]{1,0:T(8,128)(2,1)}, bf16[1024,192]{1,0:T(8,128)(2,1)}, u32[]{:S(2)}, u32[]{:S(2)}) collective-permute-start(bf16[1024,192]{1,0:T(8,128)(2,1)} %get-tuple-element.106.o3), channel_id=1, source_target_pairs={{0,5},{1,4},{2,7},{3,6},{4,1},{5,0},{6,3},{7,2},{8,13},{9,12},{10,... | collective-permute-start | bytes 1179656 | tf_op jit(solution)/shard_map/ppermute | solution.py:841
  143.9 23.5 %collective-permute-start.9 = (bf16[1024,192]{1,0:T(8,128)(2,1)}, bf16[1024,192]{1,0:T(8,128)(2,1)}, u32[]{:S(2)}, u32[]{:S(2)}) collective-permute-start(bf16[1024,192]{1,0:T(8,128)(2,1)} %get-tuple-element.104.o1), channel_id=1, source_target_pairs={{0,1},{1,0},{2,3},{3,2},{4,5},{5,4},{6,7},{7,6},{8,9},{9,8},{10,11... | collective-permute-start | bytes 1179656 | tf_op jit(solution)/shard_map/ppermute | solution.py:841
  212.8 23.8 %collective-permute-start.13 = (f32[7680]{0:T(1024)S(1)}, f32[7680]{0:T(1024)S(1)}, u32[]{:S(2)}, u32[]{:S(2)}) collective-permute-start(f32[7680]{0:T(1024)S(1)} %reduce.1), channel_id=1, source_target_pairs={{0,1},{1,0},{2,3},{3,2},{4,5},{5,4},{6,7},{7,6},{8,9},{9,8},{10,11... | collective-permute-start | bytes 92168 | tf_op jit(solution)/shard_map/ppermute | solution.py:841
  214.1 22.5 %collective-permute-start.14 = (bf16[1024,192]{1,0:T(8,128)(2,1)}, bf16[1024,192]{1,0:T(8,128)(2,1)S(1)}, u32[]{:S(2)}, u32[]{:S(2)}) collective-permute-start(bf16[1024,192]{1,0:T(8,128)(2,1)} %get-tuple-element.118), channel_id=1, source_target_pairs={{0,1},{1,0},{2,3},{3,2},{4,5},{5,4},{6,7},{7,6},{8,9},{9,8},{10,11... | collective-permute-start | bytes 1179656 | tf_op jit(solution)/shard_map/ppermute | solution.py:841
  214.3 22.3 %collective-permute-start.15 = (bf16[1024,192]{1,0:T(8,128)(2,1)}, bf16[1024,192]{1,0:T(8,128)(2,1)S(1)}, u32[]{:S(2)}, u32[]{:S(2)}) collective-permute-start(bf16[1024,192]{1,0:T(8,128)(2,1)} %get-tuple-element.119), channel_id=1, source_target_pairs={{0,4},{1,5},{2,6},{3,7},{4,0},{5,1},{6,2},{7,3},{8,12},{9,13},{10,... | collective-permute-start | bytes 1179656 | tf_op jit(solution)/shard_map/ppermute | solution.py:841
  215.1 24.0 %collective-permute-start.16 = (bf16[1024,192]{1,0:T(8,128)(2,1)}, bf16[1024,192]{1,0:T(8,128)(2,1)S(1)}, u32[]{:S(2)}, u32[]{:S(2)}) collective-permute-start(bf16[1024,192]{1,0:T(8,128)(2,1)} %get-tuple-element.120), channel_id=1, source_target_pairs={{0,5},{1,4},{2,7},{3,6},{4,1},{5,0},{6,3},{7,2},{8,13},{9,12},{10,... | collective-permute-start | bytes 1179656 | tf_op jit(solution)/shard_map/ppermute | solution.py:841
  240.0 138.6 %reduce-scatter.5.cloned.1.call-start = ((), (), s32[]{:S(2)}) async-start(), calls=%async_computation.4 | async-start | bytes 1720320 | tf_op jit(solution)/shard_map/reduce_scatter | solution.py:969
  240.8 46.3 %collective-permute-start.17 = (bf16[1024,768]{1,0:T(8,128)(2,1)S(1)}, bf16[1024,768]{1,0:T(8,128)(2,1)S(1)}, u32[]{:S(2)}, u32[]{:S(2)}) collective-permute-start(bf16[1024,768]{1,0:T(8,128)(2,1)S(1)} %copy-done.5), channel_id=1, source_target_pairs={{2,4},{3,5},{4,2},{5,3},{10,12},{11,13},{12,10},{13,11},{18,20},{1... | collective-permute-start | bytes 4718600 | tf_op jit(solution)/shard_map/ppermute | solution.py:841
  288.3 5.8 %collective-permute-start.18 = (bf16[1024,768]{1,0:T(8,128)(2,1)}, bf16[1024,768]{1,0:T(8,128)(2,1)S(1)}, u32[]{:S(2)}, u32[]{:S(2)}) collective-permute-start(bf16[1024,768]{1,0:T(8,128)(2,1)} %get-tuple-element.133), channel_id=1, source_target_pairs={{0,4},{1,5},{2,6},{3,7},{4,0},{5,1},{6,2},{7,3},{8,12},{9,13},{10,... | collective-permute-start | bytes 4718600 | tf_op jit(solution)/shard_map/ppermute | solution.py:841
  288.3 12.6 %collective-permute-start.21 = (bf16[1024,768]{1,0:T(8,128)(2,1)}, bf16[1024,768]{1,0:T(8,128)(2,1)}, u32[]{:S(2)}, u32[]{:S(2)}) collective-permute-start(bf16[1024,768]{1,0:T(8,128)(2,1)} %get-tuple-element.139), channel_id=1, source_target_pairs={{0,4},{1,5},{2,6},{3,7},{4,0},{5,1},{6,2},{7,3},{8,12},{9,13},{10,... | collective-permute-start | bytes 4718600 | tf_op jit(solution)/shard_map/ppermute | solution.py:841
  289.7 3.7 collective-permute-start.19
  297.5 2.8 collective-permute-start.22
  298.5 41.7 %collective-permute-start.20 = (bf16[1024,768]{1,0:T(8,128)(2,1)}, bf16[1024,768]{1,0:T(8,128)(2,1)}, u32[]{:S(2)}, u32[]{:S(2)}) collective-permute-start(bf16[1024,768]{1,0:T(8,128)(2,1)} %add_convert_fusion.1), channel_id=1, source_target_pairs={{0,1},{1,0},{2,3},{3,2},{4,5},{5,4},{6,7},{7,6},{8,9},{9,8},{10,11... | collective-permute-start | bytes 4718600 | tf_op jit(solution)/shard_map/ppermute | solution.py:841
  300.3 3.2 collective-permute-start.23
  324.4 8.1 %collective-permute-start.24 = (bf16[192,576]{1,0:T(8,128)(2,1)}, bf16[192,576]{1,0:T(8,128)(2,1)}, u32[]{:S(2)}, u32[]{:S(2)}) collective-permute-start(bf16[192,576]{1,0:T(8,128)(2,1)} %get-tuple-element.212), channel_id=1, source_target_pairs={{0,24},{1,25},{2,26},{3,27},{4,28},{5,29},{6,30},{7,31},{8,16},{9,... | collective-permute-start | bytes 663560 | tf_op jit(solution)/shard_map/ppermute | solution.py:841
  325.5 12.0 %collective-permute-start.25 = (bf16[192,576]{1,0:T(8,128)(2,1)}, bf16[192,576]{1,0:T(8,128)(2,1)}, u32[]{:S(2)}, u32[]{:S(2)}) collective-permute-start(bf16[192,576]{1,0:T(8,128)(2,1)} %get-tuple-element.214), channel_id=1, source_target_pairs={{0,8},{1,9},{2,10},{3,11},{4,12},{5,13},{6,14},{7,15},{8,0},{9,1},... | collective-permute-start | bytes 663560 | tf_op jit(solution)/shard_map/ppermute | solution.py:841
  326.6 12.1 %collective-permute-start.26 = (bf16[192,576]{1,0:T(8,128)(2,1)S(1)}, bf16[192,576]{1,0:T(8,128)(2,1)}, u32[]{:S(2)}, u32[]{:S(2)}) collective-permute-start(bf16[192,576]{1,0:T(8,128)(2,1)S(1)} %get-tuple-element.213), channel_id=1, source_target_pairs={{0,16},{1,17},{2,18},{3,19},{4,20},{5,21},{6,22},{7,23},{8,24},{9,... | collective-permute-start | bytes 663560 | tf_op jit(solution)/shard_map/ppermute | solution.py:841
  327.0 13.2 %collective-permute-start.27 = (f32[8064]{0:T(1024)S(1)}, f32[8064]{0:T(1024)S(1)}, u32[]{:S(2)}, u32[]{:S(2)}) collective-permute-start(f32[8064]{0:T(1024)S(1)} %add.160), channel_id=1, source_target_pairs={{0,4},{1,5},{2,6},{3,7},{4,0},{5,1},{6,2},{7,3},{8,12},{9,13},{10,... | collective-permute-start | bytes 96776 | tf_op jit(solution)/shard_map/ppermute | solution.py:841
  340.2 13.1 %copy-start.6 = (bf16[1024,768]{1,0:T(8,128)(2,1)S(1)}, bf16[1024,768]{1,0:T(8,128)(2,1)}, u32[]{:S(2)}) copy-start(bf16[1024,768]{1,0:T(8,128)(2,1)} %get-tuple-element.109) | copy-start | bytes 4718596
  340.2 13.1 %copy-start.8 = (bf16[1024,768]{1,0:T(8,128)(2,1)S(1)}, bf16[1024,768]{1,0:T(8,128)(2,1)}, u32[]{:S(2)}) copy-start(bf16[1024,768]{1,0:T(8,128)(2,1)} %copy-done.7) | copy-start | bytes 4718596
  343.3 12.6 %collective-permute-start.29 = (bf16[192,576]{1,0:T(8,128)(2,1)S(1)}, bf16[192,576]{1,0:T(8,128)(2,1)S(1)}, u32[]{:S(2)}, u32[]{:S(2)}) collective-permute-start(bf16[192,576]{1,0:T(8,128)(2,1)S(1)} %add_convert_fusion.3), channel_id=1, source_target_pairs={{2,0},{3,1},{4,6},{5,7},{10,8},{11,9},{12,14},{13,15},{18,16},{19,... | collective-permute-start | bytes 663560 | tf_op jit(solution)/shard_map/ppermute | solution.py:841
  347.3 47.3 %collective-permute-start.28 = (bf16[1024,768]{1,0:T(8,128)(2,1)}, bf16[1024,768]{1,0:T(8,128)(2,1)S(1)}, u32[]{:S(2)}, u32[]{:S(2)}) collective-permute-start(bf16[1024,768]{1,0:T(8,128)(2,1)} %add_convert_fusion), channel_id=1, source_target_pairs={{2,4},{3,5},{4,2},{5,3},{10,12},{11,13},{12,10},{13,11},{18,20},{1... | collective-permute-start | bytes 4718600 | tf_op jit(solution)/shard_map/ppermute | solution.py:841
  356.0 23.6 %collective-permute-start.30 = (bf16[96,576]{1,0:T(8,128)(2,1)S(1)}, bf16[96,576]{1,0:T(8,128)(2,1)S(1)}, u32[]{:S(2)}, u32[]{:S(2)}) collective-permute-start(bf16[96,576]{1,0:T(8,128)(2,1)S(1)} %constant_dynamic-slice_fusion), channel_id=1, source_target_pairs={{0,4},{1,5},{2,6},{3,7},{4,0},{5,1},{6,2},{7,3},{8,12},{9,13},{10,... | collective-permute-start | bytes 331784 | tf_op jit(solution)/shard_map/ppermute | solution.py:841
  (7 other events, 19.0 us)
Sparse Core Ops, SparseCore 0:
  64.9 35.9 all-gather.6
  103.7 67.9 all-gather.4
  239.3 82.9 reduce-scatter.2
  324.4 36.5 reduce-scatter.4

commit v8 on v7

--- a/solution.py
+++ b/solution.py
@@ -853,9 +853,6 @@
         return flip(value, 1, 0)
 
     rest = jnp.concatenate([w_up, w_down.T, w_output.T], axis=1)
-    below = jnp.concatenate(split_three(b_up))
-    below = jnp.pad(below, (0, -below.shape[0] % rest.shape[1])).reshape(-1, rest.shape[1])
-    rest = jnp.concatenate([rest, below], axis=0)
 
     packed = pack_columns(w_query, w_key, w_value, 1)
     columns = packed.shape[1]
@@ -872,7 +869,8 @@
     )
     own = jnp.where(here, inputs, moved)
     near_move = flip(own, 0, 1, moves)
-    own, packed_got = lax.optimization_barrier((own, packed_got))
+    own, packed_got, b_up = lax.optimization_barrier((own, packed_got, b_up))
+    up_bias = jnp.stack([b_up] + [flip(b_up, 0, n) for n in (1, 2, 3)])
     rest = lax.all_gather(rest, "tensor", axis=0)
     packed = jnp.where(here, packed, packed_got)
     small = packed[2 * w_query.shape[0] :].reshape(-1)
@@ -888,21 +886,6 @@
     b_qkv = insert_zero(pack_columns(mine[:192], b_key, mine[192:], 0), 0)
     scale = jnp.concatenate([jnp.ones((KV,), jnp.float32), jnp.full((256,), 0.125, jnp.float32)])
     near = jnp.where(here, near_stay, near_move)
-    near, own, cotangent, w_qkv, b_qkv = lax.optimization_barrier(
-        (near, own, cotangent, w_qkv, b_qkv)
-    )
-    side, far = side_of(own), side_of(near)
-    cot_moved = flip(cotangent, 1, 2, moves)
-    side, far, rest = lax.optimization_barrier((side, far, rest))
-    below = rest[:, w_up.shape[0] :].reshape(GROUP, -1)
-    rest_all = lax.all_gather(
-        rest[:, : w_up.shape[0]], "dp", axis=1, tiled=True
-    ).reshape(GROUP * width, -1)
-    b_up_all = sum(
-        below[:, n * hidden : (n + 1) * hidden].astype(jnp.float32) for n in range(3)
-    ).reshape(1, -1)
-    rows = (own, near, side, far)
-    grad_top = jnp.where(here, cotangent, cot_moved)
     block = jnp.arange(NB, dtype=jnp.int32)
     block = block ^ (rank * QB)
     fixed = jnp.clip(
@@ -925,6 +908,18 @@
     )
     table = (table ^ (rank * QB)).reshape(-1)
 
+    b_up_all = jnp.concatenate(
+        [lax.dynamic_index_in_dim(up_bias, tensor_index ^ n, 0) for n in range(GROUP)], axis=1
+    )
+    near, own, cotangent, w_qkv, b_qkv, table, b_up_all = lax.optimization_barrier(
+        (near, own, cotangent, w_qkv, b_qkv, table, b_up_all)
+    )
+    side, far = side_of(own), side_of(near)
+    cot_moved = flip(cotangent, 1, 2, moves)
+    side, far, rest = lax.optimization_barrier((side, far, rest))
+    rest_all = lax.all_gather(rest, "dp", axis=1, tiled=True).reshape(GROUP * width, -1)
+    rows = (own, near, side, far)
+    grad_top = jnp.where(here, cotangent, cot_moved)
     weights = (w_qkv, b_qkv[None], scale[None])
     out_near, out_far, out_side, probs, qkv = attend_forward((1, 3, 2), rank, table, rows, weights)
     out_own, probs = attend_forward((0,), rank, table, qkv=qkv, probs=probs)

time: 408 us -> 417 us (1.022)
  starting transfers between devices: 69 us -> 79.4 us
    all_gather x1, waiting for transfers between devices: 22 us -> 4.83 us  [per_device(): rest = lax.all_gather(rest, 'tensor', axis=0)]
    ppermute x31 -> x34, waiting for transfers between devices: 89 us -> 102 us  [flip(): return lax.ppermute(value, both, pairs)]
    ppermute x31 -> x34, starting transfers between devices: 68.9 us -> 79.3 us  [flip(): return lax.ppermute(value, both, pairs)]
  transfers between devices with their start and end apart: 35 -> 38, of which waited for: 20 -> 21; matrix products, arithmetic and copies ran while one was open for 9% -> 9% of each run, Pallas kernels for 27% -> 27%
where the time goes in v8:
time: 417 us; the launch traced here: 416 us
  Pallas kernels  152 us (36%)
  waiting for transfers between devices  120 us (29%)
  starting transfers between devices  79.4 us (19%)
  other arithmetic  31.4 us (8%)
  local copies, waits for them, and re-layouts  18.2 us (4%)
  between operations  14.7 us (4%)
    ppermute x34, waiting for transfers between devices, flip(): return lax.ppermute(value, both, pairs)  102 us
    ppermute x34, starting transfers between devices, flip(): return lax.ppermute(value, both, pairs)  79.3 us
    pallas_call x1, Pallas kernels, attend_backward(): pl.pallas_call(functools.partial(backward_kernel, steps), grid_spec=pltpu...  42.6 us
    pallas_call x1, Pallas kernels, token_block(): pl.pallas_call(functools.partial(token_kernel, tile, width, hidden), grid...  40.2 us
    pallas_call x2, Pallas kernels, attend_forward(): pl.pallas_call(functools.partial(forward_kernel, steps, count, project),...  36.8 us
    pallas_call x1, Pallas kernels, weight_block(): pl.pallas_call(functools.partial(weight_kernel, width, hidden), grid_spec...  20.5 us
    pallas_call x1, Pallas kernels, head_weight_block(): pl.pallas_call(head_weight_kernel, grid=(GROUP,), in_specs=[any_spec] * 4...  11.5 us
  transfers between devices with their start and end apart: 38, of which 21 were waited for; matrix products, arithmetic and copies ran while one was open for 9% of the time, Pallas kernels for 27%

profile of v8, /device:TPU:1, one launch (start us, length us, event | category | flops | bytes accessed | tf_op | source)
XLA Modules:
  0.0 415.6 jit_solution(10996258250584169579)
XLA Ops:
  7.2 5.7 %collective-permute-start = (bf16[1024,768]{1,0:T(8,128)(2,1)}, bf16[1024,768]{1,0:T(8,128)(2,1)S(1)}, u32[]{:S(2)}, u32[]{:S(2)}) collective-permute-start(bf16[1024,768]{1,0:T(8,128)(2,1)} %param.18), channel_id=1, source_target_pairs={{2,4},{3,5},{4,2},{5,3},{10,12},{11,13},{12,10},{13,11},{18,20},{1... | collective-permute-start | bytes 4718600 | tf_op jit(solution)/shard_map/ppermute | solution.py:841
  13.0 1.9 collective-permute-start.1
  22.0 1.8 pad_maximum_fusion.1
  25.6 1.3 collective-permute-start.3
  26.9 15.2 %collective-permute-done.3 = bf16[195,576]{1,0:T(8,128)(2,1)} collective-permute-done((bf16[195,576]{1,0:T(8,128)(2,1)}, bf16[195,576]{1,0:T(8,128)(2,1)}, u32[]{:S(2)}, u32[]{:S(2)}) %collective-permute-start.3) | collective-permute-done | bytes 224672 | tf_op jit(solution)/shard_map/ppermute | solution.py:841
  42.2 11.5 %collective-permute-done = bf16[1024,768]{1,0:T(8,128)(2,1)S(1)} collective-permute-done((bf16[1024,768]{1,0:T(8,128)(2,1)}, bf16[1024,768]{1,0:T(8,128)(2,1)S(1)}, u32[]{:S(2)}, u32[]{:S(2)}) %collective-permute-start) | collective-permute-done | bytes 1572896 | tf_op jit(solution)/shard_map/ppermute | solution.py:841
  54.8 1.6 broadcast_select_fusion.4.refs_0_.x_ref.x0
  57.0 3.0 collective-permute-start.9
  61.1 1.9 collective-permute-start.4
  66.7 4.1 collective-permute-done.5
  70.9 1.3 collective-permute-start.6
  72.9 10.3 %collective-permute-done.6 = bf16[384,576]{1,0:T(8,128)(2,1)S(1)} collective-permute-done((bf16[384,576]{1,0:T(8,128)(2,1)S(1)}, bf16[384,576]{1,0:T(8,128)(2,1)S(1)}, u32[]{:S(2)}, u32[]{:S(2)}) %collective-permute-start.6) | collective-permute-done | bytes 442400 | tf_op jit(solution)/shard_map/ppermute | solution.py:841
  83.6 1.2 pad_maximum_fusion.refs_4_.w_ref
  84.8 13.3 %collective-permute-done.4 = bf16[1024,768]{1,0:T(8,128)(2,1)} collective-permute-done((bf16[1024,768]{1,0:T(8,128)(2,1)S(1)}, bf16[1024,768]{1,0:T(8,128)(2,1)}, u32[]{:S(2)}, u32[]{:S(2)}) %collective-permute-start.4) | collective-permute-done | bytes 1572896 | tf_op jit(solution)/shard_map/ppermute | solution.py:841
  98.0 1.6 broadcast_select_fusion.3.refs_1_.x1
  100.2 4.8 %all-gather.6.cloned.1.call-done = bf16[384,1728]{1,0:T(8,128)(2,1)} async-done(((bf16[96,1728]{1,0:T(8,128)(2,1)}), bf16[384,1728]{1,0:T(8,128)(2,1)}) %all-gather.6.cloned.1.call-update) | async-done | bytes 1327120 | tf_op jit(solution)/shard_map/all_gather | solution.py:874
  105.6 12.0 %collective-permute-start.15 = (bf16[1024,768]{1,0:T(8,128)(2,1)}, bf16[1024,768]{1,0:T(8,128)(2,1)S(1)}, u32[]{:S(2)}, u32[]{:S(2)}) collective-permute-start(bf16[1024,768]{1,0:T(8,128)(2,1)} %param.19), channel_id=1, source_target_pairs={{2,4},{3,5},{4,2},{5,3},{10,12},{11,13},{12,10},{13,11},{18,20},{1... | collective-permute-start | bytes 4718600 | tf_op jit(solution)/shard_map/ppermute | solution.py:841
  118.8 27.8 %attend_forward.2 = (bf16[1024,192]{1,0:T(8,128)(2,1)}, bf16[1024,192]{1,0:T(8,128)(2,1)}, bf16[1024,192]{1,0:T(8,128)(2,1)}, bf16[64,3,64,512]{3,2,1,0:T(8,128)(2,1)}, bf16[4096,640]{1,0:T(8,128)(2,1)}) custom-call(s32[1536]{0:T(1024)} %xor.71.table, s32[4]{0:T(128)} %pad_add_fusion.1.place, bf16[1024,768]{1,0:T(8,128)(2,1)} %copy-done, ...), custom_call_target="tpu_custom_call" | custom-call | tf_op jit(solution)/shard_map/attend_forward/pallas_call | solution.py:172
  146.7 2.3 collective-permute-start.12
  150.8 9.0 %attend_forward.3 = (bf16[1024,192]{1,0:T(8,128)(2,1)}, bf16[64,3,64,512]{3,2,1,0:T(8,128)(2,1)}) custom-call(s32[1536]{0:T(1024)} %xor.71.table, s32[2]{0:T(128)} %pad_add_fusion.place, bf16[4096,640]{1,0:T(8,128)(2,1)} %get-tuple-element.106.refs_0_.qkv_hbm, bf16[64,3,64,512]{3,2,1,0:T(8,128)(2,1)} %get-tuple-element.107.refs_1_), custom_call_target="tpu_custom_call", output_to_operand_aliasing={{1}: (3, {})} | custom-call | tf_op jit(solution)/shard_map/attend_forward/pallas_call | solution.py:172
  159.8 1.3 broadcast_select_fusion.2.cot_ref
  161.1 3.2 collective-permute-done.12.o1
  164.3 11.0 %collective-permute-done.14.o3 = bf16[1024,192]{1,0:T(8,128)(2,1)} collective-permute-done((bf16[1024,192]{1,0:T(8,128)(2,1)}, bf16[1024,192]{1,0:T(8,128)(2,1)}, u32[]{:S(2)}, u32[]{:S(2)}) %collective-permute-start.14) | collective-permute-done | bytes 393248 | tf_op jit(solution)/shard_map/ppermute | solution.py:841
  175.4 5.6 %all-gather.4.cloned.1.call-done = bf16[4,768,1728]{2,1,0:T(8,128)(2,1)} async-done(((bf16[4,96,1728]{2,1,0:T(8,128)(2,1)}), bf16[4,768,1728]{2,1,0:T(8,128)(2,1)}) %all-gather.4.cloned.1.call-update) | async-done | bytes 10616848 | tf_op jit(solution)/shard_map/all_gather | solution.py:920
  180.9 40.2 %token_block.1 = (bf16[1024,768]{1,0:T(8,128)(2,1)}, bf16[1024,768]{1,0:T(8,128)(2,1)}, bf16[1024,3072]{1,0:T(8,128)(2,1)}, bf16[1024,3072]{1,0:T(8,128)(2,1)}, ...) custom-call(s32[1]{0:T(128)} %bitcast.rank_ref, ...), custom_call_target="tpu_custom_call" | custom-call | flops 46000001024 | bytes 40000000 | tf_op jit(solution)/shard_map/token_block/pallas_call | solution.py:638
  222.0 1.3 collective-permute-start.16
  225.5 20.5 %weight_block.1 = bf16[3072,1728]{1,0:T(8,128)(2,1)} custom-call(s32[1]{0:T(128)} %bitcast.rank_ref, bf16[1024,768]{1,0:T(8,128)(2,1)} %get-tuple-element.117.n1, bf16[1024,768]{1,0:T(8,128)(2,1)} %get-tuple-element.118.dfr, bf16[1024,768]{1,0:T(8,128)(2,1)} %get-tuple-element.119.dar, bf16[1024,3072]{1,0:T(8,128)(2,1)} %get-tuple-element.120.g, ...), custom_call_target="tpu_custom_call" | custom-call | flops 22000001024 | bytes 30000000 | tf_op jit(solution)/shard_map/weight_block/pallas_call | solution.py:731
  246.0 2.4 collective-permute-done.19.do3
  250.0 3.6 collective-permute-start.20
  253.6 42.6 %attend_backward.1 = (bf16[4096,640]{1,0:T(8,128)(2,1)}, f32[1024,768]{1,0:T(8,128)}, bf16[1024,768]{1,0:T(8,128)(2,1)}, bf16[1024,768]{1,0:T(8,128)(2,1)}, bf16[1024,768]{1,0:T(8,128)(2,1)}, /*index=5*/f32[8,640]{1,0:T(8,128)}) custom-call(s32[1536]{0:T(1024)} %xor.71.table, bf16[64,3,64,512]{3,2,1,0:T(8,128)(2,1)} %get-tuple-element.116.p_ref, ...), custom_call_target="tpu_custom_call" | custom-call | flops 40000000000 | bytes 25000000 | tf_op jit(solution)/shard_map/attend_backward/pallas_call | solution.py:358
  299.7 2.9 collective-permute-done.22
  303.3 3.4 add_convert_fusion.1
  310.1 1.8 convert_add_fusion
  312.6 11.5 %head_weight_block.1 = bf16[768,576]{1,0:T(8,128)(2,1)} custom-call(bf16[1024,768]{1,0:T(8,128)(2,1)} %copy-done, bf16[1024,768]{1,0:T(8,128)(2,1)} %copy-done.1, bf16[1024,768]{1,0:T(8,128)(2,1)} %collective-permute-done.10.refs_2_.x2, bf16[1024,768]{1,0:T(8,128)(2,1)} %collective-permute-done.11.refs_3_.x3, bf16[4096,640]{1,0:T(8,128)(2,1)} %get-tuple-element.149.grad_ref), custom_call_target="tpu_custom_call" | custom-call | flops 8000000000 | bytes 12000000 | tf_op jit(solution)/shard_map/head_weight_block/pallas_call | solution.py:424
  324.1 7.4 %reduce-scatter.3.cloned.1.call-done = bf16[4,96,1728]{2,1,0:T(8,128)(2,1)} async-done(((bf16[4,768,1728]{2,1,0:T(8,128)(2,1)}), bf16[4,96,1728]{2,1,0:T(8,128)(2,1)}) %reduce-scatter.3.cloned.1.call-update) | async-done | bytes 1327120 | tf_op jit(solution)/shard_map/reduce_scatter | solution.py:937
  331.5 2.0 constant_dynamic-slice_fusion.3
  333.6 1.2 collective-permute-start.27
  336.2 1.5 collective-permute-start.30
  337.7 3.9 collective-permute-done.27
  341.6 5.2 %collective-permute-done.28 = bf16[192,576]{1,0:T(8,128)(2,1)} collective-permute-done((bf16[192,576]{1,0:T(8,128)(2,1)}, bf16[192,576]{1,0:T(8,128)(2,1)}, u32[]{:S(2)}, u32[]{:S(2)}) %collective-permute-start.28) | collective-permute-done | bytes 221216 | tf_op jit(solution)/shard_map/ppermute | solution.py:841
  347.9 1.5 add_convert_fusion.3
  349.4 3.1 add_convert_fusion
  352.5 4.0 collective-permute-start.32
  356.5 5.3 %collective-permute-start.31 = (bf16[1024,768]{1,0:T(8,128)(2,1)}, bf16[1024,768]{1,0:T(8,128)(2,1)S(1)}, u32[]{:S(2)}, u32[]{:S(2)}) collective-permute-start(bf16[1024,768]{1,0:T(8,128)(2,1)} %add_convert_fusion), channel_id=1, source_target_pairs={{2,4},{3,5},{4,2},{5,3},{10,12},{11,13},{12,10},{13,11},{18,20},{1... | collective-permute-start | bytes 4718600 | tf_op jit(solution)/shard_map/ppermute | solution.py:841
  362.5 1.3 broadcast_select_fusion.1
  365.2 22.6 %collective-permute-start.33 = (bf16[96,576]{1,0:T(8,128)(2,1)S(1)}, bf16[96,576]{1,0:T(8,128)(2,1)S(1)}, u32[]{:S(2)}, u32[]{:S(2)}) collective-permute-start(bf16[96,576]{1,0:T(8,128)(2,1)S(1)} %constant_dynamic-slice_fusion), channel_id=1, source_target_pairs={{0,4},{1,5},{2,6},{3,7},{4,0},{5,1},{6,2},{7,3},{8,12},{9,13},{10,... | collective-permute-start | bytes 331784 | tf_op jit(solution)/shard_map/ppermute | solution.py:841
  388.8 15.0 %collective-permute-done.31 = bf16[1024,768]{1,0:T(8,128)(2,1)S(1)} collective-permute-done((bf16[1024,768]{1,0:T(8,128)(2,1)}, bf16[1024,768]{1,0:T(8,128)(2,1)S(1)}, u32[]{:S(2)}, u32[]{:S(2)}) %collective-permute-start.31) | collective-permute-done | bytes 1572896 | tf_op jit(solution)/shard_map/ppermute | solution.py:841
  404.9 1.3 broadcast_select_fusion
  (186 shorter events, 42.8 us)
Async XLA Ops:
  7.2 47.6 %copy-start.3 = (bf16[1024,768]{1,0:T(8,128)(2,1)S(1)}, bf16[1024,768]{1,0:T(8,128)(2,1)}, u32[]{:S(2)}) copy-start(bf16[1024,768]{1,0:T(8,128)(2,1)} %param.18) | copy-start | bytes 4718596
  7.2 97.9 %all-gather.6.cloned.1.call-start = ((), (), s32[]{:S(2)}) async-start(), calls=%async_computation.5 | async-start | bytes 1720320 | tf_op jit(solution)/shard_map/all_gather | solution.py:874
  7.2 46.4 %collective-permute-start = (bf16[1024,768]{1,0:T(8,128)(2,1)}, bf16[1024,768]{1,0:T(8,128)(2,1)S(1)}, u32[]{:S(2)}, u32[]{:S(2)}) collective-permute-start(bf16[1024,768]{1,0:T(8,128)(2,1)} %param.18), channel_id=1, source_target_pairs={{2,4},{3,5},{4,2},{5,3},{10,12},{11,13},{12,10},{13,11},{18,20},{1... | collective-permute-start | bytes 4718600 | tf_op jit(solution)/shard_map/ppermute | solution.py:841
  13.0 41.8 %collective-permute-start.1 = (bf16[1024,768]{1,0:T(8,128)(2,1)}, bf16[1024,768]{1,0:T(8,128)(2,1)}, u32[]{:S(2)}, u32[]{:S(2)}) collective-permute-start(bf16[1024,768]{1,0:T(8,128)(2,1)} %param.18), channel_id=1, source_target_pairs={{0,1},{1,0},{6,7},{7,6},{8,9},{9,8},{14,15},{15,14},{16,17},{17,16... | collective-permute-start | bytes 4718600 | tf_op jit(solution)/shard_map/ppermute | solution.py:841
  19.0 4.8 %collective-permute-start.2 = (bf16[96,576]{1,0:T(8,128)(2,1)S(1)}, bf16[96,576]{1,0:T(8,128)(2,1)}, u32[]{:S(2)}, u32[]{:S(2)}) collective-permute-start(bf16[96,576]{1,0:T(8,128)(2,1)S(1)} %concatenate.69), channel_id=1, source_target_pairs={{0,4},{1,5},{2,6},{3,7},{4,0},{5,1},{6,2},{7,3},{8,12},{9,13},{10,... | collective-permute-start | bytes 331784 | tf_op jit(solution)/shard_map/ppermute | solution.py:841
  25.6 16.6 %collective-permute-start.3 = (bf16[195,576]{1,0:T(8,128)(2,1)}, bf16[195,576]{1,0:T(8,128)(2,1)}, u32[]{:S(2)}, u32[]{:S(2)}) collective-permute-start(bf16[195,576]{1,0:T(8,128)(2,1)} %pad_maximum_fusion.2), channel_id=1, source_target_pairs={{0,2},{1,3},{6,4},{7,5},{8,10},{9,11},{14,12},{15,13},{16,18},{17,... | collective-permute-start | bytes 673928 | tf_op jit(solution)/shard_map/ppermute | solution.py:841
  26.9 29.5 %copy-start.10 = (f32[768]{0:T(1024)S(1)}, f32[768]{0:T(1024)}, u32[]{:S(2)}) copy-start(f32[768]{0:T(1024)} %param.31) | copy-start | bytes 9220
  56.4 43.2 %copy-start = (bf16[1024,768]{1,0:T(8,128)(2,1)}, bf16[1024,768]{1,0:T(8,128)(2,1)S(1)}, u32[]{:S(2)}) copy-start(bf16[1024,768]{1,0:T(8,128)(2,1)S(1)} %broadcast_select_fusion.4.refs_0_.x_ref.x0) | copy-start | bytes 4718596
  56.4 10.2 %collective-permute-start.7 = (f32[768]{0:T(1024)S(1)}, f32[768]{0:T(1024)S(1)}, u32[]{:S(2)}, u32[]{:S(2)}) collective-permute-start(f32[768]{0:T(1024)S(1)} %copy-done.10), channel_id=1, source_target_pairs={{0,1},{1,0},{2,3},{3,2},{4,5},{5,4},{6,7},{7,6},{8,9},{9,8},{10,11... | collective-permute-start | bytes 9224 | tf_op jit(solution)/shard_map/ppermute | solution.py:841
  57.0 9.6 %collective-permute-start.8 = (f32[768]{0:T(1024)S(1)}, f32[768]{0:T(1024)S(1)}, u32[]{:S(2)}, u32[]{:S(2)}) collective-permute-start(f32[768]{0:T(1024)S(1)} %copy-done.10), channel_id=1, source_target_pairs={{0,2},{1,3},{2,0},{3,1},{4,6},{5,7},{6,4},{7,5},{8,10},{9,11},{10,... | collective-permute-start | bytes 9224 | tf_op jit(solution)/shard_map/ppermute | solution.py:841
  57.0 9.6 %collective-permute-start.9 = (f32[768]{0:T(1024)S(1)}, f32[768]{0:T(1024)S(1)}, u32[]{:S(2)}, u32[]{:S(2)}) collective-permute-start(f32[768]{0:T(1024)S(1)} %copy-done.10), channel_id=1, source_target_pairs={{0,3},{1,2},{2,1},{3,0},{4,7},{5,6},{6,5},{7,4},{8,11},{9,10},{10,... | collective-permute-start | bytes 9224 | tf_op jit(solution)/shard_map/ppermute | solution.py:841
  61.1 36.9 %collective-permute-start.4 = (bf16[1024,768]{1,0:T(8,128)(2,1)S(1)}, bf16[1024,768]{1,0:T(8,128)(2,1)}, u32[]{:S(2)}, u32[]{:S(2)}) collective-permute-start(bf16[1024,768]{1,0:T(8,128)(2,1)S(1)} %broadcast_select_fusion.4.refs_0_.x_ref.x0), channel_id=1, source_target_pairs={{2,3},{3,2},{4,5},{5,4},{10,11},{11,10},{12,13},{13,12},{18,19},{1... | collective-permute-start | bytes 4718600 | tf_op jit(solution)/shard_map/ppermute | solution.py:841
  63.1 7.6 %collective-permute-start.5 = (bf16[192,576]{1,0:T(8,128)(2,1)S(1)}, bf16[192,576]{1,0:T(8,128)(2,1)S(1)}, u32[]{:S(2)}, u32[]{:S(2)}) collective-permute-start(bf16[192,576]{1,0:T(8,128)(2,1)S(1)} %slice.223), channel_id=1, source_target_pairs={{0,8},{1,9},{2,10},{3,11},{4,12},{5,13},{6,14},{7,15},{8,0},{9,1},... | collective-permute-start | bytes 663560 | tf_op jit(solution)/shard_map/ppermute | solution.py:841
  66.4 114.5 %all-gather.4.cloned.1.call-start = ((), (), s32[]{:S(2)}) async-start(), calls=%async_computation.2 | async-start | bytes 12386304 | tf_op jit(solution)/shard_map/all_gather | solution.py:920
  70.9 12.2 %collective-permute-start.6 = (bf16[384,576]{1,0:T(8,128)(2,1)S(1)}, bf16[384,576]{1,0:T(8,128)(2,1)S(1)}, u32[]{:S(2)}, u32[]{:S(2)}) collective-permute-start(bf16[384,576]{1,0:T(8,128)(2,1)S(1)} %maximum_select_fusion.1), channel_id=1, source_target_pairs={{0,16},{1,17},{2,18},{3,19},{4,20},{5,21},{6,22},{7,23},{8,24},{9,... | collective-permute-start | bytes 1327112 | tf_op jit(solution)/shard_map/ppermute | solution.py:841
  99.7 19.1 %copy-start.1 = (bf16[1024,768]{1,0:T(8,128)(2,1)}, bf16[1024,768]{1,0:T(8,128)(2,1)S(1)}, u32[]{:S(2)}) copy-start(bf16[1024,768]{1,0:T(8,128)(2,1)S(1)} %broadcast_select_fusion.3.refs_1_.x1) | copy-start | bytes 4718596
  99.7 5.4 %collective-permute-start.10 = (bf16[1024,768]{1,0:T(8,128)(2,1)S(1)}, bf16[1024,768]{1,0:T(8,128)(2,1)}, u32[]{:S(2)}, u32[]{:S(2)}) collective-permute-start(bf16[1024,768]{1,0:T(8,128)(2,1)S(1)} %broadcast_select_fusion.4.refs_0_.x_ref.x0), channel_id=1, source_target_pairs={{0,4},{1,5},{2,6},{3,7},{4,0},{5,1},{6,2},{7,3},{8,12},{9,13},{10,... | collective-permute-start | bytes 4718600 | tf_op jit(solution)/shard_map/ppermute | solution.py:841
  99.7 5.8 %collective-permute-start.11 = (bf16[1024,768]{1,0:T(8,128)(2,1)S(1)}, bf16[1024,768]{1,0:T(8,128)(2,1)}, u32[]{:S(2)}, u32[]{:S(2)}) collective-permute-start(bf16[1024,768]{1,0:T(8,128)(2,1)S(1)} %broadcast_select_fusion.3.refs_1_.x1), channel_id=1, source_target_pairs={{0,4},{1,5},{2,6},{3,7},{4,0},{5,1},{6,2},{7,3},{8,12},{9,13},{10,... | collective-permute-start | bytes 4718600 | tf_op jit(solution)/shard_map/ppermute | solution.py:841
  105.6 225.9 %reduce-scatter.3.cloned.1.call-start = ((), (), s32[]{:S(2)}) async-start(), calls=%async_computation.3 | async-start | bytes 12386304 | tf_op jit(solution)/shard_map/reduce_scatter | solution.py:937
  105.6 54.2 %collective-permute-start.15 = (bf16[1024,768]{1,0:T(8,128)(2,1)}, bf16[1024,768]{1,0:T(8,128)(2,1)S(1)}, u32[]{:S(2)}, u32[]{:S(2)}) collective-permute-start(bf16[1024,768]{1,0:T(8,128)(2,1)} %param.19), channel_id=1, source_target_pairs={{2,4},{3,5},{4,2},{5,3},{10,12},{11,13},{12,10},{13,11},{18,20},{1... | collective-permute-start | bytes 4718600 | tf_op jit(solution)/shard_map/ppermute | solution.py:841
  118.8 31.2 %copy-start.11 = (f32[768]{0:T(1024)S(1)}, f32[768]{0:T(1024)}, u32[]{:S(2)}) copy-start(f32[768]{0:T(1024)} %param.28) | copy-start | bytes 9220
  118.8 31.2 %copy-start.12 = (f32[768]{0:T(1024)S(1)}, f32[768]{0:T(1024)}, u32[]{:S(2)}) copy-start(f32[768]{0:T(1024)} %param.29) | copy-start | bytes 9220
  118.8 31.2 %copy-start.13 = (f32[768]{0:T(1024)S(1)}, f32[768]{0:T(1024)}, u32[]{:S(2)}) copy-start(f32[768]{0:T(1024)} %param.30) | copy-start | bytes 9220
  118.8 31.2 %copy-start.14 = (f32[768]{0:T(1024)S(1)}, f32[768]{0:T(1024)}, u32[]{:S(2)}) copy-start(f32[768]{0:T(1024)} %param.32) | copy-start | bytes 9220
  118.8 31.2 %copy-start.15 = (f32[768]{0:T(1024)S(1)}, f32[768]{0:T(1024)}, u32[]{:S(2)}) copy-start(f32[768]{0:T(1024)} %param.33) | copy-start | bytes 9220
  118.8 31.3 %copy-start.16 = (f32[768]{0:T(1024)S(1)}, f32[768]{0:T(1024)}, u32[]{:S(2)}) copy-start(f32[768]{0:T(1024)} %param.34) | copy-start | bytes 9220
  146.7 17.7 %collective-permute-start.12 = (bf16[1024,192]{1,0:T(8,128)(2,1)}, bf16[1024,192]{1,0:T(8,128)(2,1)S(1)}, u32[]{:S(2)}, u32[]{:S(2)}) collective-permute-start(bf16[1024,192]{1,0:T(8,128)(2,1)} %get-tuple-element.109.o1), channel_id=1, source_target_pairs={{0,1},{1,0},{2,3},{3,2},{4,5},{5,4},{6,7},{7,6},{8,9},{9,8},{10,11... | collective-permute-start | bytes 1179656 | tf_op jit(solution)/shard_map/ppermute | solution.py:841
  148.9 15.4 %collective-permute-start.13 = (bf16[1024,192]{1,0:T(8,128)(2,1)}, bf16[1024,192]{1,0:T(8,128)(2,1)S(1)}, u32[]{:S(2)}, u32[]{:S(2)}) collective-permute-start(bf16[1024,192]{1,0:T(8,128)(2,1)} %get-tuple-element.110.o2), channel_id=1, source_target_pairs={{0,4},{1,5},{2,6},{3,7},{4,0},{5,1},{6,2},{7,3},{8,12},{9,13},{10,... | collective-permute-start | bytes 1179656 | tf_op jit(solution)/shard_map/ppermute | solution.py:841
  148.9 26.4 %collective-permute-start.14 = (bf16[1024,192]{1,0:T(8,128)(2,1)}, bf16[1024,192]{1,0:T(8,128)(2,1)}, u32[]{:S(2)}, u32[]{:S(2)}) collective-permute-start(bf16[1024,192]{1,0:T(8,128)(2,1)} %get-tuple-element.111.o3), channel_id=1, source_target_pairs={{0,5},{1,4},{2,7},{3,6},{4,1},{5,0},{6,3},{7,2},{8,13},{9,12},{10,... | collective-permute-start | bytes 1179656 | tf_op jit(solution)/shard_map/ppermute | solution.py:841
  222.0 23.9 %collective-permute-start.16 = (f32[7680]{0:T(1024)S(1)}, f32[7680]{0:T(1024)S(1)}, u32[]{:S(2)}, u32[]{:S(2)}) collective-permute-start(f32[7680]{0:T(1024)S(1)} %reduce.1), channel_id=1, source_target_pairs={{0,1},{1,0},{2,3},{3,2},{4,5},{5,4},{6,7},{7,6},{8,9},{9,8},{10,11... | collective-permute-start | bytes 92168 | tf_op jit(solution)/shard_map/ppermute | solution.py:841
  223.3 22.6 %collective-permute-start.17 = (bf16[1024,192]{1,0:T(8,128)(2,1)}, bf16[1024,192]{1,0:T(8,128)(2,1)S(1)}, u32[]{:S(2)}, u32[]{:S(2)}) collective-permute-start(bf16[1024,192]{1,0:T(8,128)(2,1)} %get-tuple-element.124), channel_id=1, source_target_pairs={{0,1},{1,0},{2,3},{3,2},{4,5},{5,4},{6,7},{7,6},{8,9},{9,8},{10,11... | collective-permute-start | bytes 1179656 | tf_op jit(solution)/shard_map/ppermute | solution.py:841
  223.6 22.4 %collective-permute-start.18 = (bf16[1024,192]{1,0:T(8,128)(2,1)}, bf16[1024,192]{1,0:T(8,128)(2,1)S(1)}, u32[]{:S(2)}, u32[]{:S(2)}) collective-permute-start(bf16[1024,192]{1,0:T(8,128)(2,1)} %get-tuple-element.125), channel_id=1, source_target_pairs={{0,4},{1,5},{2,6},{3,7},{4,0},{5,1},{6,2},{7,3},{8,12},{9,13},{10,... | collective-permute-start | bytes 1179656 | tf_op jit(solution)/shard_map/ppermute | solution.py:841
  224.4 24.0 %collective-permute-start.19 = (bf16[1024,192]{1,0:T(8,128)(2,1)}, bf16[1024,192]{1,0:T(8,128)(2,1)S(1)}, u32[]{:S(2)}, u32[]{:S(2)}) collective-permute-start(bf16[1024,192]{1,0:T(8,128)(2,1)} %get-tuple-element.126), channel_id=1, source_target_pairs={{0,5},{1,4},{2,7},{3,6},{4,1},{5,0},{6,3},{7,2},{8,13},{9,12},{10,... | collective-permute-start | bytes 1179656 | tf_op jit(solution)/shard_map/ppermute | solution.py:841
  249.2 138.6 %reduce-scatter.5.cloned.1.call-start = ((), (), s32[]{:S(2)}) async-start(), calls=%async_computation.4 | async-start | bytes 1720320 | tf_op jit(solution)/shard_map/reduce_scatter | solution.py:964
  250.0 46.2 %collective-permute-start.20 = (bf16[1024,768]{1,0:T(8,128)(2,1)S(1)}, bf16[1024,768]{1,0:T(8,128)(2,1)S(1)}, u32[]{:S(2)}, u32[]{:S(2)}) collective-permute-start(bf16[1024,768]{1,0:T(8,128)(2,1)S(1)} %copy-done.5), channel_id=1, source_target_pairs={{2,4},{3,5},{4,2},{5,3},{10,12},{11,13},{12,10},{13,11},{18,20},{1... | collective-permute-start | bytes 4718600 | tf_op jit(solution)/shard_map/ppermute | solution.py:841
  297.4 5.8 %collective-permute-start.21 = (bf16[1024,768]{1,0:T(8,128)(2,1)}, bf16[1024,768]{1,0:T(8,128)(2,1)S(1)}, u32[]{:S(2)}, u32[]{:S(2)}) collective-permute-start(bf16[1024,768]{1,0:T(8,128)(2,1)} %get-tuple-element.139), channel_id=1, source_target_pairs={{0,4},{1,5},{2,6},{3,7},{4,0},{5,1},{6,2},{7,3},{8,12},{9,13},{10,... | collective-permute-start | bytes 4718600 | tf_op jit(solution)/shard_map/ppermute | solution.py:841
  297.4 12.6 %collective-permute-start.24 = (bf16[1024,768]{1,0:T(8,128)(2,1)}, bf16[1024,768]{1,0:T(8,128)(2,1)}, u32[]{:S(2)}, u32[]{:S(2)}) collective-permute-start(bf16[1024,768]{1,0:T(8,128)(2,1)} %get-tuple-element.145), channel_id=1, source_target_pairs={{0,4},{1,5},{2,6},{3,7},{4,0},{5,1},{6,2},{7,3},{8,12},{9,13},{10,... | collective-permute-start | bytes 4718600 | tf_op jit(solution)/shard_map/ppermute | solution.py:841
  298.9 3.7 collective-permute-start.22
  306.7 2.8 collective-permute-start.25
  307.7 41.7 %collective-permute-start.23 = (bf16[1024,768]{1,0:T(8,128)(2,1)}, bf16[1024,768]{1,0:T(8,128)(2,1)}, u32[]{:S(2)}, u32[]{:S(2)}) collective-permute-start(bf16[1024,768]{1,0:T(8,128)(2,1)} %add_convert_fusion.1), channel_id=1, source_target_pairs={{0,1},{1,0},{2,3},{3,2},{4,5},{5,4},{6,7},{7,6},{8,9},{9,8},{10,11... | collective-permute-start | bytes 4718600 | tf_op jit(solution)/shard_map/ppermute | solution.py:841
  309.4 3.2 collective-permute-start.26
  333.6 8.1 %collective-permute-start.27 = (bf16[192,576]{1,0:T(8,128)(2,1)}, bf16[192,576]{1,0:T(8,128)(2,1)}, u32[]{:S(2)}, u32[]{:S(2)}) collective-permute-start(bf16[192,576]{1,0:T(8,128)(2,1)} %get-tuple-element.218), channel_id=1, source_target_pairs={{0,24},{1,25},{2,26},{3,27},{4,28},{5,29},{6,30},{7,31},{8,16},{9,... | collective-permute-start | bytes 663560 | tf_op jit(solution)/shard_map/ppermute | solution.py:841
  334.7 12.1 %collective-permute-start.28 = (bf16[192,576]{1,0:T(8,128)(2,1)}, bf16[192,576]{1,0:T(8,128)(2,1)}, u32[]{:S(2)}, u32[]{:S(2)}) collective-permute-start(bf16[192,576]{1,0:T(8,128)(2,1)} %get-tuple-element.220), channel_id=1, source_target_pairs={{0,8},{1,9},{2,10},{3,11},{4,12},{5,13},{6,14},{7,15},{8,0},{9,1},... | collective-permute-start | bytes 663560 | tf_op jit(solution)/shard_map/ppermute | solution.py:841
  335.8 12.1 %collective-permute-start.29 = (bf16[192,576]{1,0:T(8,128)(2,1)S(1)}, bf16[192,576]{1,0:T(8,128)(2,1)}, u32[]{:S(2)}, u32[]{:S(2)}) collective-permute-start(bf16[192,576]{1,0:T(8,128)(2,1)S(1)} %get-tuple-element.219), channel_id=1, source_target_pairs={{0,16},{1,17},{2,18},{3,19},{4,20},{5,21},{6,22},{7,23},{8,24},{9,... | collective-permute-start | bytes 663560 | tf_op jit(solution)/shard_map/ppermute | solution.py:841
  336.2 13.2 %collective-permute-start.30 = (f32[8064]{0:T(1024)S(1)}, f32[8064]{0:T(1024)S(1)}, u32[]{:S(2)}, u32[]{:S(2)}) collective-permute-start(f32[8064]{0:T(1024)S(1)} %add.167), channel_id=1, source_target_pairs={{0,4},{1,5},{2,6},{3,7},{4,0},{5,1},{6,2},{7,3},{8,12},{9,13},{10,... | collective-permute-start | bytes 96776 | tf_op jit(solution)/shard_map/ppermute | solution.py:841
  352.5 12.6 %collective-permute-start.32 = (bf16[192,576]{1,0:T(8,128)(2,1)S(1)}, bf16[192,576]{1,0:T(8,128)(2,1)S(1)}, u32[]{:S(2)}, u32[]{:S(2)}) collective-permute-start(bf16[192,576]{1,0:T(8,128)(2,1)S(1)} %add_convert_fusion.3), channel_id=1, source_target_pairs={{2,0},{3,1},{4,6},{5,7},{10,8},{11,9},{12,14},{13,15},{18,16},{19,... | collective-permute-start | bytes 663560 | tf_op jit(solution)/shard_map/ppermute | solution.py:841
  356.5 47.3 %collective-permute-start.31 = (bf16[1024,768]{1,0:T(8,128)(2,1)}, bf16[1024,768]{1,0:T(8,128)(2,1)S(1)}, u32[]{:S(2)}, u32[]{:S(2)}) collective-permute-start(bf16[1024,768]{1,0:T(8,128)(2,1)} %add_convert_fusion), channel_id=1, source_target_pairs={{2,4},{3,5},{4,2},{5,3},{10,12},{11,13},{12,10},{13,11},{18,20},{1... | collective-permute-start | bytes 4718600 | tf_op jit(solution)/shard_map/ppermute | solution.py:841
  365.2 23.6 %collective-permute-start.33 = (bf16[96,576]{1,0:T(8,128)(2,1)S(1)}, bf16[96,576]{1,0:T(8,128)(2,1)S(1)}, u32[]{:S(2)}, u32[]{:S(2)}) collective-permute-start(bf16[96,576]{1,0:T(8,128)(2,1)S(1)} %constant_dynamic-slice_fusion), channel_id=1, source_target_pairs={{0,4},{1,5},{2,6},{3,7},{4,0},{5,1},{6,2},{7,3},{8,12},{9,13},{10,... | collective-permute-start | bytes 331784 | tf_op jit(solution)/shard_map/ppermute | solution.py:841
  (12 other events, 85.5 us)
Sparse Core Ops, SparseCore 0:
  66.6 38.4 all-gather.5
  107.0 73.9 all-gather.3
  248.5 82.8 reduce-scatter.2
  333.6 36.5 reduce-scatter.4
